TPU v7x, 32 devices: a whole 2x2x4 slice. The times are simulated.
32 devices in a mesh: tm: 8 (over z, x), col: 4 (over y, core).
Axes of the slice: x: 2, y: 2, z: 4, core: 2. Of those that a mesh axis runs over, the one named last changes fastest.
Arguments:
- blocks: float32 [16, 512, 192], P('tm', 'col'), may hold values from -0.5 to 1.5, as said below
- pattern: int32 [8, 3], replicated, may hold values from 0 to 7, as said below
- drift: float32 [16, 512], P('tm', 'col'), may hold values from -6 to 6
- cov: float32 [16, 512, 512], P('tm', 'col'), may hold values from -0.5 to 2, as said below
- cost: float32 [16, 512, 512], P('tm', 'col'), may hold values from -0.5 to 2, as said below
- eta: float32 [16, 512], P('tm', 'col'), may hold values from -6 to 6
Outputs:
- dyn_out: float32 [16, 512, 512], P('tm', 'col')
- drift_out: float32 [16, 512], P('tm', 'col')
- cov_out: float32 [16, 512, 512], P('tm', 'col')
- cost_out: float32 [16, 512, 512], P('tm', 'col')
- eta_out: float32 [16, 512], P('tm', 'col')
Inputs may be any that keep to these rules, and one draw needn't show every extreme that they name: `pattern`: row r lists r first, then two different block columns other than r. `blocks`: the first block of each row is the diagonal block. `cov`: each group's matrix is symmetric. `cost`: each group's matrix is symmetric.
All inputs are finite; a program needn't handle non-finite values.
Results may differ from a plain program's by a relative error of at most 0.00015.
Values sent between devices are 32-bit elements; how exact they have to be, the bound alone decides.
No kernel may reach another device: no remote copies, remote signals or barrier semaphores. Data moves between devices by JAX's collectives and lax.ppermute only.
A program may use at most 64 MiB of HBM per device.

v0:
```python
import functools

import jax
import jax.numpy as jnp
from jax import lax
from jax.experimental import pallas as pl
from jax.experimental.pallas import tpu as pltpu
from jax.sharding import PartitionSpec as P


HIGH = lax.Precision.HIGHEST
F32 = jnp.float32
BF16 = jnp.bfloat16


def shifted(block, axis, distance):
    devices = range(lax.axis_size(axis))
    route = [(i - distance, i) for i in devices if i - distance in devices]
    return lax.ppermute(block, axis, route)


def product(form, left, right):
    return jnp.einsum(form, left, right, precision=HIGH)


def densify(row_blocks, row_ids, pattern, block_size):
    block_count = pattern.shape[0]
    row_block = row_ids // block_size
    chooser = (row_block[:, None] == jnp.arange(block_count, dtype=jnp.int32)[None, :]).astype(
        jnp.int32
    )
    columns = jnp.sum(chooser[:, :, None] * pattern[None, :, :], axis=1)
    matches = (
        columns[:, :, None] == jnp.arange(block_count, dtype=jnp.int32)[None, None, :]
    ).astype(jnp.float32)
    pieces = row_blocks.reshape(row_blocks.shape[:-1] + (3, 1, block_size))
    filled = jnp.sum(matches[:, :, :, None] * pieces, axis=-3)
    return filled.reshape(row_blocks.shape[:-1] + (block_count * block_size,))


def combine_rows(
    dyn_prev_full,
    dyn_own_full,
    dyn_own,
    drift_prev_full,
    drift_own,
    cov_prev,
    cov_own,
    cost_prev,
    cost_own,
    eta_prev,
    eta_own,
    first_row,
):
    height = dyn_own.shape[1]
    dyn_res = product("tij,tjk->tik", dyn_own, dyn_prev_full)
    drift_res = product("tij,tj->ti", dyn_own, drift_prev_full) + drift_own
    carried = eta_own + product("tij,tj->ti", cost_own, drift_prev_full)
    value_rows = product("tij,tjk->tik", cost_own, dyn_prev_full)
    prev_columns = lax.dynamic_slice_in_dim(dyn_prev_full, first_row, height, 2)
    cov_full, carried_full, value_full = (
        lax.all_gather(cov_prev, "col", axis=1, tiled=True),
        lax.all_gather(carried, "col", axis=1, tiled=True),
        lax.all_gather(value_rows, "col", axis=1, tiled=True),
    )
    cost_res = cost_prev + product("tki,tkj->tij", prev_columns, value_full)
    cov_res = (
        product("tik,tjk->tij", product("tij,tjk->tik", dyn_own, cov_full), dyn_own_full) + cov_own
    )
    eta_res = eta_prev + product("tki,tk->ti", prev_columns, carried_full)
    return (dyn_res, drift_res, cov_res, cost_res, eta_res)


def choose(flag, combined, kept):
    return tuple(jnp.where(flag, new, old) for new, old in zip(combined, kept))


def per_device_general(blocks, pattern, drift, cov, cost, eta):
    height = cov.shape[1]
    modes = cov.shape[2]
    block_size = blocks.shape[2] // 3
    first_row = lax.axis_index("col") * height
    own_ids = first_row + jnp.arange(height, dtype=jnp.int32)
    all_ids = jnp.arange(modes, dtype=jnp.int32)
    position = lax.axis_index("tm")
    dyn_own = densify(blocks, own_ids, pattern, block_size)
    received = shifted((blocks, drift, cov, cost, eta), "tm", 1)
    blocks_prev, blocks_own, drift_prev_full = (
        lax.all_gather(received[0], "col", axis=1, tiled=True),
        lax.all_gather(blocks, "col", axis=1, tiled=True),
        lax.all_gather(received[1], "col", axis=1, tiled=True),
    )
    merged = combine_rows(
        densify(blocks_prev, all_ids, pattern, block_size),
        densify(blocks_own, all_ids, pattern, block_size),
        dyn_own,
        drift_prev_full,
        drift,
        received[2],
        cov,
        received[3],
        cost,
        received[4],
        eta,
        first_row,
    )
    current = choose(position >= 1, merged, (dyn_own, drift, cov, cost, eta))
    received = shifted(current, "tm", 2)
    dyn_prev_full = lax.all_gather(received[0], "col", axis=1, tiled=True)
    dyn_own_full = lax.all_gather(current[0], "col", axis=1, tiled=True)
    drift_prev_full = lax.all_gather(received[1], "col", axis=1, tiled=True)
    merged = combine_rows(
        dyn_prev_full,
        dyn_own_full,
        current[0],
        drift_prev_full,
        current[1],
        received[2],
        current[2],
        received[3],
        current[3],
        received[4],
        current[4],
        first_row,
    )
    return choose(position >= 2, merged, current)


def split(x):
    hi = x.astype(BF16)
    lo = (x - hi.astype(F32)).astype(BF16)
    return hi, lo


def dot(a, b):
    return jnp.dot(a, b, preferred_element_type=F32)


def dot3(ah, al, bh, bl):
    return dot(ah, bh) + (dot(ah, bl) + dot(al, bh))


def triangle(r):
    rows = lax.broadcasted_iota(jnp.int32, (r, r), 0)
    cols = lax.broadcasted_iota(jnp.int32, (r, r), 1)
    return rows, cols


def fold(first, second, r):
    rows, cols = triangle(r)
    return jnp.where(rows >= cols, first, second)


def diagonal(block, r):
    rows, cols = triangle(r)
    return jnp.sum(jnp.where(rows == cols, block, 0.0), axis=0, keepdims=True)


def unfold(folded, second_diag, r):
    rows, cols = triangle(r)
    turned = folded.T
    first = jnp.where(rows >= cols, folded, turned)
    second = jnp.where(rows < cols, folded, turned)
    second = jnp.where(rows == cols, jnp.broadcast_to(second_diag, (r, r)), second)
    return first, second


UPPER = ((0, 1), (0, 2), (0, 3), (1, 2), (1, 3), (2, 3))


def spread(packed, r, put):
    panel0, panel1, diags = packed[0:r], packed[r : 2 * r], packed[2 * r : 2 * r + 1]
    k00, k11 = unfold(panel0[:, 0:r], diags[:, 0:r], r)
    k22, k33 = unfold(panel1[:, 0:r], diags[:, r : 2 * r], r)
    for i, block in enumerate((k00, k11, k22, k33)):
        put(i, i, block)
    for at, (i, j) in enumerate(UPPER):
        panel = panel0 if at < 3 else panel1
        block = panel[:, (at % 3 + 1) * r : (at % 3 + 2) * r]
        put(i, j, block)
        put(j, i, block.T)


def column(row, r):
    rows, cols = triangle(r)
    pieces = []
    for at in range(row.shape[1] // r):
        piece = jnp.broadcast_to(row[:, at * r : (at + 1) * r], (r, r))
        pieces.append(jnp.sum(jnp.where(rows == cols, piece, 0.0), axis=1, keepdims=True))
    return jnp.concatenate(pieces, axis=0)


def row_times(row, matrix, r):
    return jnp.sum(column(row, r) * matrix, axis=0, keepdims=True)


def lanes(index, r):
    return pl.ds(pl.multiple_of(index * r, r), r)


def send_kernel(scal, cov, cost, drift, eta, to_core, to_chip, to_far):
    q, y, c = scal[0], scal[1], scal[2]
    r = cov.shape[1]

    def kind(which, element, col_block):
        at = lanes(col_block, r)
        return jnp.where(which == 0, cov[element, :, at], cost[element, :, at])

    def vectors(element):
        return drift[pl.ds(element, 1), :], eta[pl.ds(element, 1), :]

    b, e = vectors(y)
    for j in range(1, 4):
        to_core[0:r, (j - 1) * r : j * r] = kind(1 - c, y, (q ^ 1) ^ j)
    to_core[r : r + 1, 0:r] = b
    to_core[r : r + 1, r : 2 * r] = e
    b, e = vectors(1 - y)
    for j in range(2, 4):
        to_chip[0:r, (j - 2) * r : (j - 1) * r] = kind(c, 1 - y, (q ^ 2) ^ j)
    to_chip[r : r + 1, 0:r] = b
    to_chip[r : r + 1, r : 2 * r] = e
    to_far[0:r, :] = kind(1 - c, 1 - y, q)
    to_far[r : r + 1, :] = b
    to_far[r + 1 : r + 2, :] = e


def pack_near_kernel(scal, cov, cost, from_core, packed):
    q, y, c = scal[0], scal[1], scal[2]
    r = cov.shape[1]

    def own(j):
        at = lanes(q ^ j, r)
        return jnp.where(c == 0, cov[y, :, at], cost[y, :, at])

    packed[:, 0:r] = fold(own(0), from_core[0:r, 0:r], r)
    for j in range(1, 4):
        packed[:, j * r : (j + 1) * r] = own(j)
    packed[:, 4 * r :] = from_core[0:r, r : 3 * r]


def pack_far_kernel(scal, drift, eta, from_core, from_chip, from_far, packed):
    y = scal[1]
    r = drift.shape[1]
    k33 = from_far[0:r, :]
    packed[0:r, 0:r] = fold(from_chip[0:r, 0:r], k33, r)
    packed[0:r, r:] = from_chip[0:r, r : 2 * r]
    packed[r : r + 1, 0:r] = diagonal(from_core[0:r, 0:r], r)
    packed[r : r + 1, r:] = diagonal(k33, r)
    b = (
        drift[pl.ds(y, 1), :],
        from_core[r : r + 1, 0:r],
        from_chip[r : r + 1, 0:r],
        from_far[r : r + 1, :],
    )
    e = (
        eta[pl.ds(y, 1), :],
        from_core[r : r + 1, r : 2 * r],
        from_chip[r : r + 1, r : 2 * r],
        from_far[r + 1 : r + 2, :],
    )
    for j in range(4):
        at = slice(j % 2 * r, (j % 2 + 1) * r)
        packed[r + 1 + j // 2 : r + 2 + j // 2, at] = b[j]
        packed[r + 3 + j // 2 : r + 4 + j // 2, at] = e[j]
    packed[r + 5 : r + 8, :] = jnp.zeros((3, 2 * r), F32)


def far_row(packed, r, at):
    return jnp.concatenate(
        [packed[r + at : r + at + 1, :], packed[r + at + 1 : r + at + 2, :]], axis=1
    )


def pick_kernel(scal, turned, before, out):
    y = scal[1]
    height = turned.shape[1]
    out[0:height, :] = turned[1 - y]
    out[height:, :] = before[1 - y]


def halves_kernel(scal, turned, before, other, out):
    y = scal[1]
    height = turned.shape[1]
    out[0:height, :] = turned[y]
    out[height : 2 * height, :] = other[0:height, :]
    out[2 * height : 3 * height, :] = before[y]
    out[3 * height :, :] = other[height:, :]


def dense_turned(put, scal, pattern, own_half, core_half, flag, n, r, bs):
    q = scal[0]
    lane = lax.broadcasted_iota(jnp.int32, (bs, r), 1) // bs
    rows = lax.broadcasted_iota(jnp.int32, (bs, r), 0)
    cols = lax.broadcasted_iota(jnp.int32, (bs, r), 1)
    per = r // bs
    height = 3 * bs
    for j in range(4):
        half = own_half if j % 2 == 0 else core_half
        full = half[(j // 2) * height : (j // 2 + 1) * height, :]
        wanted = []
        for k in range(3):
            want = jnp.zeros((bs, r), jnp.int32)
            for h in range(per):
                block = pattern[(q ^ j) * per + h, k] ^ (q * per)
                want = jnp.where(lane == h, block, want)
            wanted.append(jnp.where(flag == 1, want, -1))
        for block in range(n // bs):
            if j * r <= block * bs < (j + 1) * r:
                value = jnp.where(
                    jnp.logical_and(rows + block * bs == cols + j * r, flag == 0), 1.0, 0.0
                )
            else:
                value = jnp.zeros((bs, r), F32)
            for k in range(3):
                piece = full[k * bs : (k + 1) * bs, :]
                value = value + jnp.where(wanted[k] == block, piece, 0.0)
            put(slice(block * bs, (block + 1) * bs), slice(j * r, (j + 1) * r), value)


def put_split(hi_ref, lo_ref, rows, cols, value):
    hi, lo = split(value)
    hi_ref[rows, cols] = hi
    lo_ref[rows, cols] = lo


def transpose_split(hi_ref, lo_ref, source, r):
    n = source.shape[0]
    for i in range(n // r):
        for j in range(n // r):
            put_split(
                hi_ref,
                lo_ref,
                slice(j * r, (j + 1) * r),
                slice(i * r, (i + 1) * r),
                source[i * r : (i + 1) * r, j * r : (j + 1) * r].T,
            )


def straight_split(hi_ref, lo_ref, source, r):
    n = source.shape[0]
    for i in range(n // r):
        put_split(
            hi_ref, lo_ref, slice(i * r, (i + 1) * r), slice(None), source[i * r : (i + 1) * r, :]
        )


def prepare_kernel(
    bs, scal, pattern, halves, core_halves, mh, ml, th, tl, a0h, a0l, a1h, a1l, dense
):
    c, has1 = scal[2], scal[3]
    n = dense.shape[0]
    r = halves.shape[1]
    half = halves.shape[0] // 2
    first = c == 0
    for at, flag, hi, lo in ((0, 1, a0h, a0l), (1, has1, a1h, a1l)):
        rows = slice(at * half, (at + 1) * half)
        mine = first if at == 0 else jnp.logical_not(first)

        def put(row, col, value):
            put_split(hi, lo, row, col, value)
            dense[row, col] = value

        dense_turned(put, scal, pattern, halves[rows, :], core_halves[rows, :], flag, n, r, bs)

        @pl.when(mine)
        def _():
            if at == 0:
                straight_split(mh, ml, dense, r)
                transpose_split(th, tl, dense, r)
            else:
                straight_split(th, tl, dense, r)
                transpose_split(mh, ml, dense, r)


def level1_kernel(
    scal, own_near, own_far, near, far, mh, ml, th, tl, out, full, xh, xl
):
    c = scal[2]
    r = own_near.shape[0]
    first = c == 0
    xn = jnp.where(first, near[...], own_near[...])
    xf = jnp.where(first, far[...], own_far[...])
    x = jnp.concatenate(
        [
            xn[:, 0 : 4 * r],
            jnp.concatenate([xf[0:r, 0:r], xn[:, 4 * r :], xf[0:r, r:]], axis=1),
            jnp.concatenate([xf[r : r + 1, :], xf[r : r + 1, :]], axis=1),
        ],
        axis=0,
    )

    def put(i, j, block):
        full[i * r : (i + 1) * r, j * r : (j + 1) * r] = block
        put_split(xh, xl, slice(i * r, (i + 1) * r), slice(j * r, (j + 1) * r), block)

    spread(x, r, put)
    b_before, b_own = far_row(far, r, 1), far_row(own_far, r, 1)
    e_before, e_own = far_row(far, r, 3), far_row(own_far, r, 3)
    carried = jnp.where(first, b_before, e_own + row_times(b_before, full[...], r))
    vec = jnp.where(first, b_own, e_before) + row_times(
        carried, mh[...].astype(F32) + ml[...].astype(F32), r
    )
    u = dot3(xh[...], xl[...], mh[...], ml[...])
    uh, ul = split(u)
    top = dot3(th[0 : 2 * r, :], tl[0 : 2 * r, :], uh, ul)
    low = dot3(th[2 * r :, :], tl[2 * r :, :], uh[:, 2 * r :], ul[:, 2 * r :])
    dn = jnp.where(first, own_near[...], near[...])
    df = jnp.where(first, own_far[...], far[...])
    z11 = top[r : 2 * r, r : 2 * r]
    z33 = low[r : 2 * r, r : 2 * r]
    out[0:r, 0:r] = fold(top[0:r, 0:r], z11, r) + dn[:, 0:r]
    out[0:r, r:] = top[0:r, r:] + dn[:, r : 4 * r]
    out[r : 2 * r, 0:r] = fold(low[0:r, 0:r], z33, r) + df[0:r, 0:r]
    out[r : 2 * r, r : 3 * r] = top[r : 2 * r, 2 * r :] + dn[:, 4 * r :]
    out[r : 2 * r, 3 * r :] = low[0:r, r : 2 * r] + df[0:r, r:]
    base = 2 * r
    out[base : base + 1, 0:r] = diagonal(z11, r) + df[r : r + 1, 0:r]
    out[base : base + 1, r : 2 * r] = diagonal(z33, r) + df[r : r + 1, r:]
    out[base : base + 1, 2 * r :] = jnp.zeros((1, 2 * r), F32)
    out[base + 1 : base + 2, :] = b_own
    out[base + 2 : base + 3, :] = vec
    out[base + 3 : base + 4, :] = b_before
    out[base + 4 : base + 8, :] = jnp.zeros((4, 4 * r), F32)


def dynamics_kernel(
    bs,
    scal,
    pattern,
    halves,
    core_halves,
    a0h,
    a0l,
    a1h,
    a1l,
    dyn_own,
    dyn_send,
    mh,
    ml,
    th,
    tl,
    a2,
    a2h,
    a2l,
    a3h,
    a3l,
    product_ref,
):
    q, c = scal[0], scal[2]
    n = a0h.shape[0]
    r = halves.shape[1]
    half = halves.shape[0] // 2
    first = c == 0

    def put2(row, col, value):
        put_split(a2h, a2l, row, col, value)
        a2[row, col] = value

    def put3(row, col, value):
        put_split(a3h, a3l, row, col, value)

    for at, flag, put in ((0, scal[4], put2), (1, scal[5], put3)):
        rows = slice(at * half, (at + 1) * half)
        dense_turned(put, scal, pattern, halves[rows, :], core_halves[rows, :], flag, n, r, bs)

    def wanted(ref):
        return jnp.concatenate([ref[:, 0:r], ref[:, 2 * r : 3 * r]], axis=1)

    t = dot3(a1h[...], a1l[...], wanted(a0h), wanted(a0l))
    t = dot3(a2h[...], a2l[...], *split(t))
    t = dot3(a3h[...], a3l[...], *split(t))
    for j in range(4):
        at = lanes(q ^ j, r)
        dyn_own[:, at] = t[j * r : (j + 1) * r, 0:r].T
        dyn_send[:, at] = t[j * r : (j + 1) * r, r : 2 * r].T

    @pl.when(first)
    def _():
        product_ref[...] = dot3(a1h[...], a1l[...], a0h[...], a0l[...])
        straight_split(mh, ml, product_ref, r)
        transpose_split(th, tl, product_ref, r)

    @pl.when(jnp.logical_not(first))
    def _():
        product_ref[...] = dot3(a3h[...], a3l[...], a2h[...], a2l[...])
        straight_split(th, tl, product_ref, r)
        transpose_split(mh, ml, product_ref, r)


def level2_kernel(
    scal, own, earlier, mh, ml, th, tl, a2, keep, to_core, to_chip, to_far, full, xh, xl
):
    q, c = scal[0], scal[2]
    r = own.shape[1] // 4
    first = c == 0
    x = jnp.where(first, earlier[...], own[...])

    def put(i, j, block):
        full[i * r : (i + 1) * r, j * r : (j + 1) * r] = block
        put_split(xh, xl, slice(i * r, (i + 1) * r), slice(j * r, (j + 1) * r), block)

    spread(x, r, put)
    base = 2 * r
    d = jnp.where(first, own[...], earlier[...])
    b1 = earlier[base + 1 : base + 2, :] + row_times(
        earlier[base + 3 : base + 4, :], a2[...], r
    )
    carried = jnp.where(first, b1, own[base + 2 : base + 3, :] + row_times(b1, full[...], r))
    vec = d[base + 2 : base + 3, :] + row_times(
        carried, mh[...].astype(F32) + ml[...].astype(F32), r
    )
    u = dot3(xh[...], xl[...], mh[...], ml[...])
    uh, ul = split(u)

    def keep_d(i, j, block):
        full[i * r : (i + 1) * r, j * r : (j + 1) * r] = block

    spread(d, r, keep_d)
    z = dot3(th[...], tl[...], uh, ul) + full[...]
    for i, ref in enumerate((keep, to_core, to_chip, to_far)):
        for j in range(4):
            ref[0:r, lanes(q ^ j, r)] = z[i * r : (i + 1) * r, j * r : (j + 1) * r]
        ref[r : r + 8, :] = jnp.zeros((8, 4 * r), F32)
        ref[r : r + 1, 0:r] = vec[:, i * r : (i + 1) * r]


def place_kernel(
    scal,
    keep,
    from_core,
    from_chip,
    from_far,
    dyn_own,
    dyn_recv,
    dyn_out,
    drift_out,
    cov_out,
    cost_out,
    eta_out,
):
    y, c = scal[1], scal[2]
    first = c == 0
    r = dyn_own.shape[0]
    dyn_out[y] = dyn_own[...]
    dyn_out[1 - y] = dyn_recv[...]
    pairs = (
        (cov_out, drift_out, keep, from_core, from_chip, from_far),
        (cost_out, eta_out, from_core, keep, from_far, from_chip),
    )
    for matrix, vector, one, two, three, four in pairs:
        matrix[y] = jnp.where(first, one[0:r, :], two[0:r, :])
        matrix[1 - y] = jnp.where(first, three[0:r, :], four[0:r, :])
        at = slice(r, r + 1)
        vector[pl.ds(y, 1), :] = jnp.where(first, one[at, 0:r], two[at, 0:r])
        vector[pl.ds(1 - y, 1), :] = jnp.where(first, three[at, 0:r], four[at, 0:r])


def kernel(body, operands, shapes, scratch=(), scalars=1, near=0, out_near=True):
    operands = [
        pltpu.with_memory_space_constraint(x, pltpu.VMEM) if i >= max(near, scalars) else x
        for i, x in enumerate(operands)
    ]
    if out_near:
        shapes = jax.tree.map(lambda s: pltpu.VMEM(s.shape, s.dtype), shapes)
    smem = pl.BlockSpec(memory_space=pltpu.SMEM)
    vmem = pl.BlockSpec(memory_space=pltpu.VMEM)
    return pl.pallas_call(
        body,
        in_specs=[smem] * scalars + [vmem] * (len(operands) - scalars),
        out_specs=jax.tree.map(lambda _: vmem, shapes),
        out_shape=shapes,
        scratch_shapes=list(scratch),
        compiler_params=pltpu.CompilerParams(vmem_limit_bytes=24 * 2**20),
    )(*operands)


def per_device_split(blocks, pattern, drift, cov, cost, eta):
    elements, r, n = cov.shape
    bs = blocks.shape[2] // 3
    tms, cols = lax.axis_size("tm"), lax.axis_size("col")
    position, q = lax.axis_index("tm"), lax.axis_index("col")

    def swap(value, bit):
        return lax.ppermute(value, "col", [(i, i ^ bit) for i in range(cols)])

    def later(value, distance):
        return lax.ppermute(value, "tm", [(i, i + distance) for i in range(tms - distance)])

    def flag(x):
        return x.astype(jnp.int32)

    scal = jnp.stack(
        [
            q,
            q >> 1,
            q & 1,
            flag(position >= 1),
            flag(position >= 2),
            flag(position >= 3),
        ]
    ).astype(jnp.int32)

    def shape(*dims):
        return jax.ShapeDtypeStruct(dims, F32)

    def half(*dims):
        return jax.ShapeDtypeStruct(dims, BF16)

    def square(dtype):
        return pltpu.VMEM((n, n), dtype)

    turned = jnp.swapaxes(blocks, 1, 2)
    before = later(turned, 1)
    to_core, to_chip, to_far = kernel(
        send_kernel,
        (scal, cov, cost, drift, eta),
        (shape(r + 8, 3 * r), shape(r + 8, 2 * r), shape(r + 8, r)),
        near=5,
    )
    from_core = swap(to_core, 1)
    from_chip = swap(to_chip, 2)
    from_far = swap(to_far, 3)
    own_near = kernel(
        pack_near_kernel, (scal, cov, cost, from_core), shape(r, 6 * r), near=3
    )
    near = later(own_near, 1)
    own_far = kernel(
        pack_far_kernel,
        (scal, drift, eta, from_core, from_chip, from_far),
        shape(r + 8, 2 * r),
        near=3,
    )
    far = later(own_far, 1)
    picked = kernel(pick_kernel, (scal, turned, before), shape(6 * bs, r), near=2)
    other = swap(picked, 2)
    halves = kernel(
        halves_kernel, (scal, turned, before, other), shape(12 * bs, r), near=2
    )
    core_halves = swap(halves, 1)
    far_halves = later(halves, 2)
    factors = kernel(
        functools.partial(prepare_kernel, bs),
        (scal, pattern, halves, core_halves),
        (half(n, n),) * 8,
        [square(F32)],
        scalars=2,
    )
    m1, a01 = factors[:4], factors[4:]
    level1 = kernel(
        level1_kernel,
        (scal, own_near, own_far, near, far) + tuple(m1),
        shape(2 * r + 8, n),
        [square(F32)] + [square(BF16)] * 2,
    )
    earlier = later(level1, 2)
    far_core_halves = swap(far_halves, 1)
    dyn_own, dyn_send, *m2 = kernel(
        functools.partial(dynamics_kernel, bs),
        (scal, pattern, far_halves, far_core_halves) + tuple(a01),
        (shape(r, n), shape(r, n)) + (half(n, n),) * 4 + (shape(n, n),),
        [square(BF16)] * 4 + [square(F32)],
        scalars=2,
    )
    dyn_recv = swap(dyn_send, 2)
    keep, to_core, to_chip, to_far = kernel(
        level2_kernel,
        (scal, level1, earlier) + tuple(m2),
        (shape(r + 8, n),) * 4,
        [square(F32)] + [square(BF16)] * 2,
    )
    from_core = swap(to_core, 1)
    from_chip = swap(to_chip, 2)
    from_far = swap(to_far, 3)
    return kernel(
        place_kernel,
        (scal, keep, from_core, from_chip, from_far, dyn_own, dyn_recv),
        (
            shape(elements, r, n),
            shape(elements, r),
            shape(elements, r, n),
            shape(elements, r, n),
            shape(elements, r),
        ),
        out_near=False,
    )


def takes_split(elements, r, bs, cols):
    return elements == 2 and cols == 4 and r % 128 == 0 and r % bs == 0 and bs % 8 == 0


def per_device(blocks, pattern, drift, cov, cost, eta):
    elements, r, _ = cov.shape
    bs = blocks.shape[2] // 3
    if takes_split(elements, r, bs, lax.axis_size("col")):
        return per_device_split(blocks, pattern, drift, cov, cost, eta)
    return per_device_general(blocks, pattern, drift, cov, cost, eta)


def solution(mesh):
    return jax.shard_map(
        per_device,
        mesh=mesh,
        in_specs=(
            P("tm", "col", None),
            P(),
            P("tm", "col"),
            P("tm", "col", None),
            P("tm", "col", None),
            P("tm", "col"),
        ),
        out_specs=(
            P("tm", "col", None),
            P("tm", "col"),
            P("tm", "col", None),
            P("tm", "col", None),
            P("tm", "col"),
        ),
        check_vma=False,
    )
```

profile of v0, /device:TPU:0, one launch (start us, length us, event | category | flops | bytes accessed | tf_op | source)
XLA Modules:
  0.0 87.6 jit_solution(2960298106977162783)
XLA Ops:
  0.6 4.9 %collective-permute-start.5 = (f32[2,192,128]{2,1,0:T(8,128)}, f32[2,192,128]{2,1,0:T(8,128)S(1)}, u32[]{:S(2)}, u32[]{:S(2)}) collective-permute-start(f32[2,192,128]{2,1,0:T(8,128)} %bitcast.7), channel_id=1, source_target_pairs={{0,4},{4,8},{8,12},{12,16},{16,20},{20,24},{24,28},{1,5},{5,9},{9,... | collective-permute-start | bytes 589832 | tf_op jit(solution)/shard_map/ppermute | solution.py:587
  6.2 1.0 %copy-done = f32[2,128,512]{2,1,0:T(8,128)S(1)} copy-done((f32[2,128,512]{2,1,0:T(8,128)S(1)}, f32[2,128,512]{2,1,0:T(8,128)}, u32[]{:S(2)}) %copy-start) | copy-done | bytes 524312
  7.3 1.0 %copy-done.2 = f32[2,128,512]{2,1,0:T(8,128)S(1)} copy-done((f32[2,128,512]{2,1,0:T(8,128)S(1)}, f32[2,128,512]{2,1,0:T(8,128)}, u32[]{:S(2)}) %copy-start.2) | copy-done | bytes 524312
  8.3 0.6 shard_map.101
  9.0 0.9 %collective-permute-done.5.before = f32[2,192,128]{2,1,0:T(8,128)S(1)} collective-permute-done((f32[2,192,128]{2,1,0:T(8,128)}, f32[2,192,128]{2,1,0:T(8,128)S(1)}, u32[]{:S(2)}, u32[]{:S(2)}) %collective-permute-start.5) | collective-permute-done | bytes 196640 | tf_op jit(solution)/shard_map/ppermute | solution.py:587
  10.6 1.6 %collective-permute-start.6 = (f32[384,128]{1,0:T(8,128)S(1)}, f32[384,128]{1,0:T(8,128)S(1)}, u32[]{:S(2)}, u32[]{:S(2)}) collective-permute-start(f32[384,128]{1,0:T(8,128)S(1)} %shard_map.104), channel_id=1, source_target_pairs={{0,2},{1,3},{2,0},{3,1},{4,6},{5,7},{6,4},{7,5},{8,10},{9,11},{10,... | collective-permute-start | bytes 589832 | tf_op jit(solution)/shard_map/ppermute | solution.py:584
  12.1 4.9 %collective-permute-done.6.other = f32[384,128]{1,0:T(8,128)S(1)} collective-permute-done((f32[384,128]{1,0:T(8,128)S(1)}, f32[384,128]{1,0:T(8,128)S(1)}, u32[]{:S(2)}, u32[]{:S(2)}) %collective-permute-start.6) | collective-permute-done | bytes 196640 | tf_op jit(solution)/shard_map/ppermute | solution.py:584
  18.3 3.7 %collective-permute-start.3 = (f32[128,768]{1,0:T(8,128)S(1)}, f32[128,768]{1,0:T(8,128)S(1)}, u32[]{:S(2)}, u32[]{:S(2)}) collective-permute-start(f32[128,768]{1,0:T(8,128)S(1)} %shard_map.102.own_near), channel_id=1, source_target_pairs={{0,4},{4,8},{8,12},{12,16},{16,20},{20,24},{24,28},{1,5},{5,9},{9,... | collective-permute-start | bytes 1179656 | tf_op jit(solution)/shard_map/ppermute | solution.py:587
  22.0 1.6 %collective-permute-start.1 = (f32[136,256]{1,0:T(8,128)S(1)}, f32[136,256]{1,0:T(8,128)S(1)}, u32[]{:S(2)}, u32[]{:S(2)}) collective-permute-start(f32[136,256]{1,0:T(8,128)S(1)} %get-tuple-element.28), channel_id=1, source_target_pairs={{0,2},{1,3},{2,0},{3,1},{4,6},{5,7},{6,4},{7,5},{8,10},{9,11},{10,... | collective-permute-start | bytes 417800 | tf_op jit(solution)/shard_map/ppermute | solution.py:584
  23.6 3.5 %collective-permute-start.9 = (f32[768,128]{1,0:T(8,128)S(1)}, f32[768,128]{1,0:T(8,128)S(1)}, u32[]{:S(2)}, u32[]{:S(2)}) collective-permute-start(f32[768,128]{1,0:T(8,128)S(1)} %shard_map.105.halves), channel_id=1, source_target_pairs={{0,8},{4,12},{8,16},{12,20},{16,24},{20,28},{1,9},{5,13},{9,17},{1... | collective-permute-start | bytes 1179656 | tf_op jit(solution)/shard_map/ppermute | solution.py:587
  27.2 4.3 %collective-permute-done.2.from_far = f32[136,128]{1,0:T(8,128)S(1)} collective-permute-done((f32[136,128]{1,0:T(8,128)S(1)}, f32[136,128]{1,0:T(8,128)S(1)}, u32[]{:S(2)}, u32[]{:S(2)}) %collective-permute-start.2) | collective-permute-done | bytes 69664 | tf_op jit(solution)/shard_map/ppermute | solution.py:584
  32.1 4.4 %collective-permute-start.4 = (f32[136,256]{1,0:T(8,128)S(1)}, f32[136,256]{1,0:T(8,128)S(1)}, u32[]{:S(2)}, u32[]{:S(2)}) collective-permute-start(f32[136,256]{1,0:T(8,128)S(1)} %shard_map.103.own_far), channel_id=1, source_target_pairs={{0,4},{4,8},{8,12},{12,16},{16,20},{20,24},{24,28},{1,5},{5,9},{9,... | collective-permute-start | bytes 417800 | tf_op jit(solution)/shard_map/ppermute | solution.py:587
  36.5 1.9 %shard_map.106 = (bf16[512,512]{1,0:T(8,128)(2,1)S(1)}, bf16[512,512]{1,0:T(8,128)(2,1)S(1)}, bf16[512,512]{1,0:T(8,128)(2,1)S(1)}, bf16[512,512]{1,0:T(8,128)(2...) custom-call(s32[6]{0:T(128)S(1)} %stack.39.scal, ...), custom_call_target="tpu_custom_call" | custom-call | tf_op jit(solution)/shard_map/pallas_call | solution.py:567
  38.4 1.0 %collective-permute-done.4.far = f32[136,256]{1,0:T(8,128)S(1)} collective-permute-done((f32[136,256]{1,0:T(8,128)S(1)}, f32[136,256]{1,0:T(8,128)S(1)}, u32[]{:S(2)}, u32[]{:S(2)}) %collective-permute-start.4) | collective-permute-done | bytes 139296 | tf_op jit(solution)/shard_map/ppermute | solution.py:587
  39.4 2.4 %shard_map.107.own = f32[264,512]{1,0:T(8,128)S(1)} custom-call(s32[6]{0:T(128)S(1)} %stack.39.scal, f32[128,768]{1,0:T(8,128)S(1)} %shard_map.102.own_near, f32[136,256]{1,0:T(8,128)S(1)} %shard_map.103.own_far, f32[128,768]{1,0:T(8,128)S(1)} %collective-permute-done.3.near, f32[136,256]{1,0:T(8,128)S(1)} %collective-permute-done.4.far, ...), custom_call_target="tpu_custom_call" | custom-call | tf_op jit(solution)/shard_map/pallas_call | solution.py:567
  41.8 9.3 %collective-permute-start.8 = (f32[264,512]{1,0:T(8,128)S(1)}, f32[264,512]{1,0:T(8,128)S(1)}, u32[]{:S(2)}, u32[]{:S(2)}) collective-permute-start(f32[264,512]{1,0:T(8,128)S(1)} %shard_map.107.own), channel_id=1, source_target_pairs={{0,8},{4,12},{8,16},{12,20},{16,24},{20,28},{1,9},{5,13},{9,17},{1... | collective-permute-start | bytes 1622024 | tf_op jit(solution)/shard_map/ppermute | solution.py:587
  51.2 1.7 %collective-permute-done.10.core_halves = f32[768,128]{1,0:T(8,128)S(1)} collective-permute-done((f32[768,128]{1,0:T(8,128)S(1)}, f32[768,128]{1,0:T(8,128)S(1)}, u32[]{:S(2)}, u32[]{:S(2)}) %collective-permute-start.10) | collective-permute-done | bytes 393248 | tf_op jit(solution)/shard_map/ppermute | solution.py:584
  52.9 4.6 %shard_map.108 = (f32[128,512]{1,0:T(8,128)S(1)}, f32[128,512]{1,0:T(8,128)S(1)}, bf16[512,512]{1,0:T(8,128)(2,1)S(1)}, bf16[512,512]{1,0:T(8,128)(2,1)S(1)}, bf...) custom-call(s32[6]{0:T(128)S(1)} %stack.39.scal, s32[8,3]{1,0:T(8,128)S(1)} %copy.11.pattern, ...), custom_call_target="tpu_custom_call" | custom-call | tf_op jit(solution)/shard_map/pallas_call | solution.py:567
  57.5 4.9 %collective-permute-done.8.earlier = f32[264,512]{1,0:T(8,128)S(1)} collective-permute-done((f32[264,512]{1,0:T(8,128)S(1)}, f32[264,512]{1,0:T(8,128)S(1)}, u32[]{:S(2)}, u32[]{:S(2)}) %collective-permute-start.8) | collective-permute-done | bytes 540704 | tf_op jit(solution)/shard_map/ppermute | solution.py:587
  62.4 2.6 %shard_map.109 = (f32[136,512]{1,0:T(8,128)S(1)}, f32[136,512]{1,0:T(8,128)S(1)}, f32[136,512]{1,0:T(8,128)S(1)}, f32[136,512]{1,0:T(8,128)S(1)}) custom-call(s32[6]{0:T(128)S(1)} %stack.39.scal, f32[264,512]{1,0:T(8,128)S(1)} %shard_map.107.own, f32[264,512]{1,0:T(8,128)S(1)} %collective-permute-done.8.earlier, bf16[512,512]{1,0:T(8,128)(2,1)S(1)} %get-tuple-element.38.mh, ...), custom_call_target="tpu_custom_call" | custom-call | tf_op jit(solution)/shard_map/pallas_call | solution.py:567
  65.1 1.6 %collective-permute-start.12 = (f32[136,512]{1,0:T(8,128)S(1)}, f32[136,512]{1,0:T(8,128)S(1)}, u32[]{:S(2)}, u32[]{:S(2)}) collective-permute-start(f32[136,512]{1,0:T(8,128)S(1)} %get-tuple-element.45), channel_id=1, source_target_pairs={{0,2},{1,3},{2,0},{3,1},{4,6},{5,7},{6,4},{7,5},{8,10},{9,11},{10,... | collective-permute-start | bytes 835592 | tf_op jit(solution)/shard_map/ppermute | solution.py:584
  67.0 1.5 %collective-permute-start.14 = (f32[128,512]{1,0:T(8,128)S(1)}, f32[128,512]{1,0:T(8,128)S(1)}, u32[]{:S(2)}, u32[]{:S(2)}) collective-permute-start(f32[128,512]{1,0:T(8,128)S(1)} %get-tuple-element.48), channel_id=1, source_target_pairs={{0,2},{1,3},{2,0},{3,1},{4,6},{5,7},{6,4},{7,5},{8,10},{9,11},{10,... | collective-permute-start | bytes 786440 | tf_op jit(solution)/shard_map/ppermute | solution.py:584
  68.5 17.3 %collective-permute-done.14.dyn_recv = f32[128,512]{1,0:T(8,128)S(1)} collective-permute-done((f32[128,512]{1,0:T(8,128)S(1)}, f32[128,512]{1,0:T(8,128)S(1)}, u32[]{:S(2)}, u32[]{:S(2)}) %collective-permute-start.14) | collective-permute-done | bytes 262176 | tf_op jit(solution)/shard_map/ppermute | solution.py:584
  85.8 1.8 %shard_map.110 = (f32[2,128,512]{2,1,0:T(8,128)}, f32[2,128]{1,0:T(2,128)}, f32[2,128,512]{2,1,0:T(8,128)}, f32[2,128,512]{2,1,0:T(8,128)}, f32[2,128]{1,0:T(2,128)}) custom-call(s32[6]{0:T(128)S(1)} %stack.39.scal, f32[136,512]{1,0:T(8,128)S(1)} %get-tuple-element.43.keep, f32[136,512]{1,0:T(8,128)S(1)} %collective-permute-done.11.from_core, ...), custom_call_target="tpu_custom_call" | custom-call | tf_op jit(solution)/shard_map/pallas_call | solution.py:567
  (34 shorter events, 3.7 us)
Async XLA Ops:
  0.6 9.3 %collective-permute-start.5 = (f32[2,192,128]{2,1,0:T(8,128)}, f32[2,192,128]{2,1,0:T(8,128)S(1)}, u32[]{:S(2)}, u32[]{:S(2)}) collective-permute-start(f32[2,192,128]{2,1,0:T(8,128)} %bitcast.7), channel_id=1, source_target_pairs={{0,4},{4,8},{8,12},{12,16},{16,20},{20,24},{24,28},{1,5},{5,9},{9,... | collective-permute-start | bytes 589832 | tf_op jit(solution)/shard_map/ppermute | solution.py:587
  5.5 0.7 copy-start.5
  5.5 0.7 copy-start.6
  6.2 1.0 %copy-start = (f32[2,128,512]{2,1,0:T(8,128)S(1)}, f32[2,128,512]{2,1,0:T(8,128)}, u32[]{:S(2)}) copy-start(f32[2,128,512]{2,1,0:T(8,128)} %cov.3) | copy-start | bytes 1572868
  7.3 1.0 %copy-start.2 = (f32[2,128,512]{2,1,0:T(8,128)S(1)}, f32[2,128,512]{2,1,0:T(8,128)}, u32[]{:S(2)}) copy-start(f32[2,128,512]{2,1,0:T(8,128)} %cost.3) | copy-start | bytes 1572868
  8.3 1.7 %copy-start.4 = (f32[2,128,192]{1,2,0:T(8,128)S(1)}, f32[2,128,192]{1,2,0:T(8,128)}, u32[]{:S(2)}) copy-start(f32[2,128,192]{1,2,0:T(8,128)} %param.6) | copy-start | bytes 589828
  9.0 8.7 %collective-permute-start = (f32[136,384]{1,0:T(8,128)S(1)}, f32[136,384]{1,0:T(8,128)S(1)}, u32[]{:S(2)}, u32[]{:S(2)}) collective-permute-start(f32[136,384]{1,0:T(8,128)S(1)} %get-tuple-element.27), channel_id=1, source_target_pairs={{0,1},{1,0},{2,3},{3,2},{4,5},{5,4},{6,7},{7,6},{8,9},{9,8},{10,11... | collective-permute-start | bytes 626696 | tf_op jit(solution)/shard_map/ppermute | solution.py:584
  10.0 7.7 %copy-start.3 = (f32[2,128,512]{2,1,0:T(8,128)S(1)}, f32[2,128,512]{2,1,0:T(8,128)}, u32[]{:S(2)}) copy-start(f32[2,128,512]{2,1,0:T(8,128)} %cost.3) | copy-start | bytes 1572868
  10.5 7.1 %copy-start.1 = (f32[2,128,512]{2,1,0:T(8,128)S(1)}, f32[2,128,512]{2,1,0:T(8,128)}, u32[]{:S(2)}) copy-start(f32[2,128,512]{2,1,0:T(8,128)} %cov.3) | copy-start | bytes 1572868
  10.6 6.4 %collective-permute-start.6 = (f32[384,128]{1,0:T(8,128)S(1)}, f32[384,128]{1,0:T(8,128)S(1)}, u32[]{:S(2)}, u32[]{:S(2)}) collective-permute-start(f32[384,128]{1,0:T(8,128)S(1)} %shard_map.104), channel_id=1, source_target_pairs={{0,2},{1,3},{2,0},{3,1},{4,6},{5,7},{6,4},{7,5},{8,10},{9,11},{10,... | collective-permute-start | bytes 589832 | tf_op jit(solution)/shard_map/ppermute | solution.py:584
  17.6 18.9 %collective-permute-start.7 = (f32[768,128]{1,0:T(8,128)S(1)}, f32[768,128]{1,0:T(8,128)S(1)}, u32[]{:S(2)}, u32[]{:S(2)}) collective-permute-start(f32[768,128]{1,0:T(8,128)S(1)} %shard_map.105.halves), channel_id=1, source_target_pairs={{0,1},{1,0},{2,3},{3,2},{4,5},{5,4},{6,7},{7,6},{8,9},{9,8},{10,11... | collective-permute-start | bytes 1179656 | tf_op jit(solution)/shard_map/ppermute | solution.py:584
  18.3 21.1 %collective-permute-start.3 = (f32[128,768]{1,0:T(8,128)S(1)}, f32[128,768]{1,0:T(8,128)S(1)}, u32[]{:S(2)}, u32[]{:S(2)}) collective-permute-start(f32[128,768]{1,0:T(8,128)S(1)} %shard_map.102.own_near), channel_id=1, source_target_pairs={{0,4},{4,8},{8,12},{12,16},{16,20},{20,24},{24,28},{1,5},{5,9},{9,... | collective-permute-start | bytes 1179656 | tf_op jit(solution)/shard_map/ppermute | solution.py:587
  22.0 9.4 %collective-permute-start.1 = (f32[136,256]{1,0:T(8,128)S(1)}, f32[136,256]{1,0:T(8,128)S(1)}, u32[]{:S(2)}, u32[]{:S(2)}) collective-permute-start(f32[136,256]{1,0:T(8,128)S(1)} %get-tuple-element.28), channel_id=1, source_target_pairs={{0,2},{1,3},{2,0},{3,1},{4,6},{5,7},{6,4},{7,5},{8,10},{9,11},{10,... | collective-permute-start | bytes 417800 | tf_op jit(solution)/shard_map/ppermute | solution.py:584
  23.6 27.5 %collective-permute-start.9 = (f32[768,128]{1,0:T(8,128)S(1)}, f32[768,128]{1,0:T(8,128)S(1)}, u32[]{:S(2)}, u32[]{:S(2)}) collective-permute-start(f32[768,128]{1,0:T(8,128)S(1)} %shard_map.105.halves), channel_id=1, source_target_pairs={{0,8},{4,12},{8,16},{12,20},{16,24},{20,28},{1,9},{5,13},{9,17},{1... | collective-permute-start | bytes 1179656 | tf_op jit(solution)/shard_map/ppermute | solution.py:587
  27.1 9.3 %copy-start.7 = (s32[8,3]{0,1:T(4,128)S(1)}, s32[8,3]{0,1:T(4,128)}, u32[]{:S(2)}) copy-start(s32[8,3]{0,1:T(4,128)} %param.7) | copy-start | bytes 292
  27.1 4.4 %collective-permute-start.2 = (f32[136,128]{1,0:T(8,128)S(1)}, f32[136,128]{1,0:T(8,128)S(1)}, u32[]{:S(2)}, u32[]{:S(2)}) collective-permute-start(f32[136,128]{1,0:T(8,128)S(1)} %get-tuple-element.29), channel_id=1, source_target_pairs={{0,3},{1,2},{2,1},{3,0},{4,7},{5,6},{6,5},{7,4},{8,11},{9,10},{10,... | collective-permute-start | bytes 208904 | tf_op jit(solution)/shard_map/ppermute | solution.py:584
  32.1 7.4 %collective-permute-start.4 = (f32[136,256]{1,0:T(8,128)S(1)}, f32[136,256]{1,0:T(8,128)S(1)}, u32[]{:S(2)}, u32[]{:S(2)}) collective-permute-start(f32[136,256]{1,0:T(8,128)S(1)} %shard_map.103.own_far), channel_id=1, source_target_pairs={{0,4},{4,8},{8,12},{12,16},{16,20},{20,24},{24,28},{1,5},{5,9},{9,... | collective-permute-start | bytes 417800 | tf_op jit(solution)/shard_map/ppermute | solution.py:587
  41.8 20.6 %collective-permute-start.8 = (f32[264,512]{1,0:T(8,128)S(1)}, f32[264,512]{1,0:T(8,128)S(1)}, u32[]{:S(2)}, u32[]{:S(2)}) collective-permute-start(f32[264,512]{1,0:T(8,128)S(1)} %shard_map.107.own), channel_id=1, source_target_pairs={{0,8},{4,12},{8,16},{12,20},{16,24},{20,28},{1,9},{5,13},{9,17},{1... | collective-permute-start | bytes 1622024 | tf_op jit(solution)/shard_map/ppermute | solution.py:587
  51.1 1.8 %collective-permute-start.10 = (f32[768,128]{1,0:T(8,128)S(1)}, f32[768,128]{1,0:T(8,128)S(1)}, u32[]{:S(2)}, u32[]{:S(2)}) collective-permute-start(f32[768,128]{1,0:T(8,128)S(1)} %collective-permute-done.9.halves), channel_id=1, source_target_pairs={{0,1},{1,0},{2,3},{3,2},{4,5},{5,4},{6,7},{7,6},{8,9},{9,8},{10,11... | collective-permute-start | bytes 1179656 | tf_op jit(solution)/shard_map/ppermute | solution.py:584
  65.1 20.7 %collective-permute-start.11 = (f32[136,512]{1,0:T(8,128)S(1)}, f32[136,512]{1,0:T(8,128)S(1)}, u32[]{:S(2)}, u32[]{:S(2)}) collective-permute-start(f32[136,512]{1,0:T(8,128)S(1)} %get-tuple-element.44), channel_id=1, source_target_pairs={{0,1},{1,0},{2,3},{3,2},{4,5},{5,4},{6,7},{7,6},{8,9},{9,8},{10,11... | collective-permute-start | bytes 835592 | tf_op jit(solution)/shard_map/ppermute | solution.py:584
  65.1 20.7 %collective-permute-start.12 = (f32[136,512]{1,0:T(8,128)S(1)}, f32[136,512]{1,0:T(8,128)S(1)}, u32[]{:S(2)}, u32[]{:S(2)}) collective-permute-start(f32[136,512]{1,0:T(8,128)S(1)} %get-tuple-element.45), channel_id=1, source_target_pairs={{0,2},{1,3},{2,0},{3,1},{4,6},{5,7},{6,4},{7,5},{8,10},{9,11},{10,... | collective-permute-start | bytes 835592 | tf_op jit(solution)/shard_map/ppermute | solution.py:584
  66.7 19.1 %collective-permute-start.13 = (f32[136,512]{1,0:T(8,128)S(1)}, f32[136,512]{1,0:T(8,128)S(1)}, u32[]{:S(2)}, u32[]{:S(2)}) collective-permute-start(f32[136,512]{1,0:T(8,128)S(1)} %get-tuple-element.46), channel_id=1, source_target_pairs={{0,3},{1,2},{2,1},{3,0},{4,7},{5,6},{6,5},{7,4},{8,11},{9,10},{10,... | collective-permute-start | bytes 835592 | tf_op jit(solution)/shard_map/ppermute | solution.py:584
  67.0 18.8 %collective-permute-start.14 = (f32[128,512]{1,0:T(8,128)S(1)}, f32[128,512]{1,0:T(8,128)S(1)}, u32[]{:S(2)}, u32[]{:S(2)}) collective-permute-start(f32[128,512]{1,0:T(8,128)S(1)} %get-tuple-element.48), channel_id=1, source_target_pairs={{0,2},{1,3},{2,0},{3,1},{4,6},{5,7},{6,4},{7,5},{8,10},{9,11},{10,... | collective-permute-start | bytes 786440 | tf_op jit(solution)/shard_map/ppermute | solution.py:584
where the time goes:
time: 87.9 us; the launch traced here: 87.6 us
  waiting for transfers between devices  35 us (40%)
  starting transfers between devices  32.6 us (37%)
  Pallas kernels  16.3 us (19%)
  local copies, waits for them, and re-layouts  2.86 us (3%)
    ppermute x10, waiting for transfers between devices, swap(): return lax.ppermute(value, 'col', [(i, i ^ bit) for i in range(cols)])  28.1 us
    ppermute x5, starting transfers between devices, later(): lax.ppermute(value, 'tm', [(i, i + distance) for i in range(tms - distanc...  25.7 us
    pallas_call x10, Pallas kernels, kernel(): pl.pallas_call(body, in_specs=[smem] * scalars + [vmem] * (len(operands)...  16.3 us
    ppermute x10, starting transfers between devices, swap(): return lax.ppermute(value, 'col', [(i, i ^ bit) for i in range(cols)])  6.89 us
    ppermute x5, waiting for transfers between devices, later(): lax.ppermute(value, 'tm', [(i, i + distance) for i in range(tms - distanc...  6.84 us
    unnamed x17, local copies, waits for them, and re-layouts  2.78 us
  transfers between devices with their start and end apart: 15, of which 7 were waited for; matrix products, arithmetic and copies ran while one was open for 0% of the time, Pallas kernels for 13%

commit v1 on v0

--- a/solution.py
+++ b/solution.py
@@ -168,17 +168,21 @@
 UPPER = ((0, 1), (0, 2), (0, 3), (1, 2), (1, 3), (2, 3))
 
 
-def spread(packed, r, put):
+def spread(packed, r, put, rows=(0, 1, 2, 3)):
     panel0, panel1, diags = packed[0:r], packed[r : 2 * r], packed[2 * r : 2 * r + 1]
-    k00, k11 = unfold(panel0[:, 0:r], diags[:, 0:r], r)
-    k22, k33 = unfold(panel1[:, 0:r], diags[:, r : 2 * r], r)
-    for i, block in enumerate((k00, k11, k22, k33)):
-        put(i, i, block)
+    for at, (panel, pair) in enumerate(((panel0, (0, 1)), (panel1, (2, 3)))):
+        if pair[0] in rows or pair[1] in rows:
+            blocks = unfold(panel[:, 0:r], diags[:, at * r : (at + 1) * r], r)
+            for i, block in zip(pair, blocks):
+                if i in rows:
+                    put(i, i, block)
     for at, (i, j) in enumerate(UPPER):
         panel = panel0 if at < 3 else panel1
         block = panel[:, (at % 3 + 1) * r : (at % 3 + 2) * r]
-        put(i, j, block)
-        put(j, i, block.T)
+        if i in rows:
+            put(i, j, block)
+        if j in rows:
+            put(j, i, block.T)
 
 
 def column(row, r):
@@ -198,62 +202,83 @@
     return pl.ds(pl.multiple_of(index * r, r), r)
 
 
-def send_kernel(scal, cov, cost, drift, eta, to_core, to_chip, to_far):
+def copy_all(pairs, sems):
+    copies = [
+        pltpu.make_async_copy(source, target, sems.at[i]) for i, (source, target) in enumerate(pairs)
+    ]
+    for copy in copies:
+        copy.start()
+    for copy in copies:
+        copy.wait()
+
+
+def send_kernel(
+    scal, cov, cost, drift, eta, to_core, to_chip, to_far, panel, vecs, b_in, e_in, sems
+):
     q, y, c = scal[0], scal[1], scal[2]
-    r = cov.shape[1]
-
-    def kind(which, element, col_block):
-        at = lanes(col_block, r)
-        return jnp.where(which == 0, cov[element, :, at], cost[element, :, at])
-
-    def vectors(element):
-        return drift[pl.ds(element, 1), :], eta[pl.ds(element, 1), :]
-
-    b, e = vectors(y)
-    for j in range(1, 4):
-        to_core[0:r, (j - 1) * r : j * r] = kind(1 - c, y, (q ^ 1) ^ j)
+    r = to_far.shape[1]
+
+    def load(mine, theirs):
+        pairs = []
+        for j in range(2, 4):
+            source = mine.at[1 - y, :, lanes((q ^ 2) ^ j, r)]
+            pairs.append((source, to_chip.at[pl.ds(0, r), pl.ds((j - 2) * r, r)]))
+        pairs.append((theirs.at[1 - y, :, lanes(q, r)], to_far.at[pl.ds(0, r), :]))
+        for j in range(1, 4):
+            source = theirs.at[y, :, lanes((q ^ 1) ^ j, r)]
+            pairs.append((source, to_core.at[pl.ds(0, r), pl.ds((j - 1) * r, r)]))
+        for j in range(4):
+            pairs.append((mine.at[y, :, lanes(q ^ j, r)], panel.at[:, pl.ds(j * r, r)]))
+        pairs.append((drift, b_in))
+        pairs.append((eta, e_in))
+        copy_all(pairs, sems)
+
+    @pl.when(c == 0)
+    def _():
+        load(cov, cost)
+
+    @pl.when(c == 1)
+    def _():
+        load(cost, cov)
+
+    b, e = b_in[pl.ds(y, 1), :], e_in[pl.ds(y, 1), :]
+    vecs[...] = jnp.zeros(vecs.shape, F32)
+    vecs[0:1, :] = b
+    vecs[1:2, :] = e
+    to_core[r : r + 8, :] = jnp.zeros((8, 3 * r), F32)
     to_core[r : r + 1, 0:r] = b
     to_core[r : r + 1, r : 2 * r] = e
-    b, e = vectors(1 - y)
-    for j in range(2, 4):
-        to_chip[0:r, (j - 2) * r : (j - 1) * r] = kind(c, 1 - y, (q ^ 2) ^ j)
+    b, e = b_in[pl.ds(1 - y, 1), :], e_in[pl.ds(1 - y, 1), :]
+    to_chip[r : r + 8, :] = jnp.zeros((8, 2 * r), F32)
     to_chip[r : r + 1, 0:r] = b
     to_chip[r : r + 1, r : 2 * r] = e
-    to_far[0:r, :] = kind(1 - c, 1 - y, q)
+    to_far[r : r + 8, :] = jnp.zeros((8, r), F32)
     to_far[r : r + 1, :] = b
     to_far[r + 1 : r + 2, :] = e
 
 
-def pack_near_kernel(scal, cov, cost, from_core, packed):
-    q, y, c = scal[0], scal[1], scal[2]
-    r = cov.shape[1]
-
-    def own(j):
-        at = lanes(q ^ j, r)
-        return jnp.where(c == 0, cov[y, :, at], cost[y, :, at])
-
-    packed[:, 0:r] = fold(own(0), from_core[0:r, 0:r], r)
-    for j in range(1, 4):
-        packed[:, j * r : (j + 1) * r] = own(j)
+def pack_near_kernel(panel, from_core, packed):
+    r = panel.shape[0]
+    packed[:, 0:r] = fold(panel[:, 0:r], from_core[0:r, 0:r], r)
+    packed[:, r : 4 * r] = panel[:, r:]
     packed[:, 4 * r :] = from_core[0:r, r : 3 * r]
 
 
-def pack_far_kernel(scal, drift, eta, from_core, from_chip, from_far, packed):
-    y = scal[1]
-    r = drift.shape[1]
+def pack_far_kernel(vecs, from_core, from_chip, from_far, packed):
+    r = vecs.shape[1]
     k33 = from_far[0:r, :]
     packed[0:r, 0:r] = fold(from_chip[0:r, 0:r], k33, r)
     packed[0:r, r:] = from_chip[0:r, r : 2 * r]
     packed[r : r + 1, 0:r] = diagonal(from_core[0:r, 0:r], r)
     packed[r : r + 1, r:] = diagonal(k33, r)
     b = (
-        drift[pl.ds(y, 1), :],
+        vecs[0:1, :],
         from_core[r : r + 1, 0:r],
         from_chip[r : r + 1, 0:r],
         from_far[r : r + 1, :],
     )
     e = (
-        eta[pl.ds(y, 1), :],
+        vecs[1:2, :],
         from_core[r : r + 1, r : 2 * r],
         from_chip[r : r + 1, r : 2 * r],
         from_far[r + 1 : r + 2, :],
@@ -344,32 +369,30 @@
         )
 
 
-def prepare_kernel(
-    bs, scal, pattern, halves, core_halves, mh, ml, th, tl, a0h, a0l, a1h, a1l, dense
-):
+def prepare_kernel(bs, scal, pattern, halves, core_halves, mh, ml, th, tl, dense):
     c, has1 = scal[2], scal[3]
     n = dense.shape[0]
     r = halves.shape[1]
     half = halves.shape[0] // 2
     first = c == 0
-    for at, flag, hi, lo in ((0, 1, a0h, a0l), (1, has1, a1h, a1l)):
-        rows = slice(at * half, (at + 1) * half)
-        mine = first if at == 0 else jnp.logical_not(first)
-
-        def put(row, col, value):
-            put_split(hi, lo, row, col, value)
-            dense[row, col] = value
-
-        dense_turned(put, scal, pattern, halves[rows, :], core_halves[rows, :], flag, n, r, bs)
-
-        @pl.when(mine)
-        def _():
-            if at == 0:
-                straight_split(mh, ml, dense, r)
-                transpose_split(th, tl, dense, r)
-            else:
-                straight_split(th, tl, dense, r)
-                transpose_split(mh, ml, dense, r)
+    own_half = jnp.where(first, halves[0:half, :], halves[half:, :])
+    core_half = jnp.where(first, core_halves[0:half, :], core_halves[half:, :])
+    flag = jnp.where(first, 1, has1)
+
+    def put(row, col, value):
+        dense[row, col] = value
+
+    dense_turned(put, scal, pattern, own_half, core_half, flag, n, r, bs)
+
+    @pl.when(first)
+    def _():
+        straight_split(mh, ml, dense, r)
+        transpose_split(th, tl, dense, r)
+
+    @pl.when(jnp.logical_not(first))
+    def _():
+        straight_split(th, tl, dense, r)
+        transpose_split(mh, ml, dense, r)
 
 
 def level1_kernel(
@@ -423,6 +446,21 @@
     out[base + 4 : base + 8, :] = jnp.zeros((4, 4 * r), F32)
 
 
+def early_kernel(bs, scal, pattern, halves, core_halves, a0h, a0l, a1h, a1l, t):
+    n = a0h.shape[0]
+    r = halves.shape[1]
+    half = halves.shape[0] // 2
+    for at, flag, hi, lo in ((0, 1, a0h, a0l), (1, scal[3], a1h, a1l)):
+        rows = slice(at * half, (at + 1) * half)
+        put = functools.partial(put_split, hi, lo)
+        dense_turned(put, scal, pattern, halves[rows, :], core_halves[rows, :], flag, n, r, bs)
+
+    def wanted(ref):
+        return jnp.concatenate([ref[:, 0:r], ref[:, 2 * r : 3 * r]], axis=1)
+
+    t[...] = dot3(a1h[...], a1l[...], wanted(a0h), wanted(a0l))
+
+
 def dynamics_kernel(
     bs,
     scal,
@@ -433,6 +471,7 @@
     a0l,
     a1h,
     a1l,
+    t,
     dyn_own,
     dyn_send,
     mh,
@@ -462,17 +501,12 @@
     for at, flag, put in ((0, scal[4], put2), (1, scal[5], put3)):
         rows = slice(at * half, (at + 1) * half)
         dense_turned(put, scal, pattern, halves[rows, :], core_halves[rows, :], flag, n, r, bs)
-
-    def wanted(ref):
-        return jnp.concatenate([ref[:, 0:r], ref[:, 2 * r : 3 * r]], axis=1)
-
-    t = dot3(a1h[...], a1l[...], wanted(a0h), wanted(a0l))
-    t = dot3(a2h[...], a2l[...], *split(t))
-    t = dot3(a3h[...], a3l[...], *split(t))
+    rows = dot3(a2h[...], a2l[...], *split(t[...]))
+    rows = dot3(a3h[...], a3l[...], *split(rows))
     for j in range(4):
         at = lanes(q ^ j, r)
-        dyn_own[:, at] = t[j * r : (j + 1) * r, 0:r].T
-        dyn_send[:, at] = t[j * r : (j + 1) * r, r : 2 * r].T
+        dyn_own[:, at] = rows[j * r : (j + 1) * r, 0:r].T
+        dyn_send[:, at] = rows[j * r : (j + 1) * r, r : 2 * r].T
 
     @pl.when(first)
     def _():
@@ -487,91 +521,200 @@
         transpose_split(mh, ml, product_ref, r)
 
 
+def ahead_kernel(scal, own, mh, ml, th, tl, full, z, xh, xl):
+    r = own.shape[1] // 4
+
+    def put(i, j, block):
+        full[i * r : (i + 1) * r, j * r : (j + 1) * r] = block
+
+    spread(own, r, put)
+
+    @pl.when(scal[2] == 1)
+    def _():
+        straight_split(xh, xl, full, r)
+        u = dot3(xh[...], xl[...], mh[...], ml[...])
+        z[...] = dot3(th[...], tl[...], *split(u))
+
+
+def put_rows(ref, value, q, r):
+    for j in range(4):
+        ref[lanes(q ^ j, r), :] = value[:, j * r : (j + 1) * r]
+
+
 def level2_kernel(
-    scal, own, earlier, mh, ml, th, tl, a2, keep, to_core, to_chip, to_far, full, xh, xl
+    scal,
+    own,
+    earlier,
+    mh,
+    ml,
+    th,
+    tl,
+    a2,
+    full,
+    z,
+    to_chip,
+    to_far,
+    uh,
+    ul,
+    vec,
+    xh,
+    xl,
+    rest,
 ):
     q, c = scal[0], scal[2]
     r = own.shape[1] // 4
-    first = c == 0
-    x = jnp.where(first, earlier[...], own[...])
-
-    def put(i, j, block):
-        full[i * r : (i + 1) * r, j * r : (j + 1) * r] = block
-        put_split(xh, xl, slice(i * r, (i + 1) * r), slice(j * r, (j + 1) * r), block)
-
-    spread(x, r, put)
+    n = 4 * r
     base = 2 * r
-    d = jnp.where(first, own[...], earlier[...])
-    b1 = earlier[base + 1 : base + 2, :] + row_times(
-        earlier[base + 3 : base + 4, :], a2[...], r
-    )
-    carried = jnp.where(first, b1, own[base + 2 : base + 3, :] + row_times(b1, full[...], r))
-    vec = d[base + 2 : base + 3, :] + row_times(
-        carried, mh[...].astype(F32) + ml[...].astype(F32), r
-    )
-    u = dot3(xh[...], xl[...], mh[...], ml[...])
-    uh, ul = split(u)
-
-    def keep_d(i, j, block):
-        full[i * r : (i + 1) * r, j * r : (j + 1) * r] = block
-
-    spread(d, r, keep_d)
-    z = dot3(th[...], tl[...], uh, ul) + full[...]
-    for i, ref in enumerate((keep, to_core, to_chip, to_far)):
-        for j in range(4):
-            ref[0:r, lanes(q ^ j, r)] = z[i * r : (i + 1) * r, j * r : (j + 1) * r]
-        ref[r : r + 8, :] = jnp.zeros((8, 4 * r), F32)
-        ref[r : r + 1, 0:r] = vec[:, i * r : (i + 1) * r]
+    b1 = earlier[base + 1 : base + 2, :] + row_times(earlier[base + 3 : base + 4, :], a2[...], r)
+
+    @pl.when(c == 0)
+    def _():
+        def put(i, j, block):
+            put_split(xh, xl, slice(i * r, (i + 1) * r), slice(j * r, (j + 1) * r), block)
+
+        spread(earlier, r, put)
+        hi, lo = split(dot3(xh[...], xl[...], mh[...], ml[...]))
+        uh[...] = hi
+        ul[...] = lo
+        rest[...] = dot3(th[2 * r :, :], tl[2 * r :, :], hi, lo) + full[2 * r :, :]
+        vec[0:1, :] = b1
+        vec[1:2, :] = own[base + 2 : base + 3, :]
+
+    @pl.when(c == 1)
+    def _():
+        def put(i, j, block):
+            rows = slice((i - 2) * r, (i - 1) * r)
+            cols = slice(j * r, (j + 1) * r)
+            rest[rows, cols] = z[i * r : (i + 1) * r, cols] + block
+
+        spread(earlier, r, put, rows=(2, 3))
+        vec[0:1, :] = own[base + 2 : base + 3, :] + row_times(b1, full[...], r)
+        vec[1:2, :] = earlier[base + 2 : base + 3, :]
+
+    out = vec[1:2, :] + row_times(vec[0:1, :], mh[...].astype(F32) + ml[...].astype(F32), r)
+    vec[0:1, :] = out
+    for i, ref in ((2, to_chip), (3, to_far)):
+        put_rows(ref, rest[(i - 2) * r : (i - 1) * r, :], q, r)
+        ref[n : n + 8, :] = jnp.broadcast_to(out[:, i * r : (i + 1) * r], (8, r))
+
+
+def rest_kernel(scal, earlier, th, tl, full, z, uh, ul, vec, keep, to_core, rest):
+    q, c = scal[0], scal[2]
+    r = earlier.shape[1] // 4
+    n = 4 * r
+
+    @pl.when(c == 0)
+    def _():
+        rest[...] = dot3(th[0 : 2 * r, :], tl[0 : 2 * r, :], uh[...], ul[...]) + full[0 : 2 * r, :]
+
+    @pl.when(c == 1)
+    def _():
+        def put(i, j, block):
+            rows = slice(i * r, (i + 1) * r)
+            cols = slice(j * r, (j + 1) * r)
+            rest[rows, cols] = z[rows, cols] + block
+
+        spread(earlier, r, put, rows=(0, 1))
+
+    for i, ref in ((0, keep), (1, to_core)):
+        put_rows(ref, rest[i * r : (i + 1) * r, :], q, r)
+        ref[n : n + 8, :] = jnp.broadcast_to(vec[0:1, i * r : (i + 1) * r], (8, r))
+
+
+def panel_copies(panel, target, element, r):
+    return [
+        (panel.at[pl.ds(g * r, r), :], target.at[element, :, pl.ds(g * r, r)]) for g in range(4)
+    ]
+
+
+def fill_kernel(scal, keep, from_core, dyn_own, dyn_recv, dyn_out, cov_out, cost_out, sems):
+    y, c = scal[1], scal[2]
+    r = dyn_own.shape[0]
+    dyn = [(dyn_own, dyn_out.at[y]), (dyn_recv, dyn_out.at[1 - y])]
+
+    @pl.when(c == 0)
+    def _():
+        copy_all(
+            dyn + panel_copies(keep, cov_out, y, r) + panel_copies(from_core, cost_out, y, r), sems
+        )
+
+    @pl.when(c == 1)
+    def _():
+        copy_all(
+            dyn + panel_copies(from_core, cov_out, y, r) + panel_copies(keep, cost_out, y, r), sems
+        )
 
 
 def place_kernel(
     scal,
+    cov_in,
+    cost_in,
     keep,
     from_core,
     from_chip,
     from_far,
-    dyn_own,
-    dyn_recv,
-    dyn_out,
-    drift_out,
     cov_out,
     cost_out,
+    drift_out,
     eta_out,
+    sems,
 ):
+    del cov_in, cost_in
     y, c = scal[1], scal[2]
     first = c == 0
-    r = dyn_own.shape[0]
-    dyn_out[y] = dyn_own[...]
-    dyn_out[1 - y] = dyn_recv[...]
-    pairs = (
-        (cov_out, drift_out, keep, from_core, from_chip, from_far),
-        (cost_out, eta_out, from_core, keep, from_far, from_chip),
-    )
-    for matrix, vector, one, two, three, four in pairs:
-        matrix[y] = jnp.where(first, one[0:r, :], two[0:r, :])
-        matrix[1 - y] = jnp.where(first, three[0:r, :], four[0:r, :])
-        at = slice(r, r + 1)
-        vector[pl.ds(y, 1), :] = jnp.where(first, one[at, 0:r], two[at, 0:r])
-        vector[pl.ds(1 - y, 1), :] = jnp.where(first, three[at, 0:r], four[at, 0:r])
-
-
-def kernel(body, operands, shapes, scratch=(), scalars=1, near=0, out_near=True):
-    operands = [
-        pltpu.with_memory_space_constraint(x, pltpu.VMEM) if i >= max(near, scalars) else x
-        for i, x in enumerate(operands)
-    ]
-    if out_near:
-        shapes = jax.tree.map(lambda s: pltpu.VMEM(s.shape, s.dtype), shapes)
-    smem = pl.BlockSpec(memory_space=pltpu.SMEM)
-    vmem = pl.BlockSpec(memory_space=pltpu.VMEM)
-    return pl.pallas_call(
+    r = keep.shape[1]
+
+    @pl.when(c == 0)
+    def _():
+        copy_all(
+            panel_copies(from_chip, cov_out, 1 - y, r) + panel_copies(from_far, cost_out, 1 - y, r),
+            sems,
+        )
+
+    @pl.when(c == 1)
+    def _():
+        copy_all(
+            panel_copies(from_far, cov_out, 1 - y, r) + panel_copies(from_chip, cost_out, 1 - y, r),
+            sems,
+        )
+
+    at = slice(4 * r, 4 * r + 1)
+    for vector, one, two, three, four in (
+        (drift_out, keep, from_core, from_chip, from_far),
+        (eta_out, from_core, keep, from_far, from_chip),
+    ):
+        vector[pl.ds(y, 1), :] = jnp.where(first, one[at, :], two[at, :])
+        vector[pl.ds(1 - y, 1), :] = jnp.where(first, three[at, :], four[at, :])
+
+
+IN_SMEM, IN_HBM, IN_VMEM, IN_OUT = 0, 1, 2, 3
+
+
+def kernel(body, operands, shapes, scratch=(), aliases=None):
+    specs = {
+        IN_SMEM: pl.BlockSpec(memory_space=pltpu.SMEM),
+        IN_HBM: pl.BlockSpec(memory_space=pltpu.HBM),
+        IN_VMEM: pl.BlockSpec(memory_space=pltpu.VMEM),
+        IN_OUT: pl.BlockSpec(memory_space=pltpu.VMEM),
+    }
+    call = pl.pallas_call(
         body,
-        in_specs=[smem] * scalars + [vmem] * (len(operands) - scalars),
-        out_specs=jax.tree.map(lambda _: vmem, shapes),
-        out_shape=shapes,
+        in_specs=[specs[where] for where, _ in operands],
+        out_specs=[specs[where] for where, _ in shapes],
+        out_shape=[
+            pltpu.VMEM(s.shape, s.dtype) if where == IN_VMEM else s for where, s in shapes
+        ],
         scratch_shapes=list(scratch),
-        compiler_params=pltpu.CompilerParams(vmem_limit_bytes=24 * 2**20),
-    )(*operands)
+        input_output_aliases=aliases or {},
+        compiler_params=pltpu.CompilerParams(vmem_limit_bytes=20 * 2**20),
+    )
+    kept = {IN_HBM: pltpu.HBM, IN_VMEM: pltpu.VMEM}
+    return call(
+        *(
+            pltpu.with_memory_space_constraint(x, kept[where]) if where in kept else x
+            for where, x in operands
+        )
+    )
 
 
 def per_device_split(blocks, pattern, drift, cov, cost, eta):
@@ -600,6 +743,15 @@
         ]
     ).astype(jnp.int32)
 
+    def smem(*arrays):
+        return [(IN_SMEM, x) for x in arrays]
+
+    def hbm(*arrays):
+        return [(IN_HBM, x) for x in arrays]
+
+    def vmem(*arrays):
+        return [(IN_VMEM, x) for x in arrays]
+
     def shape(*dims):
         return jax.ShapeDtypeStruct(dims, F32)
 
@@ -609,80 +761,97 @@
     def square(dtype):
         return pltpu.VMEM((n, n), dtype)
 
+    def sems(count):
+        return pltpu.SemaphoreType.DMA((count,))
+
     turned = jnp.swapaxes(blocks, 1, 2)
     before = later(turned, 1)
-    to_core, to_chip, to_far = kernel(
+    to_core, to_chip, to_far, panel, vecs = kernel(
         send_kernel,
-        (scal, cov, cost, drift, eta),
-        (shape(r + 8, 3 * r), shape(r + 8, 2 * r), shape(r + 8, r)),
-        near=5,
+        smem(scal) + hbm(cov, cost, drift, eta),
+        vmem(shape(r + 8, 3 * r), shape(r + 8, 2 * r), shape(r + 8, r), shape(r, n), shape(8, r)),
+        [pltpu.VMEM(drift.shape, F32), pltpu.VMEM(eta.shape, F32), sems(12)],
     )
     from_core = swap(to_core, 1)
     from_chip = swap(to_chip, 2)
     from_far = swap(to_far, 3)
-    own_near = kernel(
-        pack_near_kernel, (scal, cov, cost, from_core), shape(r, 6 * r), near=3
-    )
+    (own_near,) = kernel(pack_near_kernel, vmem(panel, from_core), vmem(shape(r, 6 * r)))
     near = later(own_near, 1)
-    own_far = kernel(
-        pack_far_kernel,
-        (scal, drift, eta, from_core, from_chip, from_far),
-        shape(r + 8, 2 * r),
-        near=3,
+    (own_far,) = kernel(
+        pack_far_kernel, vmem(vecs, from_core, from_chip, from_far), vmem(shape(r + 8, 2 * r))
     )
     far = later(own_far, 1)
-    picked = kernel(pick_kernel, (scal, turned, before), shape(6 * bs, r), near=2)
+    (picked,) = kernel(pick_kernel, smem(scal) + vmem(turned, before), vmem(shape(6 * bs, r)))
     other = swap(picked, 2)
-    halves = kernel(
-        halves_kernel, (scal, turned, before, other), shape(12 * bs, r), near=2
+    (halves,) = kernel(
+        halves_kernel, smem(scal) + vmem(turned, before, other), vmem(shape(12 * bs, r))
     )
     core_halves = swap(halves, 1)
     far_halves = later(halves, 2)
-    factors = kernel(
+    m1 = kernel(
         functools.partial(prepare_kernel, bs),
-        (scal, pattern, halves, core_halves),
-        (half(n, n),) * 8,
+        smem(scal, pattern) + vmem(halves, core_halves),
+        vmem(*[half(n, n)] * 4),
         [square(F32)],
-        scalars=2,
-    )
-    m1, a01 = factors[:4], factors[4:]
-    level1 = kernel(
+    )
+    (level1,) = kernel(
         level1_kernel,
-        (scal, own_near, own_far, near, far) + tuple(m1),
-        shape(2 * r + 8, n),
+        smem(scal) + vmem(own_near, own_far, near, far, *m1),
+        vmem(shape(2 * r + 8, n)),
         [square(F32)] + [square(BF16)] * 2,
     )
     earlier = later(level1, 2)
+    a01 = kernel(
+        functools.partial(early_kernel, bs),
+        smem(scal, pattern) + vmem(halves, core_halves),
+        vmem(*[half(n, n)] * 4, shape(n, 2 * r)),
+    )
     far_core_halves = swap(far_halves, 1)
-    dyn_own, dyn_send, *m2 = kernel(
+    dyn_own, dyn_send, *m2, a2 = kernel(
         functools.partial(dynamics_kernel, bs),
-        (scal, pattern, far_halves, far_core_halves) + tuple(a01),
-        (shape(r, n), shape(r, n)) + (half(n, n),) * 4 + (shape(n, n),),
+        smem(scal, pattern) + vmem(far_halves, far_core_halves, *a01),
+        vmem(shape(r, n), shape(r, n), *[half(n, n)] * 4, shape(n, n)),
         [square(BF16)] * 4 + [square(F32)],
-        scalars=2,
     )
     dyn_recv = swap(dyn_send, 2)
-    keep, to_core, to_chip, to_far = kernel(
+    full, z = kernel(
+        ahead_kernel,
+        smem(scal) + vmem(level1, *m2),
+        vmem(shape(n, n), shape(n, n)),
+        [square(BF16)] * 2,
+    )
+    to_chip, to_far, *u, vec = kernel(
         level2_kernel,
-        (scal, level1, earlier) + tuple(m2),
-        (shape(r + 8, n),) * 4,
-        [square(F32)] + [square(BF16)] * 2,
-    )
-    from_core = swap(to_core, 1)
+        smem(scal) + vmem(level1, earlier, *m2, a2, full, z),
+        vmem(shape(n + 8, r), shape(n + 8, r), half(n, n), half(n, n), shape(8, n)),
+        [square(BF16)] * 2 + [pltpu.VMEM((2 * r, n), F32)],
+    )
     from_chip = swap(to_chip, 2)
     from_far = swap(to_far, 3)
-    return kernel(
+    keep, to_core = kernel(
+        rest_kernel,
+        smem(scal) + vmem(earlier, *m2[2:], full, z, *u, vec),
+        vmem(shape(n + 8, r), shape(n + 8, r)),
+        [pltpu.VMEM((2 * r, n), F32)],
+    )
+    from_core = swap(to_core, 1)
+    whole = shape(elements, r, n)
+    dyn_out, cov_out, cost_out = kernel(
+        fill_kernel,
+        smem(scal) + vmem(keep, from_core, dyn_own, dyn_recv),
+        hbm(whole, whole, whole),
+        [sems(10)],
+    )
+    cov_out, cost_out, drift_out, eta_out = kernel(
         place_kernel,
-        (scal, keep, from_core, from_chip, from_far, dyn_own, dyn_recv),
-        (
-            shape(elements, r, n),
-            shape(elements, r),
-            shape(elements, r, n),
-            shape(elements, r, n),
-            shape(elements, r),
-        ),
-        out_near=False,
-    )
+        smem(scal)
+        + hbm(cov_out, cost_out)
+        + vmem(keep, from_core, from_chip, from_far),
+        hbm(whole, whole) + [(IN_OUT, shape(elements, r))] * 2,
+        [sems(8)],
+        {1: 0, 2: 1},
+    )
+    return dyn_out, drift_out, cov_out, cost_out, eta_out
 
 
 def takes_split(elements, r, bs, cols):

time: 87.9 us -> 89.7 us (1.020)
  Pallas kernels: 16.3 us -> 20.8 us
  local copies, waits for them, and re-layouts: 2.86 us -> 0.17 us
  waiting for transfers between devices: 35 us -> 33.8 us
  starting transfers between devices: 32.6 us -> 33.8 us
    pallas_call x10 -> x14, Pallas kernels: 16.3 us -> 20.8 us  [kernel(): call(*(pltpu.with_memory_space_constraint(x, kept[where]) if where in kep...]
    ppermute x10, waiting for transfers between devices: 28.1 us -> 25.3 us  [swap(): return lax.ppermute(value, 'col', [(i, i ^ bit) for i in range(cols)])]
    unnamed x17 -> x5, local copies, waits for them, and re-layouts: 2.78 us -> 0.09 us
    ppermute x5, waiting for transfers between devices: 6.84 us -> 8.47 us  [later(): lax.ppermute(value, 'tm', [(i, i + distance) for i in range(tms - distanc...]
    ppermute x5, starting transfers between devices: 25.7 us -> 26.9 us  [later(): lax.ppermute(value, 'tm', [(i, i + distance) for i in range(tms - distanc...]
  transfers between devices with their start and end apart: 15 -> 15, of which waited for: 7 -> 6; matrix products, arithmetic and copies ran while one was open for 0% -> 0% of each run, Pallas kernels for 13% -> 17%
where the time goes in v1:
time: 89.7 us; the launch traced here: 89.4 us
  starting transfers between devices  33.8 us (38%)
  waiting for transfers between devices  33.8 us (38%)
  Pallas kernels  20.8 us (23%)
    ppermute x5, starting transfers between devices, later(): lax.ppermute(value, 'tm', [(i, i + distance) for i in range(tms - distanc...  26.9 us
    ppermute x10, waiting for transfers between devices, swap(): return lax.ppermute(value, 'col', [(i, i ^ bit) for i in range(cols)])  25.3 us
    pallas_call x14, Pallas kernels, kernel(): call(*(pltpu.with_memory_space_constraint(x, kept[where]) if where in kep...  20.8 us
    ppermute x5, waiting for transfers between devices, later(): lax.ppermute(value, 'tm', [(i, i + distance) for i in range(tms - distanc...  8.47 us
    ppermute x10, starting transfers between devices, swap(): return lax.ppermute(value, 'col', [(i, i ^ bit) for i in range(cols)])  6.89 us
  transfers between devices with their start and end apart: 15, of which 6 were waited for; matrix products, arithmetic and copies ran while one was open for 0% of the time, Pallas kernels for 17%

profile of v1, /device:TPU:0, one launch (start us, length us, event | category | flops | bytes accessed | tf_op | source)
XLA Modules:
  0.0 89.4 jit_solution(2079465711498111368)
XLA Ops:
  0.6 4.9 %collective-permute-start.5 = (f32[2,192,128]{2,1,0:T(8,128)}, f32[2,192,128]{2,1,0:T(8,128)S(1)}, u32[]{:S(2)}, u32[]{:S(2)}) collective-permute-start(f32[2,192,128]{2,1,0:T(8,128)} %bitcast.7), channel_id=1, source_target_pairs={{0,4},{4,8},{8,12},{12,16},{16,20},{20,24},{24,28},{1,5},{5,9},{9,... | collective-permute-start | bytes 589832 | tf_op jit(solution)/shard_map/ppermute | solution.py:730
  5.6 1.8 %shard_map.101 = (f32[136,384]{1,0:T(8,128)S(1)}, f32[136,256]{1,0:T(8,128)S(1)}, f32[136,128]{1,0:T(8,128)S(1)}, f32[128,512]{1,0:T(8,128)S(1)}, f32[8,128]{1,0:T(8,128)S(1)}) custom-call(s32[6]{0:T(128)S(1)} %stack.39.scal, f32[2,128,512]{2,1,0:T(8,128)} %cov.1, f32[2,128,512]{2,1,0:T(8,128)} %cost.1, f32[2,128]{1,0:T(2,128)} %drift.1, f32[2,128]{1,0:T(2,128)} %eta.1), custom_call_target="tpu_custom_call" | custom-call | tf_op jit(solution)/shard_map/pallas_call | solution.py:712
  7.5 2.5 %collective-permute-done.5.before = f32[2,192,128]{2,1,0:T(8,128)S(1)} collective-permute-done((f32[2,192,128]{2,1,0:T(8,128)}, f32[2,192,128]{2,1,0:T(8,128)S(1)}, u32[]{:S(2)}, u32[]{:S(2)}) %collective-permute-start.5) | collective-permute-done | bytes 196640 | tf_op jit(solution)/shard_map/ppermute | solution.py:730
  10.5 1.6 %collective-permute-start.6 = (f32[384,128]{1,0:T(8,128)S(1)}, f32[384,128]{1,0:T(8,128)S(1)}, u32[]{:S(2)}, u32[]{:S(2)}) collective-permute-start(f32[384,128]{1,0:T(8,128)S(1)} %shard_map.104), channel_id=1, source_target_pairs={{0,2},{1,3},{2,0},{3,1},{4,6},{5,7},{6,4},{7,5},{8,10},{9,11},{10,... | collective-permute-start | bytes 589832 | tf_op jit(solution)/shard_map/ppermute | solution.py:727
  12.1 4.3 %collective-permute-done.6.other = f32[384,128]{1,0:T(8,128)S(1)} collective-permute-done((f32[384,128]{1,0:T(8,128)S(1)}, f32[384,128]{1,0:T(8,128)S(1)}, u32[]{:S(2)}, u32[]{:S(2)}) %collective-permute-start.6) | collective-permute-done | bytes 196640 | tf_op jit(solution)/shard_map/ppermute | solution.py:727
  17.1 4.3 %collective-permute-start.3 = (f32[128,768]{1,0:T(8,128)S(1)}, f32[128,768]{1,0:T(8,128)S(1)}, u32[]{:S(2)}, u32[]{:S(2)}) collective-permute-start(f32[128,768]{1,0:T(8,128)S(1)} %shard_map.102.own_near), channel_id=1, source_target_pairs={{0,4},{4,8},{8,12},{12,16},{16,20},{20,24},{24,28},{1,5},{5,9},{9,... | collective-permute-start | bytes 1179656 | tf_op jit(solution)/shard_map/ppermute | solution.py:730
  21.4 1.6 %collective-permute-start.1 = (f32[136,256]{1,0:T(8,128)S(1)}, f32[136,256]{1,0:T(8,128)S(1)}, u32[]{:S(2)}, u32[]{:S(2)}) collective-permute-start(f32[136,256]{1,0:T(8,128)S(1)} %get-tuple-element.45), channel_id=1, source_target_pairs={{0,2},{1,3},{2,0},{3,1},{4,6},{5,7},{6,4},{7,5},{8,10},{9,11},{10,... | collective-permute-start | bytes 417800 | tf_op jit(solution)/shard_map/ppermute | solution.py:727
  23.0 3.5 %collective-permute-start.9 = (f32[768,128]{1,0:T(8,128)S(1)}, f32[768,128]{1,0:T(8,128)S(1)}, u32[]{:S(2)}, u32[]{:S(2)}) collective-permute-start(f32[768,128]{1,0:T(8,128)S(1)} %shard_map.105.halves), channel_id=1, source_target_pairs={{0,8},{4,12},{8,16},{12,20},{16,24},{20,28},{1,9},{5,13},{9,17},{1... | collective-permute-start | bytes 1179656 | tf_op jit(solution)/shard_map/ppermute | solution.py:730
  26.6 4.3 %collective-permute-done.2.from_far = f32[136,128]{1,0:T(8,128)S(1)} collective-permute-done((f32[136,128]{1,0:T(8,128)S(1)}, f32[136,128]{1,0:T(8,128)S(1)}, u32[]{:S(2)}, u32[]{:S(2)}) %collective-permute-start.2) | collective-permute-done | bytes 69664 | tf_op jit(solution)/shard_map/ppermute | solution.py:727
  30.9 4.4 %collective-permute-start.4 = (f32[136,256]{1,0:T(8,128)S(1)}, f32[136,256]{1,0:T(8,128)S(1)}, u32[]{:S(2)}, u32[]{:S(2)}) collective-permute-start(f32[136,256]{1,0:T(8,128)S(1)} %shard_map.103.own_far), channel_id=1, source_target_pairs={{0,4},{4,8},{8,12},{12,16},{16,20},{20,24},{24,28},{1,5},{5,9},{9,... | collective-permute-start | bytes 417800 | tf_op jit(solution)/shard_map/ppermute | solution.py:730
  35.3 1.4 %shard_map.106 = (bf16[512,512]{1,0:T(8,128)(2,1)S(1)}, bf16[512,512]{1,0:T(8,128)(2,1)S(1)}, bf16[512,512]{1,0:T(8,128)(2,1)S(1)}, bf16[512,512]{1,0:T(8,128)(2,1)S(1)}) custom-call(s32[6]{0:T(128)S(1)} %stack.39.scal, s32[8,3]{1,0:T(8,128)S(1)} %copy.13.pattern, f32[768,128]{1,0:T(8,128)S(1)} %shard_map.105.halves, ...), custom_call_target="tpu_custom_call" | custom-call | tf_op jit(solution)/shard_map/pallas_call | solution.py:712
  36.7 1.5 %collective-permute-done.4.far = f32[136,256]{1,0:T(8,128)S(1)} collective-permute-done((f32[136,256]{1,0:T(8,128)S(1)}, f32[136,256]{1,0:T(8,128)S(1)}, u32[]{:S(2)}, u32[]{:S(2)}) %collective-permute-start.4) | collective-permute-done | bytes 139296 | tf_op jit(solution)/shard_map/ppermute | solution.py:730
  38.3 2.4 %shard_map.107.own = f32[264,512]{1,0:T(8,128)S(1)} custom-call(s32[6]{0:T(128)S(1)} %stack.39.scal, f32[128,768]{1,0:T(8,128)S(1)} %shard_map.102.own_near, f32[136,256]{1,0:T(8,128)S(1)} %shard_map.103.own_far, f32[128,768]{1,0:T(8,128)S(1)} %collective-permute-done.3.near, f32[136,256]{1,0:T(8,128)S(1)} %collective-permute-done.4.far, ...), custom_call_target="tpu_custom_call" | custom-call | tf_op jit(solution)/shard_map/pallas_call | solution.py:712
  40.7 9.8 %collective-permute-start.8 = (f32[264,512]{1,0:T(8,128)S(1)}, f32[264,512]{1,0:T(8,128)S(1)}, u32[]{:S(2)}, u32[]{:S(2)}) collective-permute-start(f32[264,512]{1,0:T(8,128)S(1)} %shard_map.107.own), channel_id=1, source_target_pairs={{0,8},{4,12},{8,16},{12,20},{16,24},{20,28},{1,9},{5,13},{9,17},{1... | collective-permute-start | bytes 1622024 | tf_op jit(solution)/shard_map/ppermute | solution.py:730
  50.6 1.9 %shard_map.108 = (bf16[512,512]{1,0:T(8,128)(2,1)S(1)}, bf16[512,512]{1,0:T(8,128)(2,1)S(1)}, bf16[512,512]{1,0:T(8,128)(2,1)S(1)}, bf16[512,512]{1,0:T(8,128)(2,1)S(1)}, f32[512,256]{1,0:T(8,128)S(1)}) custom-call(s32[6]{0:T(128)S(1)} %stack.39.scal, s32[8,3]{1,0:T(8,128)S(1)} %copy.13.pattern, f32[768,128]{1,0:T(8,128)S(1)} %shard_map.105.halves, ...), custom_call_target="tpu_custom_call" | custom-call | tf_op jit(solution)/shard_map/pallas_call | solution.py:712
  52.5 4.1 %shard_map.109 = (f32[128,512]{1,0:T(8,128)S(1)}, f32[128,512]{1,0:T(8,128)S(1)}, bf16[512,512]{1,0:T(8,128)(2,1)S(1)}, bf16[512,512]{1,0:T(8,128)(2,1)S(1)}, bf...) custom-call(s32[6]{0:T(128)S(1)} %stack.39.scal, s32[8,3]{1,0:T(8,128)S(1)} %copy.13.pattern, ...), custom_call_target="tpu_custom_call" | custom-call | tf_op jit(solution)/shard_map/pallas_call | solution.py:712
  57.3 4.5 %collective-permute-done.8.earlier = f32[264,512]{1,0:T(8,128)S(1)} collective-permute-done((f32[264,512]{1,0:T(8,128)S(1)}, f32[264,512]{1,0:T(8,128)S(1)}, u32[]{:S(2)}, u32[]{:S(2)}) %collective-permute-start.8) | collective-permute-done | bytes 540704 | tf_op jit(solution)/shard_map/ppermute | solution.py:730
  61.8 2.7 %shard_map.111 = (f32[520,128]{1,0:T(8,128)S(1)}, f32[520,128]{1,0:T(8,128)S(1)}, bf16[512,512]{1,0:T(8,128)(2,1)S(1)}, bf16[512,512]{1,0:T(8,128)(2,1)S(1)}, f32[8,512]{1,0:T(8,128)S(1)}) custom-call(s32[6]{0:T(128)S(1)} %stack.39.scal, f32[264,512]{1,0:T(8,128)S(1)} %shard_map.107.own, f32[264,512]{1,0:T(8,128)S(1)} %collective-permute-done.8.earlier, ...), custom_call_target="tpu_custom_call" | custom-call | tf_op jit(solution)/shard_map/pallas_call | solution.py:712
  64.5 1.2 %shard_map.112 = (f32[520,128]{1,0:T(8,128)S(1)}, f32[520,128]{1,0:T(8,128)S(1)}) custom-call(s32[6]{0:T(128)S(1)} %stack.39.scal, f32[264,512]{1,0:T(8,128)S(1)} %collective-permute-done.8.earlier, bf16[512,512]{1,0:T(8,128)(2,1)S(1)} %get-tuple-element.56.th, bf16[512,512]{1,0:T(8,128)(2,1)S(1)} %get-tuple-element.57.tl, ...), custom_call_target="tpu_custom_call" | custom-call | tf_op jit(solution)/shard_map/pallas_call | solution.py:712
  65.7 1.6 %collective-permute-start.13 = (f32[520,128]{1,0:T(8,128)S(1)}, f32[520,128]{1,0:T(8,128)S(1)}, u32[]{:S(2)}, u32[]{:S(2)}) collective-permute-start(f32[520,128]{1,0:T(8,128)S(1)} %get-tuple-element.73), channel_id=1, source_target_pairs={{0,2},{1,3},{2,0},{3,1},{4,6},{5,7},{6,4},{7,5},{8,10},{9,11},{10,... | collective-permute-start | bytes 798728 | tf_op jit(solution)/shard_map/ppermute | solution.py:727
  67.6 1.5 %collective-permute-start.12 = (f32[128,512]{1,0:T(8,128)S(1)}, f32[128,512]{1,0:T(8,128)S(1)}, u32[]{:S(2)}, u32[]{:S(2)}) collective-permute-start(f32[128,512]{1,0:T(8,128)S(1)} %get-tuple-element.69), channel_id=1, source_target_pairs={{0,2},{1,3},{2,0},{3,1},{4,6},{5,7},{6,4},{7,5},{8,10},{9,11},{10,... | collective-permute-start | bytes 786440 | tf_op jit(solution)/shard_map/ppermute | solution.py:727
  69.1 16.8 %collective-permute-done.12.dyn_recv = f32[128,512]{1,0:T(8,128)S(1)} collective-permute-done((f32[128,512]{1,0:T(8,128)S(1)}, f32[128,512]{1,0:T(8,128)S(1)}, u32[]{:S(2)}, u32[]{:S(2)}) %collective-permute-start.12) | collective-permute-done | bytes 262176 | tf_op jit(solution)/shard_map/ppermute | solution.py:727
  85.9 1.6 %shard_map.113 = (f32[2,128,512]{2,1,0:T(8,128)}, f32[2,128,512]{2,1,0:T(8,128)}, f32[2,128,512]{2,1,0:T(8,128)}) custom-call(s32[6]{0:T(128)S(1)} %stack.39.scal, f32[520,128]{1,0:T(8,128)S(1)} %get-tuple-element.66.keep, f32[520,128]{1,0:T(8,128)S(1)} %collective-permute-done.11.from_core, f32[128,512]{1,0:T(8,128)S(1)} %get-tuple-element.68.dyn_own, ...), custom_call_target="tpu_custom_call" | custom-call | tf_op jit(solution)/shard_map/pallas_call | solution.py:712
  87.5 2.0 %shard_map.114 = (f32[2,128,512]{2,1,0:T(8,128)}, f32[2,128,512]{2,1,0:T(8,128)}, f32[2,128]{1,0:T(2,128)}, f32[2,128]{1,0:T(2,128)}) custom-call(s32[6]{0:T(128)S(1)} %stack.39.scal, f32[2,128,512]{2,1,0:T(8,128)} %get-tuple-element.71.cov_in, f32[2,128,512]{2,1,0:T(8,128)} %get-tuple-element.72.cost_in, ...), custom_call_target="tpu_custom_call", output_to_operand_aliasing={{0}: (1, {}), {1}: (2, {})} | custom-call | tf_op jit(solution)/shard_map/pallas_call | solution.py:712
  (26 shorter events, 2.7 us)
Async XLA Ops:
  0.6 9.3 %collective-permute-start.5 = (f32[2,192,128]{2,1,0:T(8,128)}, f32[2,192,128]{2,1,0:T(8,128)S(1)}, u32[]{:S(2)}, u32[]{:S(2)}) collective-permute-start(f32[2,192,128]{2,1,0:T(8,128)} %bitcast.7), channel_id=1, source_target_pairs={{0,4},{4,8},{8,12},{12,16},{16,20},{20,24},{24,28},{1,5},{5,9},{9,... | collective-permute-start | bytes 589832 | tf_op jit(solution)/shard_map/ppermute | solution.py:730
  5.6 4.4 %copy-start = (f32[2,128,192]{1,2,0:T(8,128)S(1)}, f32[2,128,192]{1,2,0:T(8,128)}, u32[]{:S(2)}) copy-start(f32[2,128,192]{1,2,0:T(8,128)} %param.6) | copy-start | bytes 589828
  7.4 9.6 %collective-permute-start = (f32[136,384]{1,0:T(8,128)S(1)}, f32[136,384]{1,0:T(8,128)S(1)}, u32[]{:S(2)}, u32[]{:S(2)}) collective-permute-start(f32[136,384]{1,0:T(8,128)S(1)} %get-tuple-element.43), channel_id=1, source_target_pairs={{0,1},{1,0},{2,3},{3,2},{4,5},{5,4},{6,7},{7,6},{8,9},{9,8},{10,11... | collective-permute-start | bytes 626696 | tf_op jit(solution)/shard_map/ppermute | solution.py:727
  10.5 5.9 %collective-permute-start.6 = (f32[384,128]{1,0:T(8,128)S(1)}, f32[384,128]{1,0:T(8,128)S(1)}, u32[]{:S(2)}, u32[]{:S(2)}) collective-permute-start(f32[384,128]{1,0:T(8,128)S(1)} %shard_map.104), channel_id=1, source_target_pairs={{0,2},{1,3},{2,0},{3,1},{4,6},{5,7},{6,4},{7,5},{8,10},{9,11},{10,... | collective-permute-start | bytes 589832 | tf_op jit(solution)/shard_map/ppermute | solution.py:727
  17.0 18.4 %collective-permute-start.7 = (f32[768,128]{1,0:T(8,128)S(1)}, f32[768,128]{1,0:T(8,128)S(1)}, u32[]{:S(2)}, u32[]{:S(2)}) collective-permute-start(f32[768,128]{1,0:T(8,128)S(1)} %shard_map.105.halves), channel_id=1, source_target_pairs={{0,1},{1,0},{2,3},{3,2},{4,5},{5,4},{6,7},{7,6},{8,9},{9,8},{10,11... | collective-permute-start | bytes 1179656 | tf_op jit(solution)/shard_map/ppermute | solution.py:727
  17.1 21.2 %collective-permute-start.3 = (f32[128,768]{1,0:T(8,128)S(1)}, f32[128,768]{1,0:T(8,128)S(1)}, u32[]{:S(2)}, u32[]{:S(2)}) collective-permute-start(f32[128,768]{1,0:T(8,128)S(1)} %shard_map.102.own_near), channel_id=1, source_target_pairs={{0,4},{4,8},{8,12},{12,16},{16,20},{20,24},{24,28},{1,5},{5,9},{9,... | collective-permute-start | bytes 1179656 | tf_op jit(solution)/shard_map/ppermute | solution.py:730
  21.4 9.4 %collective-permute-start.1 = (f32[136,256]{1,0:T(8,128)S(1)}, f32[136,256]{1,0:T(8,128)S(1)}, u32[]{:S(2)}, u32[]{:S(2)}) collective-permute-start(f32[136,256]{1,0:T(8,128)S(1)} %get-tuple-element.45), channel_id=1, source_target_pairs={{0,2},{1,3},{2,0},{3,1},{4,6},{5,7},{6,4},{7,5},{8,10},{9,11},{10,... | collective-permute-start | bytes 417800 | tf_op jit(solution)/shard_map/ppermute | solution.py:727
  23.0 27.5 %collective-permute-start.9 = (f32[768,128]{1,0:T(8,128)S(1)}, f32[768,128]{1,0:T(8,128)S(1)}, u32[]{:S(2)}, u32[]{:S(2)}) collective-permute-start(f32[768,128]{1,0:T(8,128)S(1)} %shard_map.105.halves), channel_id=1, source_target_pairs={{0,8},{4,12},{8,16},{12,20},{16,24},{20,28},{1,9},{5,13},{9,17},{1... | collective-permute-start | bytes 1179656 | tf_op jit(solution)/shard_map/ppermute | solution.py:730
  26.5 4.4 %collective-permute-start.2 = (f32[136,128]{1,0:T(8,128)S(1)}, f32[136,128]{1,0:T(8,128)S(1)}, u32[]{:S(2)}, u32[]{:S(2)}) collective-permute-start(f32[136,128]{1,0:T(8,128)S(1)} %get-tuple-element.46), channel_id=1, source_target_pairs={{0,3},{1,2},{2,1},{3,0},{4,7},{5,6},{6,5},{7,4},{8,11},{9,10},{10,... | collective-permute-start | bytes 208904 | tf_op jit(solution)/shard_map/ppermute | solution.py:727
  30.8 4.4 %copy-start.1 = (s32[8,3]{0,1:T(4,128)S(1)}, s32[8,3]{0,1:T(4,128)}, u32[]{:S(2)}) copy-start(s32[8,3]{0,1:T(4,128)} %param.7) | copy-start | bytes 292
  30.9 7.4 %collective-permute-start.4 = (f32[136,256]{1,0:T(8,128)S(1)}, f32[136,256]{1,0:T(8,128)S(1)}, u32[]{:S(2)}, u32[]{:S(2)}) collective-permute-start(f32[136,256]{1,0:T(8,128)S(1)} %shard_map.103.own_far), channel_id=1, source_target_pairs={{0,4},{4,8},{8,12},{12,16},{16,20},{20,24},{24,28},{1,5},{5,9},{9,... | collective-permute-start | bytes 417800 | tf_op jit(solution)/shard_map/ppermute | solution.py:730
  40.7 21.1 %collective-permute-start.8 = (f32[264,512]{1,0:T(8,128)S(1)}, f32[264,512]{1,0:T(8,128)S(1)}, u32[]{:S(2)}, u32[]{:S(2)}) collective-permute-start(f32[264,512]{1,0:T(8,128)S(1)} %shard_map.107.own), channel_id=1, source_target_pairs={{0,8},{4,12},{8,16},{12,20},{16,24},{20,28},{1,9},{5,13},{9,17},{1... | collective-permute-start | bytes 1622024 | tf_op jit(solution)/shard_map/ppermute | solution.py:730
  50.5 1.9 %collective-permute-start.10 = (f32[768,128]{1,0:T(8,128)S(1)}, f32[768,128]{1,0:T(8,128)S(1)}, u32[]{:S(2)}, u32[]{:S(2)}) collective-permute-start(f32[768,128]{1,0:T(8,128)S(1)} %collective-permute-done.9.halves), channel_id=1, source_target_pairs={{0,1},{1,0},{2,3},{3,2},{4,5},{5,4},{6,7},{7,6},{8,9},{9,8},{10,11... | collective-permute-start | bytes 1179656 | tf_op jit(solution)/shard_map/ppermute | solution.py:727
  65.7 20.2 %collective-permute-start.11 = (f32[520,128]{1,0:T(8,128)S(1)}, f32[520,128]{1,0:T(8,128)S(1)}, u32[]{:S(2)}, u32[]{:S(2)}) collective-permute-start(f32[520,128]{1,0:T(8,128)S(1)} %get-tuple-element.67), channel_id=1, source_target_pairs={{0,1},{1,0},{2,3},{3,2},{4,5},{5,4},{6,7},{7,6},{8,9},{9,8},{10,11... | collective-permute-start | bytes 798728 | tf_op jit(solution)/shard_map/ppermute | solution.py:727
  65.7 21.7 %collective-permute-start.13 = (f32[520,128]{1,0:T(8,128)S(1)}, f32[520,128]{1,0:T(8,128)S(1)}, u32[]{:S(2)}, u32[]{:S(2)}) collective-permute-start(f32[520,128]{1,0:T(8,128)S(1)} %get-tuple-element.73), channel_id=1, source_target_pairs={{0,2},{1,3},{2,0},{3,1},{4,6},{5,7},{6,4},{7,5},{8,10},{9,11},{10,... | collective-permute-start | bytes 798728 | tf_op jit(solution)/shard_map/ppermute | solution.py:727
  67.3 20.1 %collective-permute-start.14 = (f32[520,128]{1,0:T(8,128)S(1)}, f32[520,128]{1,0:T(8,128)S(1)}, u32[]{:S(2)}, u32[]{:S(2)}) collective-permute-start(f32[520,128]{1,0:T(8,128)S(1)} %get-tuple-element.74), channel_id=1, source_target_pairs={{0,3},{1,2},{2,1},{3,0},{4,7},{5,6},{6,5},{7,4},{8,11},{9,10},{10,... | collective-permute-start | bytes 798728 | tf_op jit(solution)/shard_map/ppermute | solution.py:727
  67.6 18.3 %collective-permute-start.12 = (f32[128,512]{1,0:T(8,128)S(1)}, f32[128,512]{1,0:T(8,128)S(1)}, u32[]{:S(2)}, u32[]{:S(2)}) collective-permute-start(f32[128,512]{1,0:T(8,128)S(1)} %get-tuple-element.69), channel_id=1, source_target_pairs={{0,2},{1,3},{2,0},{3,1},{4,6},{5,7},{6,4},{7,5},{8,10},{9,11},{10,... | collective-permute-start | bytes 786440 | tf_op jit(solution)/shard_map/ppermute | solution.py:727

commit v2 on v1

--- a/solution.py
+++ b/solution.py
@@ -198,6 +198,15 @@
     return jnp.sum(column(row, r) * matrix, axis=0, keepdims=True)
 
 
+def place_of():
+    q = lax.axis_index("col")
+    return q, q >> 1, q & 1
+
+
+def has(distance):
+    return (lax.axis_index("tm") >= distance).astype(jnp.int32)
+
+
 def lanes(index, r):
     return pl.ds(pl.multiple_of(index * r, r), r)
 
@@ -213,9 +222,9 @@
 
 
 def send_kernel(
-    scal, cov, cost, drift, eta, to_core, to_chip, to_far, panel, vecs, b_in, e_in, sems
+    cov, cost, drift, eta, to_core, to_chip, to_far, panel, vecs, b_in, e_in, sems
 ):
-    q, y, c = scal[0], scal[1], scal[2]
+    q, y, c = place_of()
     r = to_far.shape[1]
 
     def load(mine, theirs):
@@ -296,15 +305,15 @@
     )
 
 
-def pick_kernel(scal, turned, before, out):
-    y = scal[1]
+def pick_kernel(turned, before, out):
+    y = place_of()[1]
     height = turned.shape[1]
     out[0:height, :] = turned[1 - y]
     out[height:, :] = before[1 - y]
 
 
-def halves_kernel(scal, turned, before, other, out):
-    y = scal[1]
+def halves_kernel(turned, before, other, out):
+    y = place_of()[1]
     height = turned.shape[1]
     out[0:height, :] = turned[y]
     out[height : 2 * height, :] = other[0:height, :]
@@ -312,8 +321,8 @@
     out[3 * height :, :] = other[height:, :]
 
 
-def dense_turned(put, scal, pattern, own_half, core_half, flag, n, r, bs):
-    q = scal[0]
+def dense_turned(put, pattern, own_half, core_half, flag, n, r, bs):
+    q = place_of()[0]
     lane = lax.broadcasted_iota(jnp.int32, (bs, r), 1) // bs
     rows = lax.broadcasted_iota(jnp.int32, (bs, r), 0)
     cols = lax.broadcasted_iota(jnp.int32, (bs, r), 1)
@@ -326,8 +335,8 @@
         for k in range(3):
             want = jnp.zeros((bs, r), jnp.int32)
             for h in range(per):
-                block = pattern[(q ^ j) * per + h, k] ^ (q * per)
-                want = jnp.where(lane == h, block, want)
+                block = pattern[pl.ds((q ^ j) * per + h, 1), :][:, k : k + 1] ^ (q * per)
+                want = jnp.where(lane == h, jnp.broadcast_to(block, (bs, r)), want)
             wanted.append(jnp.where(flag == 1, want, -1))
         for block in range(n // bs):
             if j * r <= block * bs < (j + 1) * r:
@@ -369,8 +378,8 @@
         )
 
 
-def prepare_kernel(bs, scal, pattern, halves, core_halves, mh, ml, th, tl, dense):
-    c, has1 = scal[2], scal[3]
+def prepare_kernel(bs, pattern, halves, core_halves, mh, ml, th, tl, dense):
+    c, has1 = place_of()[2], has(1)
     n = dense.shape[0]
     r = halves.shape[1]
     half = halves.shape[0] // 2
@@ -382,7 +391,7 @@
     def put(row, col, value):
         dense[row, col] = value
 
-    dense_turned(put, scal, pattern, own_half, core_half, flag, n, r, bs)
+    dense_turned(put, pattern, own_half, core_half, flag, n, r, bs)
 
     @pl.when(first)
     def _():
@@ -396,9 +405,9 @@
 
 
 def level1_kernel(
-    scal, own_near, own_far, near, far, mh, ml, th, tl, out, full, xh, xl
+    own_near, own_far, near, far, mh, ml, th, tl, out, full, xh, xl
 ):
-    c = scal[2]
+    c = place_of()[2]
     r = own_near.shape[0]
     first = c == 0
     xn = jnp.where(first, near[...], own_near[...])
@@ -446,14 +455,14 @@
     out[base + 4 : base + 8, :] = jnp.zeros((4, 4 * r), F32)
 
 
-def early_kernel(bs, scal, pattern, halves, core_halves, a0h, a0l, a1h, a1l, t):
+def early_kernel(bs, pattern, halves, core_halves, a0h, a0l, a1h, a1l, t):
     n = a0h.shape[0]
     r = halves.shape[1]
     half = halves.shape[0] // 2
-    for at, flag, hi, lo in ((0, 1, a0h, a0l), (1, scal[3], a1h, a1l)):
+    for at, flag, hi, lo in ((0, 1, a0h, a0l), (1, has(1), a1h, a1l)):
         rows = slice(at * half, (at + 1) * half)
         put = functools.partial(put_split, hi, lo)
-        dense_turned(put, scal, pattern, halves[rows, :], core_halves[rows, :], flag, n, r, bs)
+        dense_turned(put, pattern, halves[rows, :], core_halves[rows, :], flag, n, r, bs)
 
     def wanted(ref):
         return jnp.concatenate([ref[:, 0:r], ref[:, 2 * r : 3 * r]], axis=1)
@@ -463,7 +472,6 @@
 
 def dynamics_kernel(
     bs,
-    scal,
     pattern,
     halves,
     core_halves,
@@ -485,7 +493,7 @@
     a3l,
     product_ref,
 ):
-    q, c = scal[0], scal[2]
+    q, _, c = place_of()
     n = a0h.shape[0]
     r = halves.shape[1]
     half = halves.shape[0] // 2
@@ -498,9 +506,9 @@
     def put3(row, col, value):
         put_split(a3h, a3l, row, col, value)
 
-    for at, flag, put in ((0, scal[4], put2), (1, scal[5], put3)):
+    for at, flag, put in ((0, has(2), put2), (1, has(3), put3)):
         rows = slice(at * half, (at + 1) * half)
-        dense_turned(put, scal, pattern, halves[rows, :], core_halves[rows, :], flag, n, r, bs)
+        dense_turned(put, pattern, halves[rows, :], core_halves[rows, :], flag, n, r, bs)
     rows = dot3(a2h[...], a2l[...], *split(t[...]))
     rows = dot3(a3h[...], a3l[...], *split(rows))
     for j in range(4):
@@ -521,7 +529,7 @@
         transpose_split(mh, ml, product_ref, r)
 
 
-def ahead_kernel(scal, own, mh, ml, th, tl, full, z, xh, xl):
+def ahead_kernel(own, mh, ml, th, tl, full, z, xh, xl):
     r = own.shape[1] // 4
 
     def put(i, j, block):
@@ -529,7 +537,7 @@
 
     spread(own, r, put)
 
-    @pl.when(scal[2] == 1)
+    @pl.when(place_of()[2] == 1)
     def _():
         straight_split(xh, xl, full, r)
         u = dot3(xh[...], xl[...], mh[...], ml[...])
@@ -541,31 +549,9 @@
         ref[lanes(q ^ j, r), :] = value[:, j * r : (j + 1) * r]
 
 
-def level2_kernel(
-    scal,
-    own,
-    earlier,
-    mh,
-    ml,
-    th,
-    tl,
-    a2,
-    full,
-    z,
-    to_chip,
-    to_far,
-    uh,
-    ul,
-    vec,
-    xh,
-    xl,
-    rest,
-):
-    q, c = scal[0], scal[2]
+def level2_kernel(own, earlier, mh, ml, th, tl, full, z, to_chip, to_far, uh, ul, xh, xl, rest):
+    q, _, c = place_of()
     r = own.shape[1] // 4
-    n = 4 * r
-    base = 2 * r
-    b1 = earlier[base + 1 : base + 2, :] + row_times(earlier[base + 3 : base + 4, :], a2[...], r)
 
     @pl.when(c == 0)
     def _():
@@ -577,8 +563,6 @@
         uh[...] = hi
         ul[...] = lo
         rest[...] = dot3(th[2 * r :, :], tl[2 * r :, :], hi, lo) + full[2 * r :, :]
-        vec[0:1, :] = b1
-        vec[1:2, :] = own[base + 2 : base + 3, :]
 
     @pl.when(c == 1)
     def _():
@@ -588,24 +572,24 @@
             rest[rows, cols] = z[i * r : (i + 1) * r, cols] + block
 
         spread(earlier, r, put, rows=(2, 3))
-        vec[0:1, :] = own[base + 2 : base + 3, :] + row_times(b1, full[...], r)
-        vec[1:2, :] = earlier[base + 2 : base + 3, :]
-
-    out = vec[1:2, :] + row_times(vec[0:1, :], mh[...].astype(F32) + ml[...].astype(F32), r)
-    vec[0:1, :] = out
-    for i, ref in ((2, to_chip), (3, to_far)):
-        put_rows(ref, rest[(i - 2) * r : (i - 1) * r, :], q, r)
-        ref[n : n + 8, :] = jnp.broadcast_to(out[:, i * r : (i + 1) * r], (8, r))
-
-
-def rest_kernel(scal, earlier, th, tl, full, z, uh, ul, vec, keep, to_core, rest):
-    q, c = scal[0], scal[2]
-    r = earlier.shape[1] // 4
-    n = 4 * r
+
+    put_rows(to_chip, rest[0:r, :], q, r)
+    put_rows(to_far, rest[r : 2 * r, :], q, r)
+
+
+def rest_kernel(
+    own, earlier, mh, ml, th, tl, a2, full, z, uh, ul, keep, to_core, short, vec, rest
+):
+    q, _, c = place_of()
+    r = own.shape[1] // 4
+    base = 2 * r
+    b1 = earlier[base + 1 : base + 2, :] + row_times(earlier[base + 3 : base + 4, :], a2[...], r)
 
     @pl.when(c == 0)
     def _():
         rest[...] = dot3(th[0 : 2 * r, :], tl[0 : 2 * r, :], uh[...], ul[...]) + full[0 : 2 * r, :]
+        vec[0:1, :] = b1
+        vec[1:2, :] = own[base + 2 : base + 3, :]
 
     @pl.when(c == 1)
     def _():
@@ -615,10 +599,15 @@
             rest[rows, cols] = z[rows, cols] + block
 
         spread(earlier, r, put, rows=(0, 1))
-
-    for i, ref in ((0, keep), (1, to_core)):
-        put_rows(ref, rest[i * r : (i + 1) * r, :], q, r)
-        ref[n : n + 8, :] = jnp.broadcast_to(vec[0:1, i * r : (i + 1) * r], (8, r))
+        vec[0:1, :] = own[base + 2 : base + 3, :] + row_times(b1, full[...], r)
+        vec[1:2, :] = earlier[base + 2 : base + 3, :]
+
+    out = vec[1:2, :] + row_times(vec[0:1, :], mh[...].astype(F32) + ml[...].astype(F32), r)
+    put_rows(keep, rest[0:r, :], q, r)
+    put_rows(to_core, rest[r : 2 * r, :], q, r)
+    for i in range(4):
+        short[i : i + 1, :] = out[:, i * r : (i + 1) * r]
+    short[4:8, :] = jnp.zeros((4, r), F32)
 
 
 def panel_copies(panel, target, element, r):
@@ -627,8 +616,8 @@
     ]
 
 
-def fill_kernel(scal, keep, from_core, dyn_own, dyn_recv, dyn_out, cov_out, cost_out, sems):
-    y, c = scal[1], scal[2]
+def fill_kernel(keep, from_core, dyn_own, dyn_recv, dyn_out, cov_out, cost_out, sems):
+    _, y, c = place_of()
     r = dyn_own.shape[0]
     dyn = [(dyn_own, dyn_out.at[y]), (dyn_recv, dyn_out.at[1 - y])]
 
@@ -645,57 +634,65 @@
         )
 
 
-def place_kernel(
-    scal,
+def place_chip_kernel(
     cov_in,
     cost_in,
-    keep,
-    from_core,
-    from_chip,
-    from_far,
+    short,
+    core_short,
+    chip_short,
+    far_short,
+    panel,
     cov_out,
     cost_out,
     drift_out,
     eta_out,
+    lines,
     sems,
 ):
     del cov_in, cost_in
-    y, c = scal[1], scal[2]
+    _, y, c = place_of()
     first = c == 0
-    r = keep.shape[1]
+    r = short.shape[1]
+    for at, (one, two, three, four) in enumerate(
+        (
+            (short[0:1, :], core_short[1:2, :], chip_short[2:3, :], far_short[3:4, :]),
+            (core_short[1:2, :], short[0:1, :], far_short[3:4, :], chip_short[2:3, :]),
+        )
+    ):
+        lines[at, pl.ds(y, 1), :] = jnp.where(first, one, two)
+        lines[at, pl.ds(1 - y, 1), :] = jnp.where(first, three, four)
+    vectors = [(lines.at[0], drift_out), (lines.at[1], eta_out)]
+
+    @pl.when(first)
+    def _():
+        copy_all(vectors + panel_copies(panel, cov_out, 1 - y, r), sems)
+
+    @pl.when(c == 1)
+    def _():
+        copy_all(vectors + panel_copies(panel, cost_out, 1 - y, r), sems)
+
+
+def place_far_kernel(cov_in, cost_in, panel, cov_out, cost_out, sems):
+    del cov_in, cost_in
+    _, y, c = place_of()
+    r = panel.shape[1]
 
     @pl.when(c == 0)
     def _():
-        copy_all(
-            panel_copies(from_chip, cov_out, 1 - y, r) + panel_copies(from_far, cost_out, 1 - y, r),
-            sems,
-        )
+        copy_all(panel_copies(panel, cost_out, 1 - y, r), sems)
 
     @pl.when(c == 1)
     def _():
-        copy_all(
-            panel_copies(from_far, cov_out, 1 - y, r) + panel_copies(from_chip, cost_out, 1 - y, r),
-            sems,
-        )
-
-    at = slice(4 * r, 4 * r + 1)
-    for vector, one, two, three, four in (
-        (drift_out, keep, from_core, from_chip, from_far),
-        (eta_out, from_core, keep, from_far, from_chip),
-    ):
-        vector[pl.ds(y, 1), :] = jnp.where(first, one[at, :], two[at, :])
-        vector[pl.ds(1 - y, 1), :] = jnp.where(first, three[at, :], four[at, :])
-
-
-IN_SMEM, IN_HBM, IN_VMEM, IN_OUT = 0, 1, 2, 3
+        copy_all(panel_copies(panel, cov_out, 1 - y, r), sems)
+
+
+IN_HBM, IN_VMEM = 0, 1
 
 
 def kernel(body, operands, shapes, scratch=(), aliases=None):
     specs = {
-        IN_SMEM: pl.BlockSpec(memory_space=pltpu.SMEM),
         IN_HBM: pl.BlockSpec(memory_space=pltpu.HBM),
         IN_VMEM: pl.BlockSpec(memory_space=pltpu.VMEM),
-        IN_OUT: pl.BlockSpec(memory_space=pltpu.VMEM),
     }
     call = pl.pallas_call(
         body,
@@ -721,30 +718,12 @@
     elements, r, n = cov.shape
     bs = blocks.shape[2] // 3
     tms, cols = lax.axis_size("tm"), lax.axis_size("col")
-    position, q = lax.axis_index("tm"), lax.axis_index("col")
 
     def swap(value, bit):
         return lax.ppermute(value, "col", [(i, i ^ bit) for i in range(cols)])
 
     def later(value, distance):
         return lax.ppermute(value, "tm", [(i, i + distance) for i in range(tms - distance)])
-
-    def flag(x):
-        return x.astype(jnp.int32)
-
-    scal = jnp.stack(
-        [
-            q,
-            q >> 1,
-            q & 1,
-            flag(position >= 1),
-            flag(position >= 2),
-            flag(position >= 3),
-        ]
-    ).astype(jnp.int32)
-
-    def smem(*arrays):
-        return [(IN_SMEM, x) for x in arrays]
 
     def hbm(*arrays):
         return [(IN_HBM, x) for x in arrays]
@@ -768,7 +747,7 @@
     before = later(turned, 1)
     to_core, to_chip, to_far, panel, vecs = kernel(
         send_kernel,
-        smem(scal) + hbm(cov, cost, drift, eta),
+        hbm(cov, cost, drift, eta),
         vmem(shape(r + 8, 3 * r), shape(r + 8, 2 * r), shape(r + 8, r), shape(r, n), shape(8, r)),
         [pltpu.VMEM(drift.shape, F32), pltpu.VMEM(eta.shape, F32), sems(12)],
     )
@@ -781,75 +760,73 @@
         pack_far_kernel, vmem(vecs, from_core, from_chip, from_far), vmem(shape(r + 8, 2 * r))
     )
     far = later(own_far, 1)
-    (picked,) = kernel(pick_kernel, smem(scal) + vmem(turned, before), vmem(shape(6 * bs, r)))
+    (picked,) = kernel(pick_kernel, vmem(turned, before), vmem(shape(6 * bs, r)))
     other = swap(picked, 2)
-    (halves,) = kernel(
-        halves_kernel, smem(scal) + vmem(turned, before, other), vmem(shape(12 * bs, r))
-    )
+    (halves,) = kernel(halves_kernel, vmem(turned, before, other), vmem(shape(12 * bs, r)))
     core_halves = swap(halves, 1)
     far_halves = later(halves, 2)
     m1 = kernel(
         functools.partial(prepare_kernel, bs),
-        smem(scal, pattern) + vmem(halves, core_halves),
+        vmem(pattern, halves, core_halves),
         vmem(*[half(n, n)] * 4),
         [square(F32)],
     )
     (level1,) = kernel(
         level1_kernel,
-        smem(scal) + vmem(own_near, own_far, near, far, *m1),
+        vmem(own_near, own_far, near, far, *m1),
         vmem(shape(2 * r + 8, n)),
         [square(F32)] + [square(BF16)] * 2,
     )
     earlier = later(level1, 2)
     a01 = kernel(
         functools.partial(early_kernel, bs),
-        smem(scal, pattern) + vmem(halves, core_halves),
+        vmem(pattern, halves, core_halves),
         vmem(*[half(n, n)] * 4, shape(n, 2 * r)),
     )
     far_core_halves = swap(far_halves, 1)
     dyn_own, dyn_send, *m2, a2 = kernel(
         functools.partial(dynamics_kernel, bs),
-        smem(scal, pattern) + vmem(far_halves, far_core_halves, *a01),
+        vmem(pattern, far_halves, far_core_halves, *a01),
         vmem(shape(r, n), shape(r, n), *[half(n, n)] * 4, shape(n, n)),
         [square(BF16)] * 4 + [square(F32)],
     )
     dyn_recv = swap(dyn_send, 2)
     full, z = kernel(
-        ahead_kernel,
-        smem(scal) + vmem(level1, *m2),
-        vmem(shape(n, n), shape(n, n)),
-        [square(BF16)] * 2,
-    )
-    to_chip, to_far, *u, vec = kernel(
+        ahead_kernel, vmem(level1, *m2), vmem(shape(n, n), shape(n, n)), [square(BF16)] * 2
+    )
+    to_chip, to_far, *u = kernel(
         level2_kernel,
-        smem(scal) + vmem(level1, earlier, *m2, a2, full, z),
-        vmem(shape(n + 8, r), shape(n + 8, r), half(n, n), half(n, n), shape(8, n)),
+        vmem(level1, earlier, *m2, full, z),
+        vmem(shape(n, r), shape(n, r), half(n, n), half(n, n)),
         [square(BF16)] * 2 + [pltpu.VMEM((2 * r, n), F32)],
     )
     from_chip = swap(to_chip, 2)
     from_far = swap(to_far, 3)
-    keep, to_core = kernel(
+    keep, to_core, short = kernel(
         rest_kernel,
-        smem(scal) + vmem(earlier, *m2[2:], full, z, *u, vec),
-        vmem(shape(n + 8, r), shape(n + 8, r)),
-        [pltpu.VMEM((2 * r, n), F32)],
+        vmem(level1, earlier, *m2, a2, full, z, *u),
+        vmem(shape(n, r), shape(n, r), shape(8, r)),
+        [pltpu.VMEM((8, n), F32), pltpu.VMEM((2 * r, n), F32)],
     )
     from_core = swap(to_core, 1)
-    whole = shape(elements, r, n)
+    shorts = (short, swap(short, 1), swap(short, 2), swap(short, 3))
+    whole, line = shape(elements, r, n), shape(elements, r)
     dyn_out, cov_out, cost_out = kernel(
-        fill_kernel,
-        smem(scal) + vmem(keep, from_core, dyn_own, dyn_recv),
-        hbm(whole, whole, whole),
-        [sems(10)],
+        fill_kernel, vmem(keep, from_core, dyn_own, dyn_recv), hbm(whole, whole, whole), [sems(10)]
     )
     cov_out, cost_out, drift_out, eta_out = kernel(
-        place_kernel,
-        smem(scal)
-        + hbm(cov_out, cost_out)
-        + vmem(keep, from_core, from_chip, from_far),
-        hbm(whole, whole) + [(IN_OUT, shape(elements, r))] * 2,
-        [sems(8)],
-        {1: 0, 2: 1},
+        place_chip_kernel,
+        hbm(cov_out, cost_out) + vmem(*shorts, from_chip),
+        hbm(whole, whole, line, line),
+        [pltpu.VMEM((2, elements, r), F32), sems(6)],
+        {0: 0, 1: 1},
+    )
+    cov_out, cost_out = kernel(
+        place_far_kernel,
+        hbm(cov_out, cost_out) + vmem(from_far),
+        hbm(whole, whole),
+        [sems(4)],
+        {0: 0, 1: 1},
     )
     return dyn_out, drift_out, cov_out, cost_out, eta_out
 

time: 89.7 us -> 79.6 us (0.89)
  waiting for transfers between devices: 33.8 us -> 27.5 us
  Pallas kernels: 20.8 us -> 14.9 us
  starting transfers between devices: 33.8 us -> 35.9 us
    ppermute x10 -> x13, waiting for transfers between devices: 25.3 us -> 18.5 us  [swap(): return lax.ppermute(value, 'col', [(i, i ^ bit) for i in range(cols)])]
    pallas_call x14 -> x15, Pallas kernels: 20.8 us -> 14.9 us  [kernel(): call(*(pltpu.with_memory_space_constraint(x, kept[where]) if where in kep...]
    ppermute x10 -> x13, starting transfers between devices: 6.89 us -> 8.95 us  [swap(): return lax.ppermute(value, 'col', [(i, i ^ bit) for i in range(cols)])]
  transfers between devices with their start and end apart: 15 -> 18, of which waited for: 6 -> 8; matrix products, arithmetic and copies ran while one was open for 0% -> 0% of each run, Pallas kernels for 17% -> 18%
where the time goes in v2:
time: 79.6 us; the launch traced here: 79.3 us
  starting transfers between devices  35.9 us (45%)
  waiting for transfers between devices  27.5 us (35%)
  Pallas kernels  14.9 us (19%)
  between operations  0.85 us (1%)
    ppermute x5, starting transfers between devices, later(): lax.ppermute(value, 'tm', [(i, i + distance) for i in range(tms - distanc...  27 us
    ppermute x13, waiting for transfers between devices, swap(): return lax.ppermute(value, 'col', [(i, i ^ bit) for i in range(cols)])  18.5 us
    pallas_call x15, Pallas kernels, kernel(): call(*(pltpu.with_memory_space_constraint(x, kept[where]) if where in kep...  14.9 us
    ppermute x5, waiting for transfers between devices, later(): lax.ppermute(value, 'tm', [(i, i + distance) for i in range(tms - distanc...  9.02 us
    ppermute x13, starting transfers between devices, swap(): return lax.ppermute(value, 'col', [(i, i ^ bit) for i in range(cols)])  8.95 us
  transfers between devices with their start and end apart: 18, of which 8 were waited for; matrix products, arithmetic and copies ran while one was open for 0% of the time, Pallas kernels for 18%

profile of v2, /device:TPU:0, one launch (start us, length us, event | category | flops | bytes accessed | tf_op | source)
XLA Modules:
  0.0 79.3 jit_solution(16212270798183632760)
XLA Ops:
  0.6 5.0 %collective-permute-start.5 = (f32[2,192,128]{2,1,0:T(8,128)}, f32[2,192,128]{2,1,0:T(8,128)S(1)}, u32[]{:S(2)}, u32[]{:S(2)}) collective-permute-start(f32[2,192,128]{2,1,0:T(8,128)} %bitcast.1), channel_id=1, source_target_pairs={{0,4},{4,8},{8,12},{12,16},{16,20},{20,24},{24,28},{1,5},{5,9},{9,... | collective-permute-start | bytes 589832 | tf_op jit(solution)/shard_map/ppermute | solution.py:726
  5.7 1.3 %shard_map.101 = (f32[136,384]{1,0:T(8,128)S(1)}, f32[136,256]{1,0:T(8,128)S(1)}, f32[136,128]{1,0:T(8,128)S(1)}, f32[128,512]{1,0:T(8,128)S(1)}, f32[8,128]{1,0:T(8,128)S(1)}) custom-call(f32[2,128,512]{2,1,0:T(8,128)} %cov.1, f32[2,128,512]{2,1,0:T(8,128)} %cost.1, f32[2,128]{1,0:T(2,128)} %drift.1, f32[2,128]{1,0:T(2,128)} %eta.1), custom_call_target="tpu_custom_call" | custom-call | tf_op jit(solution)/shard_map/pallas_call | solution.py:709
  7.0 3.1 %collective-permute-done.5.before = f32[2,192,128]{2,1,0:T(8,128)S(1)} collective-permute-done((f32[2,192,128]{2,1,0:T(8,128)}, f32[2,192,128]{2,1,0:T(8,128)S(1)}, u32[]{:S(2)}, u32[]{:S(2)}) %collective-permute-start.5) | collective-permute-done | bytes 196640 | tf_op jit(solution)/shard_map/ppermute | solution.py:726
  10.1 1.6 %collective-permute-start.6 = (f32[384,128]{1,0:T(8,128)S(1)}, f32[384,128]{1,0:T(8,128)S(1)}, u32[]{:S(2)}, u32[]{:S(2)}) collective-permute-start(f32[384,128]{1,0:T(8,128)S(1)} %shard_map.104), channel_id=1, source_target_pairs={{0,2},{1,3},{2,0},{3,1},{4,6},{5,7},{6,4},{7,5},{8,10},{9,11},{10,... | collective-permute-start | bytes 589832 | tf_op jit(solution)/shard_map/ppermute | solution.py:723
  11.7 4.3 %collective-permute-done.6.other = f32[384,128]{1,0:T(8,128)S(1)} collective-permute-done((f32[384,128]{1,0:T(8,128)S(1)}, f32[384,128]{1,0:T(8,128)S(1)}, u32[]{:S(2)}, u32[]{:S(2)}) %collective-permute-start.6) | collective-permute-done | bytes 196640 | tf_op jit(solution)/shard_map/ppermute | solution.py:723
  16.1 4.3 %collective-permute-start.3 = (f32[128,768]{1,0:T(8,128)S(1)}, f32[128,768]{1,0:T(8,128)S(1)}, u32[]{:S(2)}, u32[]{:S(2)}) collective-permute-start(f32[128,768]{1,0:T(8,128)S(1)} %shard_map.102.own_near), channel_id=1, source_target_pairs={{0,4},{4,8},{8,12},{12,16},{16,20},{20,24},{24,28},{1,5},{5,9},{9,... | collective-permute-start | bytes 1179656 | tf_op jit(solution)/shard_map/ppermute | solution.py:726
  20.5 1.6 %collective-permute-start.1 = (f32[136,256]{1,0:T(8,128)S(1)}, f32[136,256]{1,0:T(8,128)S(1)}, u32[]{:S(2)}, u32[]{:S(2)}) collective-permute-start(f32[136,256]{1,0:T(8,128)S(1)} %get-tuple-element.47), channel_id=1, source_target_pairs={{0,2},{1,3},{2,0},{3,1},{4,6},{5,7},{6,4},{7,5},{8,10},{9,11},{10,... | collective-permute-start | bytes 417800 | tf_op jit(solution)/shard_map/ppermute | solution.py:723
  22.0 3.5 %collective-permute-start.9 = (f32[768,128]{1,0:T(8,128)S(1)}, f32[768,128]{1,0:T(8,128)S(1)}, u32[]{:S(2)}, u32[]{:S(2)}) collective-permute-start(f32[768,128]{1,0:T(8,128)S(1)} %shard_map.105.halves), channel_id=1, source_target_pairs={{0,8},{4,12},{8,16},{12,20},{16,24},{20,28},{1,9},{5,13},{9,17},{1... | collective-permute-start | bytes 1179656 | tf_op jit(solution)/shard_map/ppermute | solution.py:726
  25.6 4.3 %collective-permute-done.2.from_far = f32[136,128]{1,0:T(8,128)S(1)} collective-permute-done((f32[136,128]{1,0:T(8,128)S(1)}, f32[136,128]{1,0:T(8,128)S(1)}, u32[]{:S(2)}, u32[]{:S(2)}) %collective-permute-start.2) | collective-permute-done | bytes 69664 | tf_op jit(solution)/shard_map/ppermute | solution.py:723
  29.9 4.4 %collective-permute-start.4 = (f32[136,256]{1,0:T(8,128)S(1)}, f32[136,256]{1,0:T(8,128)S(1)}, u32[]{:S(2)}, u32[]{:S(2)}) collective-permute-start(f32[136,256]{1,0:T(8,128)S(1)} %shard_map.103.own_far), channel_id=1, source_target_pairs={{0,4},{4,8},{8,12},{12,16},{16,20},{20,24},{24,28},{1,5},{5,9},{9,... | collective-permute-start | bytes 417800 | tf_op jit(solution)/shard_map/ppermute | solution.py:726
  34.4 0.9 %shard_map.106 = (bf16[512,512]{1,0:T(8,128)(2,1)S(1)}, bf16[512,512]{1,0:T(8,128)(2,1)S(1)}, bf16[512,512]{1,0:T(8,128)(2,1)S(1)}, bf16[512,512]{1,0:T(8,128)(2,1)S(1)}) custom-call(s32[8,3]{1,0:T(8,128)S(1)} %copy.15.pattern, f32[768,128]{1,0:T(8,128)S(1)} %shard_map.105.halves, f32[768,128]{1,0:T(8,128)S(1)} %collective-permute-done.7.core_halves), custom_call_target="tpu_custom_call" | custom-call | tf_op jit(solution)/shard_map/pallas_call | solution.py:709
  35.3 2.0 %collective-permute-done.4.far = f32[136,256]{1,0:T(8,128)S(1)} collective-permute-done((f32[136,256]{1,0:T(8,128)S(1)}, f32[136,256]{1,0:T(8,128)S(1)}, u32[]{:S(2)}, u32[]{:S(2)}) %collective-permute-start.4) | collective-permute-done | bytes 139296 | tf_op jit(solution)/shard_map/ppermute | solution.py:726
  37.3 2.0 %shard_map.107.own = f32[264,512]{1,0:T(8,128)S(1)} custom-call(f32[128,768]{1,0:T(8,128)S(1)} %shard_map.102.own_near, f32[136,256]{1,0:T(8,128)S(1)} %shard_map.103.own_far, f32[128,768]{1,0:T(8,128)S(1)} %collective-permute-done.3.near, f32[136,256]{1,0:T(8,128)S(1)} %collective-permute-done.4.far, bf16[512,512]{1,0:T(8,128)(2,1)S(1)} %get-tuple-element.49.mh, ...), custom_call_target="tpu_custom_call" | custom-call | tf_op jit(solution)/shard_map/pallas_call | solution.py:709
  39.3 9.8 %collective-permute-start.8 = (f32[264,512]{1,0:T(8,128)S(1)}, f32[264,512]{1,0:T(8,128)S(1)}, u32[]{:S(2)}, u32[]{:S(2)}) collective-permute-start(f32[264,512]{1,0:T(8,128)S(1)} %shard_map.107.own), channel_id=1, source_target_pairs={{0,8},{4,12},{8,16},{12,20},{16,24},{20,28},{1,9},{5,13},{9,17},{1... | collective-permute-start | bytes 1622024 | tf_op jit(solution)/shard_map/ppermute | solution.py:726
  49.2 1.4 %shard_map.108 = (bf16[512,512]{1,0:T(8,128)(2,1)S(1)}, bf16[512,512]{1,0:T(8,128)(2,1)S(1)}, bf16[512,512]{1,0:T(8,128)(2,1)S(1)}, bf16[512,512]{1,0:T(8,128)(2,1)S(1)}, f32[512,256]{1,0:T(8,128)S(1)}) custom-call(s32[8,3]{1,0:T(8,128)S(1)} %copy.15.pattern, f32[768,128]{1,0:T(8,128)S(1)} %shard_map.105.halves, ...), custom_call_target="tpu_custom_call" | custom-call | tf_op jit(solution)/shard_map/pallas_call | solution.py:709
  50.9 3.7 %shard_map.109 = (f32[128,512]{1,0:T(8,128)S(1)}, f32[128,512]{1,0:T(8,128)S(1)}, bf16[512,512]{1,0:T(8,128)(2,1)S(1)}, bf16[512,512]{1,0:T(8,128)(2,1)S(1)}, bf...) custom-call(s32[8,3]{1,0:T(8,128)S(1)} %copy.15.pattern, ...), custom_call_target="tpu_custom_call" | custom-call | tf_op jit(solution)/shard_map/pallas_call | solution.py:709
  54.7 1.6 %collective-permute-start.12 = (f32[128,512]{1,0:T(8,128)S(1)}, f32[128,512]{1,0:T(8,128)S(1)}, u32[]{:S(2)}, u32[]{:S(2)}) collective-permute-start(f32[128,512]{1,0:T(8,128)S(1)} %get-tuple-element.70), channel_id=1, source_target_pairs={{0,2},{1,3},{2,0},{3,1},{4,6},{5,7},{6,4},{7,5},{8,10},{9,11},{10,... | collective-permute-start | bytes 786440 | tf_op jit(solution)/shard_map/ppermute | solution.py:723
  56.5 3.9 %collective-permute-done.8.earlier = f32[264,512]{1,0:T(8,128)S(1)} collective-permute-done((f32[264,512]{1,0:T(8,128)S(1)}, f32[264,512]{1,0:T(8,128)S(1)}, u32[]{:S(2)}, u32[]{:S(2)}) %collective-permute-start.8) | collective-permute-done | bytes 540704 | tf_op jit(solution)/shard_map/ppermute | solution.py:726
  60.4 1.6 %shard_map.111 = (f32[512,128]{1,0:T(8,128)S(1)}, f32[512,128]{1,0:T(8,128)S(1)}, bf16[512,512]{1,0:T(8,128)(2,1)S(1)}, bf16[512,512]{1,0:T(8,128)(2,1)S(1)}) custom-call(f32[264,512]{1,0:T(8,128)S(1)} %shard_map.107.own, f32[264,512]{1,0:T(8,128)S(1)} %collective-permute-done.8.earlier, bf16[512,512]{1,0:T(8,128)(2,1)S(1)} %get-tuple-element.58.mh, ...), custom_call_target="tpu_custom_call" | custom-call | tf_op jit(solution)/shard_map/pallas_call | solution.py:709
  62.0 1.1 %shard_map.112 = (f32[512,128]{1,0:T(8,128)S(1)}, f32[512,128]{1,0:T(8,128)S(1)}, f32[8,128]{1,0:T(8,128)S(1)}) custom-call(f32[264,512]{1,0:T(8,128)S(1)} %shard_map.107.own, f32[264,512]{1,0:T(8,128)S(1)} %collective-permute-done.8.earlier, bf16[512,512]{1,0:T(8,128)(2,1)S(1)} %get-tuple-element.58.mh, bf16[512,512]{1,0:T(8,128)(2,1)S(1)} %get-tuple-element.59.ml, ...), custom_call_target="tpu_custom_call" | custom-call | tf_op jit(solution)/shard_map/pallas_call | solution.py:709
  63.3 1.6 %collective-permute-start.16 = (f32[512,128]{1,0:T(8,128)S(1)}, f32[512,128]{1,0:T(8,128)S(1)}, u32[]{:S(2)}, u32[]{:S(2)}) collective-permute-start(f32[512,128]{1,0:T(8,128)S(1)} %get-tuple-element.75), channel_id=1, source_target_pairs={{0,2},{1,3},{2,0},{3,1},{4,6},{5,7},{6,4},{7,5},{8,10},{9,11},{10,... | collective-permute-start | bytes 786440 | tf_op jit(solution)/shard_map/ppermute | solution.py:723
  65.1 1.5 %collective-permute-start.15 = (f32[8,128]{1,0:T(8,128)S(1)}, f32[8,128]{1,0:T(8,128)S(1)}, u32[]{:S(2)}, u32[]{:S(2)}) collective-permute-start(f32[8,128]{1,0:T(8,128)S(1)} %get-tuple-element.74.short), channel_id=1, source_target_pairs={{0,3},{1,2},{2,1},{3,0},{4,7},{5,6},{6,5},{7,4},{8,11},{9,10},{10,... | collective-permute-start | bytes 12296 | tf_op jit(solution)/shard_map/ppermute | solution.py:723
  67.1 1.0 %shard_map.113 = (f32[2,128,512]{2,1,0:T(8,128)}, f32[2,128,512]{2,1,0:T(8,128)}, f32[2,128,512]{2,1,0:T(8,128)}) custom-call(f32[512,128]{1,0:T(8,128)S(1)} %get-tuple-element.67.keep, f32[512,128]{1,0:T(8,128)S(1)} %collective-permute-done.11.from_core, f32[128,512]{1,0:T(8,128)S(1)} %get-tuple-element.69.dyn_own, ...), custom_call_target="tpu_custom_call" | custom-call | tf_op jit(solution)/shard_map/pallas_call | solution.py:709
  68.1 9.0 %collective-permute-done.15.far_short = f32[8,128]{1,0:T(8,128)S(1)} collective-permute-done((f32[8,128]{1,0:T(8,128)S(1)}, f32[8,128]{1,0:T(8,128)S(1)}, u32[]{:S(2)}, u32[]{:S(2)}) %collective-permute-start.15) | collective-permute-done | bytes 4128 | tf_op jit(solution)/shard_map/ppermute | solution.py:723
  (32 shorter events, 4.0 us)
Async XLA Ops:
  0.6 9.5 %copy-start = (f32[2,128,192]{1,2,0:T(8,128)S(1)}, f32[2,128,192]{1,2,0:T(8,128)}, u32[]{:S(2)}) copy-start(f32[2,128,192]{1,2,0:T(8,128)} %param.6) | copy-start | bytes 589828
  0.6 9.5 %collective-permute-start.5 = (f32[2,192,128]{2,1,0:T(8,128)}, f32[2,192,128]{2,1,0:T(8,128)S(1)}, u32[]{:S(2)}, u32[]{:S(2)}) collective-permute-start(f32[2,192,128]{2,1,0:T(8,128)} %bitcast.1), channel_id=1, source_target_pairs={{0,4},{4,8},{8,12},{12,16},{16,20},{20,24},{24,28},{1,5},{5,9},{9,... | collective-permute-start | bytes 589832 | tf_op jit(solution)/shard_map/ppermute | solution.py:726
  6.9 9.2 %collective-permute-start = (f32[136,384]{1,0:T(8,128)S(1)}, f32[136,384]{1,0:T(8,128)S(1)}, u32[]{:S(2)}, u32[]{:S(2)}) collective-permute-start(f32[136,384]{1,0:T(8,128)S(1)} %get-tuple-element.45), channel_id=1, source_target_pairs={{0,1},{1,0},{2,3},{3,2},{4,5},{5,4},{6,7},{7,6},{8,9},{9,8},{10,11... | collective-permute-start | bytes 626696 | tf_op jit(solution)/shard_map/ppermute | solution.py:723
  10.1 5.9 %collective-permute-start.6 = (f32[384,128]{1,0:T(8,128)S(1)}, f32[384,128]{1,0:T(8,128)S(1)}, u32[]{:S(2)}, u32[]{:S(2)}) collective-permute-start(f32[384,128]{1,0:T(8,128)S(1)} %shard_map.104), channel_id=1, source_target_pairs={{0,2},{1,3},{2,0},{3,1},{4,6},{5,7},{6,4},{7,5},{8,10},{9,11},{10,... | collective-permute-start | bytes 589832 | tf_op jit(solution)/shard_map/ppermute | solution.py:723
  16.0 18.4 %collective-permute-start.7 = (f32[768,128]{1,0:T(8,128)S(1)}, f32[768,128]{1,0:T(8,128)S(1)}, u32[]{:S(2)}, u32[]{:S(2)}) collective-permute-start(f32[768,128]{1,0:T(8,128)S(1)} %shard_map.105.halves), channel_id=1, source_target_pairs={{0,1},{1,0},{2,3},{3,2},{4,5},{5,4},{6,7},{7,6},{8,9},{9,8},{10,11... | collective-permute-start | bytes 1179656 | tf_op jit(solution)/shard_map/ppermute | solution.py:723
  16.1 21.2 %collective-permute-start.3 = (f32[128,768]{1,0:T(8,128)S(1)}, f32[128,768]{1,0:T(8,128)S(1)}, u32[]{:S(2)}, u32[]{:S(2)}) collective-permute-start(f32[128,768]{1,0:T(8,128)S(1)} %shard_map.102.own_near), channel_id=1, source_target_pairs={{0,4},{4,8},{8,12},{12,16},{16,20},{20,24},{24,28},{1,5},{5,9},{9,... | collective-permute-start | bytes 1179656 | tf_op jit(solution)/shard_map/ppermute | solution.py:726
  20.5 9.4 %collective-permute-start.1 = (f32[136,256]{1,0:T(8,128)S(1)}, f32[136,256]{1,0:T(8,128)S(1)}, u32[]{:S(2)}, u32[]{:S(2)}) collective-permute-start(f32[136,256]{1,0:T(8,128)S(1)} %get-tuple-element.47), channel_id=1, source_target_pairs={{0,2},{1,3},{2,0},{3,1},{4,6},{5,7},{6,4},{7,5},{8,10},{9,11},{10,... | collective-permute-start | bytes 417800 | tf_op jit(solution)/shard_map/ppermute | solution.py:723
  22.0 27.1 %collective-permute-start.9 = (f32[768,128]{1,0:T(8,128)S(1)}, f32[768,128]{1,0:T(8,128)S(1)}, u32[]{:S(2)}, u32[]{:S(2)}) collective-permute-start(f32[768,128]{1,0:T(8,128)S(1)} %shard_map.105.halves), channel_id=1, source_target_pairs={{0,8},{4,12},{8,16},{12,20},{16,24},{20,28},{1,9},{5,13},{9,17},{1... | collective-permute-start | bytes 1179656 | tf_op jit(solution)/shard_map/ppermute | solution.py:726
  25.5 4.4 %collective-permute-start.2 = (f32[136,128]{1,0:T(8,128)S(1)}, f32[136,128]{1,0:T(8,128)S(1)}, u32[]{:S(2)}, u32[]{:S(2)}) collective-permute-start(f32[136,128]{1,0:T(8,128)S(1)} %get-tuple-element.48), channel_id=1, source_target_pairs={{0,3},{1,2},{2,1},{3,0},{4,7},{5,6},{6,5},{7,4},{8,11},{9,10},{10,... | collective-permute-start | bytes 208904 | tf_op jit(solution)/shard_map/ppermute | solution.py:723
  29.9 4.4 %copy-start.1 = (s32[8,3]{0,1:T(4,128)S(1)}, s32[8,3]{0,1:T(4,128)}, u32[]{:S(2)}) copy-start(s32[8,3]{0,1:T(4,128)} %param.7) | copy-start | bytes 292
  29.9 7.4 %collective-permute-start.4 = (f32[136,256]{1,0:T(8,128)S(1)}, f32[136,256]{1,0:T(8,128)S(1)}, u32[]{:S(2)}, u32[]{:S(2)}) collective-permute-start(f32[136,256]{1,0:T(8,128)S(1)} %shard_map.103.own_far), channel_id=1, source_target_pairs={{0,4},{4,8},{8,12},{12,16},{16,20},{20,24},{24,28},{1,5},{5,9},{9,... | collective-permute-start | bytes 417800 | tf_op jit(solution)/shard_map/ppermute | solution.py:726
  39.3 21.1 %collective-permute-start.8 = (f32[264,512]{1,0:T(8,128)S(1)}, f32[264,512]{1,0:T(8,128)S(1)}, u32[]{:S(2)}, u32[]{:S(2)}) collective-permute-start(f32[264,512]{1,0:T(8,128)S(1)} %shard_map.107.own), channel_id=1, source_target_pairs={{0,8},{4,12},{8,16},{12,20},{16,24},{20,28},{1,9},{5,13},{9,17},{1... | collective-permute-start | bytes 1622024 | tf_op jit(solution)/shard_map/ppermute | solution.py:726
  49.1 1.8 %collective-permute-start.10 = (f32[768,128]{1,0:T(8,128)S(1)}, f32[768,128]{1,0:T(8,128)S(1)}, u32[]{:S(2)}, u32[]{:S(2)}) collective-permute-start(f32[768,128]{1,0:T(8,128)S(1)} %collective-permute-done.9.halves), channel_id=1, source_target_pairs={{0,1},{1,0},{2,3},{3,2},{4,5},{5,4},{6,7},{7,6},{8,9},{9,8},{10,11... | collective-permute-start | bytes 1179656 | tf_op jit(solution)/shard_map/ppermute | solution.py:723
  54.7 11.9 %collective-permute-start.12 = (f32[128,512]{1,0:T(8,128)S(1)}, f32[128,512]{1,0:T(8,128)S(1)}, u32[]{:S(2)}, u32[]{:S(2)}) collective-permute-start(f32[128,512]{1,0:T(8,128)S(1)} %get-tuple-element.70), channel_id=1, source_target_pairs={{0,2},{1,3},{2,0},{3,1},{4,6},{5,7},{6,4},{7,5},{8,10},{9,11},{10,... | collective-permute-start | bytes 786440 | tf_op jit(solution)/shard_map/ppermute | solution.py:723
  63.2 3.9 %collective-permute-start.11 = (f32[512,128]{1,0:T(8,128)S(1)}, f32[512,128]{1,0:T(8,128)S(1)}, u32[]{:S(2)}, u32[]{:S(2)}) collective-permute-start(f32[512,128]{1,0:T(8,128)S(1)} %get-tuple-element.68), channel_id=1, source_target_pairs={{0,1},{1,0},{2,3},{3,2},{4,5},{5,4},{6,7},{7,6},{8,9},{9,8},{10,11... | collective-permute-start | bytes 786440 | tf_op jit(solution)/shard_map/ppermute | solution.py:723
  63.3 14.5 %collective-permute-start.16 = (f32[512,128]{1,0:T(8,128)S(1)}, f32[512,128]{1,0:T(8,128)S(1)}, u32[]{:S(2)}, u32[]{:S(2)}) collective-permute-start(f32[512,128]{1,0:T(8,128)S(1)} %get-tuple-element.75), channel_id=1, source_target_pairs={{0,2},{1,3},{2,0},{3,1},{4,6},{5,7},{6,4},{7,5},{8,10},{9,11},{10,... | collective-permute-start | bytes 786440 | tf_op jit(solution)/shard_map/ppermute | solution.py:723
  64.8 13.7 %collective-permute-start.17 = (f32[512,128]{1,0:T(8,128)S(1)}, f32[512,128]{1,0:T(8,128)S(1)}, u32[]{:S(2)}, u32[]{:S(2)}) collective-permute-start(f32[512,128]{1,0:T(8,128)S(1)} %get-tuple-element.79), channel_id=1, source_target_pairs={{0,3},{1,2},{2,1},{3,0},{4,7},{5,6},{6,5},{7,4},{8,11},{9,10},{10,... | collective-permute-start | bytes 786440 | tf_op jit(solution)/shard_map/ppermute | solution.py:723
  65.1 12.0 %collective-permute-start.15 = (f32[8,128]{1,0:T(8,128)S(1)}, f32[8,128]{1,0:T(8,128)S(1)}, u32[]{:S(2)}, u32[]{:S(2)}) collective-permute-start(f32[8,128]{1,0:T(8,128)S(1)} %get-tuple-element.74.short), channel_id=1, source_target_pairs={{0,3},{1,2},{2,1},{3,0},{4,7},{5,6},{6,5},{7,4},{8,11},{9,10},{10,... | collective-permute-start | bytes 12296 | tf_op jit(solution)/shard_map/ppermute | solution.py:723
  66.6 11.2 %collective-permute-start.14 = (f32[8,128]{1,0:T(8,128)S(1)}, f32[8,128]{1,0:T(8,128)S(1)}, u32[]{:S(2)}, u32[]{:S(2)}) collective-permute-start(f32[8,128]{1,0:T(8,128)S(1)} %get-tuple-element.74.short), channel_id=1, source_target_pairs={{0,2},{1,3},{2,0},{3,1},{4,6},{5,7},{6,4},{7,5},{8,10},{9,11},{10,... | collective-permute-start | bytes 12296 | tf_op jit(solution)/shard_map/ppermute | solution.py:723
  67.1 10.7 %collective-permute-start.13 = (f32[8,128]{1,0:T(8,128)S(1)}, f32[8,128]{1,0:T(8,128)S(1)}, u32[]{:S(2)}, u32[]{:S(2)}) collective-permute-start(f32[8,128]{1,0:T(8,128)S(1)} %get-tuple-element.74.short), channel_id=1, source_target_pairs={{0,1},{1,0},{2,3},{3,2},{4,5},{5,4},{6,7},{7,6},{8,9},{9,8},{10,11... | collective-permute-start | bytes 12296 | tf_op jit(solution)/shard_map/ppermute | solution.py:723

commit v3 on v2

--- a/solution.py
+++ b/solution.py
@@ -470,34 +470,13 @@
     t[...] = dot3(a1h[...], a1l[...], wanted(a0h), wanted(a0l))
 
 
-def dynamics_kernel(
-    bs,
-    pattern,
-    halves,
-    core_halves,
-    a0h,
-    a0l,
-    a1h,
-    a1l,
-    t,
-    dyn_own,
-    dyn_send,
-    mh,
-    ml,
-    th,
-    tl,
-    a2,
-    a2h,
-    a2l,
-    a3h,
-    a3l,
-    product_ref,
+def rows_kernel(
+    bs, pattern, halves, core_halves, t, dyn_own, dyn_send, a2, a2h, a2l, a3h, a3l
 ):
-    q, _, c = place_of()
-    n = a0h.shape[0]
+    q, _, _ = place_of()
+    n = a2.shape[0]
     r = halves.shape[1]
     half = halves.shape[0] // 2
-    first = c == 0
 
     def put2(row, col, value):
         put_split(a2h, a2l, row, col, value)
@@ -516,6 +495,13 @@
         dyn_own[:, at] = rows[j * r : (j + 1) * r, 0:r].T
         dyn_send[:, at] = rows[j * r : (j + 1) * r, r : 2 * r].T
 
+
+def product_kernel(
+    a0h, a0l, a1h, a1l, a2h, a2l, a3h, a3l, mh, ml, th, tl, product_ref
+):
+    first = place_of()[2] == 0
+    r = a0h.shape[0] // 4
+
     @pl.when(first)
     def _():
         product_ref[...] = dot3(a1h[...], a1l[...], a0h[...], a0l[...])
@@ -634,7 +620,21 @@
         )
 
 
-def place_chip_kernel(
+def place_chip_kernel(cov_in, cost_in, panel, cov_out, cost_out, sems):
+    del cov_in, cost_in
+    _, y, c = place_of()
+    r = panel.shape[1]
+
+    @pl.when(c == 0)
+    def _():
+        copy_all(panel_copies(panel, cov_out, 1 - y, r), sems)
+
+    @pl.when(c == 1)
+    def _():
+        copy_all(panel_copies(panel, cost_out, 1 - y, r), sems)
+
+
+def place_far_kernel(
     cov_in,
     cost_in,
     short,
@@ -665,25 +665,11 @@
 
     @pl.when(first)
     def _():
+        copy_all(vectors + panel_copies(panel, cost_out, 1 - y, r), sems)
+
+    @pl.when(c == 1)
+    def _():
         copy_all(vectors + panel_copies(panel, cov_out, 1 - y, r), sems)
-
-    @pl.when(c == 1)
-    def _():
-        copy_all(vectors + panel_copies(panel, cost_out, 1 - y, r), sems)
-
-
-def place_far_kernel(cov_in, cost_in, panel, cov_out, cost_out, sems):
-    del cov_in, cost_in
-    _, y, c = place_of()
-    r = panel.shape[1]
-
-    @pl.when(c == 0)
-    def _():
-        copy_all(panel_copies(panel, cost_out, 1 - y, r), sems)
-
-    @pl.when(c == 1)
-    def _():
-        copy_all(panel_copies(panel, cov_out, 1 - y, r), sems)
 
 
 IN_HBM, IN_VMEM = 0, 1
@@ -778,19 +764,19 @@
         [square(F32)] + [square(BF16)] * 2,
     )
     earlier = later(level1, 2)
-    a01 = kernel(
+    *a01, t = kernel(
         functools.partial(early_kernel, bs),
         vmem(pattern, halves, core_halves),
         vmem(*[half(n, n)] * 4, shape(n, 2 * r)),
     )
     far_core_halves = swap(far_halves, 1)
-    dyn_own, dyn_send, *m2, a2 = kernel(
-        functools.partial(dynamics_kernel, bs),
-        vmem(pattern, far_halves, far_core_halves, *a01),
-        vmem(shape(r, n), shape(r, n), *[half(n, n)] * 4, shape(n, n)),
-        [square(BF16)] * 4 + [square(F32)],
+    dyn_own, dyn_send, a2, *a23 = kernel(
+        functools.partial(rows_kernel, bs),
+        vmem(pattern, far_halves, far_core_halves, t),
+        vmem(shape(r, n), shape(r, n), shape(n, n), *[half(n, n)] * 4),
     )
     dyn_recv = swap(dyn_send, 2)
+    m2 = kernel(product_kernel, vmem(*a01, *a23), vmem(*[half(n, n)] * 4), [square(F32)])
     full, z = kernel(
         ahead_kernel, vmem(level1, *m2), vmem(shape(n, n), shape(n, n)), [square(BF16)] * 2
     )
@@ -814,18 +800,18 @@
     dyn_out, cov_out, cost_out = kernel(
         fill_kernel, vmem(keep, from_core, dyn_own, dyn_recv), hbm(whole, whole, whole), [sems(10)]
     )
+    cov_out, cost_out = kernel(
+        place_chip_kernel,
+        hbm(cov_out, cost_out) + vmem(from_chip),
+        hbm(whole, whole),
+        [sems(4)],
+        {0: 0, 1: 1},
+    )
     cov_out, cost_out, drift_out, eta_out = kernel(
-        place_chip_kernel,
-        hbm(cov_out, cost_out) + vmem(*shorts, from_chip),
+        place_far_kernel,
+        hbm(cov_out, cost_out) + vmem(*shorts, from_far),
         hbm(whole, whole, line, line),
         [pltpu.VMEM((2, elements, r), F32), sems(6)],
-        {0: 0, 1: 1},
-    )
-    cov_out, cost_out = kernel(
-        place_far_kernel,
-        hbm(cov_out, cost_out) + vmem(from_far),
-        hbm(whole, whole),
-        [sems(4)],
         {0: 0, 1: 1},
     )
     return dyn_out, drift_out, cov_out, cost_out, eta_out

time: 79.6 us -> 78.8 us (0.990)
    pallas_call x15 -> x16, Pallas kernels: 14.9 us -> 14.9 us  [kernel(): call(*(pltpu.with_memory_space_constraint(x, kept[where]) if where in kep...]
  transfers between devices with their start and end apart: 18 -> 18, of which waited for: 8 -> 9; matrix products, arithmetic and copies ran while one was open for 0% -> 0% of each run, Pallas kernels for 18% -> 18%
where the time goes in v3:
time: 78.8 us; the launch traced here: 78.5 us
  starting transfers between devices  35.9 us (46%)
  waiting for transfers between devices  26.8 us (34%)
  Pallas kernels  14.9 us (19%)
  between operations  0.85 us (1%)
    ppermute x5, starting transfers between devices, later(): lax.ppermute(value, 'tm', [(i, i + distance) for i in range(tms - distanc...  27 us
    ppermute x13, waiting for transfers between devices, swap(): return lax.ppermute(value, 'col', [(i, i ^ bit) for i in range(cols)])  17.8 us
    pallas_call x16, Pallas kernels, kernel(): call(*(pltpu.with_memory_space_constraint(x, kept[where]) if where in kep...  14.9 us
    ppermute x5, waiting for transfers between devices, later(): lax.ppermute(value, 'tm', [(i, i + distance) for i in range(tms - distanc...  9.01 us
    ppermute x13, starting transfers between devices, swap(): return lax.ppermute(value, 'col', [(i, i ^ bit) for i in range(cols)])  8.95 us
  transfers between devices with their start and end apart: 18, of which 9 were waited for; matrix products, arithmetic and copies ran while one was open for 0% of the time, Pallas kernels for 18%

profile of v3, /device:TPU:0, one launch (start us, length us, event | category | flops | bytes accessed | tf_op | source)
XLA Modules:
  0.0 78.5 jit_solution(695921263670316223)
XLA Ops:
  0.6 5.0 %collective-permute-start.5 = (f32[2,192,128]{2,1,0:T(8,128)}, f32[2,192,128]{2,1,0:T(8,128)S(1)}, u32[]{:S(2)}, u32[]{:S(2)}) collective-permute-start(f32[2,192,128]{2,1,0:T(8,128)} %bitcast.1), channel_id=1, source_target_pairs={{0,4},{4,8},{8,12},{12,16},{16,20},{20,24},{24,28},{1,5},{5,9},{9,... | collective-permute-start | bytes 589832 | tf_op jit(solution)/shard_map/ppermute | solution.py:712
  5.7 1.3 %shard_map.101 = (f32[136,384]{1,0:T(8,128)S(1)}, f32[136,256]{1,0:T(8,128)S(1)}, f32[136,128]{1,0:T(8,128)S(1)}, f32[128,512]{1,0:T(8,128)S(1)}, f32[8,128]{1,0:T(8,128)S(1)}) custom-call(f32[2,128,512]{2,1,0:T(8,128)} %cov.1, f32[2,128,512]{2,1,0:T(8,128)} %cost.1, f32[2,128]{1,0:T(2,128)} %drift.1, f32[2,128]{1,0:T(2,128)} %eta.1), custom_call_target="tpu_custom_call" | custom-call | tf_op jit(solution)/shard_map/pallas_call | solution.py:695
  7.0 3.1 %collective-permute-done.5.before = f32[2,192,128]{2,1,0:T(8,128)S(1)} collective-permute-done((f32[2,192,128]{2,1,0:T(8,128)}, f32[2,192,128]{2,1,0:T(8,128)S(1)}, u32[]{:S(2)}, u32[]{:S(2)}) %collective-permute-start.5) | collective-permute-done | bytes 196640 | tf_op jit(solution)/shard_map/ppermute | solution.py:712
  10.1 1.6 %collective-permute-start.6 = (f32[384,128]{1,0:T(8,128)S(1)}, f32[384,128]{1,0:T(8,128)S(1)}, u32[]{:S(2)}, u32[]{:S(2)}) collective-permute-start(f32[384,128]{1,0:T(8,128)S(1)} %shard_map.104), channel_id=1, source_target_pairs={{0,2},{1,3},{2,0},{3,1},{4,6},{5,7},{6,4},{7,5},{8,10},{9,11},{10,... | collective-permute-start | bytes 589832 | tf_op jit(solution)/shard_map/ppermute | solution.py:709
  11.7 4.3 %collective-permute-done.6.other = f32[384,128]{1,0:T(8,128)S(1)} collective-permute-done((f32[384,128]{1,0:T(8,128)S(1)}, f32[384,128]{1,0:T(8,128)S(1)}, u32[]{:S(2)}, u32[]{:S(2)}) %collective-permute-start.6) | collective-permute-done | bytes 196640 | tf_op jit(solution)/shard_map/ppermute | solution.py:709
  16.1 4.3 %collective-permute-start.3 = (f32[128,768]{1,0:T(8,128)S(1)}, f32[128,768]{1,0:T(8,128)S(1)}, u32[]{:S(2)}, u32[]{:S(2)}) collective-permute-start(f32[128,768]{1,0:T(8,128)S(1)} %shard_map.102.own_near), channel_id=1, source_target_pairs={{0,4},{4,8},{8,12},{12,16},{16,20},{20,24},{24,28},{1,5},{5,9},{9,... | collective-permute-start | bytes 1179656 | tf_op jit(solution)/shard_map/ppermute | solution.py:712
  20.5 1.6 %collective-permute-start.1 = (f32[136,256]{1,0:T(8,128)S(1)}, f32[136,256]{1,0:T(8,128)S(1)}, u32[]{:S(2)}, u32[]{:S(2)}) collective-permute-start(f32[136,256]{1,0:T(8,128)S(1)} %get-tuple-element.51), channel_id=1, source_target_pairs={{0,2},{1,3},{2,0},{3,1},{4,6},{5,7},{6,4},{7,5},{8,10},{9,11},{10,... | collective-permute-start | bytes 417800 | tf_op jit(solution)/shard_map/ppermute | solution.py:709
  22.0 3.5 %collective-permute-start.9 = (f32[768,128]{1,0:T(8,128)S(1)}, f32[768,128]{1,0:T(8,128)S(1)}, u32[]{:S(2)}, u32[]{:S(2)}) collective-permute-start(f32[768,128]{1,0:T(8,128)S(1)} %shard_map.105.halves), channel_id=1, source_target_pairs={{0,8},{4,12},{8,16},{12,20},{16,24},{20,28},{1,9},{5,13},{9,17},{1... | collective-permute-start | bytes 1179656 | tf_op jit(solution)/shard_map/ppermute | solution.py:712
  25.6 4.3 %collective-permute-done.2.from_far = f32[136,128]{1,0:T(8,128)S(1)} collective-permute-done((f32[136,128]{1,0:T(8,128)S(1)}, f32[136,128]{1,0:T(8,128)S(1)}, u32[]{:S(2)}, u32[]{:S(2)}) %collective-permute-start.2) | collective-permute-done | bytes 69664 | tf_op jit(solution)/shard_map/ppermute | solution.py:709
  29.9 4.4 %collective-permute-start.4 = (f32[136,256]{1,0:T(8,128)S(1)}, f32[136,256]{1,0:T(8,128)S(1)}, u32[]{:S(2)}, u32[]{:S(2)}) collective-permute-start(f32[136,256]{1,0:T(8,128)S(1)} %shard_map.103.own_far), channel_id=1, source_target_pairs={{0,4},{4,8},{8,12},{12,16},{16,20},{20,24},{24,28},{1,5},{5,9},{9,... | collective-permute-start | bytes 417800 | tf_op jit(solution)/shard_map/ppermute | solution.py:712
  35.3 2.0 %collective-permute-done.4.far = f32[136,256]{1,0:T(8,128)S(1)} collective-permute-done((f32[136,256]{1,0:T(8,128)S(1)}, f32[136,256]{1,0:T(8,128)S(1)}, u32[]{:S(2)}, u32[]{:S(2)}) %collective-permute-start.4) | collective-permute-done | bytes 139296 | tf_op jit(solution)/shard_map/ppermute | solution.py:712
  37.3 2.0 %shard_map.107.own = f32[264,512]{1,0:T(8,128)S(1)} custom-call(f32[128,768]{1,0:T(8,128)S(1)} %shard_map.102.own_near, f32[136,256]{1,0:T(8,128)S(1)} %shard_map.103.own_far, f32[128,768]{1,0:T(8,128)S(1)} %collective-permute-done.3.near, f32[136,256]{1,0:T(8,128)S(1)} %collective-permute-done.4.far, bf16[512,512]{1,0:T(8,128)(2,1)S(1)} %get-tuple-element.53.mh, ...), custom_call_target="tpu_custom_call" | custom-call | tf_op jit(solution)/shard_map/pallas_call | solution.py:695
  39.3 9.8 %collective-permute-start.8 = (f32[264,512]{1,0:T(8,128)S(1)}, f32[264,512]{1,0:T(8,128)S(1)}, u32[]{:S(2)}, u32[]{:S(2)}) collective-permute-start(f32[264,512]{1,0:T(8,128)S(1)} %shard_map.107.own), channel_id=1, source_target_pairs={{0,8},{4,12},{8,16},{12,20},{16,24},{20,28},{1,9},{5,13},{9,17},{1... | collective-permute-start | bytes 1622024 | tf_op jit(solution)/shard_map/ppermute | solution.py:712
  49.2 1.4 %shard_map.108 = (bf16[512,512]{1,0:T(8,128)(2,1)S(1)}, bf16[512,512]{1,0:T(8,128)(2,1)S(1)}, bf16[512,512]{1,0:T(8,128)(2,1)S(1)}, bf16[512,512]{1,0:T(8,128)(2,1)S(1)}, f32[512,256]{1,0:T(8,128)S(1)}) custom-call(s32[8,3]{1,0:T(8,128)S(1)} %copy.15.pattern, f32[768,128]{1,0:T(8,128)S(1)} %shard_map.105.halves, ...), custom_call_target="tpu_custom_call" | custom-call | tf_op jit(solution)/shard_map/pallas_call | solution.py:695
  50.9 2.5 %shard_map.109 = (f32[128,512]{1,0:T(8,128)S(1)}, f32[128,512]{1,0:T(8,128)S(1)}, f32[512,512]{1,0:T(8,128)S(1)}, bf16[512,512]{1,0:T(8,128)(2,1)S(1)}, bf16[512...) custom-call(s32[8,3]{1,0:T(8,128)S(1)} %copy.15.pattern, ...), custom_call_target="tpu_custom_call" | custom-call | tf_op jit(solution)/shard_map/pallas_call | solution.py:695
  53.5 1.6 %collective-permute-start.12 = (f32[128,512]{1,0:T(8,128)S(1)}, f32[128,512]{1,0:T(8,128)S(1)}, u32[]{:S(2)}, u32[]{:S(2)}) collective-permute-start(f32[128,512]{1,0:T(8,128)S(1)} %get-tuple-element.78), channel_id=1, source_target_pairs={{0,2},{1,3},{2,0},{3,1},{4,6},{5,7},{6,4},{7,5},{8,10},{9,11},{10,... | collective-permute-start | bytes 786440 | tf_op jit(solution)/shard_map/ppermute | solution.py:709
  55.0 1.2 %shard_map.110 = (bf16[512,512]{1,0:T(8,128)(2,1)S(1)}, bf16[512,512]{1,0:T(8,128)(2,1)S(1)}, bf16[512,512]{1,0:T(8,128)(2,1)S(1)}, bf16[512,512]{1,0:T(8,128)(2,1)S(1)}) custom-call(bf16[512,512]{1,0:T(8,128)(2,1)S(1)} %get-tuple-element.57.a0h, bf16[512,512]{1,0:T(8,128)(2,1)S(1)} %get-tuple-element.58.a0l, bf16[512,512]{1,0:T(8,128)(2,1)S(1)} %get-tuple-element.59.a1h, ...), custom_call_target="tpu_custom_call" | custom-call | tf_op jit(solution)/shard_map/pallas_call | solution.py:695
  56.5 3.9 %collective-permute-done.8.earlier = f32[264,512]{1,0:T(8,128)S(1)} collective-permute-done((f32[264,512]{1,0:T(8,128)S(1)}, f32[264,512]{1,0:T(8,128)S(1)}, u32[]{:S(2)}, u32[]{:S(2)}) %collective-permute-start.8) | collective-permute-done | bytes 540704 | tf_op jit(solution)/shard_map/ppermute | solution.py:712
  60.4 1.6 %shard_map.112 = (f32[512,128]{1,0:T(8,128)S(1)}, f32[512,128]{1,0:T(8,128)S(1)}, bf16[512,512]{1,0:T(8,128)(2,1)S(1)}, bf16[512,512]{1,0:T(8,128)(2,1)S(1)}) custom-call(f32[264,512]{1,0:T(8,128)S(1)} %shard_map.107.own, f32[264,512]{1,0:T(8,128)S(1)} %collective-permute-done.8.earlier, bf16[512,512]{1,0:T(8,128)(2,1)S(1)} %get-tuple-element.66.mh, ...), custom_call_target="tpu_custom_call" | custom-call | tf_op jit(solution)/shard_map/pallas_call | solution.py:695
  62.0 1.1 %shard_map.113 = (f32[512,128]{1,0:T(8,128)S(1)}, f32[512,128]{1,0:T(8,128)S(1)}, f32[8,128]{1,0:T(8,128)S(1)}) custom-call(f32[264,512]{1,0:T(8,128)S(1)} %shard_map.107.own, f32[264,512]{1,0:T(8,128)S(1)} %collective-permute-done.8.earlier, bf16[512,512]{1,0:T(8,128)(2,1)S(1)} %get-tuple-element.66.mh, bf16[512,512]{1,0:T(8,128)(2,1)S(1)} %get-tuple-element.67.ml, ...), custom_call_target="tpu_custom_call" | custom-call | tf_op jit(solution)/shard_map/pallas_call | solution.py:695
  63.3 1.6 %collective-permute-start.13 = (f32[512,128]{1,0:T(8,128)S(1)}, f32[512,128]{1,0:T(8,128)S(1)}, u32[]{:S(2)}, u32[]{:S(2)}) collective-permute-start(f32[512,128]{1,0:T(8,128)S(1)} %get-tuple-element.82), channel_id=1, source_target_pairs={{0,2},{1,3},{2,0},{3,1},{4,6},{5,7},{6,4},{7,5},{8,10},{9,11},{10,... | collective-permute-start | bytes 786440 | tf_op jit(solution)/shard_map/ppermute | solution.py:709
  65.1 1.5 %collective-permute-start.16 = (f32[8,128]{1,0:T(8,128)S(1)}, f32[8,128]{1,0:T(8,128)S(1)}, u32[]{:S(2)}, u32[]{:S(2)}) collective-permute-start(f32[8,128]{1,0:T(8,128)S(1)} %get-tuple-element.85.short), channel_id=1, source_target_pairs={{0,3},{1,2},{2,1},{3,0},{4,7},{5,6},{6,5},{7,4},{8,11},{9,10},{10,... | collective-permute-start | bytes 12296 | tf_op jit(solution)/shard_map/ppermute | solution.py:709
  68.1 4.4 %collective-permute-done.13.panel = f32[512,128]{1,0:T(8,128)S(1)} collective-permute-done((f32[512,128]{1,0:T(8,128)S(1)}, f32[512,128]{1,0:T(8,128)S(1)}, u32[]{:S(2)}, u32[]{:S(2)}) %collective-permute-start.13) | collective-permute-done | bytes 262176 | tf_op jit(solution)/shard_map/ppermute | solution.py:709
  73.2 3.9 %collective-permute-done.16.far_short = f32[8,128]{1,0:T(8,128)S(1)} collective-permute-done((f32[8,128]{1,0:T(8,128)S(1)}, f32[8,128]{1,0:T(8,128)S(1)}, u32[]{:S(2)}, u32[]{:S(2)}) %collective-permute-start.16) | collective-permute-done | bytes 4128 | tf_op jit(solution)/shard_map/ppermute | solution.py:709
  (33 shorter events, 6.0 us)
Async XLA Ops:
  0.6 9.5 %copy-start = (f32[2,128,192]{1,2,0:T(8,128)S(1)}, f32[2,128,192]{1,2,0:T(8,128)}, u32[]{:S(2)}) copy-start(f32[2,128,192]{1,2,0:T(8,128)} %param.6) | copy-start | bytes 589828
  0.6 9.5 %collective-permute-start.5 = (f32[2,192,128]{2,1,0:T(8,128)}, f32[2,192,128]{2,1,0:T(8,128)S(1)}, u32[]{:S(2)}, u32[]{:S(2)}) collective-permute-start(f32[2,192,128]{2,1,0:T(8,128)} %bitcast.1), channel_id=1, source_target_pairs={{0,4},{4,8},{8,12},{12,16},{16,20},{20,24},{24,28},{1,5},{5,9},{9,... | collective-permute-start | bytes 589832 | tf_op jit(solution)/shard_map/ppermute | solution.py:712
  6.9 9.2 %collective-permute-start = (f32[136,384]{1,0:T(8,128)S(1)}, f32[136,384]{1,0:T(8,128)S(1)}, u32[]{:S(2)}, u32[]{:S(2)}) collective-permute-start(f32[136,384]{1,0:T(8,128)S(1)} %get-tuple-element.49), channel_id=1, source_target_pairs={{0,1},{1,0},{2,3},{3,2},{4,5},{5,4},{6,7},{7,6},{8,9},{9,8},{10,11... | collective-permute-start | bytes 626696 | tf_op jit(solution)/shard_map/ppermute | solution.py:709
  10.1 5.9 %collective-permute-start.6 = (f32[384,128]{1,0:T(8,128)S(1)}, f32[384,128]{1,0:T(8,128)S(1)}, u32[]{:S(2)}, u32[]{:S(2)}) collective-permute-start(f32[384,128]{1,0:T(8,128)S(1)} %shard_map.104), channel_id=1, source_target_pairs={{0,2},{1,3},{2,0},{3,1},{4,6},{5,7},{6,4},{7,5},{8,10},{9,11},{10,... | collective-permute-start | bytes 589832 | tf_op jit(solution)/shard_map/ppermute | solution.py:709
  16.0 18.4 %collective-permute-start.7 = (f32[768,128]{1,0:T(8,128)S(1)}, f32[768,128]{1,0:T(8,128)S(1)}, u32[]{:S(2)}, u32[]{:S(2)}) collective-permute-start(f32[768,128]{1,0:T(8,128)S(1)} %shard_map.105.halves), channel_id=1, source_target_pairs={{0,1},{1,0},{2,3},{3,2},{4,5},{5,4},{6,7},{7,6},{8,9},{9,8},{10,11... | collective-permute-start | bytes 1179656 | tf_op jit(solution)/shard_map/ppermute | solution.py:709
  16.1 21.2 %collective-permute-start.3 = (f32[128,768]{1,0:T(8,128)S(1)}, f32[128,768]{1,0:T(8,128)S(1)}, u32[]{:S(2)}, u32[]{:S(2)}) collective-permute-start(f32[128,768]{1,0:T(8,128)S(1)} %shard_map.102.own_near), channel_id=1, source_target_pairs={{0,4},{4,8},{8,12},{12,16},{16,20},{20,24},{24,28},{1,5},{5,9},{9,... | collective-permute-start | bytes 1179656 | tf_op jit(solution)/shard_map/ppermute | solution.py:712
  20.5 9.4 %collective-permute-start.1 = (f32[136,256]{1,0:T(8,128)S(1)}, f32[136,256]{1,0:T(8,128)S(1)}, u32[]{:S(2)}, u32[]{:S(2)}) collective-permute-start(f32[136,256]{1,0:T(8,128)S(1)} %get-tuple-element.51), channel_id=1, source_target_pairs={{0,2},{1,3},{2,0},{3,1},{4,6},{5,7},{6,4},{7,5},{8,10},{9,11},{10,... | collective-permute-start | bytes 417800 | tf_op jit(solution)/shard_map/ppermute | solution.py:709
  22.0 27.1 %collective-permute-start.9 = (f32[768,128]{1,0:T(8,128)S(1)}, f32[768,128]{1,0:T(8,128)S(1)}, u32[]{:S(2)}, u32[]{:S(2)}) collective-permute-start(f32[768,128]{1,0:T(8,128)S(1)} %shard_map.105.halves), channel_id=1, source_target_pairs={{0,8},{4,12},{8,16},{12,20},{16,24},{20,28},{1,9},{5,13},{9,17},{1... | collective-permute-start | bytes 1179656 | tf_op jit(solution)/shard_map/ppermute | solution.py:712
  25.5 4.4 %collective-permute-start.2 = (f32[136,128]{1,0:T(8,128)S(1)}, f32[136,128]{1,0:T(8,128)S(1)}, u32[]{:S(2)}, u32[]{:S(2)}) collective-permute-start(f32[136,128]{1,0:T(8,128)S(1)} %get-tuple-element.52), channel_id=1, source_target_pairs={{0,3},{1,2},{2,1},{3,0},{4,7},{5,6},{6,5},{7,4},{8,11},{9,10},{10,... | collective-permute-start | bytes 208904 | tf_op jit(solution)/shard_map/ppermute | solution.py:709
  29.9 4.4 %copy-start.1 = (s32[8,3]{0,1:T(4,128)S(1)}, s32[8,3]{0,1:T(4,128)}, u32[]{:S(2)}) copy-start(s32[8,3]{0,1:T(4,128)} %param.7) | copy-start | bytes 292
  29.9 7.4 %collective-permute-start.4 = (f32[136,256]{1,0:T(8,128)S(1)}, f32[136,256]{1,0:T(8,128)S(1)}, u32[]{:S(2)}, u32[]{:S(2)}) collective-permute-start(f32[136,256]{1,0:T(8,128)S(1)} %shard_map.103.own_far), channel_id=1, source_target_pairs={{0,4},{4,8},{8,12},{12,16},{16,20},{20,24},{24,28},{1,5},{5,9},{9,... | collective-permute-start | bytes 417800 | tf_op jit(solution)/shard_map/ppermute | solution.py:712
  39.3 21.1 %collective-permute-start.8 = (f32[264,512]{1,0:T(8,128)S(1)}, f32[264,512]{1,0:T(8,128)S(1)}, u32[]{:S(2)}, u32[]{:S(2)}) collective-permute-start(f32[264,512]{1,0:T(8,128)S(1)} %shard_map.107.own), channel_id=1, source_target_pairs={{0,8},{4,12},{8,16},{12,20},{16,24},{20,28},{1,9},{5,13},{9,17},{1... | collective-permute-start | bytes 1622024 | tf_op jit(solution)/shard_map/ppermute | solution.py:712
  49.1 1.8 %collective-permute-start.10 = (f32[768,128]{1,0:T(8,128)S(1)}, f32[768,128]{1,0:T(8,128)S(1)}, u32[]{:S(2)}, u32[]{:S(2)}) collective-permute-start(f32[768,128]{1,0:T(8,128)S(1)} %collective-permute-done.9.halves), channel_id=1, source_target_pairs={{0,1},{1,0},{2,3},{3,2},{4,5},{5,4},{6,7},{7,6},{8,9},{9,8},{10,11... | collective-permute-start | bytes 1179656 | tf_op jit(solution)/shard_map/ppermute | solution.py:709
  53.5 13.1 %collective-permute-start.12 = (f32[128,512]{1,0:T(8,128)S(1)}, f32[128,512]{1,0:T(8,128)S(1)}, u32[]{:S(2)}, u32[]{:S(2)}) collective-permute-start(f32[128,512]{1,0:T(8,128)S(1)} %get-tuple-element.78), channel_id=1, source_target_pairs={{0,2},{1,3},{2,0},{3,1},{4,6},{5,7},{6,4},{7,5},{8,10},{9,11},{10,... | collective-permute-start | bytes 786440 | tf_op jit(solution)/shard_map/ppermute | solution.py:709
  63.2 3.9 %collective-permute-start.11 = (f32[512,128]{1,0:T(8,128)S(1)}, f32[512,128]{1,0:T(8,128)S(1)}, u32[]{:S(2)}, u32[]{:S(2)}) collective-permute-start(f32[512,128]{1,0:T(8,128)S(1)} %get-tuple-element.76), channel_id=1, source_target_pairs={{0,1},{1,0},{2,3},{3,2},{4,5},{5,4},{6,7},{7,6},{8,9},{9,8},{10,11... | collective-permute-start | bytes 786440 | tf_op jit(solution)/shard_map/ppermute | solution.py:709
  63.3 9.2 %collective-permute-start.13 = (f32[512,128]{1,0:T(8,128)S(1)}, f32[512,128]{1,0:T(8,128)S(1)}, u32[]{:S(2)}, u32[]{:S(2)}) collective-permute-start(f32[512,128]{1,0:T(8,128)S(1)} %get-tuple-element.82), channel_id=1, source_target_pairs={{0,2},{1,3},{2,0},{3,1},{4,6},{5,7},{6,4},{7,5},{8,10},{9,11},{10,... | collective-permute-start | bytes 786440 | tf_op jit(solution)/shard_map/ppermute | solution.py:709
  64.8 12.9 %collective-permute-start.17 = (f32[512,128]{1,0:T(8,128)S(1)}, f32[512,128]{1,0:T(8,128)S(1)}, u32[]{:S(2)}, u32[]{:S(2)}) collective-permute-start(f32[512,128]{1,0:T(8,128)S(1)} %get-tuple-element.86), channel_id=1, source_target_pairs={{0,3},{1,2},{2,1},{3,0},{4,7},{5,6},{6,5},{7,4},{8,11},{9,10},{10,... | collective-permute-start | bytes 786440 | tf_op jit(solution)/shard_map/ppermute | solution.py:709
  65.1 12.0 %collective-permute-start.16 = (f32[8,128]{1,0:T(8,128)S(1)}, f32[8,128]{1,0:T(8,128)S(1)}, u32[]{:S(2)}, u32[]{:S(2)}) collective-permute-start(f32[8,128]{1,0:T(8,128)S(1)} %get-tuple-element.85.short), channel_id=1, source_target_pairs={{0,3},{1,2},{2,1},{3,0},{4,7},{5,6},{6,5},{7,4},{8,11},{9,10},{10,... | collective-permute-start | bytes 12296 | tf_op jit(solution)/shard_map/ppermute | solution.py:709
  66.6 11.2 %collective-permute-start.15 = (f32[8,128]{1,0:T(8,128)S(1)}, f32[8,128]{1,0:T(8,128)S(1)}, u32[]{:S(2)}, u32[]{:S(2)}) collective-permute-start(f32[8,128]{1,0:T(8,128)S(1)} %get-tuple-element.85.short), channel_id=1, source_target_pairs={{0,2},{1,3},{2,0},{3,1},{4,6},{5,7},{6,4},{7,5},{8,10},{9,11},{10,... | collective-permute-start | bytes 12296 | tf_op jit(solution)/shard_map/ppermute | solution.py:709
  67.1 10.7 %collective-permute-start.14 = (f32[8,128]{1,0:T(8,128)S(1)}, f32[8,128]{1,0:T(8,128)S(1)}, u32[]{:S(2)}, u32[]{:S(2)}) collective-permute-start(f32[8,128]{1,0:T(8,128)S(1)} %get-tuple-element.85.short), channel_id=1, source_target_pairs={{0,1},{1,0},{2,3},{3,2},{4,5},{5,4},{6,7},{7,6},{8,9},{9,8},{10,11... | collective-permute-start | bytes 12296 | tf_op jit(solution)/shard_map/ppermute | solution.py:709

commit v4 on v3

--- a/solution.py
+++ b/solution.py
@@ -535,9 +535,13 @@
         ref[lanes(q ^ j, r), :] = value[:, j * r : (j + 1) * r]
 
 
-def level2_kernel(own, earlier, mh, ml, th, tl, full, z, to_chip, to_far, uh, ul, xh, xl, rest):
-    q, _, c = place_of()
+CROSSING = ((2, 0), (2, 1), (2, 3))
+
+
+def level2_kernel(own, earlier, mh, ml, th, tl, full, z, to_chip, uh, ul, xh, xl, rest):
+    c = place_of()[2]
     r = own.shape[1] // 4
+    two, three = slice(2 * r, 3 * r), slice(3 * r, 4 * r)
 
     @pl.when(c == 0)
     def _():
@@ -548,34 +552,70 @@
         hi, lo = split(dot3(xh[...], xl[...], mh[...], ml[...]))
         uh[...] = hi
         ul[...] = lo
-        rest[...] = dot3(th[2 * r :, :], tl[2 * r :, :], hi, lo) + full[2 * r :, :]
+        rest[:, 2 * r :] = dot3(th[2 * r :, :], tl[2 * r :, :], hi[:, 2 * r :], lo[:, 2 * r :])
+        rest[0:r, 0 : 2 * r] = dot3(th[two, :], tl[two, :], hi[:, 0 : 2 * r], lo[:, 0 : 2 * r])
+        rest[:, 2 * r :] = rest[:, 2 * r :] + full[2 * r :, 2 * r :]
+        rest[0:r, 0 : 2 * r] = rest[0:r, 0 : 2 * r] + full[two, 0 : 2 * r]
 
     @pl.when(c == 1)
     def _():
         def put(i, j, block):
-            rows = slice((i - 2) * r, (i - 1) * r)
-            cols = slice(j * r, (j + 1) * r)
-            rest[rows, cols] = z[i * r : (i + 1) * r, cols] + block
+            if (i, j) in CROSSING or i == j:
+                rows = slice((i - 2) * r, (i - 1) * r)
+                cols = slice(j * r, (j + 1) * r)
+                rest[rows, cols] = z[i * r : (i + 1) * r, cols] + block
 
         spread(earlier, r, put, rows=(2, 3))
 
-    put_rows(to_chip, rest[0:r, :], q, r)
-    put_rows(to_far, rest[r : 2 * r, :], q, r)
-
-
-def rest_kernel(
-    own, earlier, mh, ml, th, tl, a2, full, z, uh, ul, keep, to_core, short, vec, rest
+    z33 = rest[r : 2 * r, three]
+    to_chip[0:r, :] = fold(rest[0:r, two], z33, r)
+    for at, (_, j) in enumerate(CROSSING):
+        to_chip[(at + 1) * r : (at + 2) * r, :] = rest[0:r, j * r : (j + 1) * r]
+    to_chip[4 * r :, :] = jnp.broadcast_to(diagonal(z33, r), (8, r))
+
+
+def far_rows_kernel(
+    own, earlier, mh, ml, th, tl, a2, full, z, uh, ul, to_far, short, vec, rest
 ):
-    q, _, c = place_of()
+    c = place_of()[2]
     r = own.shape[1] // 4
     base = 2 * r
+    three = slice(3 * r, 4 * r)
     b1 = earlier[base + 1 : base + 2, :] + row_times(earlier[base + 3 : base + 4, :], a2[...], r)
 
     @pl.when(c == 0)
     def _():
-        rest[...] = dot3(th[0 : 2 * r, :], tl[0 : 2 * r, :], uh[...], ul[...]) + full[0 : 2 * r, :]
+        value = dot3(th[three, :], tl[three, :], uh[:, 0 : 2 * r], ul[:, 0 : 2 * r])
+        rest[...] = value + full[three, 0 : 2 * r]
         vec[0:1, :] = b1
         vec[1:2, :] = own[base + 2 : base + 3, :]
+
+    @pl.when(c == 1)
+    def _():
+        def put(i, j, block):
+            if j < 2:
+                cols = slice(j * r, (j + 1) * r)
+                rest[:, cols] = z[three, cols] + block
+
+        spread(earlier, r, put, rows=(3,))
+        vec[0:1, :] = own[base + 2 : base + 3, :] + row_times(b1, full[...], r)
+        vec[1:2, :] = earlier[base + 2 : base + 3, :]
+
+    to_far[0:r, :] = rest[:, 0:r]
+    to_far[r : 2 * r, :] = rest[:, r : 2 * r]
+    out = vec[1:2, :] + row_times(vec[0:1, :], mh[...].astype(F32) + ml[...].astype(F32), r)
+    for i in range(4):
+        short[i : i + 1, :] = out[:, i * r : (i + 1) * r]
+    short[4:8, :] = jnp.zeros((4, r), F32)
+
+
+def rest_kernel(earlier, th, tl, full, z, uh, ul, keep, to_core, rest):
+    q, _, c = place_of()
+    r = earlier.shape[1] // 4
+
+    @pl.when(c == 0)
+    def _():
+        rest[...] = dot3(th[0 : 2 * r, :], tl[0 : 2 * r, :], uh[...], ul[...]) + full[0 : 2 * r, :]
 
     @pl.when(c == 1)
     def _():
@@ -585,15 +625,17 @@
             rest[rows, cols] = z[rows, cols] + block
 
         spread(earlier, r, put, rows=(0, 1))
-        vec[0:1, :] = own[base + 2 : base + 3, :] + row_times(b1, full[...], r)
-        vec[1:2, :] = earlier[base + 2 : base + 3, :]
-
-    out = vec[1:2, :] + row_times(vec[0:1, :], mh[...].astype(F32) + ml[...].astype(F32), r)
+
     put_rows(keep, rest[0:r, :], q, r)
     put_rows(to_core, rest[r : 2 * r, :], q, r)
-    for i in range(4):
-        short[i : i + 1, :] = out[:, i * r : (i + 1) * r]
-    short[4:8, :] = jnp.zeros((4, r), F32)
+
+
+def turn_kernel(from_chip, diagonal_block, mirrored):
+    r = diagonal_block.shape[0]
+    first, second = unfold(from_chip[0:r, :], from_chip[4 * r : 4 * r + 1, :], r)
+    diagonal_block[...] = first
+    mirrored[0:r, :] = from_chip[3 * r : 4 * r, :].T
+    mirrored[r : 2 * r, :] = second
 
 
 def panel_copies(panel, target, element, r):
@@ -620,18 +662,25 @@
         )
 
 
-def place_chip_kernel(cov_in, cost_in, panel, cov_out, cost_out, sems):
+def block_copies(blocks, target, element, r):
+    return [(source, target.at[element, :, lanes(at, r)]) for source, at in blocks]
+
+
+def place_chip_kernel(cov_in, cost_in, diagonal_block, panel, cov_out, cost_out, sems):
     del cov_in, cost_in
-    _, y, c = place_of()
+    q, y, c = place_of()
     r = panel.shape[1]
+    blocks = [(diagonal_block, q)] + [
+        (panel.at[pl.ds(at * r, r), :], q ^ bit) for at, bit in ((1, 2), (2, 3), (3, 1))
+    ]
 
     @pl.when(c == 0)
     def _():
-        copy_all(panel_copies(panel, cov_out, 1 - y, r), sems)
+        copy_all(block_copies(blocks, cov_out, 1 - y, r), sems)
 
     @pl.when(c == 1)
     def _():
-        copy_all(panel_copies(panel, cost_out, 1 - y, r), sems)
+        copy_all(block_copies(blocks, cost_out, 1 - y, r), sems)
 
 
 def place_far_kernel(
@@ -641,6 +690,7 @@
     core_short,
     chip_short,
     far_short,
+    mirrored,
     panel,
     cov_out,
     cost_out,
@@ -650,7 +700,7 @@
     sems,
 ):
     del cov_in, cost_in
-    _, y, c = place_of()
+    q, y, c = place_of()
     first = c == 0
     r = short.shape[1]
     for at, (one, two, three, four) in enumerate(
@@ -662,14 +712,21 @@
         lines[at, pl.ds(y, 1), :] = jnp.where(first, one, two)
         lines[at, pl.ds(1 - y, 1), :] = jnp.where(first, three, four)
     vectors = [(lines.at[0], drift_out), (lines.at[1], eta_out)]
+    near, far = pl.ds(0, r), pl.ds(r, r)
+    blocks = [
+        (panel.at[near, :], q ^ 3),
+        (panel.at[far, :], q ^ 2),
+        (mirrored.at[near, :], q ^ 1),
+        (mirrored.at[far, :], q),
+    ]
 
     @pl.when(first)
     def _():
-        copy_all(vectors + panel_copies(panel, cost_out, 1 - y, r), sems)
+        copy_all(vectors + block_copies(blocks, cost_out, 1 - y, r), sems)
 
     @pl.when(c == 1)
     def _():
-        copy_all(vectors + panel_copies(panel, cov_out, 1 - y, r), sems)
+        copy_all(vectors + block_copies(blocks, cov_out, 1 - y, r), sems)
 
 
 IN_HBM, IN_VMEM = 0, 1
@@ -780,36 +837,47 @@
     full, z = kernel(
         ahead_kernel, vmem(level1, *m2), vmem(shape(n, n), shape(n, n)), [square(BF16)] * 2
     )
-    to_chip, to_far, *u = kernel(
+    to_chip, *u = kernel(
         level2_kernel,
         vmem(level1, earlier, *m2, full, z),
-        vmem(shape(n, r), shape(n, r), half(n, n), half(n, n)),
+        vmem(shape(n + 8, r), half(n, n), half(n, n)),
         [square(BF16)] * 2 + [pltpu.VMEM((2 * r, n), F32)],
     )
     from_chip = swap(to_chip, 2)
+    to_far, short = kernel(
+        far_rows_kernel,
+        vmem(level1, earlier, *m2, a2, full, z, *u),
+        vmem(shape(2 * r, r), shape(8, r)),
+        [pltpu.VMEM((8, n), F32), pltpu.VMEM((r, 2 * r), F32)],
+    )
+    chip_short, far_short = swap(short, 2), swap(short, 3)
     from_far = swap(to_far, 3)
-    keep, to_core, short = kernel(
+    keep, to_core = kernel(
         rest_kernel,
-        vmem(level1, earlier, *m2, a2, full, z, *u),
-        vmem(shape(n, r), shape(n, r), shape(8, r)),
-        [pltpu.VMEM((8, n), F32), pltpu.VMEM((2 * r, n), F32)],
+        vmem(earlier, *m2[2:], full, z, *u),
+        vmem(shape(n, r), shape(n, r)),
+        [pltpu.VMEM((2 * r, n), F32)],
     )
     from_core = swap(to_core, 1)
-    shorts = (short, swap(short, 1), swap(short, 2), swap(short, 3))
+    shorts = (short, swap(short, 1), chip_short, far_short)
+    diagonal_block, mirrored = kernel(
+        turn_kernel, vmem(from_chip), vmem(shape(r, r), shape(2 * r, r))
+    )
+    mirrored = swap(mirrored, 1)
     whole, line = shape(elements, r, n), shape(elements, r)
     dyn_out, cov_out, cost_out = kernel(
         fill_kernel, vmem(keep, from_core, dyn_own, dyn_recv), hbm(whole, whole, whole), [sems(10)]
     )
     cov_out, cost_out = kernel(
         place_chip_kernel,
-        hbm(cov_out, cost_out) + vmem(from_chip),
+        hbm(cov_out, cost_out) + vmem(diagonal_block, from_chip),
         hbm(whole, whole),
         [sems(4)],
         {0: 0, 1: 1},
     )
     cov_out, cost_out, drift_out, eta_out = kernel(
         place_far_kernel,
-        hbm(cov_out, cost_out) + vmem(*shorts, from_far),
+        hbm(cov_out, cost_out) + vmem(*shorts, mirrored, from_far),
         hbm(whole, whole, line, line),
         [pltpu.VMEM((2, elements, r), F32), sems(6)],
         {0: 0, 1: 1},

time: 78.8 us -> 80.3 us (1.019)
    ppermute x5, waiting for transfers between devices: 9.01 us -> 10.6 us  [later(): lax.ppermute(value, 'tm', [(i, i + distance) for i in range(tms - distanc...]
    ppermute x13 -> x14, waiting for transfers between devices: 17.8 us -> 16.7 us  [swap(): return lax.ppermute(value, 'col', [(i, i ^ bit) for i in range(cols)])]
    ppermute x13 -> x14, starting transfers between devices: 8.95 us -> 9.43 us  [swap(): return lax.ppermute(value, 'col', [(i, i ^ bit) for i in range(cols)])]
    pallas_call x16 -> x18, Pallas kernels: 14.9 us -> 15.3 us  [kernel(): call(*(pltpu.with_memory_space_constraint(x, kept[where]) if where in kep...]
  transfers between devices with their start and end apart: 18 -> 19, of which waited for: 9 -> 10; matrix products, arithmetic and copies ran while one was open for 0% -> 0% of each run, Pallas kernels for 18% -> 16%
where the time goes in v4:
time: 80.3 us; the launch traced here: 80.1 us
  starting transfers between devices  36.4 us (45%)
  waiting for transfers between devices  27.3 us (34%)
  Pallas kernels  15.3 us (19%)
  between operations  0.87 us (1%)
    ppermute x5, starting transfers between devices, later(): lax.ppermute(value, 'tm', [(i, i + distance) for i in range(tms - distanc...  27 us
    ppermute x14, waiting for transfers between devices, swap(): return lax.ppermute(value, 'col', [(i, i ^ bit) for i in range(cols)])  16.7 us
    pallas_call x18, Pallas kernels, kernel(): call(*(pltpu.with_memory_space_constraint(x, kept[where]) if where in kep...  15.3 us
    ppermute x5, waiting for transfers between devices, later(): lax.ppermute(value, 'tm', [(i, i + distance) for i in range(tms - distanc...  10.6 us
    ppermute x14, starting transfers between devices, swap(): return lax.ppermute(value, 'col', [(i, i ^ bit) for i in range(cols)])  9.43 us
  transfers between devices with their start and end apart: 19, of which 10 were waited for; matrix products, arithmetic and copies ran while one was open for 0% of the time, Pallas kernels for 16%

profile of v4, /device:TPU:0, one launch (start us, length us, event | category | flops | bytes accessed | tf_op | source)
XLA Modules:
  0.0 80.1 jit_solution(16223405668445998586)
XLA Ops:
  0.6 5.0 %collective-permute-start.5 = (f32[2,192,128]{2,1,0:T(8,128)}, f32[2,192,128]{2,1,0:T(8,128)S(1)}, u32[]{:S(2)}, u32[]{:S(2)}) collective-permute-start(f32[2,192,128]{2,1,0:T(8,128)} %bitcast.1), channel_id=1, source_target_pairs={{0,4},{4,8},{8,12},{12,16},{16,20},{20,24},{24,28},{1,5},{5,9},{9,... | collective-permute-start | bytes 589832 | tf_op jit(solution)/shard_map/ppermute | solution.py:769
  5.7 1.3 %shard_map.101 = (f32[136,384]{1,0:T(8,128)S(1)}, f32[136,256]{1,0:T(8,128)S(1)}, f32[136,128]{1,0:T(8,128)S(1)}, f32[128,512]{1,0:T(8,128)S(1)}, f32[8,128]{1,0:T(8,128)S(1)}) custom-call(f32[2,128,512]{2,1,0:T(8,128)} %cov.1, f32[2,128,512]{2,1,0:T(8,128)} %cost.1, f32[2,128]{1,0:T(2,128)} %drift.1, f32[2,128]{1,0:T(2,128)} %eta.1), custom_call_target="tpu_custom_call" | custom-call | tf_op jit(solution)/shard_map/pallas_call | solution.py:752
  7.0 3.1 %collective-permute-done.5.before = f32[2,192,128]{2,1,0:T(8,128)S(1)} collective-permute-done((f32[2,192,128]{2,1,0:T(8,128)}, f32[2,192,128]{2,1,0:T(8,128)S(1)}, u32[]{:S(2)}, u32[]{:S(2)}) %collective-permute-start.5) | collective-permute-done | bytes 196640 | tf_op jit(solution)/shard_map/ppermute | solution.py:769
  10.1 1.6 %collective-permute-start.6 = (f32[384,128]{1,0:T(8,128)S(1)}, f32[384,128]{1,0:T(8,128)S(1)}, u32[]{:S(2)}, u32[]{:S(2)}) collective-permute-start(f32[384,128]{1,0:T(8,128)S(1)} %shard_map.104), channel_id=1, source_target_pairs={{0,2},{1,3},{2,0},{3,1},{4,6},{5,7},{6,4},{7,5},{8,10},{9,11},{10,... | collective-permute-start | bytes 589832 | tf_op jit(solution)/shard_map/ppermute | solution.py:766
  11.7 4.3 %collective-permute-done.6.other = f32[384,128]{1,0:T(8,128)S(1)} collective-permute-done((f32[384,128]{1,0:T(8,128)S(1)}, f32[384,128]{1,0:T(8,128)S(1)}, u32[]{:S(2)}, u32[]{:S(2)}) %collective-permute-start.6) | collective-permute-done | bytes 196640 | tf_op jit(solution)/shard_map/ppermute | solution.py:766
  16.1 4.3 %collective-permute-start.3 = (f32[128,768]{1,0:T(8,128)S(1)}, f32[128,768]{1,0:T(8,128)S(1)}, u32[]{:S(2)}, u32[]{:S(2)}) collective-permute-start(f32[128,768]{1,0:T(8,128)S(1)} %shard_map.102.own_near), channel_id=1, source_target_pairs={{0,4},{4,8},{8,12},{12,16},{16,20},{20,24},{24,28},{1,5},{5,9},{9,... | collective-permute-start | bytes 1179656 | tf_op jit(solution)/shard_map/ppermute | solution.py:769
  20.5 1.6 %collective-permute-start.1 = (f32[136,256]{1,0:T(8,128)S(1)}, f32[136,256]{1,0:T(8,128)S(1)}, u32[]{:S(2)}, u32[]{:S(2)}) collective-permute-start(f32[136,256]{1,0:T(8,128)S(1)} %get-tuple-element.53), channel_id=1, source_target_pairs={{0,2},{1,3},{2,0},{3,1},{4,6},{5,7},{6,4},{7,5},{8,10},{9,11},{10,... | collective-permute-start | bytes 417800 | tf_op jit(solution)/shard_map/ppermute | solution.py:766
  22.0 3.5 %collective-permute-start.9 = (f32[768,128]{1,0:T(8,128)S(1)}, f32[768,128]{1,0:T(8,128)S(1)}, u32[]{:S(2)}, u32[]{:S(2)}) collective-permute-start(f32[768,128]{1,0:T(8,128)S(1)} %shard_map.105.halves), channel_id=1, source_target_pairs={{0,8},{4,12},{8,16},{12,20},{16,24},{20,28},{1,9},{5,13},{9,17},{1... | collective-permute-start | bytes 1179656 | tf_op jit(solution)/shard_map/ppermute | solution.py:769
  25.6 4.3 %collective-permute-done.2.from_far = f32[136,128]{1,0:T(8,128)S(1)} collective-permute-done((f32[136,128]{1,0:T(8,128)S(1)}, f32[136,128]{1,0:T(8,128)S(1)}, u32[]{:S(2)}, u32[]{:S(2)}) %collective-permute-start.2) | collective-permute-done | bytes 69664 | tf_op jit(solution)/shard_map/ppermute | solution.py:766
  29.9 4.4 %collective-permute-start.4 = (f32[136,256]{1,0:T(8,128)S(1)}, f32[136,256]{1,0:T(8,128)S(1)}, u32[]{:S(2)}, u32[]{:S(2)}) collective-permute-start(f32[136,256]{1,0:T(8,128)S(1)} %shard_map.103.own_far), channel_id=1, source_target_pairs={{0,4},{4,8},{8,12},{12,16},{16,20},{20,24},{24,28},{1,5},{5,9},{9,... | collective-permute-start | bytes 417800 | tf_op jit(solution)/shard_map/ppermute | solution.py:769
  35.3 2.0 %collective-permute-done.4.far = f32[136,256]{1,0:T(8,128)S(1)} collective-permute-done((f32[136,256]{1,0:T(8,128)S(1)}, f32[136,256]{1,0:T(8,128)S(1)}, u32[]{:S(2)}, u32[]{:S(2)}) %collective-permute-start.4) | collective-permute-done | bytes 139296 | tf_op jit(solution)/shard_map/ppermute | solution.py:769
  37.3 2.0 %shard_map.107.own = f32[264,512]{1,0:T(8,128)S(1)} custom-call(f32[128,768]{1,0:T(8,128)S(1)} %shard_map.102.own_near, f32[136,256]{1,0:T(8,128)S(1)} %shard_map.103.own_far, f32[128,768]{1,0:T(8,128)S(1)} %collective-permute-done.3.near, f32[136,256]{1,0:T(8,128)S(1)} %collective-permute-done.4.far, bf16[512,512]{1,0:T(8,128)(2,1)S(1)} %get-tuple-element.55.mh, ...), custom_call_target="tpu_custom_call" | custom-call | tf_op jit(solution)/shard_map/pallas_call | solution.py:752
  39.3 9.8 %collective-permute-start.8 = (f32[264,512]{1,0:T(8,128)S(1)}, f32[264,512]{1,0:T(8,128)S(1)}, u32[]{:S(2)}, u32[]{:S(2)}) collective-permute-start(f32[264,512]{1,0:T(8,128)S(1)} %shard_map.107.own), channel_id=1, source_target_pairs={{0,8},{4,12},{8,16},{12,20},{16,24},{20,28},{1,9},{5,13},{9,17},{1... | collective-permute-start | bytes 1622024 | tf_op jit(solution)/shard_map/ppermute | solution.py:769
  49.2 1.4 %shard_map.108 = (bf16[512,512]{1,0:T(8,128)(2,1)S(1)}, bf16[512,512]{1,0:T(8,128)(2,1)S(1)}, bf16[512,512]{1,0:T(8,128)(2,1)S(1)}, bf16[512,512]{1,0:T(8,128)(2,1)S(1)}, f32[512,256]{1,0:T(8,128)S(1)}) custom-call(s32[8,3]{1,0:T(8,128)S(1)} %copy.15.pattern, f32[768,128]{1,0:T(8,128)S(1)} %shard_map.105.halves, ...), custom_call_target="tpu_custom_call" | custom-call | tf_op jit(solution)/shard_map/pallas_call | solution.py:752
  50.9 2.5 %shard_map.109 = (f32[128,512]{1,0:T(8,128)S(1)}, f32[128,512]{1,0:T(8,128)S(1)}, f32[512,512]{1,0:T(8,128)S(1)}, bf16[512,512]{1,0:T(8,128)(2,1)S(1)}, bf16[512...) custom-call(s32[8,3]{1,0:T(8,128)S(1)} %copy.15.pattern, ...), custom_call_target="tpu_custom_call" | custom-call | tf_op jit(solution)/shard_map/pallas_call | solution.py:752
  53.5 1.2 %shard_map.110 = (bf16[512,512]{1,0:T(8,128)(2,1)S(1)}, bf16[512,512]{1,0:T(8,128)(2,1)S(1)}, bf16[512,512]{1,0:T(8,128)(2,1)S(1)}, bf16[512,512]{1,0:T(8,128)(2,1)S(1)}) custom-call(bf16[512,512]{1,0:T(8,128)(2,1)S(1)} %get-tuple-element.59.a0h, bf16[512,512]{1,0:T(8,128)(2,1)S(1)} %get-tuple-element.60.a0l, bf16[512,512]{1,0:T(8,128)(2,1)S(1)} %get-tuple-element.61.a1h, ...), custom_call_target="tpu_custom_call" | custom-call | tf_op jit(solution)/shard_map/pallas_call | solution.py:752
  54.9 5.5 %collective-permute-done.8.earlier = f32[264,512]{1,0:T(8,128)S(1)} collective-permute-done((f32[264,512]{1,0:T(8,128)S(1)}, f32[264,512]{1,0:T(8,128)S(1)}, u32[]{:S(2)}, u32[]{:S(2)}) %collective-permute-start.8) | collective-permute-done | bytes 540704 | tf_op jit(solution)/shard_map/ppermute | solution.py:769
  60.4 1.7 %shard_map.112 = (f32[520,128]{1,0:T(8,128)S(1)}, bf16[512,512]{1,0:T(8,128)(2,1)S(1)}, bf16[512,512]{1,0:T(8,128)(2,1)S(1)}) custom-call(f32[264,512]{1,0:T(8,128)S(1)} %shard_map.107.own, f32[264,512]{1,0:T(8,128)S(1)} %collective-permute-done.8.earlier, bf16[512,512]{1,0:T(8,128)(2,1)S(1)} %get-tuple-element.70.mh, ...), custom_call_target="tpu_custom_call" | custom-call | tf_op jit(solution)/shard_map/pallas_call | solution.py:752
  62.1 1.6 %collective-permute-start.13 = (f32[520,128]{1,0:T(8,128)S(1)}, f32[520,128]{1,0:T(8,128)S(1)}, u32[]{:S(2)}, u32[]{:S(2)}) collective-permute-start(f32[520,128]{1,0:T(8,128)S(1)} %get-tuple-element.83), channel_id=1, source_target_pairs={{0,2},{1,3},{2,0},{3,1},{4,6},{5,7},{6,4},{7,5},{8,10},{9,11},{10,... | collective-permute-start | bytes 798728 | tf_op jit(solution)/shard_map/ppermute | solution.py:766
  65.7 1.7 %collective-permute-start.18 = (f32[256,128]{1,0:T(8,128)S(1)}, f32[256,128]{1,0:T(8,128)S(1)}, u32[]{:S(2)}, u32[]{:S(2)}) collective-permute-start(f32[256,128]{1,0:T(8,128)S(1)} %get-tuple-element.90), channel_id=1, source_target_pairs={{0,3},{1,2},{2,1},{3,0},{4,7},{5,6},{6,5},{7,4},{8,11},{9,10},{10,... | collective-permute-start | bytes 393224 | tf_op jit(solution)/shard_map/ppermute | solution.py:766
  67.4 4.0 %collective-permute-done.13.from_chip.panel = f32[520,128]{1,0:T(8,128)S(1)} collective-permute-done((f32[520,128]{1,0:T(8,128)S(1)}, f32[520,128]{1,0:T(8,128)S(1)}, u32[]{:S(2)}, u32[]{:S(2)}) %collective-permute-start.13) | collective-permute-done | bytes 266272 | tf_op jit(solution)/shard_map/ppermute | solution.py:766
  72.1 2.6 %collective-permute-done.12.dyn_recv = f32[128,512]{1,0:T(8,128)S(1)} collective-permute-done((f32[128,512]{1,0:T(8,128)S(1)}, f32[128,512]{1,0:T(8,128)S(1)}, u32[]{:S(2)}, u32[]{:S(2)}) %collective-permute-start.12) | collective-permute-done | bytes 262176 | tf_op jit(solution)/shard_map/ppermute | solution.py:766
  74.7 1.5 %collective-permute-start.15 = (f32[8,128]{1,0:T(8,128)S(1)}, f32[8,128]{1,0:T(8,128)S(1)}, u32[]{:S(2)}, u32[]{:S(2)}) collective-permute-start(f32[8,128]{1,0:T(8,128)S(1)} %get-tuple-element.88.short), channel_id=1, source_target_pairs={{0,2},{1,3},{2,0},{3,1},{4,6},{5,7},{6,4},{7,5},{8,10},{9,11},{10,... | collective-permute-start | bytes 12296 | tf_op jit(solution)/shard_map/ppermute | solution.py:766
  76.3 1.0 %shard_map.114 = (f32[2,128,512]{2,1,0:T(8,128)}, f32[2,128,512]{2,1,0:T(8,128)}, f32[2,128,512]{2,1,0:T(8,128)}) custom-call(f32[512,128]{1,0:T(8,128)S(1)} %get-tuple-element.76.keep, f32[512,128]{1,0:T(8,128)S(1)} %collective-permute-done.11.from_core, f32[128,512]{1,0:T(8,128)S(1)} %get-tuple-element.78.dyn_own, ...), custom_call_target="tpu_custom_call" | custom-call | tf_op jit(solution)/shard_map/pallas_call | solution.py:752
  (37 shorter events, 7.3 us)
Async XLA Ops:
  0.6 9.5 %copy-start = (f32[2,128,192]{1,2,0:T(8,128)S(1)}, f32[2,128,192]{1,2,0:T(8,128)}, u32[]{:S(2)}) copy-start(f32[2,128,192]{1,2,0:T(8,128)} %param.6) | copy-start | bytes 589828
  0.6 9.5 %collective-permute-start.5 = (f32[2,192,128]{2,1,0:T(8,128)}, f32[2,192,128]{2,1,0:T(8,128)S(1)}, u32[]{:S(2)}, u32[]{:S(2)}) collective-permute-start(f32[2,192,128]{2,1,0:T(8,128)} %bitcast.1), channel_id=1, source_target_pairs={{0,4},{4,8},{8,12},{12,16},{16,20},{20,24},{24,28},{1,5},{5,9},{9,... | collective-permute-start | bytes 589832 | tf_op jit(solution)/shard_map/ppermute | solution.py:769
  6.9 9.2 %collective-permute-start = (f32[136,384]{1,0:T(8,128)S(1)}, f32[136,384]{1,0:T(8,128)S(1)}, u32[]{:S(2)}, u32[]{:S(2)}) collective-permute-start(f32[136,384]{1,0:T(8,128)S(1)} %get-tuple-element.51), channel_id=1, source_target_pairs={{0,1},{1,0},{2,3},{3,2},{4,5},{5,4},{6,7},{7,6},{8,9},{9,8},{10,11... | collective-permute-start | bytes 626696 | tf_op jit(solution)/shard_map/ppermute | solution.py:766
  10.1 5.9 %collective-permute-start.6 = (f32[384,128]{1,0:T(8,128)S(1)}, f32[384,128]{1,0:T(8,128)S(1)}, u32[]{:S(2)}, u32[]{:S(2)}) collective-permute-start(f32[384,128]{1,0:T(8,128)S(1)} %shard_map.104), channel_id=1, source_target_pairs={{0,2},{1,3},{2,0},{3,1},{4,6},{5,7},{6,4},{7,5},{8,10},{9,11},{10,... | collective-permute-start | bytes 589832 | tf_op jit(solution)/shard_map/ppermute | solution.py:766
  16.0 18.4 %collective-permute-start.7 = (f32[768,128]{1,0:T(8,128)S(1)}, f32[768,128]{1,0:T(8,128)S(1)}, u32[]{:S(2)}, u32[]{:S(2)}) collective-permute-start(f32[768,128]{1,0:T(8,128)S(1)} %shard_map.105.halves), channel_id=1, source_target_pairs={{0,1},{1,0},{2,3},{3,2},{4,5},{5,4},{6,7},{7,6},{8,9},{9,8},{10,11... | collective-permute-start | bytes 1179656 | tf_op jit(solution)/shard_map/ppermute | solution.py:766
  16.1 21.2 %collective-permute-start.3 = (f32[128,768]{1,0:T(8,128)S(1)}, f32[128,768]{1,0:T(8,128)S(1)}, u32[]{:S(2)}, u32[]{:S(2)}) collective-permute-start(f32[128,768]{1,0:T(8,128)S(1)} %shard_map.102.own_near), channel_id=1, source_target_pairs={{0,4},{4,8},{8,12},{12,16},{16,20},{20,24},{24,28},{1,5},{5,9},{9,... | collective-permute-start | bytes 1179656 | tf_op jit(solution)/shard_map/ppermute | solution.py:769
  20.5 9.4 %collective-permute-start.1 = (f32[136,256]{1,0:T(8,128)S(1)}, f32[136,256]{1,0:T(8,128)S(1)}, u32[]{:S(2)}, u32[]{:S(2)}) collective-permute-start(f32[136,256]{1,0:T(8,128)S(1)} %get-tuple-element.53), channel_id=1, source_target_pairs={{0,2},{1,3},{2,0},{3,1},{4,6},{5,7},{6,4},{7,5},{8,10},{9,11},{10,... | collective-permute-start | bytes 417800 | tf_op jit(solution)/shard_map/ppermute | solution.py:766
  22.0 27.1 %collective-permute-start.9 = (f32[768,128]{1,0:T(8,128)S(1)}, f32[768,128]{1,0:T(8,128)S(1)}, u32[]{:S(2)}, u32[]{:S(2)}) collective-permute-start(f32[768,128]{1,0:T(8,128)S(1)} %shard_map.105.halves), channel_id=1, source_target_pairs={{0,8},{4,12},{8,16},{12,20},{16,24},{20,28},{1,9},{5,13},{9,17},{1... | collective-permute-start | bytes 1179656 | tf_op jit(solution)/shard_map/ppermute | solution.py:769
  25.5 4.4 %collective-permute-start.2 = (f32[136,128]{1,0:T(8,128)S(1)}, f32[136,128]{1,0:T(8,128)S(1)}, u32[]{:S(2)}, u32[]{:S(2)}) collective-permute-start(f32[136,128]{1,0:T(8,128)S(1)} %get-tuple-element.54), channel_id=1, source_target_pairs={{0,3},{1,2},{2,1},{3,0},{4,7},{5,6},{6,5},{7,4},{8,11},{9,10},{10,... | collective-permute-start | bytes 208904 | tf_op jit(solution)/shard_map/ppermute | solution.py:766
  29.9 4.4 %copy-start.1 = (s32[8,3]{0,1:T(4,128)S(1)}, s32[8,3]{0,1:T(4,128)}, u32[]{:S(2)}) copy-start(s32[8,3]{0,1:T(4,128)} %param.7) | copy-start | bytes 292
  29.9 7.4 %collective-permute-start.4 = (f32[136,256]{1,0:T(8,128)S(1)}, f32[136,256]{1,0:T(8,128)S(1)}, u32[]{:S(2)}, u32[]{:S(2)}) collective-permute-start(f32[136,256]{1,0:T(8,128)S(1)} %shard_map.103.own_far), channel_id=1, source_target_pairs={{0,4},{4,8},{8,12},{12,16},{16,20},{20,24},{24,28},{1,5},{5,9},{9,... | collective-permute-start | bytes 417800 | tf_op jit(solution)/shard_map/ppermute | solution.py:769
  39.3 21.1 %collective-permute-start.8 = (f32[264,512]{1,0:T(8,128)S(1)}, f32[264,512]{1,0:T(8,128)S(1)}, u32[]{:S(2)}, u32[]{:S(2)}) collective-permute-start(f32[264,512]{1,0:T(8,128)S(1)} %shard_map.107.own), channel_id=1, source_target_pairs={{0,8},{4,12},{8,16},{12,20},{16,24},{20,28},{1,9},{5,13},{9,17},{1... | collective-permute-start | bytes 1622024 | tf_op jit(solution)/shard_map/ppermute | solution.py:769
  49.1 1.8 %collective-permute-start.10 = (f32[768,128]{1,0:T(8,128)S(1)}, f32[768,128]{1,0:T(8,128)S(1)}, u32[]{:S(2)}, u32[]{:S(2)}) collective-permute-start(f32[768,128]{1,0:T(8,128)S(1)} %collective-permute-done.9.halves), channel_id=1, source_target_pairs={{0,1},{1,0},{2,3},{3,2},{4,5},{5,4},{6,7},{7,6},{8,9},{9,8},{10,11... | collective-permute-start | bytes 1179656 | tf_op jit(solution)/shard_map/ppermute | solution.py:766
  62.1 9.3 %collective-permute-start.13 = (f32[520,128]{1,0:T(8,128)S(1)}, f32[520,128]{1,0:T(8,128)S(1)}, u32[]{:S(2)}, u32[]{:S(2)}) collective-permute-start(f32[520,128]{1,0:T(8,128)S(1)} %get-tuple-element.83), channel_id=1, source_target_pairs={{0,2},{1,3},{2,0},{3,1},{4,6},{5,7},{6,4},{7,5},{8,10},{9,11},{10,... | collective-permute-start | bytes 798728 | tf_op jit(solution)/shard_map/ppermute | solution.py:766
  63.7 11.0 %collective-permute-start.12 = (f32[128,512]{1,0:T(8,128)S(1)}, f32[128,512]{1,0:T(8,128)S(1)}, u32[]{:S(2)}, u32[]{:S(2)}) collective-permute-start(f32[128,512]{1,0:T(8,128)S(1)} %get-tuple-element.79), channel_id=1, source_target_pairs={{0,2},{1,3},{2,0},{3,1},{4,6},{5,7},{6,4},{7,5},{8,10},{9,11},{10,... | collective-permute-start | bytes 786440 | tf_op jit(solution)/shard_map/ppermute | solution.py:766
  64.8 11.4 %collective-permute-start.11 = (f32[512,128]{1,0:T(8,128)S(1)}, f32[512,128]{1,0:T(8,128)S(1)}, u32[]{:S(2)}, u32[]{:S(2)}) collective-permute-start(f32[512,128]{1,0:T(8,128)S(1)} %get-tuple-element.77), channel_id=1, source_target_pairs={{0,1},{1,0},{2,3},{3,2},{4,5},{5,4},{6,7},{7,6},{8,9},{9,8},{10,11... | collective-permute-start | bytes 786440 | tf_op jit(solution)/shard_map/ppermute | solution.py:766
  65.7 13.6 %collective-permute-start.18 = (f32[256,128]{1,0:T(8,128)S(1)}, f32[256,128]{1,0:T(8,128)S(1)}, u32[]{:S(2)}, u32[]{:S(2)}) collective-permute-start(f32[256,128]{1,0:T(8,128)S(1)} %get-tuple-element.90), channel_id=1, source_target_pairs={{0,3},{1,2},{2,1},{3,0},{4,7},{5,6},{6,5},{7,4},{8,11},{9,10},{10,... | collective-permute-start | bytes 393224 | tf_op jit(solution)/shard_map/ppermute | solution.py:766
  71.5 7.7 %collective-permute-start.17 = (f32[256,128]{1,0:T(8,128)S(1)}, f32[256,128]{1,0:T(8,128)S(1)}, u32[]{:S(2)}, u32[]{:S(2)}) collective-permute-start(f32[256,128]{1,0:T(8,128)S(1)} %get-tuple-element.89), channel_id=1, source_target_pairs={{0,1},{1,0},{2,3},{3,2},{4,5},{5,4},{6,7},{7,6},{8,9},{9,8},{10,11... | collective-permute-start | bytes 393224 | tf_op jit(solution)/shard_map/ppermute | solution.py:766
  71.6 6.4 %collective-permute-start.14 = (f32[8,128]{1,0:T(8,128)S(1)}, f32[8,128]{1,0:T(8,128)S(1)}, u32[]{:S(2)}, u32[]{:S(2)}) collective-permute-start(f32[8,128]{1,0:T(8,128)S(1)} %get-tuple-element.88.short), channel_id=1, source_target_pairs={{0,1},{1,0},{2,3},{3,2},{4,5},{5,4},{6,7},{7,6},{8,9},{9,8},{10,11... | collective-permute-start | bytes 12296 | tf_op jit(solution)/shard_map/ppermute | solution.py:766
  74.7 3.6 %collective-permute-start.15 = (f32[8,128]{1,0:T(8,128)S(1)}, f32[8,128]{1,0:T(8,128)S(1)}, u32[]{:S(2)}, u32[]{:S(2)}) collective-permute-start(f32[8,128]{1,0:T(8,128)S(1)} %get-tuple-element.88.short), channel_id=1, source_target_pairs={{0,2},{1,3},{2,0},{3,1},{4,6},{5,7},{6,4},{7,5},{8,10},{9,11},{10,... | collective-permute-start | bytes 12296 | tf_op jit(solution)/shard_map/ppermute | solution.py:766
  76.2 3.0 %collective-permute-start.16 = (f32[8,128]{1,0:T(8,128)S(1)}, f32[8,128]{1,0:T(8,128)S(1)}, u32[]{:S(2)}, u32[]{:S(2)}) collective-permute-start(f32[8,128]{1,0:T(8,128)S(1)} %get-tuple-element.88.short), channel_id=1, source_target_pairs={{0,3},{1,2},{2,1},{3,0},{4,7},{5,6},{6,5},{7,4},{8,11},{9,10},{10,... | collective-permute-start | bytes 12296 | tf_op jit(solution)/shard_map/ppermute | solution.py:766

commit v5 on v4

--- a/solution.py
+++ b/solution.py
@@ -604,12 +604,13 @@
     to_far[0:r, :] = rest[:, 0:r]
     to_far[r : 2 * r, :] = rest[:, r : 2 * r]
     out = vec[1:2, :] + row_times(vec[0:1, :], mh[...].astype(F32) + ml[...].astype(F32), r)
+    to_far[2 * r :, :] = jnp.broadcast_to(out[:, 3 * r :], (8, r))
     for i in range(4):
         short[i : i + 1, :] = out[:, i * r : (i + 1) * r]
     short[4:8, :] = jnp.zeros((4, r), F32)
 
 
-def rest_kernel(earlier, th, tl, full, z, uh, ul, keep, to_core, rest):
+def rest_kernel(earlier, th, tl, full, z, uh, ul, short, keep, to_core, rest):
     q, _, c = place_of()
     r = earlier.shape[1] // 4
 
@@ -628,6 +629,7 @@
 
     put_rows(keep, rest[0:r, :], q, r)
     put_rows(to_core, rest[r : 2 * r, :], q, r)
+    to_core[4 * r :, :] = jnp.broadcast_to(short[1:2, :], (8, r))
 
 
 def turn_kernel(from_chip, diagonal_block, mirrored):
@@ -644,52 +646,53 @@
     ]
 
 
-def fill_kernel(keep, from_core, dyn_own, dyn_recv, dyn_out, cov_out, cost_out, sems):
-    _, y, c = place_of()
+def block_copies(blocks, target, element, r):
+    return [(source, target.at[element, :, lanes(at, r)]) for source, at in blocks]
+
+
+def fill_kernel(
+    keep,
+    from_core,
+    dyn_own,
+    dyn_recv,
+    diagonal_block,
+    from_chip,
+    dyn_out,
+    cov_out,
+    cost_out,
+    sems,
+):
+    q, y, c = place_of()
     r = dyn_own.shape[0]
     dyn = [(dyn_own, dyn_out.at[y]), (dyn_recv, dyn_out.at[1 - y])]
+    blocks = [(diagonal_block, q)] + [
+        (from_chip.at[pl.ds(at * r, r), :], q ^ bit) for at, bit in ((1, 2), (2, 3), (3, 1))
+    ]
+
+    def write(mine, other):
+        copy_all(
+            dyn
+            + panel_copies(keep, mine, y, r)
+            + panel_copies(from_core, other, y, r)
+            + block_copies(blocks, mine, 1 - y, r),
+            sems,
+        )
 
     @pl.when(c == 0)
     def _():
-        copy_all(
-            dyn + panel_copies(keep, cov_out, y, r) + panel_copies(from_core, cost_out, y, r), sems
-        )
+        write(cov_out, cost_out)
 
     @pl.when(c == 1)
     def _():
-        copy_all(
-            dyn + panel_copies(from_core, cov_out, y, r) + panel_copies(keep, cost_out, y, r), sems
-        )
-
-
-def block_copies(blocks, target, element, r):
-    return [(source, target.at[element, :, lanes(at, r)]) for source, at in blocks]
-
-
-def place_chip_kernel(cov_in, cost_in, diagonal_block, panel, cov_out, cost_out, sems):
-    del cov_in, cost_in
-    q, y, c = place_of()
-    r = panel.shape[1]
-    blocks = [(diagonal_block, q)] + [
-        (panel.at[pl.ds(at * r, r), :], q ^ bit) for at, bit in ((1, 2), (2, 3), (3, 1))
-    ]
-
-    @pl.when(c == 0)
-    def _():
-        copy_all(block_copies(blocks, cov_out, 1 - y, r), sems)
-
-    @pl.when(c == 1)
-    def _():
-        copy_all(block_copies(blocks, cost_out, 1 - y, r), sems)
-
-
-def place_far_kernel(
+        write(cost_out, cov_out)
+
+
+def place_kernel(
     cov_in,
     cost_in,
     short,
-    core_short,
     chip_short,
-    far_short,
+    from_core,
     mirrored,
     panel,
     cov_out,
@@ -703,11 +706,10 @@
     q, y, c = place_of()
     first = c == 0
     r = short.shape[1]
+    mine, other = short[0:1, :], from_core[4 * r : 4 * r + 1, :]
+    chip, far = chip_short[2:3, :], panel[2 * r : 2 * r + 1, :]
     for at, (one, two, three, four) in enumerate(
-        (
-            (short[0:1, :], core_short[1:2, :], chip_short[2:3, :], far_short[3:4, :]),
-            (core_short[1:2, :], short[0:1, :], far_short[3:4, :], chip_short[2:3, :]),
-        )
+        ((mine, other, chip, far), (other, mine, far, chip))
     ):
         lines[at, pl.ds(y, 1), :] = jnp.where(first, one, two)
         lines[at, pl.ds(1 - y, 1), :] = jnp.where(first, three, four)
@@ -847,37 +849,32 @@
     to_far, short = kernel(
         far_rows_kernel,
         vmem(level1, earlier, *m2, a2, full, z, *u),
-        vmem(shape(2 * r, r), shape(8, r)),
+        vmem(shape(2 * r + 8, r), shape(8, r)),
         [pltpu.VMEM((8, n), F32), pltpu.VMEM((r, 2 * r), F32)],
     )
-    chip_short, far_short = swap(short, 2), swap(short, 3)
+    chip_short = swap(short, 2)
     from_far = swap(to_far, 3)
     keep, to_core = kernel(
         rest_kernel,
-        vmem(earlier, *m2[2:], full, z, *u),
-        vmem(shape(n, r), shape(n, r)),
+        vmem(earlier, *m2[2:], full, z, *u, short),
+        vmem(shape(n, r), shape(n + 8, r)),
         [pltpu.VMEM((2 * r, n), F32)],
     )
     from_core = swap(to_core, 1)
-    shorts = (short, swap(short, 1), chip_short, far_short)
     diagonal_block, mirrored = kernel(
         turn_kernel, vmem(from_chip), vmem(shape(r, r), shape(2 * r, r))
     )
     mirrored = swap(mirrored, 1)
     whole, line = shape(elements, r, n), shape(elements, r)
     dyn_out, cov_out, cost_out = kernel(
-        fill_kernel, vmem(keep, from_core, dyn_own, dyn_recv), hbm(whole, whole, whole), [sems(10)]
-    )
-    cov_out, cost_out = kernel(
-        place_chip_kernel,
-        hbm(cov_out, cost_out) + vmem(diagonal_block, from_chip),
-        hbm(whole, whole),
-        [sems(4)],
-        {0: 0, 1: 1},
+        fill_kernel,
+        vmem(keep, from_core, dyn_own, dyn_recv, diagonal_block, from_chip),
+        hbm(whole, whole, whole),
+        [sems(14)],
     )
     cov_out, cost_out, drift_out, eta_out = kernel(
-        place_far_kernel,
-        hbm(cov_out, cost_out) + vmem(*shorts, mirrored, from_far),
+        place_kernel,
+        hbm(cov_out, cost_out) + vmem(short, chip_short, from_core, mirrored, from_far),
         hbm(whole, whole, line, line),
         [pltpu.VMEM((2, elements, r), F32), sems(6)],
         {0: 0, 1: 1},

time: 80.3 us -> 78.2 us (0.974)
  waiting for transfers between devices: 27.3 us -> 25.7 us
    ppermute x14 -> x12, waiting for transfers between devices: 16.7 us -> 15.1 us  [swap(): return lax.ppermute(value, 'col', [(i, i ^ bit) for i in range(cols)])]
    pallas_call x18 -> x17, Pallas kernels: 15.3 us -> 14.7 us  [kernel(): call(*(pltpu.with_memory_space_constraint(x, kept[where]) if where in kep...]
    ppermute x14 -> x12, starting transfers between devices: 9.43 us -> 9.57 us  [swap(): return lax.ppermute(value, 'col', [(i, i ^ bit) for i in range(cols)])]
  transfers between devices with their start and end apart: 19 -> 17, of which waited for: 10 -> 9; matrix products, arithmetic and copies ran while one was open for 0% -> 0% of each run, Pallas kernels for 16% -> 16%
where the time goes in v5:
time: 78.2 us; the launch traced here: 77.9 us
  starting transfers between devices  36.6 us (47%)
  waiting for transfers between devices  25.7 us (33%)
  Pallas kernels  14.7 us (19%)
  between operations  0.86 us (1%)
    ppermute x5, starting transfers between devices, later(): lax.ppermute(value, 'tm', [(i, i + distance) for i in range(tms - distanc...  27 us
    ppermute x12, waiting for transfers between devices, swap(): return lax.ppermute(value, 'col', [(i, i ^ bit) for i in range(cols)])  15.1 us
    pallas_call x17, Pallas kernels, kernel(): call(*(pltpu.with_memory_space_constraint(x, kept[where]) if where in kep...  14.7 us
    ppermute x5, waiting for transfers between devices, later(): lax.ppermute(value, 'tm', [(i, i + distance) for i in range(tms - distanc...  10.6 us
    ppermute x12, starting transfers between devices, swap(): return lax.ppermute(value, 'col', [(i, i ^ bit) for i in range(cols)])  9.57 us
  transfers between devices with their start and end apart: 17, of which 9 were waited for; matrix products, arithmetic and copies ran while one was open for 0% of the time, Pallas kernels for 16%

profile of v5, /device:TPU:0, one launch (start us, length us, event | category | flops | bytes accessed | tf_op | source)
XLA Modules:
  0.0 77.9 jit_solution(11071559175361579709)
XLA Ops:
  0.6 5.0 %collective-permute-start.5 = (f32[2,192,128]{2,1,0:T(8,128)}, f32[2,192,128]{2,1,0:T(8,128)S(1)}, u32[]{:S(2)}, u32[]{:S(2)}) collective-permute-start(f32[2,192,128]{2,1,0:T(8,128)} %bitcast.1), channel_id=1, source_target_pairs={{0,4},{4,8},{8,12},{12,16},{16,20},{20,24},{24,28},{1,5},{5,9},{9,... | collective-permute-start | bytes 589832 | tf_op jit(solution)/shard_map/ppermute | solution.py:771
  5.7 1.3 %shard_map.101 = (f32[136,384]{1,0:T(8,128)S(1)}, f32[136,256]{1,0:T(8,128)S(1)}, f32[136,128]{1,0:T(8,128)S(1)}, f32[128,512]{1,0:T(8,128)S(1)}, f32[8,128]{1,0:T(8,128)S(1)}) custom-call(f32[2,128,512]{2,1,0:T(8,128)} %cov.1, f32[2,128,512]{2,1,0:T(8,128)} %cost.1, f32[2,128]{1,0:T(2,128)} %drift.1, f32[2,128]{1,0:T(2,128)} %eta.1), custom_call_target="tpu_custom_call" | custom-call | tf_op jit(solution)/shard_map/pallas_call | solution.py:754
  7.0 3.1 %collective-permute-done.5.before = f32[2,192,128]{2,1,0:T(8,128)S(1)} collective-permute-done((f32[2,192,128]{2,1,0:T(8,128)}, f32[2,192,128]{2,1,0:T(8,128)S(1)}, u32[]{:S(2)}, u32[]{:S(2)}) %collective-permute-start.5) | collective-permute-done | bytes 196640 | tf_op jit(solution)/shard_map/ppermute | solution.py:771
  10.1 1.6 %collective-permute-start.6 = (f32[384,128]{1,0:T(8,128)S(1)}, f32[384,128]{1,0:T(8,128)S(1)}, u32[]{:S(2)}, u32[]{:S(2)}) collective-permute-start(f32[384,128]{1,0:T(8,128)S(1)} %shard_map.104), channel_id=1, source_target_pairs={{0,2},{1,3},{2,0},{3,1},{4,6},{5,7},{6,4},{7,5},{8,10},{9,11},{10,... | collective-permute-start | bytes 589832 | tf_op jit(solution)/shard_map/ppermute | solution.py:768
  11.7 4.3 %collective-permute-done.6.other = f32[384,128]{1,0:T(8,128)S(1)} collective-permute-done((f32[384,128]{1,0:T(8,128)S(1)}, f32[384,128]{1,0:T(8,128)S(1)}, u32[]{:S(2)}, u32[]{:S(2)}) %collective-permute-start.6) | collective-permute-done | bytes 196640 | tf_op jit(solution)/shard_map/ppermute | solution.py:768
  16.1 4.3 %collective-permute-start.3 = (f32[128,768]{1,0:T(8,128)S(1)}, f32[128,768]{1,0:T(8,128)S(1)}, u32[]{:S(2)}, u32[]{:S(2)}) collective-permute-start(f32[128,768]{1,0:T(8,128)S(1)} %shard_map.102.own_near), channel_id=1, source_target_pairs={{0,4},{4,8},{8,12},{12,16},{16,20},{20,24},{24,28},{1,5},{5,9},{9,... | collective-permute-start | bytes 1179656 | tf_op jit(solution)/shard_map/ppermute | solution.py:771
  20.5 1.6 %collective-permute-start.1 = (f32[136,256]{1,0:T(8,128)S(1)}, f32[136,256]{1,0:T(8,128)S(1)}, u32[]{:S(2)}, u32[]{:S(2)}) collective-permute-start(f32[136,256]{1,0:T(8,128)S(1)} %get-tuple-element.51), channel_id=1, source_target_pairs={{0,2},{1,3},{2,0},{3,1},{4,6},{5,7},{6,4},{7,5},{8,10},{9,11},{10,... | collective-permute-start | bytes 417800 | tf_op jit(solution)/shard_map/ppermute | solution.py:768
  22.0 3.5 %collective-permute-start.9 = (f32[768,128]{1,0:T(8,128)S(1)}, f32[768,128]{1,0:T(8,128)S(1)}, u32[]{:S(2)}, u32[]{:S(2)}) collective-permute-start(f32[768,128]{1,0:T(8,128)S(1)} %shard_map.105.halves), channel_id=1, source_target_pairs={{0,8},{4,12},{8,16},{12,20},{16,24},{20,28},{1,9},{5,13},{9,17},{1... | collective-permute-start | bytes 1179656 | tf_op jit(solution)/shard_map/ppermute | solution.py:771
  25.6 4.3 %collective-permute-done.2.from_far = f32[136,128]{1,0:T(8,128)S(1)} collective-permute-done((f32[136,128]{1,0:T(8,128)S(1)}, f32[136,128]{1,0:T(8,128)S(1)}, u32[]{:S(2)}, u32[]{:S(2)}) %collective-permute-start.2) | collective-permute-done | bytes 69664 | tf_op jit(solution)/shard_map/ppermute | solution.py:768
  29.9 4.4 %collective-permute-start.4 = (f32[136,256]{1,0:T(8,128)S(1)}, f32[136,256]{1,0:T(8,128)S(1)}, u32[]{:S(2)}, u32[]{:S(2)}) collective-permute-start(f32[136,256]{1,0:T(8,128)S(1)} %shard_map.103.own_far), channel_id=1, source_target_pairs={{0,4},{4,8},{8,12},{12,16},{16,20},{20,24},{24,28},{1,5},{5,9},{9,... | collective-permute-start | bytes 417800 | tf_op jit(solution)/shard_map/ppermute | solution.py:771
  35.3 2.0 %collective-permute-done.4.far = f32[136,256]{1,0:T(8,128)S(1)} collective-permute-done((f32[136,256]{1,0:T(8,128)S(1)}, f32[136,256]{1,0:T(8,128)S(1)}, u32[]{:S(2)}, u32[]{:S(2)}) %collective-permute-start.4) | collective-permute-done | bytes 139296 | tf_op jit(solution)/shard_map/ppermute | solution.py:771
  37.3 2.0 %shard_map.107.own = f32[264,512]{1,0:T(8,128)S(1)} custom-call(f32[128,768]{1,0:T(8,128)S(1)} %shard_map.102.own_near, f32[136,256]{1,0:T(8,128)S(1)} %shard_map.103.own_far, f32[128,768]{1,0:T(8,128)S(1)} %collective-permute-done.3.near, f32[136,256]{1,0:T(8,128)S(1)} %collective-permute-done.4.far, bf16[512,512]{1,0:T(8,128)(2,1)S(1)} %get-tuple-element.53.mh, ...), custom_call_target="tpu_custom_call" | custom-call | tf_op jit(solution)/shard_map/pallas_call | solution.py:754
  39.3 9.8 %collective-permute-start.8 = (f32[264,512]{1,0:T(8,128)S(1)}, f32[264,512]{1,0:T(8,128)S(1)}, u32[]{:S(2)}, u32[]{:S(2)}) collective-permute-start(f32[264,512]{1,0:T(8,128)S(1)} %shard_map.107.own), channel_id=1, source_target_pairs={{0,8},{4,12},{8,16},{12,20},{16,24},{20,28},{1,9},{5,13},{9,17},{1... | collective-permute-start | bytes 1622024 | tf_op jit(solution)/shard_map/ppermute | solution.py:771
  49.2 1.4 %shard_map.108 = (bf16[512,512]{1,0:T(8,128)(2,1)S(1)}, bf16[512,512]{1,0:T(8,128)(2,1)S(1)}, bf16[512,512]{1,0:T(8,128)(2,1)S(1)}, bf16[512,512]{1,0:T(8,128)(2,1)S(1)}, f32[512,256]{1,0:T(8,128)S(1)}) custom-call(s32[8,3]{1,0:T(8,128)S(1)} %copy.13.pattern, f32[768,128]{1,0:T(8,128)S(1)} %shard_map.105.halves, ...), custom_call_target="tpu_custom_call" | custom-call | tf_op jit(solution)/shard_map/pallas_call | solution.py:754
  50.9 2.5 %shard_map.109 = (f32[128,512]{1,0:T(8,128)S(1)}, f32[128,512]{1,0:T(8,128)S(1)}, f32[512,512]{1,0:T(8,128)S(1)}, bf16[512,512]{1,0:T(8,128)(2,1)S(1)}, bf16[512...) custom-call(s32[8,3]{1,0:T(8,128)S(1)} %copy.13.pattern, ...), custom_call_target="tpu_custom_call" | custom-call | tf_op jit(solution)/shard_map/pallas_call | solution.py:754
  53.5 1.2 %shard_map.110 = (bf16[512,512]{1,0:T(8,128)(2,1)S(1)}, bf16[512,512]{1,0:T(8,128)(2,1)S(1)}, bf16[512,512]{1,0:T(8,128)(2,1)S(1)}, bf16[512,512]{1,0:T(8,128)(2,1)S(1)}) custom-call(bf16[512,512]{1,0:T(8,128)(2,1)S(1)} %get-tuple-element.57.a0h, bf16[512,512]{1,0:T(8,128)(2,1)S(1)} %get-tuple-element.58.a0l, bf16[512,512]{1,0:T(8,128)(2,1)S(1)} %get-tuple-element.59.a1h, ...), custom_call_target="tpu_custom_call" | custom-call | tf_op jit(solution)/shard_map/pallas_call | solution.py:754
  54.9 5.5 %collective-permute-done.8.earlier = f32[264,512]{1,0:T(8,128)S(1)} collective-permute-done((f32[264,512]{1,0:T(8,128)S(1)}, f32[264,512]{1,0:T(8,128)S(1)}, u32[]{:S(2)}, u32[]{:S(2)}) %collective-permute-start.8) | collective-permute-done | bytes 540704 | tf_op jit(solution)/shard_map/ppermute | solution.py:771
  60.4 1.7 %shard_map.112 = (f32[520,128]{1,0:T(8,128)S(1)}, bf16[512,512]{1,0:T(8,128)(2,1)S(1)}, bf16[512,512]{1,0:T(8,128)(2,1)S(1)}) custom-call(f32[264,512]{1,0:T(8,128)S(1)} %shard_map.107.own, f32[264,512]{1,0:T(8,128)S(1)} %collective-permute-done.8.earlier, bf16[512,512]{1,0:T(8,128)(2,1)S(1)} %get-tuple-element.68.mh, ...), custom_call_target="tpu_custom_call" | custom-call | tf_op jit(solution)/shard_map/pallas_call | solution.py:754
  62.1 1.6 %collective-permute-start.13 = (f32[520,128]{1,0:T(8,128)S(1)}, f32[520,128]{1,0:T(8,128)S(1)}, u32[]{:S(2)}, u32[]{:S(2)}) collective-permute-start(f32[520,128]{1,0:T(8,128)S(1)} %get-tuple-element.80), channel_id=1, source_target_pairs={{0,2},{1,3},{2,0},{3,1},{4,6},{5,7},{6,4},{7,5},{8,10},{9,11},{10,... | collective-permute-start | bytes 798728 | tf_op jit(solution)/shard_map/ppermute | solution.py:768
  65.7 1.3 %collective-permute-start.16 = (f32[264,128]{1,0:T(8,128)S(1)}, f32[264,128]{1,0:T(8,128)S(1)}, u32[]{:S(2)}, u32[]{:S(2)}) collective-permute-start(f32[264,128]{1,0:T(8,128)S(1)} %get-tuple-element.86), channel_id=1, source_target_pairs={{0,3},{1,2},{2,1},{3,0},{4,7},{5,6},{6,5},{7,4},{8,11},{9,10},{10,... | collective-permute-start | bytes 405512 | tf_op jit(solution)/shard_map/ppermute | solution.py:768
  67.0 1.9 %collective-permute-done.13.from_chip = f32[520,128]{1,0:T(8,128)S(1)} collective-permute-done((f32[520,128]{1,0:T(8,128)S(1)}, f32[520,128]{1,0:T(8,128)S(1)}, u32[]{:S(2)}, u32[]{:S(2)}) %collective-permute-start.13) | collective-permute-done | bytes 266272 | tf_op jit(solution)/shard_map/ppermute | solution.py:768
  69.1 2.5 %collective-permute-start.14 = (f32[8,128]{1,0:T(8,128)S(1)}, f32[8,128]{1,0:T(8,128)S(1)}, u32[]{:S(2)}, u32[]{:S(2)}) collective-permute-start(f32[8,128]{1,0:T(8,128)S(1)} %get-tuple-element.75.short), channel_id=1, source_target_pairs={{0,2},{1,3},{2,0},{3,1},{4,6},{5,7},{6,4},{7,5},{8,10},{9,11},{10,... | collective-permute-start | bytes 12296 | tf_op jit(solution)/shard_map/ppermute | solution.py:768
  71.6 2.9 %collective-permute-done.12.dyn_recv = f32[128,512]{1,0:T(8,128)S(1)} collective-permute-done((f32[128,512]{1,0:T(8,128)S(1)}, f32[128,512]{1,0:T(8,128)S(1)}, u32[]{:S(2)}, u32[]{:S(2)}) %collective-permute-start.12) | collective-permute-done | bytes 262176 | tf_op jit(solution)/shard_map/ppermute | solution.py:768
  75.7 1.5 %collective-permute-done.14.chip_short = f32[8,128]{1,0:T(8,128)S(1)} collective-permute-done((f32[8,128]{1,0:T(8,128)S(1)}, f32[8,128]{1,0:T(8,128)S(1)}, u32[]{:S(2)}, u32[]{:S(2)}) %collective-permute-start.14) | collective-permute-done | bytes 4128 | tf_op jit(solution)/shard_map/ppermute | solution.py:768
  (32 shorter events, 6.1 us)
Async XLA Ops:
  0.6 9.5 %copy-start = (f32[2,128,192]{1,2,0:T(8,128)S(1)}, f32[2,128,192]{1,2,0:T(8,128)}, u32[]{:S(2)}) copy-start(f32[2,128,192]{1,2,0:T(8,128)} %param.6) | copy-start | bytes 589828
  0.6 9.5 %collective-permute-start.5 = (f32[2,192,128]{2,1,0:T(8,128)}, f32[2,192,128]{2,1,0:T(8,128)S(1)}, u32[]{:S(2)}, u32[]{:S(2)}) collective-permute-start(f32[2,192,128]{2,1,0:T(8,128)} %bitcast.1), channel_id=1, source_target_pairs={{0,4},{4,8},{8,12},{12,16},{16,20},{20,24},{24,28},{1,5},{5,9},{9,... | collective-permute-start | bytes 589832 | tf_op jit(solution)/shard_map/ppermute | solution.py:771
  6.9 9.2 %collective-permute-start = (f32[136,384]{1,0:T(8,128)S(1)}, f32[136,384]{1,0:T(8,128)S(1)}, u32[]{:S(2)}, u32[]{:S(2)}) collective-permute-start(f32[136,384]{1,0:T(8,128)S(1)} %get-tuple-element.49), channel_id=1, source_target_pairs={{0,1},{1,0},{2,3},{3,2},{4,5},{5,4},{6,7},{7,6},{8,9},{9,8},{10,11... | collective-permute-start | bytes 626696 | tf_op jit(solution)/shard_map/ppermute | solution.py:768
  10.1 5.9 %collective-permute-start.6 = (f32[384,128]{1,0:T(8,128)S(1)}, f32[384,128]{1,0:T(8,128)S(1)}, u32[]{:S(2)}, u32[]{:S(2)}) collective-permute-start(f32[384,128]{1,0:T(8,128)S(1)} %shard_map.104), channel_id=1, source_target_pairs={{0,2},{1,3},{2,0},{3,1},{4,6},{5,7},{6,4},{7,5},{8,10},{9,11},{10,... | collective-permute-start | bytes 589832 | tf_op jit(solution)/shard_map/ppermute | solution.py:768
  16.0 18.4 %collective-permute-start.7 = (f32[768,128]{1,0:T(8,128)S(1)}, f32[768,128]{1,0:T(8,128)S(1)}, u32[]{:S(2)}, u32[]{:S(2)}) collective-permute-start(f32[768,128]{1,0:T(8,128)S(1)} %shard_map.105.halves), channel_id=1, source_target_pairs={{0,1},{1,0},{2,3},{3,2},{4,5},{5,4},{6,7},{7,6},{8,9},{9,8},{10,11... | collective-permute-start | bytes 1179656 | tf_op jit(solution)/shard_map/ppermute | solution.py:768
  16.1 21.2 %collective-permute-start.3 = (f32[128,768]{1,0:T(8,128)S(1)}, f32[128,768]{1,0:T(8,128)S(1)}, u32[]{:S(2)}, u32[]{:S(2)}) collective-permute-start(f32[128,768]{1,0:T(8,128)S(1)} %shard_map.102.own_near), channel_id=1, source_target_pairs={{0,4},{4,8},{8,12},{12,16},{16,20},{20,24},{24,28},{1,5},{5,9},{9,... | collective-permute-start | bytes 1179656 | tf_op jit(solution)/shard_map/ppermute | solution.py:771
  20.5 9.4 %collective-permute-start.1 = (f32[136,256]{1,0:T(8,128)S(1)}, f32[136,256]{1,0:T(8,128)S(1)}, u32[]{:S(2)}, u32[]{:S(2)}) collective-permute-start(f32[136,256]{1,0:T(8,128)S(1)} %get-tuple-element.51), channel_id=1, source_target_pairs={{0,2},{1,3},{2,0},{3,1},{4,6},{5,7},{6,4},{7,5},{8,10},{9,11},{10,... | collective-permute-start | bytes 417800 | tf_op jit(solution)/shard_map/ppermute | solution.py:768
  22.0 27.1 %collective-permute-start.9 = (f32[768,128]{1,0:T(8,128)S(1)}, f32[768,128]{1,0:T(8,128)S(1)}, u32[]{:S(2)}, u32[]{:S(2)}) collective-permute-start(f32[768,128]{1,0:T(8,128)S(1)} %shard_map.105.halves), channel_id=1, source_target_pairs={{0,8},{4,12},{8,16},{12,20},{16,24},{20,28},{1,9},{5,13},{9,17},{1... | collective-permute-start | bytes 1179656 | tf_op jit(solution)/shard_map/ppermute | solution.py:771
  25.5 4.4 %collective-permute-start.2 = (f32[136,128]{1,0:T(8,128)S(1)}, f32[136,128]{1,0:T(8,128)S(1)}, u32[]{:S(2)}, u32[]{:S(2)}) collective-permute-start(f32[136,128]{1,0:T(8,128)S(1)} %get-tuple-element.52), channel_id=1, source_target_pairs={{0,3},{1,2},{2,1},{3,0},{4,7},{5,6},{6,5},{7,4},{8,11},{9,10},{10,... | collective-permute-start | bytes 208904 | tf_op jit(solution)/shard_map/ppermute | solution.py:768
  29.9 4.4 %copy-start.1 = (s32[8,3]{0,1:T(4,128)S(1)}, s32[8,3]{0,1:T(4,128)}, u32[]{:S(2)}) copy-start(s32[8,3]{0,1:T(4,128)} %param.7) | copy-start | bytes 292
  29.9 7.4 %collective-permute-start.4 = (f32[136,256]{1,0:T(8,128)S(1)}, f32[136,256]{1,0:T(8,128)S(1)}, u32[]{:S(2)}, u32[]{:S(2)}) collective-permute-start(f32[136,256]{1,0:T(8,128)S(1)} %shard_map.103.own_far), channel_id=1, source_target_pairs={{0,4},{4,8},{8,12},{12,16},{16,20},{20,24},{24,28},{1,5},{5,9},{9,... | collective-permute-start | bytes 417800 | tf_op jit(solution)/shard_map/ppermute | solution.py:771
  39.3 21.1 %collective-permute-start.8 = (f32[264,512]{1,0:T(8,128)S(1)}, f32[264,512]{1,0:T(8,128)S(1)}, u32[]{:S(2)}, u32[]{:S(2)}) collective-permute-start(f32[264,512]{1,0:T(8,128)S(1)} %shard_map.107.own), channel_id=1, source_target_pairs={{0,8},{4,12},{8,16},{12,20},{16,24},{20,28},{1,9},{5,13},{9,17},{1... | collective-permute-start | bytes 1622024 | tf_op jit(solution)/shard_map/ppermute | solution.py:771
  49.1 1.8 %collective-permute-start.10 = (f32[768,128]{1,0:T(8,128)S(1)}, f32[768,128]{1,0:T(8,128)S(1)}, u32[]{:S(2)}, u32[]{:S(2)}) collective-permute-start(f32[768,128]{1,0:T(8,128)S(1)} %collective-permute-done.9.halves), channel_id=1, source_target_pairs={{0,1},{1,0},{2,3},{3,2},{4,5},{5,4},{6,7},{7,6},{8,9},{9,8},{10,11... | collective-permute-start | bytes 1179656 | tf_op jit(solution)/shard_map/ppermute | solution.py:768
  62.1 6.8 %collective-permute-start.13 = (f32[520,128]{1,0:T(8,128)S(1)}, f32[520,128]{1,0:T(8,128)S(1)}, u32[]{:S(2)}, u32[]{:S(2)}) collective-permute-start(f32[520,128]{1,0:T(8,128)S(1)} %get-tuple-element.80), channel_id=1, source_target_pairs={{0,2},{1,3},{2,0},{3,1},{4,6},{5,7},{6,4},{7,5},{8,10},{9,11},{10,... | collective-permute-start | bytes 798728 | tf_op jit(solution)/shard_map/ppermute | solution.py:768
  65.1 9.4 %collective-permute-start.11 = (f32[520,128]{1,0:T(8,128)S(1)}, f32[520,128]{1,0:T(8,128)S(1)}, u32[]{:S(2)}, u32[]{:S(2)}) collective-permute-start(f32[520,128]{1,0:T(8,128)S(1)} %get-tuple-element.77), channel_id=1, source_target_pairs={{0,1},{1,0},{2,3},{3,2},{4,5},{5,4},{6,7},{7,6},{8,9},{9,8},{10,11... | collective-permute-start | bytes 798728 | tf_op jit(solution)/shard_map/ppermute | solution.py:768
  65.2 9.4 %collective-permute-start.12 = (f32[128,512]{1,0:T(8,128)S(1)}, f32[128,512]{1,0:T(8,128)S(1)}, u32[]{:S(2)}, u32[]{:S(2)}) collective-permute-start(f32[128,512]{1,0:T(8,128)S(1)} %get-tuple-element.79), channel_id=1, source_target_pairs={{0,2},{1,3},{2,0},{3,1},{4,6},{5,7},{6,4},{7,5},{8,10},{9,11},{10,... | collective-permute-start | bytes 786440 | tf_op jit(solution)/shard_map/ppermute | solution.py:768
  65.7 11.4 %collective-permute-start.16 = (f32[264,128]{1,0:T(8,128)S(1)}, f32[264,128]{1,0:T(8,128)S(1)}, u32[]{:S(2)}, u32[]{:S(2)}) collective-permute-start(f32[264,128]{1,0:T(8,128)S(1)} %get-tuple-element.86), channel_id=1, source_target_pairs={{0,3},{1,2},{2,1},{3,0},{4,7},{5,6},{6,5},{7,4},{8,11},{9,10},{10,... | collective-permute-start | bytes 405512 | tf_op jit(solution)/shard_map/ppermute | solution.py:768
  69.0 8.2 %collective-permute-start.15 = (f32[256,128]{1,0:T(8,128)S(1)}, f32[256,128]{1,0:T(8,128)S(1)}, u32[]{:S(2)}, u32[]{:S(2)}) collective-permute-start(f32[256,128]{1,0:T(8,128)S(1)} %get-tuple-element.85), channel_id=1, source_target_pairs={{0,1},{1,0},{2,3},{3,2},{4,5},{5,4},{6,7},{7,6},{8,9},{9,8},{10,11... | collective-permute-start | bytes 393224 | tf_op jit(solution)/shard_map/ppermute | solution.py:768
  69.1 8.1 %collective-permute-start.14 = (f32[8,128]{1,0:T(8,128)S(1)}, f32[8,128]{1,0:T(8,128)S(1)}, u32[]{:S(2)}, u32[]{:S(2)}) collective-permute-start(f32[8,128]{1,0:T(8,128)S(1)} %get-tuple-element.75.short), channel_id=1, source_target_pairs={{0,2},{1,3},{2,0},{3,1},{4,6},{5,7},{6,4},{7,5},{8,10},{9,11},{10,... | collective-permute-start | bytes 12296 | tf_op jit(solution)/shard_map/ppermute | solution.py:768

commit v6 on v5

--- a/solution.py
+++ b/solution.py
@@ -404,11 +404,11 @@
         transpose_split(mh, ml, dense, r)
 
 
-def level1_kernel(
-    own_near, own_far, near, far, mh, ml, th, tl, out, full, xh, xl
-):
+def level1_kernel(own_near, own_far, near, far, mh, ml, th, tl, out, xh, xl, sh, sl):
     c = place_of()[2]
     r = own_near.shape[0]
+    n = 4 * r
+    extra = slice(n, n + 16)
     first = c == 0
     xn = jnp.where(first, near[...], own_near[...])
     xf = jnp.where(first, far[...], own_far[...])
@@ -422,20 +422,22 @@
     )
 
     def put(i, j, block):
-        full[i * r : (i + 1) * r, j * r : (j + 1) * r] = block
         put_split(xh, xl, slice(i * r, (i + 1) * r), slice(j * r, (j + 1) * r), block)
 
     spread(x, r, put)
     b_before, b_own = far_row(far, r, 1), far_row(own_far, r, 1)
     e_before, e_own = far_row(far, r, 3), far_row(own_far, r, 3)
-    carried = jnp.where(first, b_before, e_own + row_times(b_before, full[...], r))
-    vec = jnp.where(first, b_own, e_before) + row_times(
-        carried, mh[...].astype(F32) + ml[...].astype(F32), r
-    )
+    row = jnp.broadcast_to(jnp.where(first, b_before, e_own), (16, n))
+    put_split(xh, xl, extra, slice(None), row)
     u = dot3(xh[...], xl[...], mh[...], ml[...])
-    uh, ul = split(u)
-    top = dot3(th[0 : 2 * r, :], tl[0 : 2 * r, :], uh, ul)
+    uh, ul = split(u[0:n, :])
+    sh[0 : 2 * r, :] = th[0 : 2 * r, :]
+    sl[0 : 2 * r, :] = tl[0 : 2 * r, :]
+    row = jnp.broadcast_to(jnp.where(first, 0.0, b_before), (16, n))
+    put_split(sh, sl, slice(2 * r, 2 * r + 16), slice(None), row)
+    top = dot3(sh[...], sl[...], uh, ul)
     low = dot3(th[2 * r :, :], tl[2 * r :, :], uh[:, 2 * r :], ul[:, 2 * r :])
+    vec = jnp.where(first, b_own, e_before) + u[n : n + 1, :] + top[2 * r : 2 * r + 1, :]
     dn = jnp.where(first, own_near[...], near[...])
     df = jnp.where(first, own_far[...], far[...])
     z11 = top[r : 2 * r, r : 2 * r]
@@ -820,7 +822,7 @@
         level1_kernel,
         vmem(own_near, own_far, near, far, *m1),
         vmem(shape(2 * r + 8, n)),
-        [square(F32)] + [square(BF16)] * 2,
+        [pltpu.VMEM((n + 16, n), BF16)] * 2 + [pltpu.VMEM((2 * r + 16, n), BF16)] * 2,
     )
     earlier = later(level1, 2)
     *a01, t = kernel(

time: 78.2 us -> 78.2 us (level)
  no operation moved by 1% of the time
where the time goes in v6:
time: 78.2 us; the launch traced here: 77.9 us
  starting transfers between devices  36.6 us (47%)
  waiting for transfers between devices  25.7 us (33%)
  Pallas kernels  14.6 us (19%)
  between operations  0.86 us (1%)
    ppermute x5, starting transfers between devices, later(): lax.ppermute(value, 'tm', [(i, i + distance) for i in range(tms - distanc...  27 us
    ppermute x12, waiting for transfers between devices, swap(): return lax.ppermute(value, 'col', [(i, i ^ bit) for i in range(cols)])  15.2 us
    pallas_call x17, Pallas kernels, kernel(): call(*(pltpu.with_memory_space_constraint(x, kept[where]) if where in kep...  14.6 us
    ppermute x5, waiting for transfers between devices, later(): lax.ppermute(value, 'tm', [(i, i + distance) for i in range(tms - distanc...  10.6 us
    ppermute x12, starting transfers between devices, swap(): return lax.ppermute(value, 'col', [(i, i ^ bit) for i in range(cols)])  9.57 us
  transfers between devices with their start and end apart: 17, of which 9 were waited for; matrix products, arithmetic and copies ran while one was open for 0% of the time, Pallas kernels for 16%

profile of v6, /device:TPU:0, one launch (start us, length us, event | category | flops | bytes accessed | tf_op | source)
XLA Modules:
  0.0 77.9 jit_solution(16268551119597160498)
XLA Ops:
  0.6 5.0 %collective-permute-start.5 = (f32[2,192,128]{2,1,0:T(8,128)}, f32[2,192,128]{2,1,0:T(8,128)S(1)}, u32[]{:S(2)}, u32[]{:S(2)}) collective-permute-start(f32[2,192,128]{2,1,0:T(8,128)} %bitcast.1), channel_id=1, source_target_pairs={{0,4},{4,8},{8,12},{12,16},{16,20},{20,24},{24,28},{1,5},{5,9},{9,... | collective-permute-start | bytes 589832 | tf_op jit(solution)/shard_map/ppermute | solution.py:773
  5.7 1.3 %shard_map.101 = (f32[136,384]{1,0:T(8,128)S(1)}, f32[136,256]{1,0:T(8,128)S(1)}, f32[136,128]{1,0:T(8,128)S(1)}, f32[128,512]{1,0:T(8,128)S(1)}, f32[8,128]{1,0:T(8,128)S(1)}) custom-call(f32[2,128,512]{2,1,0:T(8,128)} %cov.1, f32[2,128,512]{2,1,0:T(8,128)} %cost.1, f32[2,128]{1,0:T(2,128)} %drift.1, f32[2,128]{1,0:T(2,128)} %eta.1), custom_call_target="tpu_custom_call" | custom-call | tf_op jit(solution)/shard_map/pallas_call | solution.py:756
  7.0 3.1 %collective-permute-done.5.before = f32[2,192,128]{2,1,0:T(8,128)S(1)} collective-permute-done((f32[2,192,128]{2,1,0:T(8,128)}, f32[2,192,128]{2,1,0:T(8,128)S(1)}, u32[]{:S(2)}, u32[]{:S(2)}) %collective-permute-start.5) | collective-permute-done | bytes 196640 | tf_op jit(solution)/shard_map/ppermute | solution.py:773
  10.1 1.6 %collective-permute-start.6 = (f32[384,128]{1,0:T(8,128)S(1)}, f32[384,128]{1,0:T(8,128)S(1)}, u32[]{:S(2)}, u32[]{:S(2)}) collective-permute-start(f32[384,128]{1,0:T(8,128)S(1)} %shard_map.104), channel_id=1, source_target_pairs={{0,2},{1,3},{2,0},{3,1},{4,6},{5,7},{6,4},{7,5},{8,10},{9,11},{10,... | collective-permute-start | bytes 589832 | tf_op jit(solution)/shard_map/ppermute | solution.py:770
  11.7 4.3 %collective-permute-done.6.other = f32[384,128]{1,0:T(8,128)S(1)} collective-permute-done((f32[384,128]{1,0:T(8,128)S(1)}, f32[384,128]{1,0:T(8,128)S(1)}, u32[]{:S(2)}, u32[]{:S(2)}) %collective-permute-start.6) | collective-permute-done | bytes 196640 | tf_op jit(solution)/shard_map/ppermute | solution.py:770
  16.1 4.3 %collective-permute-start.3 = (f32[128,768]{1,0:T(8,128)S(1)}, f32[128,768]{1,0:T(8,128)S(1)}, u32[]{:S(2)}, u32[]{:S(2)}) collective-permute-start(f32[128,768]{1,0:T(8,128)S(1)} %shard_map.102.own_near), channel_id=1, source_target_pairs={{0,4},{4,8},{8,12},{12,16},{16,20},{20,24},{24,28},{1,5},{5,9},{9,... | collective-permute-start | bytes 1179656 | tf_op jit(solution)/shard_map/ppermute | solution.py:773
  20.5 1.6 %collective-permute-start.1 = (f32[136,256]{1,0:T(8,128)S(1)}, f32[136,256]{1,0:T(8,128)S(1)}, u32[]{:S(2)}, u32[]{:S(2)}) collective-permute-start(f32[136,256]{1,0:T(8,128)S(1)} %get-tuple-element.51), channel_id=1, source_target_pairs={{0,2},{1,3},{2,0},{3,1},{4,6},{5,7},{6,4},{7,5},{8,10},{9,11},{10,... | collective-permute-start | bytes 417800 | tf_op jit(solution)/shard_map/ppermute | solution.py:770
  22.0 3.5 %collective-permute-start.9 = (f32[768,128]{1,0:T(8,128)S(1)}, f32[768,128]{1,0:T(8,128)S(1)}, u32[]{:S(2)}, u32[]{:S(2)}) collective-permute-start(f32[768,128]{1,0:T(8,128)S(1)} %shard_map.105.halves), channel_id=1, source_target_pairs={{0,8},{4,12},{8,16},{12,20},{16,24},{20,28},{1,9},{5,13},{9,17},{1... | collective-permute-start | bytes 1179656 | tf_op jit(solution)/shard_map/ppermute | solution.py:773
  25.6 4.3 %collective-permute-done.2.from_far = f32[136,128]{1,0:T(8,128)S(1)} collective-permute-done((f32[136,128]{1,0:T(8,128)S(1)}, f32[136,128]{1,0:T(8,128)S(1)}, u32[]{:S(2)}, u32[]{:S(2)}) %collective-permute-start.2) | collective-permute-done | bytes 69664 | tf_op jit(solution)/shard_map/ppermute | solution.py:770
  29.9 4.4 %collective-permute-start.4 = (f32[136,256]{1,0:T(8,128)S(1)}, f32[136,256]{1,0:T(8,128)S(1)}, u32[]{:S(2)}, u32[]{:S(2)}) collective-permute-start(f32[136,256]{1,0:T(8,128)S(1)} %shard_map.103.own_far), channel_id=1, source_target_pairs={{0,4},{4,8},{8,12},{12,16},{16,20},{20,24},{24,28},{1,5},{5,9},{9,... | collective-permute-start | bytes 417800 | tf_op jit(solution)/shard_map/ppermute | solution.py:773
  35.3 2.0 %collective-permute-done.4.far = f32[136,256]{1,0:T(8,128)S(1)} collective-permute-done((f32[136,256]{1,0:T(8,128)S(1)}, f32[136,256]{1,0:T(8,128)S(1)}, u32[]{:S(2)}, u32[]{:S(2)}) %collective-permute-start.4) | collective-permute-done | bytes 139296 | tf_op jit(solution)/shard_map/ppermute | solution.py:773
  37.3 1.9 %shard_map.107.own = f32[264,512]{1,0:T(8,128)S(1)} custom-call(f32[128,768]{1,0:T(8,128)S(1)} %shard_map.102.own_near, f32[136,256]{1,0:T(8,128)S(1)} %shard_map.103.own_far, f32[128,768]{1,0:T(8,128)S(1)} %collective-permute-done.3.near, f32[136,256]{1,0:T(8,128)S(1)} %collective-permute-done.4.far, bf16[512,512]{1,0:T(8,128)(2,1)S(1)} %get-tuple-element.53.mh, ...), custom_call_target="tpu_custom_call" | custom-call | tf_op jit(solution)/shard_map/pallas_call | solution.py:756
  39.2 9.8 %collective-permute-start.8 = (f32[264,512]{1,0:T(8,128)S(1)}, f32[264,512]{1,0:T(8,128)S(1)}, u32[]{:S(2)}, u32[]{:S(2)}) collective-permute-start(f32[264,512]{1,0:T(8,128)S(1)} %shard_map.107.own), channel_id=1, source_target_pairs={{0,8},{4,12},{8,16},{12,20},{16,24},{20,28},{1,9},{5,13},{9,17},{1... | collective-permute-start | bytes 1622024 | tf_op jit(solution)/shard_map/ppermute | solution.py:773
  49.2 1.4 %shard_map.108 = (bf16[512,512]{1,0:T(8,128)(2,1)S(1)}, bf16[512,512]{1,0:T(8,128)(2,1)S(1)}, bf16[512,512]{1,0:T(8,128)(2,1)S(1)}, bf16[512,512]{1,0:T(8,128)(2,1)S(1)}, f32[512,256]{1,0:T(8,128)S(1)}) custom-call(s32[8,3]{1,0:T(8,128)S(1)} %copy.13.pattern, f32[768,128]{1,0:T(8,128)S(1)} %shard_map.105.halves, ...), custom_call_target="tpu_custom_call" | custom-call | tf_op jit(solution)/shard_map/pallas_call | solution.py:756
  50.9 2.5 %shard_map.109 = (f32[128,512]{1,0:T(8,128)S(1)}, f32[128,512]{1,0:T(8,128)S(1)}, f32[512,512]{1,0:T(8,128)S(1)}, bf16[512,512]{1,0:T(8,128)(2,1)S(1)}, bf16[512...) custom-call(s32[8,3]{1,0:T(8,128)S(1)} %copy.13.pattern, ...), custom_call_target="tpu_custom_call" | custom-call | tf_op jit(solution)/shard_map/pallas_call | solution.py:756
  53.4 1.2 %shard_map.110 = (bf16[512,512]{1,0:T(8,128)(2,1)S(1)}, bf16[512,512]{1,0:T(8,128)(2,1)S(1)}, bf16[512,512]{1,0:T(8,128)(2,1)S(1)}, bf16[512,512]{1,0:T(8,128)(2,1)S(1)}) custom-call(bf16[512,512]{1,0:T(8,128)(2,1)S(1)} %get-tuple-element.57.a0h, bf16[512,512]{1,0:T(8,128)(2,1)S(1)} %get-tuple-element.58.a0l, bf16[512,512]{1,0:T(8,128)(2,1)S(1)} %get-tuple-element.59.a1h, ...), custom_call_target="tpu_custom_call" | custom-call | tf_op jit(solution)/shard_map/pallas_call | solution.py:756
  54.9 5.5 %collective-permute-done.8.earlier = f32[264,512]{1,0:T(8,128)S(1)} collective-permute-done((f32[264,512]{1,0:T(8,128)S(1)}, f32[264,512]{1,0:T(8,128)S(1)}, u32[]{:S(2)}, u32[]{:S(2)}) %collective-permute-start.8) | collective-permute-done | bytes 540704 | tf_op jit(solution)/shard_map/ppermute | solution.py:773
  60.4 1.7 %shard_map.112 = (f32[520,128]{1,0:T(8,128)S(1)}, bf16[512,512]{1,0:T(8,128)(2,1)S(1)}, bf16[512,512]{1,0:T(8,128)(2,1)S(1)}) custom-call(f32[264,512]{1,0:T(8,128)S(1)} %shard_map.107.own, f32[264,512]{1,0:T(8,128)S(1)} %collective-permute-done.8.earlier, bf16[512,512]{1,0:T(8,128)(2,1)S(1)} %get-tuple-element.68.mh, ...), custom_call_target="tpu_custom_call" | custom-call | tf_op jit(solution)/shard_map/pallas_call | solution.py:756
  62.0 1.6 %collective-permute-start.13 = (f32[520,128]{1,0:T(8,128)S(1)}, f32[520,128]{1,0:T(8,128)S(1)}, u32[]{:S(2)}, u32[]{:S(2)}) collective-permute-start(f32[520,128]{1,0:T(8,128)S(1)} %get-tuple-element.80), channel_id=1, source_target_pairs={{0,2},{1,3},{2,0},{3,1},{4,6},{5,7},{6,4},{7,5},{8,10},{9,11},{10,... | collective-permute-start | bytes 798728 | tf_op jit(solution)/shard_map/ppermute | solution.py:770
  65.7 1.3 %collective-permute-start.16 = (f32[264,128]{1,0:T(8,128)S(1)}, f32[264,128]{1,0:T(8,128)S(1)}, u32[]{:S(2)}, u32[]{:S(2)}) collective-permute-start(f32[264,128]{1,0:T(8,128)S(1)} %get-tuple-element.86), channel_id=1, source_target_pairs={{0,3},{1,2},{2,1},{3,0},{4,7},{5,6},{6,5},{7,4},{8,11},{9,10},{10,... | collective-permute-start | bytes 405512 | tf_op jit(solution)/shard_map/ppermute | solution.py:770
  67.0 1.9 %collective-permute-done.13.from_chip = f32[520,128]{1,0:T(8,128)S(1)} collective-permute-done((f32[520,128]{1,0:T(8,128)S(1)}, f32[520,128]{1,0:T(8,128)S(1)}, u32[]{:S(2)}, u32[]{:S(2)}) %collective-permute-start.13) | collective-permute-done | bytes 266272 | tf_op jit(solution)/shard_map/ppermute | solution.py:770
  69.0 2.5 %collective-permute-start.14 = (f32[8,128]{1,0:T(8,128)S(1)}, f32[8,128]{1,0:T(8,128)S(1)}, u32[]{:S(2)}, u32[]{:S(2)}) collective-permute-start(f32[8,128]{1,0:T(8,128)S(1)} %get-tuple-element.75.short), channel_id=1, source_target_pairs={{0,2},{1,3},{2,0},{3,1},{4,6},{5,7},{6,4},{7,5},{8,10},{9,11},{10,... | collective-permute-start | bytes 12296 | tf_op jit(solution)/shard_map/ppermute | solution.py:770
  71.6 2.9 %collective-permute-done.12.dyn_recv = f32[128,512]{1,0:T(8,128)S(1)} collective-permute-done((f32[128,512]{1,0:T(8,128)S(1)}, f32[128,512]{1,0:T(8,128)S(1)}, u32[]{:S(2)}, u32[]{:S(2)}) %collective-permute-start.12) | collective-permute-done | bytes 262176 | tf_op jit(solution)/shard_map/ppermute | solution.py:770
  75.6 1.5 %collective-permute-done.14.chip_short = f32[8,128]{1,0:T(8,128)S(1)} collective-permute-done((f32[8,128]{1,0:T(8,128)S(1)}, f32[8,128]{1,0:T(8,128)S(1)}, u32[]{:S(2)}, u32[]{:S(2)}) %collective-permute-start.14) | collective-permute-done | bytes 4128 | tf_op jit(solution)/shard_map/ppermute | solution.py:770
  (32 shorter events, 6.1 us)
Async XLA Ops:
  0.6 9.5 %copy-start = (f32[2,128,192]{1,2,0:T(8,128)S(1)}, f32[2,128,192]{1,2,0:T(8,128)}, u32[]{:S(2)}) copy-start(f32[2,128,192]{1,2,0:T(8,128)} %param.6) | copy-start | bytes 589828
  0.6 9.5 %collective-permute-start.5 = (f32[2,192,128]{2,1,0:T(8,128)}, f32[2,192,128]{2,1,0:T(8,128)S(1)}, u32[]{:S(2)}, u32[]{:S(2)}) collective-permute-start(f32[2,192,128]{2,1,0:T(8,128)} %bitcast.1), channel_id=1, source_target_pairs={{0,4},{4,8},{8,12},{12,16},{16,20},{20,24},{24,28},{1,5},{5,9},{9,... | collective-permute-start | bytes 589832 | tf_op jit(solution)/shard_map/ppermute | solution.py:773
  6.9 9.2 %collective-permute-start = (f32[136,384]{1,0:T(8,128)S(1)}, f32[136,384]{1,0:T(8,128)S(1)}, u32[]{:S(2)}, u32[]{:S(2)}) collective-permute-start(f32[136,384]{1,0:T(8,128)S(1)} %get-tuple-element.49), channel_id=1, source_target_pairs={{0,1},{1,0},{2,3},{3,2},{4,5},{5,4},{6,7},{7,6},{8,9},{9,8},{10,11... | collective-permute-start | bytes 626696 | tf_op jit(solution)/shard_map/ppermute | solution.py:770
  10.1 5.9 %collective-permute-start.6 = (f32[384,128]{1,0:T(8,128)S(1)}, f32[384,128]{1,0:T(8,128)S(1)}, u32[]{:S(2)}, u32[]{:S(2)}) collective-permute-start(f32[384,128]{1,0:T(8,128)S(1)} %shard_map.104), channel_id=1, source_target_pairs={{0,2},{1,3},{2,0},{3,1},{4,6},{5,7},{6,4},{7,5},{8,10},{9,11},{10,... | collective-permute-start | bytes 589832 | tf_op jit(solution)/shard_map/ppermute | solution.py:770
  16.0 18.4 %collective-permute-start.7 = (f32[768,128]{1,0:T(8,128)S(1)}, f32[768,128]{1,0:T(8,128)S(1)}, u32[]{:S(2)}, u32[]{:S(2)}) collective-permute-start(f32[768,128]{1,0:T(8,128)S(1)} %shard_map.105.halves), channel_id=1, source_target_pairs={{0,1},{1,0},{2,3},{3,2},{4,5},{5,4},{6,7},{7,6},{8,9},{9,8},{10,11... | collective-permute-start | bytes 1179656 | tf_op jit(solution)/shard_map/ppermute | solution.py:770
  16.1 21.2 %collective-permute-start.3 = (f32[128,768]{1,0:T(8,128)S(1)}, f32[128,768]{1,0:T(8,128)S(1)}, u32[]{:S(2)}, u32[]{:S(2)}) collective-permute-start(f32[128,768]{1,0:T(8,128)S(1)} %shard_map.102.own_near), channel_id=1, source_target_pairs={{0,4},{4,8},{8,12},{12,16},{16,20},{20,24},{24,28},{1,5},{5,9},{9,... | collective-permute-start | bytes 1179656 | tf_op jit(solution)/shard_map/ppermute | solution.py:773
  20.5 9.4 %collective-permute-start.1 = (f32[136,256]{1,0:T(8,128)S(1)}, f32[136,256]{1,0:T(8,128)S(1)}, u32[]{:S(2)}, u32[]{:S(2)}) collective-permute-start(f32[136,256]{1,0:T(8,128)S(1)} %get-tuple-element.51), channel_id=1, source_target_pairs={{0,2},{1,3},{2,0},{3,1},{4,6},{5,7},{6,4},{7,5},{8,10},{9,11},{10,... | collective-permute-start | bytes 417800 | tf_op jit(solution)/shard_map/ppermute | solution.py:770
  22.0 27.0 %collective-permute-start.9 = (f32[768,128]{1,0:T(8,128)S(1)}, f32[768,128]{1,0:T(8,128)S(1)}, u32[]{:S(2)}, u32[]{:S(2)}) collective-permute-start(f32[768,128]{1,0:T(8,128)S(1)} %shard_map.105.halves), channel_id=1, source_target_pairs={{0,8},{4,12},{8,16},{12,20},{16,24},{20,28},{1,9},{5,13},{9,17},{1... | collective-permute-start | bytes 1179656 | tf_op jit(solution)/shard_map/ppermute | solution.py:773
  25.5 4.4 %collective-permute-start.2 = (f32[136,128]{1,0:T(8,128)S(1)}, f32[136,128]{1,0:T(8,128)S(1)}, u32[]{:S(2)}, u32[]{:S(2)}) collective-permute-start(f32[136,128]{1,0:T(8,128)S(1)} %get-tuple-element.52), channel_id=1, source_target_pairs={{0,3},{1,2},{2,1},{3,0},{4,7},{5,6},{6,5},{7,4},{8,11},{9,10},{10,... | collective-permute-start | bytes 208904 | tf_op jit(solution)/shard_map/ppermute | solution.py:770
  29.9 4.4 %copy-start.1 = (s32[8,3]{0,1:T(4,128)S(1)}, s32[8,3]{0,1:T(4,128)}, u32[]{:S(2)}) copy-start(s32[8,3]{0,1:T(4,128)} %param.7) | copy-start | bytes 292
  29.9 7.4 %collective-permute-start.4 = (f32[136,256]{1,0:T(8,128)S(1)}, f32[136,256]{1,0:T(8,128)S(1)}, u32[]{:S(2)}, u32[]{:S(2)}) collective-permute-start(f32[136,256]{1,0:T(8,128)S(1)} %shard_map.103.own_far), channel_id=1, source_target_pairs={{0,4},{4,8},{8,12},{12,16},{16,20},{20,24},{24,28},{1,5},{5,9},{9,... | collective-permute-start | bytes 417800 | tf_op jit(solution)/shard_map/ppermute | solution.py:773
  39.2 21.1 %collective-permute-start.8 = (f32[264,512]{1,0:T(8,128)S(1)}, f32[264,512]{1,0:T(8,128)S(1)}, u32[]{:S(2)}, u32[]{:S(2)}) collective-permute-start(f32[264,512]{1,0:T(8,128)S(1)} %shard_map.107.own), channel_id=1, source_target_pairs={{0,8},{4,12},{8,16},{12,20},{16,24},{20,28},{1,9},{5,13},{9,17},{1... | collective-permute-start | bytes 1622024 | tf_op jit(solution)/shard_map/ppermute | solution.py:773
  49.1 1.8 %collective-permute-start.10 = (f32[768,128]{1,0:T(8,128)S(1)}, f32[768,128]{1,0:T(8,128)S(1)}, u32[]{:S(2)}, u32[]{:S(2)}) collective-permute-start(f32[768,128]{1,0:T(8,128)S(1)} %collective-permute-done.9.halves), channel_id=1, source_target_pairs={{0,1},{1,0},{2,3},{3,2},{4,5},{5,4},{6,7},{7,6},{8,9},{9,8},{10,11... | collective-permute-start | bytes 1179656 | tf_op jit(solution)/shard_map/ppermute | solution.py:770
  62.0 6.8 %collective-permute-start.13 = (f32[520,128]{1,0:T(8,128)S(1)}, f32[520,128]{1,0:T(8,128)S(1)}, u32[]{:S(2)}, u32[]{:S(2)}) collective-permute-start(f32[520,128]{1,0:T(8,128)S(1)} %get-tuple-element.80), channel_id=1, source_target_pairs={{0,2},{1,3},{2,0},{3,1},{4,6},{5,7},{6,4},{7,5},{8,10},{9,11},{10,... | collective-permute-start | bytes 798728 | tf_op jit(solution)/shard_map/ppermute | solution.py:770
  65.0 9.5 %collective-permute-start.11 = (f32[520,128]{1,0:T(8,128)S(1)}, f32[520,128]{1,0:T(8,128)S(1)}, u32[]{:S(2)}, u32[]{:S(2)}) collective-permute-start(f32[520,128]{1,0:T(8,128)S(1)} %get-tuple-element.77), channel_id=1, source_target_pairs={{0,1},{1,0},{2,3},{3,2},{4,5},{5,4},{6,7},{7,6},{8,9},{9,8},{10,11... | collective-permute-start | bytes 798728 | tf_op jit(solution)/shard_map/ppermute | solution.py:770
  65.1 9.4 %collective-permute-start.12 = (f32[128,512]{1,0:T(8,128)S(1)}, f32[128,512]{1,0:T(8,128)S(1)}, u32[]{:S(2)}, u32[]{:S(2)}) collective-permute-start(f32[128,512]{1,0:T(8,128)S(1)} %get-tuple-element.79), channel_id=1, source_target_pairs={{0,2},{1,3},{2,0},{3,1},{4,6},{5,7},{6,4},{7,5},{8,10},{9,11},{10,... | collective-permute-start | bytes 786440 | tf_op jit(solution)/shard_map/ppermute | solution.py:770
  65.7 11.4 %collective-permute-start.16 = (f32[264,128]{1,0:T(8,128)S(1)}, f32[264,128]{1,0:T(8,128)S(1)}, u32[]{:S(2)}, u32[]{:S(2)}) collective-permute-start(f32[264,128]{1,0:T(8,128)S(1)} %get-tuple-element.86), channel_id=1, source_target_pairs={{0,3},{1,2},{2,1},{3,0},{4,7},{5,6},{6,5},{7,4},{8,11},{9,10},{10,... | collective-permute-start | bytes 405512 | tf_op jit(solution)/shard_map/ppermute | solution.py:770
  69.0 8.1 %collective-permute-start.15 = (f32[256,128]{1,0:T(8,128)S(1)}, f32[256,128]{1,0:T(8,128)S(1)}, u32[]{:S(2)}, u32[]{:S(2)}) collective-permute-start(f32[256,128]{1,0:T(8,128)S(1)} %get-tuple-element.85), channel_id=1, source_target_pairs={{0,1},{1,0},{2,3},{3,2},{4,5},{5,4},{6,7},{7,6},{8,9},{9,8},{10,11... | collective-permute-start | bytes 393224 | tf_op jit(solution)/shard_map/ppermute | solution.py:770
  69.0 8.1 %collective-permute-start.14 = (f32[8,128]{1,0:T(8,128)S(1)}, f32[8,128]{1,0:T(8,128)S(1)}, u32[]{:S(2)}, u32[]{:S(2)}) collective-permute-start(f32[8,128]{1,0:T(8,128)S(1)} %get-tuple-element.75.short), channel_id=1, source_target_pairs={{0,2},{1,3},{2,0},{3,1},{4,6},{5,7},{6,4},{7,5},{8,10},{9,11},{10,... | collective-permute-start | bytes 12296 | tf_op jit(solution)/shard_map/ppermute | solution.py:770

commit v7 on v6

--- a/solution.py
+++ b/solution.py
@@ -410,7 +410,8 @@
     n = 4 * r
     extra = slice(n, n + 16)
     first = c == 0
-    xn = jnp.where(first, near[...], own_near[...])
+    came = jnp.where(has(1) == 1, near[...], 0.0)
+    xn = jnp.where(first, came, own_near[...])
     xf = jnp.where(first, far[...], own_far[...])
     x = jnp.concatenate(
         [
@@ -438,7 +439,7 @@
     top = dot3(sh[...], sl[...], uh, ul)
     low = dot3(th[2 * r :, :], tl[2 * r :, :], uh[:, 2 * r :], ul[:, 2 * r :])
     vec = jnp.where(first, b_own, e_before) + u[n : n + 1, :] + top[2 * r : 2 * r + 1, :]
-    dn = jnp.where(first, own_near[...], near[...])
+    dn = jnp.where(first, own_near[...], came)
     df = jnp.where(first, own_far[...], far[...])
     z11 = top[r : 2 * r, r : 2 * r]
     z33 = low[r : 2 * r, r : 2 * r]
@@ -769,8 +770,9 @@
     def swap(value, bit):
         return lax.ppermute(value, "col", [(i, i ^ bit) for i in range(cols)])
 
-    def later(value, distance):
-        return lax.ppermute(value, "tm", [(i, i + distance) for i in range(tms - distance)])
+    def later(value, distance, cyclic=False):
+        count = tms if cyclic else tms - distance
+        return lax.ppermute(value, "tm", [(i, (i + distance) % tms) for i in range(count)])
 
     def hbm(*arrays):
         return [(IN_HBM, x) for x in arrays]
@@ -791,7 +793,7 @@
         return pltpu.SemaphoreType.DMA((count,))
 
     turned = jnp.swapaxes(blocks, 1, 2)
-    before = later(turned, 1)
+    before = later(turned, 1, cyclic=True)
     to_core, to_chip, to_far, panel, vecs = kernel(
         send_kernel,
         hbm(cov, cost, drift, eta),
@@ -802,7 +804,7 @@
     from_chip = swap(to_chip, 2)
     from_far = swap(to_far, 3)
     (own_near,) = kernel(pack_near_kernel, vmem(panel, from_core), vmem(shape(r, 6 * r)))
-    near = later(own_near, 1)
+    near = later(own_near, 1, cyclic=True)
     (own_far,) = kernel(
         pack_far_kernel, vmem(vecs, from_core, from_chip, from_far), vmem(shape(r + 8, 2 * r))
     )
@@ -811,7 +813,7 @@
     other = swap(picked, 2)
     (halves,) = kernel(halves_kernel, vmem(turned, before, other), vmem(shape(12 * bs, r)))
     core_halves = swap(halves, 1)
-    far_halves = later(halves, 2)
+    far_halves = later(halves, 2, cyclic=True)
     m1 = kernel(
         functools.partial(prepare_kernel, bs),
         vmem(pattern, halves, core_halves),

time: 78.2 us -> 74.3 us (0.950)
  starting transfers between devices: 36.6 us -> 26.4 us
  waiting for transfers between devices: 25.7 us -> 32.1 us
    ppermute x5, starting transfers between devices: 27 us -> 16.7 us  [later(): lax.ppermute(value, 'tm', [(i, (i + distance) % tms) for i in range(count)])]
    ppermute x5, waiting for transfers between devices: 10.6 us -> 15.7 us  [later(): lax.ppermute(value, 'tm', [(i, (i + distance) % tms) for i in range(count)])]
    ppermute x12, waiting for transfers between devices: 15.2 us -> 16.4 us  [swap(): return lax.ppermute(value, 'col', [(i, i ^ bit) for i in range(cols)])]
  transfers between devices with their start and end apart: 17 -> 17, of which waited for: 9 -> 10; matrix products, arithmetic and copies ran while one was open for 0% -> 0% of each run, Pallas kernels for 16% -> 16%
where the time goes in v7:
time: 74.3 us; the launch traced here: 74.1 us
  waiting for transfers between devices  32.1 us (43%)
  starting transfers between devices  26.4 us (36%)
  Pallas kernels  14.6 us (20%)
  between operations  0.83 us (1%)
    ppermute x5, starting transfers between devices, later(): lax.ppermute(value, 'tm', [(i, (i + distance) % tms) for i in range(count)])  16.7 us
    ppermute x12, waiting for transfers between devices, swap(): return lax.ppermute(value, 'col', [(i, i ^ bit) for i in range(cols)])  16.4 us
    ppermute x5, waiting for transfers between devices, later(): lax.ppermute(value, 'tm', [(i, (i + distance) % tms) for i in range(count)])  15.7 us
    pallas_call x17, Pallas kernels, kernel(): call(*(pltpu.with_memory_space_constraint(x, kept[where]) if where in kep...  14.6 us
    ppermute x12, starting transfers between devices, swap(): return lax.ppermute(value, 'col', [(i, i ^ bit) for i in range(cols)])  9.73 us
  transfers between devices with their start and end apart: 17, of which 10 were waited for; matrix products, arithmetic and copies ran while one was open for 0% of the time, Pallas kernels for 16%

profile of v7, /device:TPU:0, one launch (start us, length us, event | category | flops | bytes accessed | tf_op | source)
XLA Modules:
  0.0 74.1 jit_solution(12555920471927369526)
XLA Ops:
  0.6 3.0 %collective-permute-start.5 = (f32[2,192,128]{2,1,0:T(8,128)}, f32[2,192,128]{2,1,0:T(8,128)S(1)}, u32[]{:S(2)}, u32[]{:S(2)}) collective-permute-start(f32[2,192,128]{2,1,0:T(8,128)} %bitcast.1), channel_id=1, source_target_pairs={{0,4},{4,8},{8,12},{12,16},{16,20},{20,24},{24,28},{28,0},{1,5},{5... | collective-permute-start | bytes 589832 | tf_op jit(solution)/shard_map/ppermute | solution.py:775
  3.7 1.2 %shard_map.101 = (f32[136,384]{1,0:T(8,128)S(1)}, f32[136,256]{1,0:T(8,128)S(1)}, f32[136,128]{1,0:T(8,128)S(1)}, f32[128,512]{1,0:T(8,128)S(1)}, f32[8,128]{1,0:T(8,128)S(1)}) custom-call(f32[2,128,512]{2,1,0:T(8,128)} %cov.1, f32[2,128,512]{2,1,0:T(8,128)} %cost.1, f32[2,128]{1,0:T(2,128)} %drift.1, f32[2,128]{1,0:T(2,128)} %eta.1), custom_call_target="tpu_custom_call" | custom-call | tf_op jit(solution)/shard_map/pallas_call | solution.py:757
  5.0 6.8 %collective-permute-done.5.before = f32[2,192,128]{2,1,0:T(8,128)S(1)} collective-permute-done((f32[2,192,128]{2,1,0:T(8,128)}, f32[2,192,128]{2,1,0:T(8,128)S(1)}, u32[]{:S(2)}, u32[]{:S(2)}) %collective-permute-start.5) | collective-permute-done | bytes 196640 | tf_op jit(solution)/shard_map/ppermute | solution.py:775
  11.8 1.6 %collective-permute-start.6 = (f32[384,128]{1,0:T(8,128)S(1)}, f32[384,128]{1,0:T(8,128)S(1)}, u32[]{:S(2)}, u32[]{:S(2)}) collective-permute-start(f32[384,128]{1,0:T(8,128)S(1)} %shard_map.104), channel_id=1, source_target_pairs={{0,2},{1,3},{2,0},{3,1},{4,6},{5,7},{6,4},{7,5},{8,10},{9,11},{10,... | collective-permute-start | bytes 589832 | tf_op jit(solution)/shard_map/ppermute | solution.py:771
  13.4 4.5 %collective-permute-done.6.other = f32[384,128]{1,0:T(8,128)S(1)} collective-permute-done((f32[384,128]{1,0:T(8,128)S(1)}, f32[384,128]{1,0:T(8,128)S(1)}, u32[]{:S(2)}, u32[]{:S(2)}) %collective-permute-start.6) | collective-permute-done | bytes 196640 | tf_op jit(solution)/shard_map/ppermute | solution.py:771
  18.2 1.4 %collective-permute-start.1 = (f32[136,256]{1,0:T(8,128)S(1)}, f32[136,256]{1,0:T(8,128)S(1)}, u32[]{:S(2)}, u32[]{:S(2)}) collective-permute-start(f32[136,256]{1,0:T(8,128)S(1)} %get-tuple-element.51), channel_id=1, source_target_pairs={{0,2},{1,3},{2,0},{3,1},{4,6},{5,7},{6,4},{7,5},{8,10},{9,11},{10,... | collective-permute-start | bytes 417800 | tf_op jit(solution)/shard_map/ppermute | solution.py:771
  20.1 5.2 %collective-permute-done.2.from_far = f32[136,128]{1,0:T(8,128)S(1)} collective-permute-done((f32[136,128]{1,0:T(8,128)S(1)}, f32[136,128]{1,0:T(8,128)S(1)}, u32[]{:S(2)}, u32[]{:S(2)}) %collective-permute-start.2) | collective-permute-done | bytes 69664 | tf_op jit(solution)/shard_map/ppermute | solution.py:771
  25.4 3.0 %collective-permute-start.4 = (f32[136,256]{1,0:T(8,128)S(1)}, f32[136,256]{1,0:T(8,128)S(1)}, u32[]{:S(2)}, u32[]{:S(2)}) collective-permute-start(f32[136,256]{1,0:T(8,128)S(1)} %shard_map.103.own_far), channel_id=1, source_target_pairs={{0,4},{4,8},{8,12},{12,16},{16,20},{20,24},{24,28},{1,5},{5,9},{9,... | collective-permute-start | bytes 417800 | tf_op jit(solution)/shard_map/ppermute | solution.py:775
  29.5 2.0 %collective-permute-done.4.far = f32[136,256]{1,0:T(8,128)S(1)} collective-permute-done((f32[136,256]{1,0:T(8,128)S(1)}, f32[136,256]{1,0:T(8,128)S(1)}, u32[]{:S(2)}, u32[]{:S(2)}) %collective-permute-start.4) | collective-permute-done | bytes 139296 | tf_op jit(solution)/shard_map/ppermute | solution.py:775
  31.4 1.4 %collective-permute-done.3.near = f32[128,768]{1,0:T(8,128)S(1)} collective-permute-done((f32[128,768]{1,0:T(8,128)S(1)}, f32[128,768]{1,0:T(8,128)S(1)}, u32[]{:S(2)}, u32[]{:S(2)}) %collective-permute-start.3) | collective-permute-done | bytes 393248 | tf_op jit(solution)/shard_map/ppermute | solution.py:775
  32.9 1.9 %shard_map.107.own = f32[264,512]{1,0:T(8,128)S(1)} custom-call(f32[128,768]{1,0:T(8,128)S(1)} %shard_map.102.own_near, f32[136,256]{1,0:T(8,128)S(1)} %shard_map.103.own_far, f32[128,768]{1,0:T(8,128)S(1)} %collective-permute-done.3.near, f32[136,256]{1,0:T(8,128)S(1)} %collective-permute-done.4.far, bf16[512,512]{1,0:T(8,128)(2,1)S(1)} %get-tuple-element.53.mh, ...), custom_call_target="tpu_custom_call" | custom-call | tf_op jit(solution)/shard_map/pallas_call | solution.py:757
  34.8 10.5 %collective-permute-start.8 = (f32[264,512]{1,0:T(8,128)S(1)}, f32[264,512]{1,0:T(8,128)S(1)}, u32[]{:S(2)}, u32[]{:S(2)}) collective-permute-start(f32[264,512]{1,0:T(8,128)S(1)} %shard_map.107.own), channel_id=1, source_target_pairs={{0,8},{4,12},{8,16},{12,20},{16,24},{20,28},{1,9},{5,13},{9,17},{1... | collective-permute-start | bytes 1622024 | tf_op jit(solution)/shard_map/ppermute | solution.py:775
  45.4 1.4 %shard_map.108 = (bf16[512,512]{1,0:T(8,128)(2,1)S(1)}, bf16[512,512]{1,0:T(8,128)(2,1)S(1)}, bf16[512,512]{1,0:T(8,128)(2,1)S(1)}, bf16[512,512]{1,0:T(8,128)(2,1)S(1)}, f32[512,256]{1,0:T(8,128)S(1)}) custom-call(s32[8,3]{1,0:T(8,128)S(1)} %copy.13.pattern, f32[768,128]{1,0:T(8,128)S(1)} %shard_map.105.halves, ...), custom_call_target="tpu_custom_call" | custom-call | tf_op jit(solution)/shard_map/pallas_call | solution.py:757
  47.1 2.5 %shard_map.109 = (f32[128,512]{1,0:T(8,128)S(1)}, f32[128,512]{1,0:T(8,128)S(1)}, f32[512,512]{1,0:T(8,128)S(1)}, bf16[512,512]{1,0:T(8,128)(2,1)S(1)}, bf16[512...) custom-call(s32[8,3]{1,0:T(8,128)S(1)} %copy.13.pattern, ...), custom_call_target="tpu_custom_call" | custom-call | tf_op jit(solution)/shard_map/pallas_call | solution.py:757
  49.6 1.2 %shard_map.110 = (bf16[512,512]{1,0:T(8,128)(2,1)S(1)}, bf16[512,512]{1,0:T(8,128)(2,1)S(1)}, bf16[512,512]{1,0:T(8,128)(2,1)S(1)}, bf16[512,512]{1,0:T(8,128)(2,1)S(1)}) custom-call(bf16[512,512]{1,0:T(8,128)(2,1)S(1)} %get-tuple-element.57.a0h, bf16[512,512]{1,0:T(8,128)(2,1)S(1)} %get-tuple-element.58.a0l, bf16[512,512]{1,0:T(8,128)(2,1)S(1)} %get-tuple-element.59.a1h, ...), custom_call_target="tpu_custom_call" | custom-call | tf_op jit(solution)/shard_map/pallas_call | solution.py:757
  51.1 5.5 %collective-permute-done.8.earlier = f32[264,512]{1,0:T(8,128)S(1)} collective-permute-done((f32[264,512]{1,0:T(8,128)S(1)}, f32[264,512]{1,0:T(8,128)S(1)}, u32[]{:S(2)}, u32[]{:S(2)}) %collective-permute-start.8) | collective-permute-done | bytes 540704 | tf_op jit(solution)/shard_map/ppermute | solution.py:775
  56.5 1.7 %shard_map.112 = (f32[520,128]{1,0:T(8,128)S(1)}, bf16[512,512]{1,0:T(8,128)(2,1)S(1)}, bf16[512,512]{1,0:T(8,128)(2,1)S(1)}) custom-call(f32[264,512]{1,0:T(8,128)S(1)} %shard_map.107.own, f32[264,512]{1,0:T(8,128)S(1)} %collective-permute-done.8.earlier, bf16[512,512]{1,0:T(8,128)(2,1)S(1)} %get-tuple-element.68.mh, ...), custom_call_target="tpu_custom_call" | custom-call | tf_op jit(solution)/shard_map/pallas_call | solution.py:757
  58.2 1.6 %collective-permute-start.13 = (f32[520,128]{1,0:T(8,128)S(1)}, f32[520,128]{1,0:T(8,128)S(1)}, u32[]{:S(2)}, u32[]{:S(2)}) collective-permute-start(f32[520,128]{1,0:T(8,128)S(1)} %get-tuple-element.80), channel_id=1, source_target_pairs={{0,2},{1,3},{2,0},{3,1},{4,6},{5,7},{6,4},{7,5},{8,10},{9,11},{10,... | collective-permute-start | bytes 798728 | tf_op jit(solution)/shard_map/ppermute | solution.py:771
  61.9 1.3 %collective-permute-start.16 = (f32[264,128]{1,0:T(8,128)S(1)}, f32[264,128]{1,0:T(8,128)S(1)}, u32[]{:S(2)}, u32[]{:S(2)}) collective-permute-start(f32[264,128]{1,0:T(8,128)S(1)} %get-tuple-element.86), channel_id=1, source_target_pairs={{0,3},{1,2},{2,1},{3,0},{4,7},{5,6},{6,5},{7,4},{8,11},{9,10},{10,... | collective-permute-start | bytes 405512 | tf_op jit(solution)/shard_map/ppermute | solution.py:771
  63.2 1.9 %collective-permute-done.13.from_chip = f32[520,128]{1,0:T(8,128)S(1)} collective-permute-done((f32[520,128]{1,0:T(8,128)S(1)}, f32[520,128]{1,0:T(8,128)S(1)}, u32[]{:S(2)}, u32[]{:S(2)}) %collective-permute-start.13) | collective-permute-done | bytes 266272 | tf_op jit(solution)/shard_map/ppermute | solution.py:771
  65.2 2.5 %collective-permute-start.14 = (f32[8,128]{1,0:T(8,128)S(1)}, f32[8,128]{1,0:T(8,128)S(1)}, u32[]{:S(2)}, u32[]{:S(2)}) collective-permute-start(f32[8,128]{1,0:T(8,128)S(1)} %get-tuple-element.75.short), channel_id=1, source_target_pairs={{0,2},{1,3},{2,0},{3,1},{4,6},{5,7},{6,4},{7,5},{8,10},{9,11},{10,... | collective-permute-start | bytes 12296 | tf_op jit(solution)/shard_map/ppermute | solution.py:771
  67.8 2.9 %collective-permute-done.12.dyn_recv = f32[128,512]{1,0:T(8,128)S(1)} collective-permute-done((f32[128,512]{1,0:T(8,128)S(1)}, f32[128,512]{1,0:T(8,128)S(1)}, u32[]{:S(2)}, u32[]{:S(2)}) %collective-permute-start.12) | collective-permute-done | bytes 262176 | tf_op jit(solution)/shard_map/ppermute | solution.py:771
  70.7 1.2 %shard_map.116 = (f32[2,128,512]{2,1,0:T(8,128)}, f32[2,128,512]{2,1,0:T(8,128)}, f32[2,128,512]{2,1,0:T(8,128)}) custom-call(f32[512,128]{1,0:T(8,128)S(1)} %get-tuple-element.76.keep, f32[520,128]{1,0:T(8,128)S(1)} %collective-permute-done.11.from_core, f32[128,512]{1,0:T(8,128)S(1)} %get-tuple-element.78.dyn_own, ...), custom_call_target="tpu_custom_call" | custom-call | tf_op jit(solution)/shard_map/pallas_call | solution.py:757
  71.8 1.5 %collective-permute-done.14.chip_short = f32[8,128]{1,0:T(8,128)S(1)} collective-permute-done((f32[8,128]{1,0:T(8,128)S(1)}, f32[8,128]{1,0:T(8,128)S(1)}, u32[]{:S(2)}, u32[]{:S(2)}) %collective-permute-start.14) | collective-permute-done | bytes 4128 | tf_op jit(solution)/shard_map/ppermute | solution.py:771
  (32 shorter events, 5.4 us)
Async XLA Ops:
  0.6 11.2 %copy-start = (f32[2,128,192]{1,2,0:T(8,128)S(1)}, f32[2,128,192]{1,2,0:T(8,128)}, u32[]{:S(2)}) copy-start(f32[2,128,192]{1,2,0:T(8,128)} %param.6) | copy-start | bytes 589828
  0.6 11.2 %collective-permute-start.5 = (f32[2,192,128]{2,1,0:T(8,128)}, f32[2,192,128]{2,1,0:T(8,128)S(1)}, u32[]{:S(2)}, u32[]{:S(2)}) collective-permute-start(f32[2,192,128]{2,1,0:T(8,128)} %bitcast.1), channel_id=1, source_target_pairs={{0,4},{4,8},{8,12},{12,16},{16,20},{20,24},{24,28},{28,0},{1,5},{5... | collective-permute-start | bytes 589832 | tf_op jit(solution)/shard_map/ppermute | solution.py:775
  4.9 13.2 %collective-permute-start = (f32[136,384]{1,0:T(8,128)S(1)}, f32[136,384]{1,0:T(8,128)S(1)}, u32[]{:S(2)}, u32[]{:S(2)}) collective-permute-start(f32[136,384]{1,0:T(8,128)S(1)} %get-tuple-element.49), channel_id=1, source_target_pairs={{0,1},{1,0},{2,3},{3,2},{4,5},{5,4},{6,7},{7,6},{8,9},{9,8},{10,11... | collective-permute-start | bytes 626696 | tf_op jit(solution)/shard_map/ppermute | solution.py:771
  11.8 6.1 %collective-permute-start.6 = (f32[384,128]{1,0:T(8,128)S(1)}, f32[384,128]{1,0:T(8,128)S(1)}, u32[]{:S(2)}, u32[]{:S(2)}) collective-permute-start(f32[384,128]{1,0:T(8,128)S(1)} %shard_map.104), channel_id=1, source_target_pairs={{0,2},{1,3},{2,0},{3,1},{4,6},{5,7},{6,4},{7,5},{8,10},{9,11},{10,... | collective-permute-start | bytes 589832 | tf_op jit(solution)/shard_map/ppermute | solution.py:771
  18.0 10.5 %collective-permute-start.7 = (f32[768,128]{1,0:T(8,128)S(1)}, f32[768,128]{1,0:T(8,128)S(1)}, u32[]{:S(2)}, u32[]{:S(2)}) collective-permute-start(f32[768,128]{1,0:T(8,128)S(1)} %shard_map.105.halves), channel_id=1, source_target_pairs={{0,1},{1,0},{2,3},{3,2},{4,5},{5,4},{6,7},{7,6},{8,9},{9,8},{10,11... | collective-permute-start | bytes 1179656 | tf_op jit(solution)/shard_map/ppermute | solution.py:771
  18.1 14.7 %collective-permute-start.3 = (f32[128,768]{1,0:T(8,128)S(1)}, f32[128,768]{1,0:T(8,128)S(1)}, u32[]{:S(2)}, u32[]{:S(2)}) collective-permute-start(f32[128,768]{1,0:T(8,128)S(1)} %shard_map.102.own_near), channel_id=1, source_target_pairs={{0,4},{4,8},{8,12},{12,16},{16,20},{20,24},{24,28},{28,0},{1,5},{5... | collective-permute-start | bytes 1179656 | tf_op jit(solution)/shard_map/ppermute | solution.py:775
  18.2 7.1 %collective-permute-start.1 = (f32[136,256]{1,0:T(8,128)S(1)}, f32[136,256]{1,0:T(8,128)S(1)}, u32[]{:S(2)}, u32[]{:S(2)}) collective-permute-start(f32[136,256]{1,0:T(8,128)S(1)} %get-tuple-element.51), channel_id=1, source_target_pairs={{0,2},{1,3},{2,0},{3,1},{4,6},{5,7},{6,4},{7,5},{8,10},{9,11},{10,... | collective-permute-start | bytes 417800 | tf_op jit(solution)/shard_map/ppermute | solution.py:771
  19.6 25.7 %collective-permute-start.9 = (f32[768,128]{1,0:T(8,128)S(1)}, f32[768,128]{1,0:T(8,128)S(1)}, u32[]{:S(2)}, u32[]{:S(2)}) collective-permute-start(f32[768,128]{1,0:T(8,128)S(1)} %shard_map.105.halves), channel_id=1, source_target_pairs={{0,8},{4,12},{8,16},{12,20},{16,24},{20,28},{24,0},{28,4},{1,9},{5... | collective-permute-start | bytes 1179656 | tf_op jit(solution)/shard_map/ppermute | solution.py:775
  19.7 5.6 %collective-permute-start.2 = (f32[136,128]{1,0:T(8,128)S(1)}, f32[136,128]{1,0:T(8,128)S(1)}, u32[]{:S(2)}, u32[]{:S(2)}) collective-permute-start(f32[136,128]{1,0:T(8,128)S(1)} %get-tuple-element.52), channel_id=1, source_target_pairs={{0,3},{1,2},{2,1},{3,0},{4,7},{5,6},{6,5},{7,4},{8,11},{9,10},{10,... | collective-permute-start | bytes 208904 | tf_op jit(solution)/shard_map/ppermute | solution.py:771
  25.3 3.1 %copy-start.1 = (s32[8,3]{0,1:T(4,128)S(1)}, s32[8,3]{0,1:T(4,128)}, u32[]{:S(2)}) copy-start(s32[8,3]{0,1:T(4,128)} %param.7) | copy-start | bytes 292
  25.4 6.0 %collective-permute-start.4 = (f32[136,256]{1,0:T(8,128)S(1)}, f32[136,256]{1,0:T(8,128)S(1)}, u32[]{:S(2)}, u32[]{:S(2)}) collective-permute-start(f32[136,256]{1,0:T(8,128)S(1)} %shard_map.103.own_far), channel_id=1, source_target_pairs={{0,4},{4,8},{8,12},{12,16},{16,20},{20,24},{24,28},{1,5},{5,9},{9,... | collective-permute-start | bytes 417800 | tf_op jit(solution)/shard_map/ppermute | solution.py:775
  34.8 21.8 %collective-permute-start.8 = (f32[264,512]{1,0:T(8,128)S(1)}, f32[264,512]{1,0:T(8,128)S(1)}, u32[]{:S(2)}, u32[]{:S(2)}) collective-permute-start(f32[264,512]{1,0:T(8,128)S(1)} %shard_map.107.own), channel_id=1, source_target_pairs={{0,8},{4,12},{8,16},{12,20},{16,24},{20,28},{1,9},{5,13},{9,17},{1... | collective-permute-start | bytes 1622024 | tf_op jit(solution)/shard_map/ppermute | solution.py:775
  45.3 1.8 %collective-permute-start.10 = (f32[768,128]{1,0:T(8,128)S(1)}, f32[768,128]{1,0:T(8,128)S(1)}, u32[]{:S(2)}, u32[]{:S(2)}) collective-permute-start(f32[768,128]{1,0:T(8,128)S(1)} %collective-permute-done.9.halves), channel_id=1, source_target_pairs={{0,1},{1,0},{2,3},{3,2},{4,5},{5,4},{6,7},{7,6},{8,9},{9,8},{10,11... | collective-permute-start | bytes 1179656 | tf_op jit(solution)/shard_map/ppermute | solution.py:771
  58.2 6.8 %collective-permute-start.13 = (f32[520,128]{1,0:T(8,128)S(1)}, f32[520,128]{1,0:T(8,128)S(1)}, u32[]{:S(2)}, u32[]{:S(2)}) collective-permute-start(f32[520,128]{1,0:T(8,128)S(1)} %get-tuple-element.80), channel_id=1, source_target_pairs={{0,2},{1,3},{2,0},{3,1},{4,6},{5,7},{6,4},{7,5},{8,10},{9,11},{10,... | collective-permute-start | bytes 798728 | tf_op jit(solution)/shard_map/ppermute | solution.py:771
  61.2 9.4 %collective-permute-start.11 = (f32[520,128]{1,0:T(8,128)S(1)}, f32[520,128]{1,0:T(8,128)S(1)}, u32[]{:S(2)}, u32[]{:S(2)}) collective-permute-start(f32[520,128]{1,0:T(8,128)S(1)} %get-tuple-element.77), channel_id=1, source_target_pairs={{0,1},{1,0},{2,3},{3,2},{4,5},{5,4},{6,7},{7,6},{8,9},{9,8},{10,11... | collective-permute-start | bytes 798728 | tf_op jit(solution)/shard_map/ppermute | solution.py:771
  61.3 9.4 %collective-permute-start.12 = (f32[128,512]{1,0:T(8,128)S(1)}, f32[128,512]{1,0:T(8,128)S(1)}, u32[]{:S(2)}, u32[]{:S(2)}) collective-permute-start(f32[128,512]{1,0:T(8,128)S(1)} %get-tuple-element.79), channel_id=1, source_target_pairs={{0,2},{1,3},{2,0},{3,1},{4,6},{5,7},{6,4},{7,5},{8,10},{9,11},{10,... | collective-permute-start | bytes 786440 | tf_op jit(solution)/shard_map/ppermute | solution.py:771
  61.9 11.4 %collective-permute-start.16 = (f32[264,128]{1,0:T(8,128)S(1)}, f32[264,128]{1,0:T(8,128)S(1)}, u32[]{:S(2)}, u32[]{:S(2)}) collective-permute-start(f32[264,128]{1,0:T(8,128)S(1)} %get-tuple-element.86), channel_id=1, source_target_pairs={{0,3},{1,2},{2,1},{3,0},{4,7},{5,6},{6,5},{7,4},{8,11},{9,10},{10,... | collective-permute-start | bytes 405512 | tf_op jit(solution)/shard_map/ppermute | solution.py:771
  65.2 8.1 %collective-permute-start.15 = (f32[256,128]{1,0:T(8,128)S(1)}, f32[256,128]{1,0:T(8,128)S(1)}, u32[]{:S(2)}, u32[]{:S(2)}) collective-permute-start(f32[256,128]{1,0:T(8,128)S(1)} %get-tuple-element.85), channel_id=1, source_target_pairs={{0,1},{1,0},{2,3},{3,2},{4,5},{5,4},{6,7},{7,6},{8,9},{9,8},{10,11... | collective-permute-start | bytes 393224 | tf_op jit(solution)/shard_map/ppermute | solution.py:771
  65.2 8.1 %collective-permute-start.14 = (f32[8,128]{1,0:T(8,128)S(1)}, f32[8,128]{1,0:T(8,128)S(1)}, u32[]{:S(2)}, u32[]{:S(2)}) collective-permute-start(f32[8,128]{1,0:T(8,128)S(1)} %get-tuple-element.75.short), channel_id=1, source_target_pairs={{0,2},{1,3},{2,0},{3,1},{4,6},{5,7},{6,4},{7,5},{8,10},{9,11},{10,... | collective-permute-start | bytes 12296 | tf_op jit(solution)/shard_map/ppermute | solution.py:771

commit v8 on v7

--- a/solution.py
+++ b/solution.py
@@ -323,32 +323,37 @@
 
 def dense_turned(put, pattern, own_half, core_half, flag, n, r, bs):
     q = place_of()[0]
-    lane = lax.broadcasted_iota(jnp.int32, (bs, r), 1) // bs
+    sub = 8
+    lane = lax.broadcasted_iota(jnp.int32, (sub, r), 1) // bs
     rows = lax.broadcasted_iota(jnp.int32, (bs, r), 0)
     cols = lax.broadcasted_iota(jnp.int32, (bs, r), 1)
     per = r // bs
     height = 3 * bs
     for j in range(4):
         half = own_half if j % 2 == 0 else core_half
-        full = half[(j // 2) * height : (j // 2 + 1) * height, :]
-        wanted = []
+        pieces, wanted = [], []
         for k in range(3):
-            want = jnp.zeros((bs, r), jnp.int32)
+            at = (j // 2) * height + k * bs
+            pieces.append(half[at : at + bs, :].reshape(bs // sub, sub, r))
+            want = jnp.zeros((sub, r), jnp.int32)
             for h in range(per):
                 block = pattern[pl.ds((q ^ j) * per + h, 1), :][:, k : k + 1] ^ (q * per)
-                want = jnp.where(lane == h, jnp.broadcast_to(block, (bs, r)), want)
+                want = jnp.where(lane == h, jnp.broadcast_to(block, (sub, r)), want)
             wanted.append(jnp.where(flag == 1, want, -1))
         for block in range(n // bs):
             if j * r <= block * bs < (j + 1) * r:
                 value = jnp.where(
                     jnp.logical_and(rows + block * bs == cols + j * r, flag == 0), 1.0, 0.0
-                )
+                ).reshape(bs // sub, sub, r)
             else:
-                value = jnp.zeros((bs, r), F32)
+                value = jnp.zeros((bs // sub, sub, r), F32)
             for k in range(3):
-                piece = full[k * bs : (k + 1) * bs, :]
-                value = value + jnp.where(wanted[k] == block, piece, 0.0)
-            put(slice(block * bs, (block + 1) * bs), slice(j * r, (j + 1) * r), value)
+                value = jnp.where((wanted[k] == block)[None], pieces[k], value)
+            put(
+                slice(block * bs, (block + 1) * bs),
+                slice(j * r, (j + 1) * r),
+                value.reshape(bs, r),
+            )
 
 
 def put_split(hi_ref, lo_ref, rows, cols, value):

time: 74.3 us -> 74.3 us (level)
  no operation moved by 1% of the time
where the time goes in v8:
time: 74.3 us; the launch traced here: 74.1 us
  waiting for transfers between devices  32.1 us (43%)
  starting transfers between devices  26.4 us (36%)
  Pallas kernels  14.6 us (20%)
  between operations  0.84 us (1%)
    ppermute x5, starting transfers between devices, later(): lax.ppermute(value, 'tm', [(i, (i + distance) % tms) for i in range(count)])  16.7 us
    ppermute x12, waiting for transfers between devices, swap(): return lax.ppermute(value, 'col', [(i, i ^ bit) for i in range(cols)])  16.3 us
    ppermute x5, waiting for transfers between devices, later(): lax.ppermute(value, 'tm', [(i, (i + distance) % tms) for i in range(count)])  15.8 us
    pallas_call x17, Pallas kernels, kernel(): call(*(pltpu.with_memory_space_constraint(x, kept[where]) if where in kep...  14.6 us
    ppermute x12, starting transfers between devices, swap(): return lax.ppermute(value, 'col', [(i, i ^ bit) for i in range(cols)])  9.73 us
  transfers between devices with their start and end apart: 17, of which 10 were waited for; matrix products, arithmetic and copies ran while one was open for 0% of the time, Pallas kernels for 16%

profile of v8, /device:TPU:0, one launch (start us, length us, event | category | flops | bytes accessed | tf_op | source)
XLA Modules:
  0.0 74.1 jit_solution(10257966430732229579)
XLA Ops:
  0.6 3.0 %collective-permute-start.5 = (f32[2,192,128]{2,1,0:T(8,128)}, f32[2,192,128]{2,1,0:T(8,128)S(1)}, u32[]{:S(2)}, u32[]{:S(2)}) collective-permute-start(f32[2,192,128]{2,1,0:T(8,128)} %bitcast.1), channel_id=1, source_target_pairs={{0,4},{4,8},{8,12},{12,16},{16,20},{20,24},{24,28},{28,0},{1,5},{5... | collective-permute-start | bytes 589832 | tf_op jit(solution)/shard_map/ppermute | solution.py:780
  3.7 1.2 %shard_map.101 = (f32[136,384]{1,0:T(8,128)S(1)}, f32[136,256]{1,0:T(8,128)S(1)}, f32[136,128]{1,0:T(8,128)S(1)}, f32[128,512]{1,0:T(8,128)S(1)}, f32[8,128]{1,0:T(8,128)S(1)}) custom-call(f32[2,128,512]{2,1,0:T(8,128)} %cov.1, f32[2,128,512]{2,1,0:T(8,128)} %cost.1, f32[2,128]{1,0:T(2,128)} %drift.1, f32[2,128]{1,0:T(2,128)} %eta.1), custom_call_target="tpu_custom_call" | custom-call | tf_op jit(solution)/shard_map/pallas_call | solution.py:762
  5.0 6.8 %collective-permute-done.5.before = f32[2,192,128]{2,1,0:T(8,128)S(1)} collective-permute-done((f32[2,192,128]{2,1,0:T(8,128)}, f32[2,192,128]{2,1,0:T(8,128)S(1)}, u32[]{:S(2)}, u32[]{:S(2)}) %collective-permute-start.5) | collective-permute-done | bytes 196640 | tf_op jit(solution)/shard_map/ppermute | solution.py:780
  11.8 1.6 %collective-permute-start.6 = (f32[384,128]{1,0:T(8,128)S(1)}, f32[384,128]{1,0:T(8,128)S(1)}, u32[]{:S(2)}, u32[]{:S(2)}) collective-permute-start(f32[384,128]{1,0:T(8,128)S(1)} %shard_map.104), channel_id=1, source_target_pairs={{0,2},{1,3},{2,0},{3,1},{4,6},{5,7},{6,4},{7,5},{8,10},{9,11},{10,... | collective-permute-start | bytes 589832 | tf_op jit(solution)/shard_map/ppermute | solution.py:776
  13.4 4.5 %collective-permute-done.6.other = f32[384,128]{1,0:T(8,128)S(1)} collective-permute-done((f32[384,128]{1,0:T(8,128)S(1)}, f32[384,128]{1,0:T(8,128)S(1)}, u32[]{:S(2)}, u32[]{:S(2)}) %collective-permute-start.6) | collective-permute-done | bytes 196640 | tf_op jit(solution)/shard_map/ppermute | solution.py:776
  18.2 1.4 %collective-permute-start.1 = (f32[136,256]{1,0:T(8,128)S(1)}, f32[136,256]{1,0:T(8,128)S(1)}, u32[]{:S(2)}, u32[]{:S(2)}) collective-permute-start(f32[136,256]{1,0:T(8,128)S(1)} %get-tuple-element.51), channel_id=1, source_target_pairs={{0,2},{1,3},{2,0},{3,1},{4,6},{5,7},{6,4},{7,5},{8,10},{9,11},{10,... | collective-permute-start | bytes 417800 | tf_op jit(solution)/shard_map/ppermute | solution.py:776
  20.1 5.2 %collective-permute-done.2.from_far = f32[136,128]{1,0:T(8,128)S(1)} collective-permute-done((f32[136,128]{1,0:T(8,128)S(1)}, f32[136,128]{1,0:T(8,128)S(1)}, u32[]{:S(2)}, u32[]{:S(2)}) %collective-permute-start.2) | collective-permute-done | bytes 69664 | tf_op jit(solution)/shard_map/ppermute | solution.py:776
  25.4 3.0 %collective-permute-start.4 = (f32[136,256]{1,0:T(8,128)S(1)}, f32[136,256]{1,0:T(8,128)S(1)}, u32[]{:S(2)}, u32[]{:S(2)}) collective-permute-start(f32[136,256]{1,0:T(8,128)S(1)} %shard_map.103.own_far), channel_id=1, source_target_pairs={{0,4},{4,8},{8,12},{12,16},{16,20},{20,24},{24,28},{1,5},{5,9},{9,... | collective-permute-start | bytes 417800 | tf_op jit(solution)/shard_map/ppermute | solution.py:780
  29.4 2.0 %collective-permute-done.4.far = f32[136,256]{1,0:T(8,128)S(1)} collective-permute-done((f32[136,256]{1,0:T(8,128)S(1)}, f32[136,256]{1,0:T(8,128)S(1)}, u32[]{:S(2)}, u32[]{:S(2)}) %collective-permute-start.4) | collective-permute-done | bytes 139296 | tf_op jit(solution)/shard_map/ppermute | solution.py:780
  31.4 1.4 %collective-permute-done.3.near = f32[128,768]{1,0:T(8,128)S(1)} collective-permute-done((f32[128,768]{1,0:T(8,128)S(1)}, f32[128,768]{1,0:T(8,128)S(1)}, u32[]{:S(2)}, u32[]{:S(2)}) %collective-permute-start.3) | collective-permute-done | bytes 393248 | tf_op jit(solution)/shard_map/ppermute | solution.py:780
  32.9 1.9 %shard_map.107.own = f32[264,512]{1,0:T(8,128)S(1)} custom-call(f32[128,768]{1,0:T(8,128)S(1)} %shard_map.102.own_near, f32[136,256]{1,0:T(8,128)S(1)} %shard_map.103.own_far, f32[128,768]{1,0:T(8,128)S(1)} %collective-permute-done.3.near, f32[136,256]{1,0:T(8,128)S(1)} %collective-permute-done.4.far, bf16[512,512]{1,0:T(8,128)(2,1)S(1)} %get-tuple-element.53.mh, ...), custom_call_target="tpu_custom_call" | custom-call | tf_op jit(solution)/shard_map/pallas_call | solution.py:762
  34.8 10.5 %collective-permute-start.8 = (f32[264,512]{1,0:T(8,128)S(1)}, f32[264,512]{1,0:T(8,128)S(1)}, u32[]{:S(2)}, u32[]{:S(2)}) collective-permute-start(f32[264,512]{1,0:T(8,128)S(1)} %shard_map.107.own), channel_id=1, source_target_pairs={{0,8},{4,12},{8,16},{12,20},{16,24},{20,28},{1,9},{5,13},{9,17},{1... | collective-permute-start | bytes 1622024 | tf_op jit(solution)/shard_map/ppermute | solution.py:780
  45.4 1.4 %shard_map.108 = (bf16[512,512]{1,0:T(8,128)(2,1)S(1)}, bf16[512,512]{1,0:T(8,128)(2,1)S(1)}, bf16[512,512]{1,0:T(8,128)(2,1)S(1)}, bf16[512,512]{1,0:T(8,128)(2,1)S(1)}, f32[512,256]{1,0:T(8,128)S(1)}) custom-call(s32[8,3]{1,0:T(8,128)S(1)} %copy.13.pattern, f32[768,128]{1,0:T(8,128)S(1)} %shard_map.105.halves, ...), custom_call_target="tpu_custom_call" | custom-call | tf_op jit(solution)/shard_map/pallas_call | solution.py:762
  47.1 2.6 %shard_map.109 = (f32[128,512]{1,0:T(8,128)S(1)}, f32[128,512]{1,0:T(8,128)S(1)}, f32[512,512]{1,0:T(8,128)S(1)}, bf16[512,512]{1,0:T(8,128)(2,1)S(1)}, bf16[512...) custom-call(s32[8,3]{1,0:T(8,128)S(1)} %copy.13.pattern, ...), custom_call_target="tpu_custom_call" | custom-call | tf_op jit(solution)/shard_map/pallas_call | solution.py:762
  49.6 1.2 %shard_map.110 = (bf16[512,512]{1,0:T(8,128)(2,1)S(1)}, bf16[512,512]{1,0:T(8,128)(2,1)S(1)}, bf16[512,512]{1,0:T(8,128)(2,1)S(1)}, bf16[512,512]{1,0:T(8,128)(2,1)S(1)}) custom-call(bf16[512,512]{1,0:T(8,128)(2,1)S(1)} %get-tuple-element.57.a0h, bf16[512,512]{1,0:T(8,128)(2,1)S(1)} %get-tuple-element.58.a0l, bf16[512,512]{1,0:T(8,128)(2,1)S(1)} %get-tuple-element.59.a1h, ...), custom_call_target="tpu_custom_call" | custom-call | tf_op jit(solution)/shard_map/pallas_call | solution.py:762
  51.1 5.5 %collective-permute-done.8.earlier = f32[264,512]{1,0:T(8,128)S(1)} collective-permute-done((f32[264,512]{1,0:T(8,128)S(1)}, f32[264,512]{1,0:T(8,128)S(1)}, u32[]{:S(2)}, u32[]{:S(2)}) %collective-permute-start.8) | collective-permute-done | bytes 540704 | tf_op jit(solution)/shard_map/ppermute | solution.py:780
  56.5 1.7 %shard_map.112 = (f32[520,128]{1,0:T(8,128)S(1)}, bf16[512,512]{1,0:T(8,128)(2,1)S(1)}, bf16[512,512]{1,0:T(8,128)(2,1)S(1)}) custom-call(f32[264,512]{1,0:T(8,128)S(1)} %shard_map.107.own, f32[264,512]{1,0:T(8,128)S(1)} %collective-permute-done.8.earlier, bf16[512,512]{1,0:T(8,128)(2,1)S(1)} %get-tuple-element.68.mh, ...), custom_call_target="tpu_custom_call" | custom-call | tf_op jit(solution)/shard_map/pallas_call | solution.py:762
  58.2 1.6 %collective-permute-start.13 = (f32[520,128]{1,0:T(8,128)S(1)}, f32[520,128]{1,0:T(8,128)S(1)}, u32[]{:S(2)}, u32[]{:S(2)}) collective-permute-start(f32[520,128]{1,0:T(8,128)S(1)} %get-tuple-element.80), channel_id=1, source_target_pairs={{0,2},{1,3},{2,0},{3,1},{4,6},{5,7},{6,4},{7,5},{8,10},{9,11},{10,... | collective-permute-start | bytes 798728 | tf_op jit(solution)/shard_map/ppermute | solution.py:776
  61.9 1.3 %collective-permute-start.16 = (f32[264,128]{1,0:T(8,128)S(1)}, f32[264,128]{1,0:T(8,128)S(1)}, u32[]{:S(2)}, u32[]{:S(2)}) collective-permute-start(f32[264,128]{1,0:T(8,128)S(1)} %get-tuple-element.86), channel_id=1, source_target_pairs={{0,3},{1,2},{2,1},{3,0},{4,7},{5,6},{6,5},{7,4},{8,11},{9,10},{10,... | collective-permute-start | bytes 405512 | tf_op jit(solution)/shard_map/ppermute | solution.py:776
  63.2 1.9 %collective-permute-done.13.from_chip = f32[520,128]{1,0:T(8,128)S(1)} collective-permute-done((f32[520,128]{1,0:T(8,128)S(1)}, f32[520,128]{1,0:T(8,128)S(1)}, u32[]{:S(2)}, u32[]{:S(2)}) %collective-permute-start.13) | collective-permute-done | bytes 266272 | tf_op jit(solution)/shard_map/ppermute | solution.py:776
  65.2 2.5 %collective-permute-start.14 = (f32[8,128]{1,0:T(8,128)S(1)}, f32[8,128]{1,0:T(8,128)S(1)}, u32[]{:S(2)}, u32[]{:S(2)}) collective-permute-start(f32[8,128]{1,0:T(8,128)S(1)} %get-tuple-element.75.short), channel_id=1, source_target_pairs={{0,2},{1,3},{2,0},{3,1},{4,6},{5,7},{6,4},{7,5},{8,10},{9,11},{10,... | collective-permute-start | bytes 12296 | tf_op jit(solution)/shard_map/ppermute | solution.py:776
  67.8 2.9 %collective-permute-done.12.dyn_recv = f32[128,512]{1,0:T(8,128)S(1)} collective-permute-done((f32[128,512]{1,0:T(8,128)S(1)}, f32[128,512]{1,0:T(8,128)S(1)}, u32[]{:S(2)}, u32[]{:S(2)}) %collective-permute-start.12) | collective-permute-done | bytes 262176 | tf_op jit(solution)/shard_map/ppermute | solution.py:776
  70.7 1.2 %shard_map.116 = (f32[2,128,512]{2,1,0:T(8,128)}, f32[2,128,512]{2,1,0:T(8,128)}, f32[2,128,512]{2,1,0:T(8,128)}) custom-call(f32[512,128]{1,0:T(8,128)S(1)} %get-tuple-element.76.keep, f32[520,128]{1,0:T(8,128)S(1)} %collective-permute-done.11.from_core, f32[128,512]{1,0:T(8,128)S(1)} %get-tuple-element.78.dyn_own, ...), custom_call_target="tpu_custom_call" | custom-call | tf_op jit(solution)/shard_map/pallas_call | solution.py:762
  71.8 1.5 %collective-permute-done.14.chip_short = f32[8,128]{1,0:T(8,128)S(1)} collective-permute-done((f32[8,128]{1,0:T(8,128)S(1)}, f32[8,128]{1,0:T(8,128)S(1)}, u32[]{:S(2)}, u32[]{:S(2)}) %collective-permute-start.14) | collective-permute-done | bytes 4128 | tf_op jit(solution)/shard_map/ppermute | solution.py:776
  (32 shorter events, 5.4 us)
Async XLA Ops:
  0.6 11.2 %copy-start = (f32[2,128,192]{1,2,0:T(8,128)S(1)}, f32[2,128,192]{1,2,0:T(8,128)}, u32[]{:S(2)}) copy-start(f32[2,128,192]{1,2,0:T(8,128)} %param.6) | copy-start | bytes 589828
  0.6 11.2 %collective-permute-start.5 = (f32[2,192,128]{2,1,0:T(8,128)}, f32[2,192,128]{2,1,0:T(8,128)S(1)}, u32[]{:S(2)}, u32[]{:S(2)}) collective-permute-start(f32[2,192,128]{2,1,0:T(8,128)} %bitcast.1), channel_id=1, source_target_pairs={{0,4},{4,8},{8,12},{12,16},{16,20},{20,24},{24,28},{28,0},{1,5},{5... | collective-permute-start | bytes 589832 | tf_op jit(solution)/shard_map/ppermute | solution.py:780
  4.9 13.2 %collective-permute-start = (f32[136,384]{1,0:T(8,128)S(1)}, f32[136,384]{1,0:T(8,128)S(1)}, u32[]{:S(2)}, u32[]{:S(2)}) collective-permute-start(f32[136,384]{1,0:T(8,128)S(1)} %get-tuple-element.49), channel_id=1, source_target_pairs={{0,1},{1,0},{2,3},{3,2},{4,5},{5,4},{6,7},{7,6},{8,9},{9,8},{10,11... | collective-permute-start | bytes 626696 | tf_op jit(solution)/shard_map/ppermute | solution.py:776
  11.8 6.1 %collective-permute-start.6 = (f32[384,128]{1,0:T(8,128)S(1)}, f32[384,128]{1,0:T(8,128)S(1)}, u32[]{:S(2)}, u32[]{:S(2)}) collective-permute-start(f32[384,128]{1,0:T(8,128)S(1)} %shard_map.104), channel_id=1, source_target_pairs={{0,2},{1,3},{2,0},{3,1},{4,6},{5,7},{6,4},{7,5},{8,10},{9,11},{10,... | collective-permute-start | bytes 589832 | tf_op jit(solution)/shard_map/ppermute | solution.py:776
  18.0 10.5 %collective-permute-start.7 = (f32[768,128]{1,0:T(8,128)S(1)}, f32[768,128]{1,0:T(8,128)S(1)}, u32[]{:S(2)}, u32[]{:S(2)}) collective-permute-start(f32[768,128]{1,0:T(8,128)S(1)} %shard_map.105.halves), channel_id=1, source_target_pairs={{0,1},{1,0},{2,3},{3,2},{4,5},{5,4},{6,7},{7,6},{8,9},{9,8},{10,11... | collective-permute-start | bytes 1179656 | tf_op jit(solution)/shard_map/ppermute | solution.py:776
  18.1 14.7 %collective-permute-start.3 = (f32[128,768]{1,0:T(8,128)S(1)}, f32[128,768]{1,0:T(8,128)S(1)}, u32[]{:S(2)}, u32[]{:S(2)}) collective-permute-start(f32[128,768]{1,0:T(8,128)S(1)} %shard_map.102.own_near), channel_id=1, source_target_pairs={{0,4},{4,8},{8,12},{12,16},{16,20},{20,24},{24,28},{28,0},{1,5},{5... | collective-permute-start | bytes 1179656 | tf_op jit(solution)/shard_map/ppermute | solution.py:780
  18.2 7.1 %collective-permute-start.1 = (f32[136,256]{1,0:T(8,128)S(1)}, f32[136,256]{1,0:T(8,128)S(1)}, u32[]{:S(2)}, u32[]{:S(2)}) collective-permute-start(f32[136,256]{1,0:T(8,128)S(1)} %get-tuple-element.51), channel_id=1, source_target_pairs={{0,2},{1,3},{2,0},{3,1},{4,6},{5,7},{6,4},{7,5},{8,10},{9,11},{10,... | collective-permute-start | bytes 417800 | tf_op jit(solution)/shard_map/ppermute | solution.py:776
  19.6 25.7 %collective-permute-start.9 = (f32[768,128]{1,0:T(8,128)S(1)}, f32[768,128]{1,0:T(8,128)S(1)}, u32[]{:S(2)}, u32[]{:S(2)}) collective-permute-start(f32[768,128]{1,0:T(8,128)S(1)} %shard_map.105.halves), channel_id=1, source_target_pairs={{0,8},{4,12},{8,16},{12,20},{16,24},{20,28},{24,0},{28,4},{1,9},{5... | collective-permute-start | bytes 1179656 | tf_op jit(solution)/shard_map/ppermute | solution.py:780
  19.7 5.6 %collective-permute-start.2 = (f32[136,128]{1,0:T(8,128)S(1)}, f32[136,128]{1,0:T(8,128)S(1)}, u32[]{:S(2)}, u32[]{:S(2)}) collective-permute-start(f32[136,128]{1,0:T(8,128)S(1)} %get-tuple-element.52), channel_id=1, source_target_pairs={{0,3},{1,2},{2,1},{3,0},{4,7},{5,6},{6,5},{7,4},{8,11},{9,10},{10,... | collective-permute-start | bytes 208904 | tf_op jit(solution)/shard_map/ppermute | solution.py:776
  25.3 3.1 %copy-start.1 = (s32[8,3]{0,1:T(4,128)S(1)}, s32[8,3]{0,1:T(4,128)}, u32[]{:S(2)}) copy-start(s32[8,3]{0,1:T(4,128)} %param.7) | copy-start | bytes 292
  25.4 6.0 %collective-permute-start.4 = (f32[136,256]{1,0:T(8,128)S(1)}, f32[136,256]{1,0:T(8,128)S(1)}, u32[]{:S(2)}, u32[]{:S(2)}) collective-permute-start(f32[136,256]{1,0:T(8,128)S(1)} %shard_map.103.own_far), channel_id=1, source_target_pairs={{0,4},{4,8},{8,12},{12,16},{16,20},{20,24},{24,28},{1,5},{5,9},{9,... | collective-permute-start | bytes 417800 | tf_op jit(solution)/shard_map/ppermute | solution.py:780
  34.8 21.8 %collective-permute-start.8 = (f32[264,512]{1,0:T(8,128)S(1)}, f32[264,512]{1,0:T(8,128)S(1)}, u32[]{:S(2)}, u32[]{:S(2)}) collective-permute-start(f32[264,512]{1,0:T(8,128)S(1)} %shard_map.107.own), channel_id=1, source_target_pairs={{0,8},{4,12},{8,16},{12,20},{16,24},{20,28},{1,9},{5,13},{9,17},{1... | collective-permute-start | bytes 1622024 | tf_op jit(solution)/shard_map/ppermute | solution.py:780
  45.3 1.8 %collective-permute-start.10 = (f32[768,128]{1,0:T(8,128)S(1)}, f32[768,128]{1,0:T(8,128)S(1)}, u32[]{:S(2)}, u32[]{:S(2)}) collective-permute-start(f32[768,128]{1,0:T(8,128)S(1)} %collective-permute-done.9.halves), channel_id=1, source_target_pairs={{0,1},{1,0},{2,3},{3,2},{4,5},{5,4},{6,7},{7,6},{8,9},{9,8},{10,11... | collective-permute-start | bytes 1179656 | tf_op jit(solution)/shard_map/ppermute | solution.py:776
  58.2 6.8 %collective-permute-start.13 = (f32[520,128]{1,0:T(8,128)S(1)}, f32[520,128]{1,0:T(8,128)S(1)}, u32[]{:S(2)}, u32[]{:S(2)}) collective-permute-start(f32[520,128]{1,0:T(8,128)S(1)} %get-tuple-element.80), channel_id=1, source_target_pairs={{0,2},{1,3},{2,0},{3,1},{4,6},{5,7},{6,4},{7,5},{8,10},{9,11},{10,... | collective-permute-start | bytes 798728 | tf_op jit(solution)/shard_map/ppermute | solution.py:776
  61.2 9.4 %collective-permute-start.11 = (f32[520,128]{1,0:T(8,128)S(1)}, f32[520,128]{1,0:T(8,128)S(1)}, u32[]{:S(2)}, u32[]{:S(2)}) collective-permute-start(f32[520,128]{1,0:T(8,128)S(1)} %get-tuple-element.77), channel_id=1, source_target_pairs={{0,1},{1,0},{2,3},{3,2},{4,5},{5,4},{6,7},{7,6},{8,9},{9,8},{10,11... | collective-permute-start | bytes 798728 | tf_op jit(solution)/shard_map/ppermute | solution.py:776
  61.3 9.4 %collective-permute-start.12 = (f32[128,512]{1,0:T(8,128)S(1)}, f32[128,512]{1,0:T(8,128)S(1)}, u32[]{:S(2)}, u32[]{:S(2)}) collective-permute-start(f32[128,512]{1,0:T(8,128)S(1)} %get-tuple-element.79), channel_id=1, source_target_pairs={{0,2},{1,3},{2,0},{3,1},{4,6},{5,7},{6,4},{7,5},{8,10},{9,11},{10,... | collective-permute-start | bytes 786440 | tf_op jit(solution)/shard_map/ppermute | solution.py:776
  61.9 11.4 %collective-permute-start.16 = (f32[264,128]{1,0:T(8,128)S(1)}, f32[264,128]{1,0:T(8,128)S(1)}, u32[]{:S(2)}, u32[]{:S(2)}) collective-permute-start(f32[264,128]{1,0:T(8,128)S(1)} %get-tuple-element.86), channel_id=1, source_target_pairs={{0,3},{1,2},{2,1},{3,0},{4,7},{5,6},{6,5},{7,4},{8,11},{9,10},{10,... | collective-permute-start | bytes 405512 | tf_op jit(solution)/shard_map/ppermute | solution.py:776
  65.2 8.1 %collective-permute-start.15 = (f32[256,128]{1,0:T(8,128)S(1)}, f32[256,128]{1,0:T(8,128)S(1)}, u32[]{:S(2)}, u32[]{:S(2)}) collective-permute-start(f32[256,128]{1,0:T(8,128)S(1)} %get-tuple-element.85), channel_id=1, source_target_pairs={{0,1},{1,0},{2,3},{3,2},{4,5},{5,4},{6,7},{7,6},{8,9},{9,8},{10,11... | collective-permute-start | bytes 393224 | tf_op jit(solution)/shard_map/ppermute | solution.py:776
  65.2 8.1 %collective-permute-start.14 = (f32[8,128]{1,0:T(8,128)S(1)}, f32[8,128]{1,0:T(8,128)S(1)}, u32[]{:S(2)}, u32[]{:S(2)}) collective-permute-start(f32[8,128]{1,0:T(8,128)S(1)} %get-tuple-element.75.short), channel_id=1, source_target_pairs={{0,2},{1,3},{2,0},{3,1},{4,6},{5,7},{6,4},{7,5},{8,10},{9,11},{10,... | collective-permute-start | bytes 12296 | tf_op jit(solution)/shard_map/ppermute | solution.py:776

commit v9 on v8

--- a/solution.py
+++ b/solution.py
@@ -312,13 +312,13 @@
     out[height:, :] = before[1 - y]
 
 
-def halves_kernel(turned, before, other, out):
+def halves_kernel(turned, before, other, own, earlier):
     y = place_of()[1]
     height = turned.shape[1]
-    out[0:height, :] = turned[y]
-    out[height : 2 * height, :] = other[0:height, :]
-    out[2 * height : 3 * height, :] = before[y]
-    out[3 * height :, :] = other[height:, :]
+    own[0:height, :] = turned[y]
+    own[height:, :] = other[0:height, :]
+    earlier[0:height, :] = before[y]
+    earlier[height:, :] = other[height:, :]
 
 
 def dense_turned(put, pattern, own_half, core_half, flag, n, r, bs):
@@ -383,14 +383,13 @@
         )
 
 
-def prepare_kernel(bs, pattern, halves, core_halves, mh, ml, th, tl, dense):
+def prepare_kernel(bs, pattern, own, own_core, before, before_core, mh, ml, th, tl, dense):
     c, has1 = place_of()[2], has(1)
     n = dense.shape[0]
-    r = halves.shape[1]
-    half = halves.shape[0] // 2
+    r = own.shape[1]
     first = c == 0
-    own_half = jnp.where(first, halves[0:half, :], halves[half:, :])
-    core_half = jnp.where(first, core_halves[0:half, :], core_halves[half:, :])
+    own_half = jnp.where(first, own[...], before[...])
+    core_half = jnp.where(first, own_core[...], before_core[...])
     flag = jnp.where(first, 1, has1)
 
     def put(row, col, value):
@@ -463,14 +462,15 @@
     out[base + 4 : base + 8, :] = jnp.zeros((4, 4 * r), F32)
 
 
-def early_kernel(bs, pattern, halves, core_halves, a0h, a0l, a1h, a1l, t):
+def early_kernel(bs, pattern, own, own_core, before, before_core, a0h, a0l, a1h, a1l, t):
     n = a0h.shape[0]
-    r = halves.shape[1]
-    half = halves.shape[0] // 2
-    for at, flag, hi, lo in ((0, 1, a0h, a0l), (1, has(1), a1h, a1l)):
-        rows = slice(at * half, (at + 1) * half)
+    r = own.shape[1]
+    for flag, mine, theirs, hi, lo in (
+        (1, own, own_core, a0h, a0l),
+        (has(1), before, before_core, a1h, a1l),
+    ):
         put = functools.partial(put_split, hi, lo)
-        dense_turned(put, pattern, halves[rows, :], core_halves[rows, :], flag, n, r, bs)
+        dense_turned(put, pattern, mine[...], theirs[...], flag, n, r, bs)
 
     def wanted(ref):
         return jnp.concatenate([ref[:, 0:r], ref[:, 2 * r : 3 * r]], axis=1)
@@ -478,26 +478,25 @@
     t[...] = dot3(a1h[...], a1l[...], wanted(a0h), wanted(a0l))
 
 
-def rows_kernel(
-    bs, pattern, halves, core_halves, t, dyn_own, dyn_send, a2, a2h, a2l, a3h, a3l
-):
-    q, _, _ = place_of()
+def third_kernel(bs, pattern, mine, theirs, t, out, a2, a2h, a2l):
     n = a2.shape[0]
-    r = halves.shape[1]
-    half = halves.shape[0] // 2
-
-    def put2(row, col, value):
+    r = mine.shape[1]
+
+    def put(row, col, value):
         put_split(a2h, a2l, row, col, value)
         a2[row, col] = value
 
-    def put3(row, col, value):
-        put_split(a3h, a3l, row, col, value)
-
-    for at, flag, put in ((0, has(2), put2), (1, has(3), put3)):
-        rows = slice(at * half, (at + 1) * half)
-        dense_turned(put, pattern, halves[rows, :], core_halves[rows, :], flag, n, r, bs)
-    rows = dot3(a2h[...], a2l[...], *split(t[...]))
-    rows = dot3(a3h[...], a3l[...], *split(rows))
+    dense_turned(put, pattern, mine[...], theirs[...], has(2), n, r, bs)
+    out[...] = dot3(a2h[...], a2l[...], *split(t[...]))
+
+
+def rows_kernel(bs, pattern, mine, theirs, t, dyn_own, dyn_send, a3h, a3l):
+    q, _, _ = place_of()
+    n = a3h.shape[0]
+    r = mine.shape[1]
+    put = functools.partial(put_split, a3h, a3l)
+    dense_turned(put, pattern, mine[...], theirs[...], has(3), n, r, bs)
+    rows = dot3(a3h[...], a3l[...], *split(t[...]))
     for j in range(4):
         at = lanes(q ^ j, r)
         dyn_own[:, at] = rows[j * r : (j + 1) * r, 0:r].T
@@ -543,12 +542,17 @@
         ref[lanes(q ^ j, r), :] = value[:, j * r : (j + 1) * r]
 
 
+def came(earlier):
+    return jnp.where(has(2) == 1, earlier[...], 0.0)
+
+
 CROSSING = ((2, 0), (2, 1), (2, 3))
 
 
 def level2_kernel(own, earlier, mh, ml, th, tl, full, z, to_chip, uh, ul, xh, xl, rest):
     c = place_of()[2]
     r = own.shape[1] // 4
+    earlier = came(earlier)
     two, three = slice(2 * r, 3 * r), slice(3 * r, 4 * r)
 
     @pl.when(c == 0)
@@ -587,6 +591,7 @@
 ):
     c = place_of()[2]
     r = own.shape[1] // 4
+    earlier = came(earlier)
     base = 2 * r
     three = slice(3 * r, 4 * r)
     b1 = earlier[base + 1 : base + 2, :] + row_times(earlier[base + 3 : base + 4, :], a2[...], r)
@@ -621,6 +626,7 @@
 def rest_kernel(earlier, th, tl, full, z, uh, ul, short, keep, to_core, rest):
     q, _, c = place_of()
     r = earlier.shape[1] // 4
+    earlier = came(earlier)
 
     @pl.when(c == 0)
     def _():
@@ -816,12 +822,15 @@
     far = later(own_far, 1)
     (picked,) = kernel(pick_kernel, vmem(turned, before), vmem(shape(6 * bs, r)))
     other = swap(picked, 2)
-    (halves,) = kernel(halves_kernel, vmem(turned, before, other), vmem(shape(12 * bs, r)))
-    core_halves = swap(halves, 1)
-    far_halves = later(halves, 2, cyclic=True)
+    own_half, before_half = kernel(
+        halves_kernel, vmem(turned, before, other), vmem(shape(6 * bs, r), shape(6 * bs, r))
+    )
+    pairs = (own_half, swap(own_half, 1), before_half, swap(before_half, 1))
+    third = later(own_half, 2, cyclic=True)
+    fourth = later(before_half, 2, cyclic=True)
     m1 = kernel(
         functools.partial(prepare_kernel, bs),
-        vmem(pattern, halves, core_halves),
+        vmem(pattern, *pairs),
         vmem(*[half(n, n)] * 4),
         [square(F32)],
     )
@@ -831,18 +840,23 @@
         vmem(shape(2 * r + 8, n)),
         [pltpu.VMEM((n + 16, n), BF16)] * 2 + [pltpu.VMEM((2 * r + 16, n), BF16)] * 2,
     )
-    earlier = later(level1, 2)
+    earlier = later(level1, 2, cyclic=True)
     *a01, t = kernel(
         functools.partial(early_kernel, bs),
-        vmem(pattern, halves, core_halves),
+        vmem(pattern, *pairs),
         vmem(*[half(n, n)] * 4, shape(n, 2 * r)),
     )
-    far_core_halves = swap(far_halves, 1)
-    dyn_own, dyn_send, a2, *a23 = kernel(
+    t, a2, *a2_split = kernel(
+        functools.partial(third_kernel, bs),
+        vmem(pattern, third, swap(third, 1), t),
+        vmem(shape(n, 2 * r), shape(n, n), half(n, n), half(n, n)),
+    )
+    dyn_own, dyn_send, *a3_split = kernel(
         functools.partial(rows_kernel, bs),
-        vmem(pattern, far_halves, far_core_halves, t),
-        vmem(shape(r, n), shape(r, n), shape(n, n), *[half(n, n)] * 4),
-    )
+        vmem(pattern, fourth, swap(fourth, 1), t),
+        vmem(shape(r, n), shape(r, n), half(n, n), half(n, n)),
+    )
+    a23 = (*a2_split, *a3_split)
     dyn_recv = swap(dyn_send, 2)
     m2 = kernel(product_kernel, vmem(*a01, *a23), vmem(*[half(n, n)] * 4), [square(F32)])
     full, z = kernel(

time: 74.3 us -> 83.2 us (1.12)
  waiting for transfers between devices: 32.1 us -> 48.4 us
  starting transfers between devices: 26.4 us -> 19.3 us
    ppermute x5 -> x6, waiting for transfers between devices: 15.8 us -> 31.2 us  [later(): lax.ppermute(value, 'tm', [(i, (i + distance) % tms) for i in range(count)])]
    ppermute x5 -> x6, starting transfers between devices: 16.7 us -> 10.6 us  [later(): lax.ppermute(value, 'tm', [(i, (i + distance) % tms) for i in range(count)])]
    ppermute x12 -> x14, starting transfers between devices: 9.73 us -> 8.72 us  [swap(): return lax.ppermute(value, 'col', [(i, i ^ bit) for i in range(cols)])]
    ppermute x12 -> x14, waiting for transfers between devices: 16.3 us -> 17.3 us  [swap(): return lax.ppermute(value, 'col', [(i, i ^ bit) for i in range(cols)])]
    pallas_call x17 -> x18, Pallas kernels: 14.6 us -> 14.4 us  [kernel(): call(*(pltpu.with_memory_space_constraint(x, kept[where]) if where in kep...]
  transfers between devices with their start and end apart: 17 -> 20, of which waited for: 10 -> 10; matrix products, arithmetic and copies ran while one was open for 0% -> 0% of each run, Pallas kernels for 16% -> 11%
where the time goes in v9:
time: 83.2 us; the launch traced here: 83 us
  waiting for transfers between devices  48.4 us (58%)
  starting transfers between devices  19.3 us (23%)
  Pallas kernels  14.4 us (17%)
    ppermute x6, waiting for transfers between devices, later(): lax.ppermute(value, 'tm', [(i, (i + distance) % tms) for i in range(count)])  31.2 us
    ppermute x14, waiting for transfers between devices, swap(): return lax.ppermute(value, 'col', [(i, i ^ bit) for i in range(cols)])  17.3 us
    pallas_call x18, Pallas kernels, kernel(): call(*(pltpu.with_memory_space_constraint(x, kept[where]) if where in kep...  14.4 us
    ppermute x6, starting transfers between devices, later(): lax.ppermute(value, 'tm', [(i, (i + distance) % tms) for i in range(count)])  10.6 us
    ppermute x14, starting transfers between devices, swap(): return lax.ppermute(value, 'col', [(i, i ^ bit) for i in range(cols)])  8.72 us
  transfers between devices with their start and end apart: 20, of which 10 were waited for; matrix products, arithmetic and copies ran while one was open for 0% of the time, Pallas kernels for 11%

profile of v9, /device:TPU:0, one launch (start us, length us, event | category | flops | bytes accessed | tf_op | source)
XLA Modules:
  0.0 83.0 jit_solution(3884357658006883643)
XLA Ops:
  0.6 1.3 %shard_map.101 = (f32[136,384]{1,0:T(8,128)S(1)}, f32[136,256]{1,0:T(8,128)S(1)}, f32[136,128]{1,0:T(8,128)S(1)}, f32[128,512]{1,0:T(8,128)S(1)}, f32[8,128]{1,0:T(8,128)S(1)}) custom-call(f32[2,128,512]{2,1,0:T(8,128)} %cov.1, f32[2,128,512]{2,1,0:T(8,128)} %cost.1, f32[2,128]{1,0:T(2,128)} %drift.1, f32[2,128]{1,0:T(2,128)} %eta.1), custom_call_target="tpu_custom_call" | custom-call | tf_op jit(solution)/shard_map/pallas_call | solution.py:768
  2.5 2.5 %collective-permute-start.5 = (f32[2,192,128]{2,1,0:T(8,128)S(1)}, f32[2,192,128]{2,1,0:T(8,128)S(1)}, u32[]{:S(2)}, u32[]{:S(2)}) collective-permute-start(f32[2,192,128]{2,1,0:T(8,128)S(1)} %bitcast.1), channel_id=1, source_target_pairs={{0,4},{4,8},{8,12},{12,16},{16,20},{20,24},{24,28},{28,0},{1,5},{5... | collective-permute-start | bytes 589832 | tf_op jit(solution)/shard_map/ppermute | solution.py:786
  5.0 8.5 %collective-permute-done.5.before = f32[2,192,128]{2,1,0:T(8,128)S(1)} collective-permute-done((f32[2,192,128]{2,1,0:T(8,128)S(1)}, f32[2,192,128]{2,1,0:T(8,128)S(1)}, u32[]{:S(2)}, u32[]{:S(2)}) %collective-permute-start.5) | collective-permute-done | bytes 196640 | tf_op jit(solution)/shard_map/ppermute | solution.py:786
  13.6 1.6 %collective-permute-start.6 = (f32[384,128]{1,0:T(8,128)S(1)}, f32[384,128]{1,0:T(8,128)S(1)}, u32[]{:S(2)}, u32[]{:S(2)}) collective-permute-start(f32[384,128]{1,0:T(8,128)S(1)} %shard_map.104), channel_id=1, source_target_pairs={{0,2},{1,3},{2,0},{3,1},{4,6},{5,7},{6,4},{7,5},{8,10},{9,11},{10,... | collective-permute-start | bytes 589832 | tf_op jit(solution)/shard_map/ppermute | solution.py:782
  16.1 5.3 %collective-permute-done.6.other = f32[384,128]{1,0:T(8,128)S(1)} collective-permute-done((f32[384,128]{1,0:T(8,128)S(1)}, f32[384,128]{1,0:T(8,128)S(1)}, u32[]{:S(2)}, u32[]{:S(2)}) %collective-permute-start.6) | collective-permute-done | bytes 196640 | tf_op jit(solution)/shard_map/ppermute | solution.py:782
  22.0 1.6 %collective-permute-done.2.from_far = f32[136,128]{1,0:T(8,128)S(1)} collective-permute-done((f32[136,128]{1,0:T(8,128)S(1)}, f32[136,128]{1,0:T(8,128)S(1)}, u32[]{:S(2)}, u32[]{:S(2)}) %collective-permute-start.2) | collective-permute-done | bytes 69664 | tf_op jit(solution)/shard_map/ppermute | solution.py:782
  24.1 1.3 %collective-permute-start.4 = (f32[136,256]{1,0:T(8,128)S(1)}, f32[136,256]{1,0:T(8,128)S(1)}, u32[]{:S(2)}, u32[]{:S(2)}) collective-permute-start(f32[136,256]{1,0:T(8,128)S(1)} %shard_map.103.own_far), channel_id=1, source_target_pairs={{0,4},{4,8},{8,12},{12,16},{16,20},{20,24},{24,28},{1,5},{5,9},{9,... | collective-permute-start | bytes 417800 | tf_op jit(solution)/shard_map/ppermute | solution.py:786
  26.4 2.9 %collective-permute-done.4.far = f32[136,256]{1,0:T(8,128)S(1)} collective-permute-done((f32[136,256]{1,0:T(8,128)S(1)}, f32[136,256]{1,0:T(8,128)S(1)}, u32[]{:S(2)}, u32[]{:S(2)}) %collective-permute-start.4) | collective-permute-done | bytes 139296 | tf_op jit(solution)/shard_map/ppermute | solution.py:786
  29.3 1.9 %shard_map.107.own = f32[264,512]{1,0:T(8,128)S(1)} custom-call(f32[128,768]{1,0:T(8,128)S(1)} %shard_map.102.own_near, f32[136,256]{1,0:T(8,128)S(1)} %shard_map.103.own_far, f32[128,768]{1,0:T(8,128)S(1)} %collective-permute-done.3.near, f32[136,256]{1,0:T(8,128)S(1)} %collective-permute-done.4.far, bf16[512,512]{1,0:T(8,128)(2,1)S(1)} %get-tuple-element.58.mh, ...), custom_call_target="tpu_custom_call" | custom-call | tf_op jit(solution)/shard_map/pallas_call | solution.py:768
  31.2 3.6 %collective-permute-start.9 = (f32[264,512]{1,0:T(8,128)S(1)}, f32[264,512]{1,0:T(8,128)S(1)}, u32[]{:S(2)}, u32[]{:S(2)}) collective-permute-start(f32[264,512]{1,0:T(8,128)S(1)} %shard_map.107.own), channel_id=1, source_target_pairs={{0,8},{4,12},{8,16},{12,20},{16,24},{20,28},{24,0},{28,4},{1,9},{5... | collective-permute-start | bytes 1622024 | tf_op jit(solution)/shard_map/ppermute | solution.py:786
  34.7 1.6 %collective-permute-start.10 = (f32[384,128]{1,0:T(8,128)S(1)}, f32[384,128]{1,0:T(8,128)S(1)}, u32[]{:S(2)}, u32[]{:S(2)}) collective-permute-start(f32[384,128]{1,0:T(8,128)S(1)} %get-tuple-element.56.own), channel_id=1, source_target_pairs={{0,8},{4,12},{8,16},{12,20},{16,24},{20,28},{24,0},{28,4},{1,9},{5... | collective-permute-start | bytes 589832 | tf_op jit(solution)/shard_map/ppermute | solution.py:786
  36.3 1.6 %collective-permute-start.12 = (f32[384,128]{1,0:T(8,128)S(1)}, f32[384,128]{1,0:T(8,128)S(1)}, u32[]{:S(2)}, u32[]{:S(2)}) collective-permute-start(f32[384,128]{1,0:T(8,128)S(1)} %get-tuple-element.57.before), channel_id=1, source_target_pairs={{0,8},{4,12},{8,16},{12,20},{16,24},{20,28},{24,0},{28,4},{1,9},{5... | collective-permute-start | bytes 589832 | tf_op jit(solution)/shard_map/ppermute | solution.py:786
  37.9 16.2 %collective-permute-done.10.mine = f32[384,128]{1,0:T(8,128)S(1)} collective-permute-done((f32[384,128]{1,0:T(8,128)S(1)}, f32[384,128]{1,0:T(8,128)S(1)}, u32[]{:S(2)}, u32[]{:S(2)}) %collective-permute-start.10) | collective-permute-done | bytes 196640 | tf_op jit(solution)/shard_map/ppermute | solution.py:786
  54.1 3.5 %collective-permute-done.12.mine = f32[384,128]{1,0:T(8,128)S(1)} collective-permute-done((f32[384,128]{1,0:T(8,128)S(1)}, f32[384,128]{1,0:T(8,128)S(1)}, u32[]{:S(2)}, u32[]{:S(2)}) %collective-permute-start.12) | collective-permute-done | bytes 196640 | tf_op jit(solution)/shard_map/ppermute | solution.py:786
  57.6 1.4 %shard_map.108 = (bf16[512,512]{1,0:T(8,128)(2,1)S(1)}, bf16[512,512]{1,0:T(8,128)(2,1)S(1)}, bf16[512,512]{1,0:T(8,128)(2,1)S(1)}, bf16[512,512]{1,0:T(8,128)(2,1)S(1)}, f32[512,256]{1,0:T(8,128)S(1)}) custom-call(s32[8,3]{1,0:T(8,128)S(1)} %copy.13.pattern, f32[384,128]{1,0:T(8,128)S(1)} %get-tuple-element.56.own, ...), custom_call_target="tpu_custom_call" | custom-call | tf_op jit(solution)/shard_map/pallas_call | solution.py:768
  61.3 1.2 %shard_map.111 = (bf16[512,512]{1,0:T(8,128)(2,1)S(1)}, bf16[512,512]{1,0:T(8,128)(2,1)S(1)}, bf16[512,512]{1,0:T(8,128)(2,1)S(1)}, bf16[512,512]{1,0:T(8,128)(2,1)S(1)}) custom-call(bf16[512,512]{1,0:T(8,128)(2,1)S(1)} %get-tuple-element.62.a0h, bf16[512,512]{1,0:T(8,128)(2,1)S(1)} %get-tuple-element.63.a0l, bf16[512,512]{1,0:T(8,128)(2,1)S(1)} %get-tuple-element.64.a1h, ...), custom_call_target="tpu_custom_call" | custom-call | tf_op jit(solution)/shard_map/pallas_call | solution.py:768
  62.7 1.7 %shard_map.113 = (f32[520,128]{1,0:T(8,128)S(1)}, bf16[512,512]{1,0:T(8,128)(2,1)S(1)}, bf16[512,512]{1,0:T(8,128)(2,1)S(1)}) custom-call(f32[264,512]{1,0:T(8,128)S(1)} %shard_map.107.own, f32[264,512]{1,0:T(8,128)S(1)} %collective-permute-done.9.earlier, bf16[512,512]{1,0:T(8,128)(2,1)S(1)} %get-tuple-element.74.mh, ...), custom_call_target="tpu_custom_call" | custom-call | tf_op jit(solution)/shard_map/pallas_call | solution.py:768
  64.4 1.6 %collective-permute-start.16 = (f32[520,128]{1,0:T(8,128)S(1)}, f32[520,128]{1,0:T(8,128)S(1)}, u32[]{:S(2)}, u32[]{:S(2)}) collective-permute-start(f32[520,128]{1,0:T(8,128)S(1)} %get-tuple-element.86), channel_id=1, source_target_pairs={{0,2},{1,3},{2,0},{3,1},{4,6},{5,7},{6,4},{7,5},{8,10},{9,11},{10,... | collective-permute-start | bytes 798728 | tf_op jit(solution)/shard_map/ppermute | solution.py:782
  68.2 1.2 %collective-permute-start.19 = (f32[264,128]{1,0:T(8,128)S(1)}, f32[264,128]{1,0:T(8,128)S(1)}, u32[]{:S(2)}, u32[]{:S(2)}) collective-permute-start(f32[264,128]{1,0:T(8,128)S(1)} %get-tuple-element.92), channel_id=1, source_target_pairs={{0,3},{1,2},{2,1},{3,0},{4,7},{5,6},{6,5},{7,4},{8,11},{9,10},{10,... | collective-permute-start | bytes 405512 | tf_op jit(solution)/shard_map/ppermute | solution.py:782
  69.4 4.4 %collective-permute-done.16.from_chip = f32[520,128]{1,0:T(8,128)S(1)} collective-permute-done((f32[520,128]{1,0:T(8,128)S(1)}, f32[520,128]{1,0:T(8,128)S(1)}, u32[]{:S(2)}, u32[]{:S(2)}) %collective-permute-start.16) | collective-permute-done | bytes 266272 | tf_op jit(solution)/shard_map/ppermute | solution.py:782
  73.9 1.6 %collective-permute-start.17 = (f32[8,128]{1,0:T(8,128)S(1)}, f32[8,128]{1,0:T(8,128)S(1)}, u32[]{:S(2)}, u32[]{:S(2)}) collective-permute-start(f32[8,128]{1,0:T(8,128)S(1)} %get-tuple-element.81.short), channel_id=1, source_target_pairs={{0,2},{1,3},{2,0},{3,1},{4,6},{5,7},{6,4},{7,5},{8,10},{9,11},{10,... | collective-permute-start | bytes 12296 | tf_op jit(solution)/shard_map/ppermute | solution.py:782
  75.5 3.8 %collective-permute-done.15.dyn_recv = f32[128,512]{1,0:T(8,128)S(1)} collective-permute-done((f32[128,512]{1,0:T(8,128)S(1)}, f32[128,512]{1,0:T(8,128)S(1)}, u32[]{:S(2)}, u32[]{:S(2)}) %collective-permute-start.15) | collective-permute-done | bytes 262176 | tf_op jit(solution)/shard_map/ppermute | solution.py:782
  79.4 1.2 %shard_map.117 = (f32[2,128,512]{2,1,0:T(8,128)}, f32[2,128,512]{2,1,0:T(8,128)}, f32[2,128,512]{2,1,0:T(8,128)}) custom-call(f32[512,128]{1,0:T(8,128)S(1)} %get-tuple-element.82.keep, f32[520,128]{1,0:T(8,128)S(1)} %collective-permute-done.14.from_core, f32[128,512]{1,0:T(8,128)S(1)} %get-tuple-element.84.dyn_own, ...), custom_call_target="tpu_custom_call" | custom-call | tf_op jit(solution)/shard_map/pallas_call | solution.py:768
  80.5 1.7 %collective-permute-done.17.chip_short = f32[8,128]{1,0:T(8,128)S(1)} collective-permute-done((f32[8,128]{1,0:T(8,128)S(1)}, f32[8,128]{1,0:T(8,128)S(1)}, u32[]{:S(2)}, u32[]{:S(2)}) %collective-permute-start.17) | collective-permute-done | bytes 4128 | tf_op jit(solution)/shard_map/ppermute | solution.py:782
  (39 shorter events, 9.0 us)
Async XLA Ops:
  0.6 1.9 %copy-start = (f32[2,128,192]{1,2,0:T(8,128)S(1)}, f32[2,128,192]{1,2,0:T(8,128)}, u32[]{:S(2)}) copy-start(f32[2,128,192]{1,2,0:T(8,128)} %param.6) | copy-start | bytes 589828
  1.9 13.3 %collective-permute-start = (f32[136,384]{1,0:T(8,128)S(1)}, f32[136,384]{1,0:T(8,128)S(1)}, u32[]{:S(2)}, u32[]{:S(2)}) collective-permute-start(f32[136,384]{1,0:T(8,128)S(1)} %get-tuple-element.52), channel_id=1, source_target_pairs={{0,1},{1,0},{2,3},{3,2},{4,5},{5,4},{6,7},{7,6},{8,9},{9,8},{10,11... | collective-permute-start | bytes 626696 | tf_op jit(solution)/shard_map/ppermute | solution.py:782
  2.5 11.1 %collective-permute-start.5 = (f32[2,192,128]{2,1,0:T(8,128)S(1)}, f32[2,192,128]{2,1,0:T(8,128)S(1)}, u32[]{:S(2)}, u32[]{:S(2)}) collective-permute-start(f32[2,192,128]{2,1,0:T(8,128)S(1)} %bitcast.1), channel_id=1, source_target_pairs={{0,4},{4,8},{8,12},{12,16},{16,20},{20,24},{24,28},{28,0},{1,5},{5... | collective-permute-start | bytes 589832 | tf_op jit(solution)/shard_map/ppermute | solution.py:786
  13.6 7.8 %collective-permute-start.6 = (f32[384,128]{1,0:T(8,128)S(1)}, f32[384,128]{1,0:T(8,128)S(1)}, u32[]{:S(2)}, u32[]{:S(2)}) collective-permute-start(f32[384,128]{1,0:T(8,128)S(1)} %shard_map.104), channel_id=1, source_target_pairs={{0,2},{1,3},{2,0},{3,1},{4,6},{5,7},{6,4},{7,5},{8,10},{9,11},{10,... | collective-permute-start | bytes 589832 | tf_op jit(solution)/shard_map/ppermute | solution.py:782
  15.2 14.0 %collective-permute-start.3 = (f32[128,768]{1,0:T(8,128)S(1)}, f32[128,768]{1,0:T(8,128)S(1)}, u32[]{:S(2)}, u32[]{:S(2)}) collective-permute-start(f32[128,768]{1,0:T(8,128)S(1)} %shard_map.102.own_near), channel_id=1, source_target_pairs={{0,4},{4,8},{8,12},{12,16},{16,20},{20,24},{24,28},{28,0},{1,5},{5... | collective-permute-start | bytes 1179656 | tf_op jit(solution)/shard_map/ppermute | solution.py:786
  15.3 8.8 %collective-permute-start.1 = (f32[136,256]{1,0:T(8,128)S(1)}, f32[136,256]{1,0:T(8,128)S(1)}, u32[]{:S(2)}, u32[]{:S(2)}) collective-permute-start(f32[136,256]{1,0:T(8,128)S(1)} %get-tuple-element.54), channel_id=1, source_target_pairs={{0,2},{1,3},{2,0},{3,1},{4,6},{5,7},{6,4},{7,5},{8,10},{9,11},{10,... | collective-permute-start | bytes 417800 | tf_op jit(solution)/shard_map/ppermute | solution.py:782
  15.9 7.8 %collective-permute-start.2 = (f32[136,128]{1,0:T(8,128)S(1)}, f32[136,128]{1,0:T(8,128)S(1)}, u32[]{:S(2)}, u32[]{:S(2)}) collective-permute-start(f32[136,128]{1,0:T(8,128)S(1)} %get-tuple-element.55), channel_id=1, source_target_pairs={{0,3},{1,2},{2,1},{3,0},{4,7},{5,6},{6,5},{7,4},{8,11},{9,10},{10,... | collective-permute-start | bytes 208904 | tf_op jit(solution)/shard_map/ppermute | solution.py:782
  21.5 4.0 %collective-permute-start.7 = (f32[384,128]{1,0:T(8,128)S(1)}, f32[384,128]{1,0:T(8,128)S(1)}, u32[]{:S(2)}, u32[]{:S(2)}) collective-permute-start(f32[384,128]{1,0:T(8,128)S(1)} %get-tuple-element.56.own), channel_id=1, source_target_pairs={{0,1},{1,0},{2,3},{3,2},{4,5},{5,4},{6,7},{7,6},{8,9},{9,8},{10,11... | collective-permute-start | bytes 589832 | tf_op jit(solution)/shard_map/ppermute | solution.py:782
  21.5 4.0 %collective-permute-start.8 = (f32[384,128]{1,0:T(8,128)S(1)}, f32[384,128]{1,0:T(8,128)S(1)}, u32[]{:S(2)}, u32[]{:S(2)}) collective-permute-start(f32[384,128]{1,0:T(8,128)S(1)} %get-tuple-element.57.before), channel_id=1, source_target_pairs={{0,1},{1,0},{2,3},{3,2},{4,5},{5,4},{6,7},{7,6},{8,9},{9,8},{10,11... | collective-permute-start | bytes 589832 | tf_op jit(solution)/shard_map/ppermute | solution.py:782
  24.1 1.3 %copy-start.1 = (s32[8,3]{0,1:T(4,128)S(1)}, s32[8,3]{0,1:T(4,128)}, u32[]{:S(2)}) copy-start(s32[8,3]{0,1:T(4,128)} %param.7) | copy-start | bytes 292
  24.1 5.2 %collective-permute-start.4 = (f32[136,256]{1,0:T(8,128)S(1)}, f32[136,256]{1,0:T(8,128)S(1)}, u32[]{:S(2)}, u32[]{:S(2)}) collective-permute-start(f32[136,256]{1,0:T(8,128)S(1)} %shard_map.103.own_far), channel_id=1, source_target_pairs={{0,4},{4,8},{8,12},{12,16},{16,20},{20,24},{24,28},{1,5},{5,9},{9,... | collective-permute-start | bytes 417800 | tf_op jit(solution)/shard_map/ppermute | solution.py:786
  31.2 31.5 %collective-permute-start.9 = (f32[264,512]{1,0:T(8,128)S(1)}, f32[264,512]{1,0:T(8,128)S(1)}, u32[]{:S(2)}, u32[]{:S(2)}) collective-permute-start(f32[264,512]{1,0:T(8,128)S(1)} %shard_map.107.own), channel_id=1, source_target_pairs={{0,8},{4,12},{8,16},{12,20},{16,24},{20,28},{24,0},{28,4},{1,9},{5... | collective-permute-start | bytes 1622024 | tf_op jit(solution)/shard_map/ppermute | solution.py:786
  34.7 19.4 %collective-permute-start.10 = (f32[384,128]{1,0:T(8,128)S(1)}, f32[384,128]{1,0:T(8,128)S(1)}, u32[]{:S(2)}, u32[]{:S(2)}) collective-permute-start(f32[384,128]{1,0:T(8,128)S(1)} %get-tuple-element.56.own), channel_id=1, source_target_pairs={{0,8},{4,12},{8,16},{12,20},{16,24},{20,28},{24,0},{28,4},{1,9},{5... | collective-permute-start | bytes 589832 | tf_op jit(solution)/shard_map/ppermute | solution.py:786
  36.3 21.3 %collective-permute-start.12 = (f32[384,128]{1,0:T(8,128)S(1)}, f32[384,128]{1,0:T(8,128)S(1)}, u32[]{:S(2)}, u32[]{:S(2)}) collective-permute-start(f32[384,128]{1,0:T(8,128)S(1)} %get-tuple-element.57.before), channel_id=1, source_target_pairs={{0,8},{4,12},{8,16},{12,20},{16,24},{20,28},{24,0},{28,4},{1,9},{5... | collective-permute-start | bytes 589832 | tf_op jit(solution)/shard_map/ppermute | solution.py:786
  54.1 4.9 %collective-permute-start.11 = (f32[384,128]{1,0:T(8,128)S(1)}, f32[384,128]{1,0:T(8,128)S(1)}, u32[]{:S(2)}, u32[]{:S(2)}) collective-permute-start(f32[384,128]{1,0:T(8,128)S(1)} %collective-permute-done.10.mine), channel_id=1, source_target_pairs={{0,1},{1,0},{2,3},{3,2},{4,5},{5,4},{6,7},{7,6},{8,9},{9,8},{10,11... | collective-permute-start | bytes 589832 | tf_op jit(solution)/shard_map/ppermute | solution.py:782
  57.6 2.5 %collective-permute-start.13 = (f32[384,128]{1,0:T(8,128)S(1)}, f32[384,128]{1,0:T(8,128)S(1)}, u32[]{:S(2)}, u32[]{:S(2)}) collective-permute-start(f32[384,128]{1,0:T(8,128)S(1)} %collective-permute-done.12.mine), channel_id=1, source_target_pairs={{0,1},{1,0},{2,3},{3,2},{4,5},{5,4},{6,7},{7,6},{8,9},{9,8},{10,11... | collective-permute-start | bytes 589832 | tf_op jit(solution)/shard_map/ppermute | solution.py:782
  64.4 9.3 %collective-permute-start.16 = (f32[520,128]{1,0:T(8,128)S(1)}, f32[520,128]{1,0:T(8,128)S(1)}, u32[]{:S(2)}, u32[]{:S(2)}) collective-permute-start(f32[520,128]{1,0:T(8,128)S(1)} %get-tuple-element.86), channel_id=1, source_target_pairs={{0,2},{1,3},{2,0},{3,1},{4,6},{5,7},{6,4},{7,5},{8,10},{9,11},{10,... | collective-permute-start | bytes 798728 | tf_op jit(solution)/shard_map/ppermute | solution.py:782
  67.5 11.9 %collective-permute-start.14 = (f32[520,128]{1,0:T(8,128)S(1)}, f32[520,128]{1,0:T(8,128)S(1)}, u32[]{:S(2)}, u32[]{:S(2)}) collective-permute-start(f32[520,128]{1,0:T(8,128)S(1)} %get-tuple-element.83), channel_id=1, source_target_pairs={{0,1},{1,0},{2,3},{3,2},{4,5},{5,4},{6,7},{7,6},{8,9},{9,8},{10,11... | collective-permute-start | bytes 798728 | tf_op jit(solution)/shard_map/ppermute | solution.py:782
  67.7 11.7 %collective-permute-start.15 = (f32[128,512]{1,0:T(8,128)S(1)}, f32[128,512]{1,0:T(8,128)S(1)}, u32[]{:S(2)}, u32[]{:S(2)}) collective-permute-start(f32[128,512]{1,0:T(8,128)S(1)} %get-tuple-element.85), channel_id=1, source_target_pairs={{0,2},{1,3},{2,0},{3,1},{4,6},{5,7},{6,4},{7,5},{8,10},{9,11},{10,... | collective-permute-start | bytes 786440 | tf_op jit(solution)/shard_map/ppermute | solution.py:782
  68.2 14.1 %collective-permute-start.19 = (f32[264,128]{1,0:T(8,128)S(1)}, f32[264,128]{1,0:T(8,128)S(1)}, u32[]{:S(2)}, u32[]{:S(2)}) collective-permute-start(f32[264,128]{1,0:T(8,128)S(1)} %get-tuple-element.92), channel_id=1, source_target_pairs={{0,3},{1,2},{2,1},{3,0},{4,7},{5,6},{6,5},{7,4},{8,11},{9,10},{10,... | collective-permute-start | bytes 405512 | tf_op jit(solution)/shard_map/ppermute | solution.py:782
  73.9 8.4 %collective-permute-start.18 = (f32[256,128]{1,0:T(8,128)S(1)}, f32[256,128]{1,0:T(8,128)S(1)}, u32[]{:S(2)}, u32[]{:S(2)}) collective-permute-start(f32[256,128]{1,0:T(8,128)S(1)} %get-tuple-element.91), channel_id=1, source_target_pairs={{0,1},{1,0},{2,3},{3,2},{4,5},{5,4},{6,7},{7,6},{8,9},{9,8},{10,11... | collective-permute-start | bytes 393224 | tf_op jit(solution)/shard_map/ppermute | solution.py:782
  73.9 8.3 %collective-permute-start.17 = (f32[8,128]{1,0:T(8,128)S(1)}, f32[8,128]{1,0:T(8,128)S(1)}, u32[]{:S(2)}, u32[]{:S(2)}) collective-permute-start(f32[8,128]{1,0:T(8,128)S(1)} %get-tuple-element.81.short), channel_id=1, source_target_pairs={{0,2},{1,3},{2,0},{3,1},{4,6},{5,7},{6,4},{7,5},{8,10},{9,11},{10,... | collective-permute-start | bytes 12296 | tf_op jit(solution)/shard_map/ppermute | solution.py:782

commit v10 on v9

--- a/solution.py
+++ b/solution.py
@@ -542,17 +542,12 @@
         ref[lanes(q ^ j, r), :] = value[:, j * r : (j + 1) * r]
 
 
-def came(earlier):
-    return jnp.where(has(2) == 1, earlier[...], 0.0)
-
-
 CROSSING = ((2, 0), (2, 1), (2, 3))
 
 
 def level2_kernel(own, earlier, mh, ml, th, tl, full, z, to_chip, uh, ul, xh, xl, rest):
     c = place_of()[2]
     r = own.shape[1] // 4
-    earlier = came(earlier)
     two, three = slice(2 * r, 3 * r), slice(3 * r, 4 * r)
 
     @pl.when(c == 0)
@@ -591,7 +586,6 @@
 ):
     c = place_of()[2]
     r = own.shape[1] // 4
-    earlier = came(earlier)
     base = 2 * r
     three = slice(3 * r, 4 * r)
     b1 = earlier[base + 1 : base + 2, :] + row_times(earlier[base + 3 : base + 4, :], a2[...], r)
@@ -626,7 +620,6 @@
 def rest_kernel(earlier, th, tl, full, z, uh, ul, short, keep, to_core, rest):
     q, _, c = place_of()
     r = earlier.shape[1] // 4
-    earlier = came(earlier)
 
     @pl.when(c == 0)
     def _():
@@ -840,7 +833,7 @@
         vmem(shape(2 * r + 8, n)),
         [pltpu.VMEM((n + 16, n), BF16)] * 2 + [pltpu.VMEM((2 * r + 16, n), BF16)] * 2,
     )
-    earlier = later(level1, 2, cyclic=True)
+    earlier = later(level1, 2)
     *a01, t = kernel(
         functools.partial(early_kernel, bs),
         vmem(pattern, *pairs),

time: 83.2 us -> 82.3 us (0.989)
  waiting for transfers between devices: 48.4 us -> 45.7 us
  starting transfers between devices: 19.3 us -> 21.2 us
    ppermute x6, waiting for transfers between devices: 31.2 us -> 28.3 us  [later(): lax.ppermute(value, 'tm', [(i, (i + distance) % tms) for i in range(count)])]
    ppermute x6, starting transfers between devices: 10.6 us -> 12.5 us  [later(): lax.ppermute(value, 'tm', [(i, (i + distance) % tms) for i in range(count)])]
where the time goes in v10:
time: 82.3 us; the launch traced here: 82.1 us
  waiting for transfers between devices  45.7 us (56%)
  starting transfers between devices  21.2 us (26%)
  Pallas kernels  14.3 us (17%)
  between operations  0.83 us (1%)
    ppermute x6, waiting for transfers between devices, later(): lax.ppermute(value, 'tm', [(i, (i + distance) % tms) for i in range(count)])  28.3 us
    ppermute x14, waiting for transfers between devices, swap(): return lax.ppermute(value, 'col', [(i, i ^ bit) for i in range(cols)])  17.3 us
    pallas_call x18, Pallas kernels, kernel(): call(*(pltpu.with_memory_space_constraint(x, kept[where]) if where in kep...  14.3 us
    ppermute x6, starting transfers between devices, later(): lax.ppermute(value, 'tm', [(i, (i + distance) % tms) for i in range(count)])  12.5 us
    ppermute x14, starting transfers between devices, swap(): return lax.ppermute(value, 'col', [(i, i ^ bit) for i in range(cols)])  8.72 us
  transfers between devices with their start and end apart: 20, of which 10 were waited for; matrix products, arithmetic and copies ran while one was open for 0% of the time, Pallas kernels for 11%

profile of v10, /device:TPU:0, one launch (start us, length us, event | category | flops | bytes accessed | tf_op | source)
XLA Modules:
  0.0 82.1 jit_solution(15174122323324592693)
XLA Ops:
  0.6 1.3 %shard_map.101 = (f32[136,384]{1,0:T(8,128)S(1)}, f32[136,256]{1,0:T(8,128)S(1)}, f32[136,128]{1,0:T(8,128)S(1)}, f32[128,512]{1,0:T(8,128)S(1)}, f32[8,128]{1,0:T(8,128)S(1)}) custom-call(f32[2,128,512]{2,1,0:T(8,128)} %cov.1, f32[2,128,512]{2,1,0:T(8,128)} %cost.1, f32[2,128]{1,0:T(2,128)} %drift.1, f32[2,128]{1,0:T(2,128)} %eta.1), custom_call_target="tpu_custom_call" | custom-call | tf_op jit(solution)/shard_map/pallas_call | solution.py:761
  2.5 2.5 %collective-permute-start.5 = (f32[2,192,128]{2,1,0:T(8,128)S(1)}, f32[2,192,128]{2,1,0:T(8,128)S(1)}, u32[]{:S(2)}, u32[]{:S(2)}) collective-permute-start(f32[2,192,128]{2,1,0:T(8,128)S(1)} %bitcast.1), channel_id=1, source_target_pairs={{0,4},{4,8},{8,12},{12,16},{16,20},{20,24},{24,28},{28,0},{1,5},{5... | collective-permute-start | bytes 589832 | tf_op jit(solution)/shard_map/ppermute | solution.py:779
  5.0 8.5 %collective-permute-done.5.before = f32[2,192,128]{2,1,0:T(8,128)S(1)} collective-permute-done((f32[2,192,128]{2,1,0:T(8,128)S(1)}, f32[2,192,128]{2,1,0:T(8,128)S(1)}, u32[]{:S(2)}, u32[]{:S(2)}) %collective-permute-start.5) | collective-permute-done | bytes 196640 | tf_op jit(solution)/shard_map/ppermute | solution.py:779
  13.6 1.6 %collective-permute-start.6 = (f32[384,128]{1,0:T(8,128)S(1)}, f32[384,128]{1,0:T(8,128)S(1)}, u32[]{:S(2)}, u32[]{:S(2)}) collective-permute-start(f32[384,128]{1,0:T(8,128)S(1)} %shard_map.104), channel_id=1, source_target_pairs={{0,2},{1,3},{2,0},{3,1},{4,6},{5,7},{6,4},{7,5},{8,10},{9,11},{10,... | collective-permute-start | bytes 589832 | tf_op jit(solution)/shard_map/ppermute | solution.py:775
  16.1 5.3 %collective-permute-done.6.other = f32[384,128]{1,0:T(8,128)S(1)} collective-permute-done((f32[384,128]{1,0:T(8,128)S(1)}, f32[384,128]{1,0:T(8,128)S(1)}, u32[]{:S(2)}, u32[]{:S(2)}) %collective-permute-start.6) | collective-permute-done | bytes 196640 | tf_op jit(solution)/shard_map/ppermute | solution.py:775
  22.0 1.6 %collective-permute-done.2.from_far = f32[136,128]{1,0:T(8,128)S(1)} collective-permute-done((f32[136,128]{1,0:T(8,128)S(1)}, f32[136,128]{1,0:T(8,128)S(1)}, u32[]{:S(2)}, u32[]{:S(2)}) %collective-permute-start.2) | collective-permute-done | bytes 69664 | tf_op jit(solution)/shard_map/ppermute | solution.py:775
  24.1 1.3 %collective-permute-start.4 = (f32[136,256]{1,0:T(8,128)S(1)}, f32[136,256]{1,0:T(8,128)S(1)}, u32[]{:S(2)}, u32[]{:S(2)}) collective-permute-start(f32[136,256]{1,0:T(8,128)S(1)} %shard_map.103.own_far), channel_id=1, source_target_pairs={{0,4},{4,8},{8,12},{12,16},{16,20},{20,24},{24,28},{1,5},{5,9},{9,... | collective-permute-start | bytes 417800 | tf_op jit(solution)/shard_map/ppermute | solution.py:779
  26.4 2.9 %collective-permute-done.4.far = f32[136,256]{1,0:T(8,128)S(1)} collective-permute-done((f32[136,256]{1,0:T(8,128)S(1)}, f32[136,256]{1,0:T(8,128)S(1)}, u32[]{:S(2)}, u32[]{:S(2)}) %collective-permute-start.4) | collective-permute-done | bytes 139296 | tf_op jit(solution)/shard_map/ppermute | solution.py:779
  29.3 1.9 %shard_map.107.own = f32[264,512]{1,0:T(8,128)S(1)} custom-call(f32[128,768]{1,0:T(8,128)S(1)} %shard_map.102.own_near, f32[136,256]{1,0:T(8,128)S(1)} %shard_map.103.own_far, f32[128,768]{1,0:T(8,128)S(1)} %collective-permute-done.3.near, f32[136,256]{1,0:T(8,128)S(1)} %collective-permute-done.4.far, bf16[512,512]{1,0:T(8,128)(2,1)S(1)} %get-tuple-element.58.mh, ...), custom_call_target="tpu_custom_call" | custom-call | tf_op jit(solution)/shard_map/pallas_call | solution.py:761
  31.2 5.4 %collective-permute-start.9 = (f32[264,512]{1,0:T(8,128)S(1)}, f32[264,512]{1,0:T(8,128)S(1)}, u32[]{:S(2)}, u32[]{:S(2)}) collective-permute-start(f32[264,512]{1,0:T(8,128)S(1)} %shard_map.107.own), channel_id=1, source_target_pairs={{0,8},{4,12},{8,16},{12,20},{16,24},{20,28},{1,9},{5,13},{9,17},{1... | collective-permute-start | bytes 1622024 | tf_op jit(solution)/shard_map/ppermute | solution.py:779
  36.6 1.6 %collective-permute-start.10 = (f32[384,128]{1,0:T(8,128)S(1)}, f32[384,128]{1,0:T(8,128)S(1)}, u32[]{:S(2)}, u32[]{:S(2)}) collective-permute-start(f32[384,128]{1,0:T(8,128)S(1)} %get-tuple-element.56.own), channel_id=1, source_target_pairs={{0,8},{4,12},{8,16},{12,20},{16,24},{20,28},{24,0},{28,4},{1,9},{5... | collective-permute-start | bytes 589832 | tf_op jit(solution)/shard_map/ppermute | solution.py:779
  38.2 1.6 %collective-permute-start.12 = (f32[384,128]{1,0:T(8,128)S(1)}, f32[384,128]{1,0:T(8,128)S(1)}, u32[]{:S(2)}, u32[]{:S(2)}) collective-permute-start(f32[384,128]{1,0:T(8,128)S(1)} %get-tuple-element.57.before), channel_id=1, source_target_pairs={{0,8},{4,12},{8,16},{12,20},{16,24},{20,28},{24,0},{28,4},{1,9},{5... | collective-permute-start | bytes 589832 | tf_op jit(solution)/shard_map/ppermute | solution.py:779
  39.8 13.6 %collective-permute-done.10.mine = f32[384,128]{1,0:T(8,128)S(1)} collective-permute-done((f32[384,128]{1,0:T(8,128)S(1)}, f32[384,128]{1,0:T(8,128)S(1)}, u32[]{:S(2)}, u32[]{:S(2)}) %collective-permute-start.10) | collective-permute-done | bytes 196640 | tf_op jit(solution)/shard_map/ppermute | solution.py:779
  53.4 3.2 %collective-permute-done.12.mine = f32[384,128]{1,0:T(8,128)S(1)} collective-permute-done((f32[384,128]{1,0:T(8,128)S(1)}, f32[384,128]{1,0:T(8,128)S(1)}, u32[]{:S(2)}, u32[]{:S(2)}) %collective-permute-start.12) | collective-permute-done | bytes 196640 | tf_op jit(solution)/shard_map/ppermute | solution.py:779
  56.7 1.4 %shard_map.108 = (bf16[512,512]{1,0:T(8,128)(2,1)S(1)}, bf16[512,512]{1,0:T(8,128)(2,1)S(1)}, bf16[512,512]{1,0:T(8,128)(2,1)S(1)}, bf16[512,512]{1,0:T(8,128)(2,1)S(1)}, f32[512,256]{1,0:T(8,128)S(1)}) custom-call(s32[8,3]{1,0:T(8,128)S(1)} %copy.13.pattern, f32[384,128]{1,0:T(8,128)S(1)} %get-tuple-element.56.own, ...), custom_call_target="tpu_custom_call" | custom-call | tf_op jit(solution)/shard_map/pallas_call | solution.py:761
  60.3 1.2 %shard_map.111 = (bf16[512,512]{1,0:T(8,128)(2,1)S(1)}, bf16[512,512]{1,0:T(8,128)(2,1)S(1)}, bf16[512,512]{1,0:T(8,128)(2,1)S(1)}, bf16[512,512]{1,0:T(8,128)(2,1)S(1)}) custom-call(bf16[512,512]{1,0:T(8,128)(2,1)S(1)} %get-tuple-element.62.a0h, bf16[512,512]{1,0:T(8,128)(2,1)S(1)} %get-tuple-element.63.a0l, bf16[512,512]{1,0:T(8,128)(2,1)S(1)} %get-tuple-element.64.a1h, ...), custom_call_target="tpu_custom_call" | custom-call | tf_op jit(solution)/shard_map/pallas_call | solution.py:761
  61.8 1.7 %shard_map.113 = (f32[520,128]{1,0:T(8,128)S(1)}, bf16[512,512]{1,0:T(8,128)(2,1)S(1)}, bf16[512,512]{1,0:T(8,128)(2,1)S(1)}) custom-call(f32[264,512]{1,0:T(8,128)S(1)} %shard_map.107.own, f32[264,512]{1,0:T(8,128)S(1)} %collective-permute-done.9.earlier, bf16[512,512]{1,0:T(8,128)(2,1)S(1)} %get-tuple-element.74.mh, ...), custom_call_target="tpu_custom_call" | custom-call | tf_op jit(solution)/shard_map/pallas_call | solution.py:761
  63.5 1.6 %collective-permute-start.16 = (f32[520,128]{1,0:T(8,128)S(1)}, f32[520,128]{1,0:T(8,128)S(1)}, u32[]{:S(2)}, u32[]{:S(2)}) collective-permute-start(f32[520,128]{1,0:T(8,128)S(1)} %get-tuple-element.86), channel_id=1, source_target_pairs={{0,2},{1,3},{2,0},{3,1},{4,6},{5,7},{6,4},{7,5},{8,10},{9,11},{10,... | collective-permute-start | bytes 798728 | tf_op jit(solution)/shard_map/ppermute | solution.py:775
  67.2 1.2 %collective-permute-start.19 = (f32[264,128]{1,0:T(8,128)S(1)}, f32[264,128]{1,0:T(8,128)S(1)}, u32[]{:S(2)}, u32[]{:S(2)}) collective-permute-start(f32[264,128]{1,0:T(8,128)S(1)} %get-tuple-element.92), channel_id=1, source_target_pairs={{0,3},{1,2},{2,1},{3,0},{4,7},{5,6},{6,5},{7,4},{8,11},{9,10},{10,... | collective-permute-start | bytes 405512 | tf_op jit(solution)/shard_map/ppermute | solution.py:775
  68.4 4.4 %collective-permute-done.16.from_chip = f32[520,128]{1,0:T(8,128)S(1)} collective-permute-done((f32[520,128]{1,0:T(8,128)S(1)}, f32[520,128]{1,0:T(8,128)S(1)}, u32[]{:S(2)}, u32[]{:S(2)}) %collective-permute-start.16) | collective-permute-done | bytes 266272 | tf_op jit(solution)/shard_map/ppermute | solution.py:775
  73.0 1.6 %collective-permute-start.17 = (f32[8,128]{1,0:T(8,128)S(1)}, f32[8,128]{1,0:T(8,128)S(1)}, u32[]{:S(2)}, u32[]{:S(2)}) collective-permute-start(f32[8,128]{1,0:T(8,128)S(1)} %get-tuple-element.81.short), channel_id=1, source_target_pairs={{0,2},{1,3},{2,0},{3,1},{4,6},{5,7},{6,4},{7,5},{8,10},{9,11},{10,... | collective-permute-start | bytes 12296 | tf_op jit(solution)/shard_map/ppermute | solution.py:775
  74.6 3.8 %collective-permute-done.15.dyn_recv = f32[128,512]{1,0:T(8,128)S(1)} collective-permute-done((f32[128,512]{1,0:T(8,128)S(1)}, f32[128,512]{1,0:T(8,128)S(1)}, u32[]{:S(2)}, u32[]{:S(2)}) %collective-permute-start.15) | collective-permute-done | bytes 262176 | tf_op jit(solution)/shard_map/ppermute | solution.py:775
  78.4 1.2 %shard_map.117 = (f32[2,128,512]{2,1,0:T(8,128)}, f32[2,128,512]{2,1,0:T(8,128)}, f32[2,128,512]{2,1,0:T(8,128)}) custom-call(f32[512,128]{1,0:T(8,128)S(1)} %get-tuple-element.82.keep, f32[520,128]{1,0:T(8,128)S(1)} %collective-permute-done.14.from_core, f32[128,512]{1,0:T(8,128)S(1)} %get-tuple-element.84.dyn_own, ...), custom_call_target="tpu_custom_call" | custom-call | tf_op jit(solution)/shard_map/pallas_call | solution.py:761
  79.6 1.7 %collective-permute-done.17.chip_short = f32[8,128]{1,0:T(8,128)S(1)} collective-permute-done((f32[8,128]{1,0:T(8,128)S(1)}, f32[8,128]{1,0:T(8,128)S(1)}, u32[]{:S(2)}, u32[]{:S(2)}) %collective-permute-start.17) | collective-permute-done | bytes 4128 | tf_op jit(solution)/shard_map/ppermute | solution.py:775
  (39 shorter events, 9.0 us)
Async XLA Ops:
  0.6 1.9 %copy-start = (f32[2,128,192]{1,2,0:T(8,128)S(1)}, f32[2,128,192]{1,2,0:T(8,128)}, u32[]{:S(2)}) copy-start(f32[2,128,192]{1,2,0:T(8,128)} %param.6) | copy-start | bytes 589828
  1.9 13.3 %collective-permute-start = (f32[136,384]{1,0:T(8,128)S(1)}, f32[136,384]{1,0:T(8,128)S(1)}, u32[]{:S(2)}, u32[]{:S(2)}) collective-permute-start(f32[136,384]{1,0:T(8,128)S(1)} %get-tuple-element.52), channel_id=1, source_target_pairs={{0,1},{1,0},{2,3},{3,2},{4,5},{5,4},{6,7},{7,6},{8,9},{9,8},{10,11... | collective-permute-start | bytes 626696 | tf_op jit(solution)/shard_map/ppermute | solution.py:775
  2.5 11.1 %collective-permute-start.5 = (f32[2,192,128]{2,1,0:T(8,128)S(1)}, f32[2,192,128]{2,1,0:T(8,128)S(1)}, u32[]{:S(2)}, u32[]{:S(2)}) collective-permute-start(f32[2,192,128]{2,1,0:T(8,128)S(1)} %bitcast.1), channel_id=1, source_target_pairs={{0,4},{4,8},{8,12},{12,16},{16,20},{20,24},{24,28},{28,0},{1,5},{5... | collective-permute-start | bytes 589832 | tf_op jit(solution)/shard_map/ppermute | solution.py:779
  13.6 7.8 %collective-permute-start.6 = (f32[384,128]{1,0:T(8,128)S(1)}, f32[384,128]{1,0:T(8,128)S(1)}, u32[]{:S(2)}, u32[]{:S(2)}) collective-permute-start(f32[384,128]{1,0:T(8,128)S(1)} %shard_map.104), channel_id=1, source_target_pairs={{0,2},{1,3},{2,0},{3,1},{4,6},{5,7},{6,4},{7,5},{8,10},{9,11},{10,... | collective-permute-start | bytes 589832 | tf_op jit(solution)/shard_map/ppermute | solution.py:775
  15.2 14.0 %collective-permute-start.3 = (f32[128,768]{1,0:T(8,128)S(1)}, f32[128,768]{1,0:T(8,128)S(1)}, u32[]{:S(2)}, u32[]{:S(2)}) collective-permute-start(f32[128,768]{1,0:T(8,128)S(1)} %shard_map.102.own_near), channel_id=1, source_target_pairs={{0,4},{4,8},{8,12},{12,16},{16,20},{20,24},{24,28},{28,0},{1,5},{5... | collective-permute-start | bytes 1179656 | tf_op jit(solution)/shard_map/ppermute | solution.py:779
  15.3 8.8 %collective-permute-start.1 = (f32[136,256]{1,0:T(8,128)S(1)}, f32[136,256]{1,0:T(8,128)S(1)}, u32[]{:S(2)}, u32[]{:S(2)}) collective-permute-start(f32[136,256]{1,0:T(8,128)S(1)} %get-tuple-element.54), channel_id=1, source_target_pairs={{0,2},{1,3},{2,0},{3,1},{4,6},{5,7},{6,4},{7,5},{8,10},{9,11},{10,... | collective-permute-start | bytes 417800 | tf_op jit(solution)/shard_map/ppermute | solution.py:775
  15.9 7.8 %collective-permute-start.2 = (f32[136,128]{1,0:T(8,128)S(1)}, f32[136,128]{1,0:T(8,128)S(1)}, u32[]{:S(2)}, u32[]{:S(2)}) collective-permute-start(f32[136,128]{1,0:T(8,128)S(1)} %get-tuple-element.55), channel_id=1, source_target_pairs={{0,3},{1,2},{2,1},{3,0},{4,7},{5,6},{6,5},{7,4},{8,11},{9,10},{10,... | collective-permute-start | bytes 208904 | tf_op jit(solution)/shard_map/ppermute | solution.py:775
  21.5 4.0 %collective-permute-start.7 = (f32[384,128]{1,0:T(8,128)S(1)}, f32[384,128]{1,0:T(8,128)S(1)}, u32[]{:S(2)}, u32[]{:S(2)}) collective-permute-start(f32[384,128]{1,0:T(8,128)S(1)} %get-tuple-element.56.own), channel_id=1, source_target_pairs={{0,1},{1,0},{2,3},{3,2},{4,5},{5,4},{6,7},{7,6},{8,9},{9,8},{10,11... | collective-permute-start | bytes 589832 | tf_op jit(solution)/shard_map/ppermute | solution.py:775
  21.5 4.0 %collective-permute-start.8 = (f32[384,128]{1,0:T(8,128)S(1)}, f32[384,128]{1,0:T(8,128)S(1)}, u32[]{:S(2)}, u32[]{:S(2)}) collective-permute-start(f32[384,128]{1,0:T(8,128)S(1)} %get-tuple-element.57.before), channel_id=1, source_target_pairs={{0,1},{1,0},{2,3},{3,2},{4,5},{5,4},{6,7},{7,6},{8,9},{9,8},{10,11... | collective-permute-start | bytes 589832 | tf_op jit(solution)/shard_map/ppermute | solution.py:775
  24.1 1.3 %copy-start.1 = (s32[8,3]{0,1:T(4,128)S(1)}, s32[8,3]{0,1:T(4,128)}, u32[]{:S(2)}) copy-start(s32[8,3]{0,1:T(4,128)} %param.7) | copy-start | bytes 292
  24.1 5.2 %collective-permute-start.4 = (f32[136,256]{1,0:T(8,128)S(1)}, f32[136,256]{1,0:T(8,128)S(1)}, u32[]{:S(2)}, u32[]{:S(2)}) collective-permute-start(f32[136,256]{1,0:T(8,128)S(1)} %shard_map.103.own_far), channel_id=1, source_target_pairs={{0,4},{4,8},{8,12},{12,16},{16,20},{20,24},{24,28},{1,5},{5,9},{9,... | collective-permute-start | bytes 417800 | tf_op jit(solution)/shard_map/ppermute | solution.py:779
  31.2 30.6 %collective-permute-start.9 = (f32[264,512]{1,0:T(8,128)S(1)}, f32[264,512]{1,0:T(8,128)S(1)}, u32[]{:S(2)}, u32[]{:S(2)}) collective-permute-start(f32[264,512]{1,0:T(8,128)S(1)} %shard_map.107.own), channel_id=1, source_target_pairs={{0,8},{4,12},{8,16},{12,20},{16,24},{20,28},{1,9},{5,13},{9,17},{1... | collective-permute-start | bytes 1622024 | tf_op jit(solution)/shard_map/ppermute | solution.py:779
  36.6 16.8 %collective-permute-start.10 = (f32[384,128]{1,0:T(8,128)S(1)}, f32[384,128]{1,0:T(8,128)S(1)}, u32[]{:S(2)}, u32[]{:S(2)}) collective-permute-start(f32[384,128]{1,0:T(8,128)S(1)} %get-tuple-element.56.own), channel_id=1, source_target_pairs={{0,8},{4,12},{8,16},{12,20},{16,24},{20,28},{24,0},{28,4},{1,9},{5... | collective-permute-start | bytes 589832 | tf_op jit(solution)/shard_map/ppermute | solution.py:779
  38.2 18.5 %collective-permute-start.12 = (f32[384,128]{1,0:T(8,128)S(1)}, f32[384,128]{1,0:T(8,128)S(1)}, u32[]{:S(2)}, u32[]{:S(2)}) collective-permute-start(f32[384,128]{1,0:T(8,128)S(1)} %get-tuple-element.57.before), channel_id=1, source_target_pairs={{0,8},{4,12},{8,16},{12,20},{16,24},{20,28},{24,0},{28,4},{1,9},{5... | collective-permute-start | bytes 589832 | tf_op jit(solution)/shard_map/ppermute | solution.py:779
  53.4 4.7 %collective-permute-start.11 = (f32[384,128]{1,0:T(8,128)S(1)}, f32[384,128]{1,0:T(8,128)S(1)}, u32[]{:S(2)}, u32[]{:S(2)}) collective-permute-start(f32[384,128]{1,0:T(8,128)S(1)} %collective-permute-done.10.mine), channel_id=1, source_target_pairs={{0,1},{1,0},{2,3},{3,2},{4,5},{5,4},{6,7},{7,6},{8,9},{9,8},{10,11... | collective-permute-start | bytes 589832 | tf_op jit(solution)/shard_map/ppermute | solution.py:775
  56.7 2.5 %collective-permute-start.13 = (f32[384,128]{1,0:T(8,128)S(1)}, f32[384,128]{1,0:T(8,128)S(1)}, u32[]{:S(2)}, u32[]{:S(2)}) collective-permute-start(f32[384,128]{1,0:T(8,128)S(1)} %collective-permute-done.12.mine), channel_id=1, source_target_pairs={{0,1},{1,0},{2,3},{3,2},{4,5},{5,4},{6,7},{7,6},{8,9},{9,8},{10,11... | collective-permute-start | bytes 589832 | tf_op jit(solution)/shard_map/ppermute | solution.py:775
  63.5 9.3 %collective-permute-start.16 = (f32[520,128]{1,0:T(8,128)S(1)}, f32[520,128]{1,0:T(8,128)S(1)}, u32[]{:S(2)}, u32[]{:S(2)}) collective-permute-start(f32[520,128]{1,0:T(8,128)S(1)} %get-tuple-element.86), channel_id=1, source_target_pairs={{0,2},{1,3},{2,0},{3,1},{4,6},{5,7},{6,4},{7,5},{8,10},{9,11},{10,... | collective-permute-start | bytes 798728 | tf_op jit(solution)/shard_map/ppermute | solution.py:775
  66.5 11.9 %collective-permute-start.14 = (f32[520,128]{1,0:T(8,128)S(1)}, f32[520,128]{1,0:T(8,128)S(1)}, u32[]{:S(2)}, u32[]{:S(2)}) collective-permute-start(f32[520,128]{1,0:T(8,128)S(1)} %get-tuple-element.83), channel_id=1, source_target_pairs={{0,1},{1,0},{2,3},{3,2},{4,5},{5,4},{6,7},{7,6},{8,9},{9,8},{10,11... | collective-permute-start | bytes 798728 | tf_op jit(solution)/shard_map/ppermute | solution.py:775
  66.7 11.7 %collective-permute-start.15 = (f32[128,512]{1,0:T(8,128)S(1)}, f32[128,512]{1,0:T(8,128)S(1)}, u32[]{:S(2)}, u32[]{:S(2)}) collective-permute-start(f32[128,512]{1,0:T(8,128)S(1)} %get-tuple-element.85), channel_id=1, source_target_pairs={{0,2},{1,3},{2,0},{3,1},{4,6},{5,7},{6,4},{7,5},{8,10},{9,11},{10,... | collective-permute-start | bytes 786440 | tf_op jit(solution)/shard_map/ppermute | solution.py:775
  67.2 14.1 %collective-permute-start.19 = (f32[264,128]{1,0:T(8,128)S(1)}, f32[264,128]{1,0:T(8,128)S(1)}, u32[]{:S(2)}, u32[]{:S(2)}) collective-permute-start(f32[264,128]{1,0:T(8,128)S(1)} %get-tuple-element.92), channel_id=1, source_target_pairs={{0,3},{1,2},{2,1},{3,0},{4,7},{5,6},{6,5},{7,4},{8,11},{9,10},{10,... | collective-permute-start | bytes 405512 | tf_op jit(solution)/shard_map/ppermute | solution.py:775
  72.9 8.4 %collective-permute-start.18 = (f32[256,128]{1,0:T(8,128)S(1)}, f32[256,128]{1,0:T(8,128)S(1)}, u32[]{:S(2)}, u32[]{:S(2)}) collective-permute-start(f32[256,128]{1,0:T(8,128)S(1)} %get-tuple-element.91), channel_id=1, source_target_pairs={{0,1},{1,0},{2,3},{3,2},{4,5},{5,4},{6,7},{7,6},{8,9},{9,8},{10,11... | collective-permute-start | bytes 393224 | tf_op jit(solution)/shard_map/ppermute | solution.py:775
  73.0 8.3 %collective-permute-start.17 = (f32[8,128]{1,0:T(8,128)S(1)}, f32[8,128]{1,0:T(8,128)S(1)}, u32[]{:S(2)}, u32[]{:S(2)}) collective-permute-start(f32[8,128]{1,0:T(8,128)S(1)} %get-tuple-element.81.short), channel_id=1, source_target_pairs={{0,2},{1,3},{2,0},{3,1},{4,6},{5,7},{6,4},{7,5},{8,10},{9,11},{10,... | collective-permute-start | bytes 12296 | tf_op jit(solution)/shard_map/ppermute | solution.py:775

commit v11 on v10

--- a/solution.py
+++ b/solution.py
@@ -545,7 +545,7 @@
 CROSSING = ((2, 0), (2, 1), (2, 3))
 
 
-def level2_kernel(own, earlier, mh, ml, th, tl, full, z, to_chip, uh, ul, xh, xl, rest):
+def level2_kernel(own, earlier, mh, ml, th, tl, full, z, to_chip, vh, vl, xh, xl, rest):
     c = place_of()[2]
     r = own.shape[1] // 4
     two, three = slice(2 * r, 3 * r), slice(3 * r, 4 * r)
@@ -556,11 +556,11 @@
             put_split(xh, xl, slice(i * r, (i + 1) * r), slice(j * r, (j + 1) * r), block)
 
         spread(earlier, r, put)
-        hi, lo = split(dot3(xh[...], xl[...], mh[...], ml[...]))
-        uh[...] = hi
-        ul[...] = lo
-        rest[:, 2 * r :] = dot3(th[2 * r :, :], tl[2 * r :, :], hi[:, 2 * r :], lo[:, 2 * r :])
-        rest[0:r, 0 : 2 * r] = dot3(th[two, :], tl[two, :], hi[:, 0 : 2 * r], lo[:, 0 : 2 * r])
+        hi, lo = split(dot3(th[2 * r :, :], tl[2 * r :, :], xh[...], xl[...]))
+        vh[...] = hi
+        vl[...] = lo
+        rest[:, 2 * r :] = dot3(hi, lo, mh[:, 2 * r :], ml[:, 2 * r :])
+        rest[0:r, 0 : 2 * r] = dot3(hi[0:r, :], lo[0:r, :], mh[:, 0 : 2 * r], ml[:, 0 : 2 * r])
         rest[:, 2 * r :] = rest[:, 2 * r :] + full[2 * r :, 2 * r :]
         rest[0:r, 0 : 2 * r] = rest[0:r, 0 : 2 * r] + full[two, 0 : 2 * r]
 
@@ -582,7 +582,7 @@
 
 
 def far_rows_kernel(
-    own, earlier, mh, ml, th, tl, a2, full, z, uh, ul, to_far, short, vec, rest
+    own, earlier, mh, ml, a2, full, z, vh, vl, to_far, short, vec, rest
 ):
     c = place_of()[2]
     r = own.shape[1] // 4
@@ -592,7 +592,7 @@
 
     @pl.when(c == 0)
     def _():
-        value = dot3(th[three, :], tl[three, :], uh[:, 0 : 2 * r], ul[:, 0 : 2 * r])
+        value = dot3(vh[r:, :], vl[r:, :], mh[:, 0 : 2 * r], ml[:, 0 : 2 * r])
         rest[...] = value + full[three, 0 : 2 * r]
         vec[0:1, :] = b1
         vec[1:2, :] = own[base + 2 : base + 3, :]
@@ -617,13 +617,14 @@
     short[4:8, :] = jnp.zeros((4, r), F32)
 
 
-def rest_kernel(earlier, th, tl, full, z, uh, ul, short, keep, to_core, rest):
+def rest_kernel(earlier, mh, ml, th, tl, full, z, xh, xl, short, keep, to_core, rest):
     q, _, c = place_of()
     r = earlier.shape[1] // 4
 
     @pl.when(c == 0)
     def _():
-        rest[...] = dot3(th[0 : 2 * r, :], tl[0 : 2 * r, :], uh[...], ul[...]) + full[0 : 2 * r, :]
+        hi, lo = split(dot3(th[0 : 2 * r, :], tl[0 : 2 * r, :], xh[...], xl[...]))
+        rest[...] = dot3(hi, lo, mh[...], ml[...]) + full[0 : 2 * r, :]
 
     @pl.when(c == 1)
     def _():
@@ -820,7 +821,7 @@
     )
     pairs = (own_half, swap(own_half, 1), before_half, swap(before_half, 1))
     third = later(own_half, 2, cyclic=True)
-    fourth = later(before_half, 2, cyclic=True)
+    fourth = later(before_half, 2)
     m1 = kernel(
         functools.partial(prepare_kernel, bs),
         vmem(pattern, *pairs),
@@ -855,16 +856,16 @@
     full, z = kernel(
         ahead_kernel, vmem(level1, *m2), vmem(shape(n, n), shape(n, n)), [square(BF16)] * 2
     )
-    to_chip, *u = kernel(
+    to_chip, vh, vl, *x = kernel(
         level2_kernel,
         vmem(level1, earlier, *m2, full, z),
-        vmem(shape(n + 8, r), half(n, n), half(n, n)),
-        [square(BF16)] * 2 + [pltpu.VMEM((2 * r, n), F32)],
+        vmem(shape(n + 8, r), *[half(2 * r, n)] * 2, *[half(n, n)] * 2),
+        [pltpu.VMEM((2 * r, n), F32)],
     )
     from_chip = swap(to_chip, 2)
     to_far, short = kernel(
         far_rows_kernel,
-        vmem(level1, earlier, *m2, a2, full, z, *u),
+        vmem(level1, earlier, *m2[:2], a2, full, z, vh, vl),
         vmem(shape(2 * r + 8, r), shape(8, r)),
         [pltpu.VMEM((8, n), F32), pltpu.VMEM((r, 2 * r), F32)],
     )
@@ -872,7 +873,7 @@
     from_far = swap(to_far, 3)
     keep, to_core = kernel(
         rest_kernel,
-        vmem(earlier, *m2[2:], full, z, *u, short),
+        vmem(earlier, *m2, full, z, *x, short),
         vmem(shape(n, r), shape(n + 8, r)),
         [pltpu.VMEM((2 * r, n), F32)],
     )

time: 82.3 us -> 81.9 us (level)
  waiting for transfers between devices: 45.7 us -> 42.6 us
  starting transfers between devices: 21.2 us -> 23.8 us
    ppermute x6, waiting for transfers between devices: 28.3 us -> 26.4 us  [later(): lax.ppermute(value, 'tm', [(i, (i + distance) % tms) for i in range(count)])]
    ppermute x6, starting transfers between devices: 12.5 us -> 14.4 us  [later(): lax.ppermute(value, 'tm', [(i, (i + distance) % tms) for i in range(count)])]
    ppermute x14, waiting for transfers between devices: 17.3 us -> 16.2 us  [swap(): return lax.ppermute(value, 'col', [(i, i ^ bit) for i in range(cols)])]
  transfers between devices with their start and end apart: 20 -> 20, of which waited for: 10 -> 11; matrix products, arithmetic and copies ran while one was open for 0% -> 0% of each run, Pallas kernels for 11% -> 11%
where the time goes in v11:
time: 81.9 us; the launch traced here: 81.7 us
  waiting for transfers between devices  42.6 us (52%)
  starting transfers between devices  23.8 us (29%)
  Pallas kernels  14.4 us (18%)
  between operations  0.83 us (1%)
    ppermute x6, waiting for transfers between devices, later(): lax.ppermute(value, 'tm', [(i, (i + distance) % tms) for i in range(count)])  26.4 us
    ppermute x14, waiting for transfers between devices, swap(): return lax.ppermute(value, 'col', [(i, i ^ bit) for i in range(cols)])  16.2 us
    ppermute x6, starting transfers between devices, later(): lax.ppermute(value, 'tm', [(i, (i + distance) % tms) for i in range(count)])  14.4 us
    pallas_call x18, Pallas kernels, kernel(): call(*(pltpu.with_memory_space_constraint(x, kept[where]) if where in kep...  14.4 us
    ppermute x14, starting transfers between devices, swap(): return lax.ppermute(value, 'col', [(i, i ^ bit) for i in range(cols)])  9.39 us
  transfers between devices with their start and end apart: 20, of which 11 were waited for; matrix products, arithmetic and copies ran while one was open for 0% of the time, Pallas kernels for 11%

profile of v11, /device:TPU:0, one launch (start us, length us, event | category | flops | bytes accessed | tf_op | source)
XLA Modules:
  0.0 81.7 jit_solution(14154825444856436602)
XLA Ops:
  0.6 1.3 %shard_map.101 = (f32[136,384]{1,0:T(8,128)S(1)}, f32[136,256]{1,0:T(8,128)S(1)}, f32[136,128]{1,0:T(8,128)S(1)}, f32[128,512]{1,0:T(8,128)S(1)}, f32[8,128]{1,0:T(8,128)S(1)}) custom-call(f32[2,128,512]{2,1,0:T(8,128)} %cov.1, f32[2,128,512]{2,1,0:T(8,128)} %cost.1, f32[2,128]{1,0:T(2,128)} %drift.1, f32[2,128]{1,0:T(2,128)} %eta.1), custom_call_target="tpu_custom_call" | custom-call | tf_op jit(solution)/shard_map/pallas_call | solution.py:762
  2.5 2.5 %collective-permute-start.5 = (f32[2,192,128]{2,1,0:T(8,128)S(1)}, f32[2,192,128]{2,1,0:T(8,128)S(1)}, u32[]{:S(2)}, u32[]{:S(2)}) collective-permute-start(f32[2,192,128]{2,1,0:T(8,128)S(1)} %bitcast.1), channel_id=1, source_target_pairs={{0,4},{4,8},{8,12},{12,16},{16,20},{20,24},{24,28},{28,0},{1,5},{5... | collective-permute-start | bytes 589832 | tf_op jit(solution)/shard_map/ppermute | solution.py:780
  5.0 8.5 %collective-permute-done.5.before = f32[2,192,128]{2,1,0:T(8,128)S(1)} collective-permute-done((f32[2,192,128]{2,1,0:T(8,128)S(1)}, f32[2,192,128]{2,1,0:T(8,128)S(1)}, u32[]{:S(2)}, u32[]{:S(2)}) %collective-permute-start.5) | collective-permute-done | bytes 196640 | tf_op jit(solution)/shard_map/ppermute | solution.py:780
  13.6 1.6 %collective-permute-start.6 = (f32[384,128]{1,0:T(8,128)S(1)}, f32[384,128]{1,0:T(8,128)S(1)}, u32[]{:S(2)}, u32[]{:S(2)}) collective-permute-start(f32[384,128]{1,0:T(8,128)S(1)} %shard_map.104), channel_id=1, source_target_pairs={{0,2},{1,3},{2,0},{3,1},{4,6},{5,7},{6,4},{7,5},{8,10},{9,11},{10,... | collective-permute-start | bytes 589832 | tf_op jit(solution)/shard_map/ppermute | solution.py:776
  16.1 5.3 %collective-permute-done.6.other = f32[384,128]{1,0:T(8,128)S(1)} collective-permute-done((f32[384,128]{1,0:T(8,128)S(1)}, f32[384,128]{1,0:T(8,128)S(1)}, u32[]{:S(2)}, u32[]{:S(2)}) %collective-permute-start.6) | collective-permute-done | bytes 196640 | tf_op jit(solution)/shard_map/ppermute | solution.py:776
  22.0 1.6 %collective-permute-done.2.from_far = f32[136,128]{1,0:T(8,128)S(1)} collective-permute-done((f32[136,128]{1,0:T(8,128)S(1)}, f32[136,128]{1,0:T(8,128)S(1)}, u32[]{:S(2)}, u32[]{:S(2)}) %collective-permute-start.2) | collective-permute-done | bytes 69664 | tf_op jit(solution)/shard_map/ppermute | solution.py:776
  24.1 1.3 %collective-permute-start.4 = (f32[136,256]{1,0:T(8,128)S(1)}, f32[136,256]{1,0:T(8,128)S(1)}, u32[]{:S(2)}, u32[]{:S(2)}) collective-permute-start(f32[136,256]{1,0:T(8,128)S(1)} %shard_map.103.own_far), channel_id=1, source_target_pairs={{0,4},{4,8},{8,12},{12,16},{16,20},{20,24},{24,28},{1,5},{5,9},{9,... | collective-permute-start | bytes 417800 | tf_op jit(solution)/shard_map/ppermute | solution.py:780
  26.4 2.9 %collective-permute-done.4.far = f32[136,256]{1,0:T(8,128)S(1)} collective-permute-done((f32[136,256]{1,0:T(8,128)S(1)}, f32[136,256]{1,0:T(8,128)S(1)}, u32[]{:S(2)}, u32[]{:S(2)}) %collective-permute-start.4) | collective-permute-done | bytes 139296 | tf_op jit(solution)/shard_map/ppermute | solution.py:780
  29.3 1.9 %shard_map.107.own = f32[264,512]{1,0:T(8,128)S(1)} custom-call(f32[128,768]{1,0:T(8,128)S(1)} %shard_map.102.own_near, f32[136,256]{1,0:T(8,128)S(1)} %shard_map.103.own_far, f32[128,768]{1,0:T(8,128)S(1)} %collective-permute-done.3.near, f32[136,256]{1,0:T(8,128)S(1)} %collective-permute-done.4.far, bf16[512,512]{1,0:T(8,128)(2,1)S(1)} %get-tuple-element.60.mh, ...), custom_call_target="tpu_custom_call" | custom-call | tf_op jit(solution)/shard_map/pallas_call | solution.py:762
  31.2 5.4 %collective-permute-start.9 = (f32[264,512]{1,0:T(8,128)S(1)}, f32[264,512]{1,0:T(8,128)S(1)}, u32[]{:S(2)}, u32[]{:S(2)}) collective-permute-start(f32[264,512]{1,0:T(8,128)S(1)} %shard_map.107.own), channel_id=1, source_target_pairs={{0,8},{4,12},{8,16},{12,20},{16,24},{20,28},{1,9},{5,13},{9,17},{1... | collective-permute-start | bytes 1622024 | tf_op jit(solution)/shard_map/ppermute | solution.py:780
  36.6 1.6 %collective-permute-start.10 = (f32[384,128]{1,0:T(8,128)S(1)}, f32[384,128]{1,0:T(8,128)S(1)}, u32[]{:S(2)}, u32[]{:S(2)}) collective-permute-start(f32[384,128]{1,0:T(8,128)S(1)} %get-tuple-element.58.own), channel_id=1, source_target_pairs={{0,8},{4,12},{8,16},{12,20},{16,24},{20,28},{24,0},{28,4},{1,9},{5... | collective-permute-start | bytes 589832 | tf_op jit(solution)/shard_map/ppermute | solution.py:780
  38.2 3.5 %collective-permute-start.12 = (f32[384,128]{1,0:T(8,128)S(1)}, f32[384,128]{1,0:T(8,128)S(1)}, u32[]{:S(2)}, u32[]{:S(2)}) collective-permute-start(f32[384,128]{1,0:T(8,128)S(1)} %get-tuple-element.59.before), channel_id=1, source_target_pairs={{0,8},{4,12},{8,16},{12,20},{16,24},{20,28},{1,9},{5,13},{9,17},{1... | collective-permute-start | bytes 589832 | tf_op jit(solution)/shard_map/ppermute | solution.py:780
  41.7 11.7 %collective-permute-done.10.mine = f32[384,128]{1,0:T(8,128)S(1)} collective-permute-done((f32[384,128]{1,0:T(8,128)S(1)}, f32[384,128]{1,0:T(8,128)S(1)}, u32[]{:S(2)}, u32[]{:S(2)}) %collective-permute-start.10) | collective-permute-done | bytes 196640 | tf_op jit(solution)/shard_map/ppermute | solution.py:780
  53.4 3.2 %collective-permute-done.12.mine = f32[384,128]{1,0:T(8,128)S(1)} collective-permute-done((f32[384,128]{1,0:T(8,128)S(1)}, f32[384,128]{1,0:T(8,128)S(1)}, u32[]{:S(2)}, u32[]{:S(2)}) %collective-permute-start.12) | collective-permute-done | bytes 196640 | tf_op jit(solution)/shard_map/ppermute | solution.py:780
  56.7 1.4 %shard_map.108 = (bf16[512,512]{1,0:T(8,128)(2,1)S(1)}, bf16[512,512]{1,0:T(8,128)(2,1)S(1)}, bf16[512,512]{1,0:T(8,128)(2,1)S(1)}, bf16[512,512]{1,0:T(8,128)(2,1)S(1)}, f32[512,256]{1,0:T(8,128)S(1)}) custom-call(s32[8,3]{1,0:T(8,128)S(1)} %copy.13.pattern, f32[384,128]{1,0:T(8,128)S(1)} %get-tuple-element.58.own, ...), custom_call_target="tpu_custom_call" | custom-call | tf_op jit(solution)/shard_map/pallas_call | solution.py:762
  60.3 1.2 %shard_map.111 = (bf16[512,512]{1,0:T(8,128)(2,1)S(1)}, bf16[512,512]{1,0:T(8,128)(2,1)S(1)}, bf16[512,512]{1,0:T(8,128)(2,1)S(1)}, bf16[512,512]{1,0:T(8,128)(2,1)S(1)}) custom-call(bf16[512,512]{1,0:T(8,128)(2,1)S(1)} %get-tuple-element.64.a0h, bf16[512,512]{1,0:T(8,128)(2,1)S(1)} %get-tuple-element.65.a0l, bf16[512,512]{1,0:T(8,128)(2,1)S(1)} %get-tuple-element.66.a1h, ...), custom_call_target="tpu_custom_call" | custom-call | tf_op jit(solution)/shard_map/pallas_call | solution.py:762
  61.8 1.3 %shard_map.113 = (f32[520,128]{1,0:T(8,128)S(1)}, bf16[256,512]{1,0:T(8,128)(2,1)S(1)}, bf16[256,512]{1,0:T(8,128)(2,1)S(1)}, bf16[512,512]{1,0:T(8,128)(2,1)S(1)}, bf16[512,512]{1,0:T(8,128)(2,1)S(1)}) custom-call(f32[264,512]{1,0:T(8,128)S(1)} %shard_map.107.own, f32[264,512]{1,0:T(8,128)S(1)} %collective-permute-done.9.earlier, ...), custom_call_target="tpu_custom_call" | custom-call | tf_op jit(solution)/shard_map/pallas_call | solution.py:762
  63.1 1.6 %collective-permute-start.16 = (f32[520,128]{1,0:T(8,128)S(1)}, f32[520,128]{1,0:T(8,128)S(1)}, u32[]{:S(2)}, u32[]{:S(2)}) collective-permute-start(f32[520,128]{1,0:T(8,128)S(1)} %get-tuple-element.90), channel_id=1, source_target_pairs={{0,2},{1,3},{2,0},{3,1},{4,6},{5,7},{6,4},{7,5},{8,10},{9,11},{10,... | collective-permute-start | bytes 798728 | tf_op jit(solution)/shard_map/ppermute | solution.py:776
  67.2 1.3 %collective-permute-start.19 = (f32[264,128]{1,0:T(8,128)S(1)}, f32[264,128]{1,0:T(8,128)S(1)}, u32[]{:S(2)}, u32[]{:S(2)}) collective-permute-start(f32[264,128]{1,0:T(8,128)S(1)} %get-tuple-element.96), channel_id=1, source_target_pairs={{0,3},{1,2},{2,1},{3,0},{4,7},{5,6},{6,5},{7,4},{8,11},{9,10},{10,... | collective-permute-start | bytes 405512 | tf_op jit(solution)/shard_map/ppermute | solution.py:776
  68.5 3.6 %collective-permute-done.16.from_chip = f32[520,128]{1,0:T(8,128)S(1)} collective-permute-done((f32[520,128]{1,0:T(8,128)S(1)}, f32[520,128]{1,0:T(8,128)S(1)}, u32[]{:S(2)}, u32[]{:S(2)}) %collective-permute-start.16) | collective-permute-done | bytes 266272 | tf_op jit(solution)/shard_map/ppermute | solution.py:776
  73.0 1.5 %collective-permute-start.17 = (f32[8,128]{1,0:T(8,128)S(1)}, f32[8,128]{1,0:T(8,128)S(1)}, u32[]{:S(2)}, u32[]{:S(2)}) collective-permute-start(f32[8,128]{1,0:T(8,128)S(1)} %get-tuple-element.85.short), channel_id=1, source_target_pairs={{0,2},{1,3},{2,0},{3,1},{4,6},{5,7},{6,4},{7,5},{8,10},{9,11},{10,... | collective-permute-start | bytes 12296 | tf_op jit(solution)/shard_map/ppermute | solution.py:776
  74.5 3.2 %collective-permute-done.15.dyn_recv = f32[128,512]{1,0:T(8,128)S(1)} collective-permute-done((f32[128,512]{1,0:T(8,128)S(1)}, f32[128,512]{1,0:T(8,128)S(1)}, u32[]{:S(2)}, u32[]{:S(2)}) %collective-permute-start.15) | collective-permute-done | bytes 262176 | tf_op jit(solution)/shard_map/ppermute | solution.py:776
  77.7 1.2 %shard_map.117 = (f32[2,128,512]{2,1,0:T(8,128)}, f32[2,128,512]{2,1,0:T(8,128)}, f32[2,128,512]{2,1,0:T(8,128)}) custom-call(f32[512,128]{1,0:T(8,128)S(1)} %get-tuple-element.86.keep, f32[520,128]{1,0:T(8,128)S(1)} %collective-permute-done.14.from_core, f32[128,512]{1,0:T(8,128)S(1)} %get-tuple-element.88.dyn_own, ...), custom_call_target="tpu_custom_call" | custom-call | tf_op jit(solution)/shard_map/pallas_call | solution.py:762
  78.9 1.8 %collective-permute-done.17.chip_short = f32[8,128]{1,0:T(8,128)S(1)} collective-permute-done((f32[8,128]{1,0:T(8,128)S(1)}, f32[8,128]{1,0:T(8,128)S(1)}, u32[]{:S(2)}, u32[]{:S(2)}) %collective-permute-start.17) | collective-permute-done | bytes 4128 | tf_op jit(solution)/shard_map/ppermute | solution.py:776
  (39 shorter events, 10.4 us)
Async XLA Ops:
  0.6 1.9 %copy-start = (f32[2,128,192]{1,2,0:T(8,128)S(1)}, f32[2,128,192]{1,2,0:T(8,128)}, u32[]{:S(2)}) copy-start(f32[2,128,192]{1,2,0:T(8,128)} %param.6) | copy-start | bytes 589828
  1.9 13.3 %collective-permute-start = (f32[136,384]{1,0:T(8,128)S(1)}, f32[136,384]{1,0:T(8,128)S(1)}, u32[]{:S(2)}, u32[]{:S(2)}) collective-permute-start(f32[136,384]{1,0:T(8,128)S(1)} %get-tuple-element.54), channel_id=1, source_target_pairs={{0,1},{1,0},{2,3},{3,2},{4,5},{5,4},{6,7},{7,6},{8,9},{9,8},{10,11... | collective-permute-start | bytes 626696 | tf_op jit(solution)/shard_map/ppermute | solution.py:776
  2.5 11.1 %collective-permute-start.5 = (f32[2,192,128]{2,1,0:T(8,128)S(1)}, f32[2,192,128]{2,1,0:T(8,128)S(1)}, u32[]{:S(2)}, u32[]{:S(2)}) collective-permute-start(f32[2,192,128]{2,1,0:T(8,128)S(1)} %bitcast.1), channel_id=1, source_target_pairs={{0,4},{4,8},{8,12},{12,16},{16,20},{20,24},{24,28},{28,0},{1,5},{5... | collective-permute-start | bytes 589832 | tf_op jit(solution)/shard_map/ppermute | solution.py:780
  13.6 7.8 %collective-permute-start.6 = (f32[384,128]{1,0:T(8,128)S(1)}, f32[384,128]{1,0:T(8,128)S(1)}, u32[]{:S(2)}, u32[]{:S(2)}) collective-permute-start(f32[384,128]{1,0:T(8,128)S(1)} %shard_map.104), channel_id=1, source_target_pairs={{0,2},{1,3},{2,0},{3,1},{4,6},{5,7},{6,4},{7,5},{8,10},{9,11},{10,... | collective-permute-start | bytes 589832 | tf_op jit(solution)/shard_map/ppermute | solution.py:776
  15.2 14.0 %collective-permute-start.3 = (f32[128,768]{1,0:T(8,128)S(1)}, f32[128,768]{1,0:T(8,128)S(1)}, u32[]{:S(2)}, u32[]{:S(2)}) collective-permute-start(f32[128,768]{1,0:T(8,128)S(1)} %shard_map.102.own_near), channel_id=1, source_target_pairs={{0,4},{4,8},{8,12},{12,16},{16,20},{20,24},{24,28},{28,0},{1,5},{5... | collective-permute-start | bytes 1179656 | tf_op jit(solution)/shard_map/ppermute | solution.py:780
  15.3 8.8 %collective-permute-start.1 = (f32[136,256]{1,0:T(8,128)S(1)}, f32[136,256]{1,0:T(8,128)S(1)}, u32[]{:S(2)}, u32[]{:S(2)}) collective-permute-start(f32[136,256]{1,0:T(8,128)S(1)} %get-tuple-element.56), channel_id=1, source_target_pairs={{0,2},{1,3},{2,0},{3,1},{4,6},{5,7},{6,4},{7,5},{8,10},{9,11},{10,... | collective-permute-start | bytes 417800 | tf_op jit(solution)/shard_map/ppermute | solution.py:776
  15.9 7.8 %collective-permute-start.2 = (f32[136,128]{1,0:T(8,128)S(1)}, f32[136,128]{1,0:T(8,128)S(1)}, u32[]{:S(2)}, u32[]{:S(2)}) collective-permute-start(f32[136,128]{1,0:T(8,128)S(1)} %get-tuple-element.57), channel_id=1, source_target_pairs={{0,3},{1,2},{2,1},{3,0},{4,7},{5,6},{6,5},{7,4},{8,11},{9,10},{10,... | collective-permute-start | bytes 208904 | tf_op jit(solution)/shard_map/ppermute | solution.py:776
  21.5 4.0 %collective-permute-start.7 = (f32[384,128]{1,0:T(8,128)S(1)}, f32[384,128]{1,0:T(8,128)S(1)}, u32[]{:S(2)}, u32[]{:S(2)}) collective-permute-start(f32[384,128]{1,0:T(8,128)S(1)} %get-tuple-element.58.own), channel_id=1, source_target_pairs={{0,1},{1,0},{2,3},{3,2},{4,5},{5,4},{6,7},{7,6},{8,9},{9,8},{10,11... | collective-permute-start | bytes 589832 | tf_op jit(solution)/shard_map/ppermute | solution.py:776
  21.5 4.0 %collective-permute-start.8 = (f32[384,128]{1,0:T(8,128)S(1)}, f32[384,128]{1,0:T(8,128)S(1)}, u32[]{:S(2)}, u32[]{:S(2)}) collective-permute-start(f32[384,128]{1,0:T(8,128)S(1)} %get-tuple-element.59.before), channel_id=1, source_target_pairs={{0,1},{1,0},{2,3},{3,2},{4,5},{5,4},{6,7},{7,6},{8,9},{9,8},{10,11... | collective-permute-start | bytes 589832 | tf_op jit(solution)/shard_map/ppermute | solution.py:776
  24.1 1.3 %copy-start.1 = (s32[8,3]{0,1:T(4,128)S(1)}, s32[8,3]{0,1:T(4,128)}, u32[]{:S(2)}) copy-start(s32[8,3]{0,1:T(4,128)} %param.7) | copy-start | bytes 292
  24.1 5.2 %collective-permute-start.4 = (f32[136,256]{1,0:T(8,128)S(1)}, f32[136,256]{1,0:T(8,128)S(1)}, u32[]{:S(2)}, u32[]{:S(2)}) collective-permute-start(f32[136,256]{1,0:T(8,128)S(1)} %shard_map.103.own_far), channel_id=1, source_target_pairs={{0,4},{4,8},{8,12},{12,16},{16,20},{20,24},{24,28},{1,5},{5,9},{9,... | collective-permute-start | bytes 417800 | tf_op jit(solution)/shard_map/ppermute | solution.py:780
  31.2 30.6 %collective-permute-start.9 = (f32[264,512]{1,0:T(8,128)S(1)}, f32[264,512]{1,0:T(8,128)S(1)}, u32[]{:S(2)}, u32[]{:S(2)}) collective-permute-start(f32[264,512]{1,0:T(8,128)S(1)} %shard_map.107.own), channel_id=1, source_target_pairs={{0,8},{4,12},{8,16},{12,20},{16,24},{20,28},{1,9},{5,13},{9,17},{1... | collective-permute-start | bytes 1622024 | tf_op jit(solution)/shard_map/ppermute | solution.py:780
  36.6 16.8 %collective-permute-start.10 = (f32[384,128]{1,0:T(8,128)S(1)}, f32[384,128]{1,0:T(8,128)S(1)}, u32[]{:S(2)}, u32[]{:S(2)}) collective-permute-start(f32[384,128]{1,0:T(8,128)S(1)} %get-tuple-element.58.own), channel_id=1, source_target_pairs={{0,8},{4,12},{8,16},{12,20},{16,24},{20,28},{24,0},{28,4},{1,9},{5... | collective-permute-start | bytes 589832 | tf_op jit(solution)/shard_map/ppermute | solution.py:780
  38.2 18.5 %collective-permute-start.12 = (f32[384,128]{1,0:T(8,128)S(1)}, f32[384,128]{1,0:T(8,128)S(1)}, u32[]{:S(2)}, u32[]{:S(2)}) collective-permute-start(f32[384,128]{1,0:T(8,128)S(1)} %get-tuple-element.59.before), channel_id=1, source_target_pairs={{0,8},{4,12},{8,16},{12,20},{16,24},{20,28},{1,9},{5,13},{9,17},{1... | collective-permute-start | bytes 589832 | tf_op jit(solution)/shard_map/ppermute | solution.py:780
  53.4 4.7 %collective-permute-start.11 = (f32[384,128]{1,0:T(8,128)S(1)}, f32[384,128]{1,0:T(8,128)S(1)}, u32[]{:S(2)}, u32[]{:S(2)}) collective-permute-start(f32[384,128]{1,0:T(8,128)S(1)} %collective-permute-done.10.mine), channel_id=1, source_target_pairs={{0,1},{1,0},{2,3},{3,2},{4,5},{5,4},{6,7},{7,6},{8,9},{9,8},{10,11... | collective-permute-start | bytes 589832 | tf_op jit(solution)/shard_map/ppermute | solution.py:776
  56.7 2.5 %collective-permute-start.13 = (f32[384,128]{1,0:T(8,128)S(1)}, f32[384,128]{1,0:T(8,128)S(1)}, u32[]{:S(2)}, u32[]{:S(2)}) collective-permute-start(f32[384,128]{1,0:T(8,128)S(1)} %collective-permute-done.12.mine), channel_id=1, source_target_pairs={{0,1},{1,0},{2,3},{3,2},{4,5},{5,4},{6,7},{7,6},{8,9},{9,8},{10,11... | collective-permute-start | bytes 589832 | tf_op jit(solution)/shard_map/ppermute | solution.py:776
  63.1 9.0 %collective-permute-start.16 = (f32[520,128]{1,0:T(8,128)S(1)}, f32[520,128]{1,0:T(8,128)S(1)}, u32[]{:S(2)}, u32[]{:S(2)}) collective-permute-start(f32[520,128]{1,0:T(8,128)S(1)} %get-tuple-element.90), channel_id=1, source_target_pairs={{0,2},{1,3},{2,0},{3,1},{4,6},{5,7},{6,4},{7,5},{8,10},{9,11},{10,... | collective-permute-start | bytes 798728 | tf_op jit(solution)/shard_map/ppermute | solution.py:776
  66.6 11.1 %collective-permute-start.14 = (f32[520,128]{1,0:T(8,128)S(1)}, f32[520,128]{1,0:T(8,128)S(1)}, u32[]{:S(2)}, u32[]{:S(2)}) collective-permute-start(f32[520,128]{1,0:T(8,128)S(1)} %get-tuple-element.87), channel_id=1, source_target_pairs={{0,1},{1,0},{2,3},{3,2},{4,5},{5,4},{6,7},{7,6},{8,9},{9,8},{10,11... | collective-permute-start | bytes 798728 | tf_op jit(solution)/shard_map/ppermute | solution.py:776
  66.7 11.0 %collective-permute-start.15 = (f32[128,512]{1,0:T(8,128)S(1)}, f32[128,512]{1,0:T(8,128)S(1)}, u32[]{:S(2)}, u32[]{:S(2)}) collective-permute-start(f32[128,512]{1,0:T(8,128)S(1)} %get-tuple-element.89), channel_id=1, source_target_pairs={{0,2},{1,3},{2,0},{3,1},{4,6},{5,7},{6,4},{7,5},{8,10},{9,11},{10,... | collective-permute-start | bytes 786440 | tf_op jit(solution)/shard_map/ppermute | solution.py:776
  67.2 13.7 %collective-permute-start.19 = (f32[264,128]{1,0:T(8,128)S(1)}, f32[264,128]{1,0:T(8,128)S(1)}, u32[]{:S(2)}, u32[]{:S(2)}) collective-permute-start(f32[264,128]{1,0:T(8,128)S(1)} %get-tuple-element.96), channel_id=1, source_target_pairs={{0,3},{1,2},{2,1},{3,0},{4,7},{5,6},{6,5},{7,4},{8,11},{9,10},{10,... | collective-permute-start | bytes 405512 | tf_op jit(solution)/shard_map/ppermute | solution.py:776
  72.2 8.8 %collective-permute-start.18 = (f32[256,128]{1,0:T(8,128)S(1)}, f32[256,128]{1,0:T(8,128)S(1)}, u32[]{:S(2)}, u32[]{:S(2)}) collective-permute-start(f32[256,128]{1,0:T(8,128)S(1)} %get-tuple-element.95), channel_id=1, source_target_pairs={{0,1},{1,0},{2,3},{3,2},{4,5},{5,4},{6,7},{7,6},{8,9},{9,8},{10,11... | collective-permute-start | bytes 393224 | tf_op jit(solution)/shard_map/ppermute | solution.py:776
  73.0 7.7 %collective-permute-start.17 = (f32[8,128]{1,0:T(8,128)S(1)}, f32[8,128]{1,0:T(8,128)S(1)}, u32[]{:S(2)}, u32[]{:S(2)}) collective-permute-start(f32[8,128]{1,0:T(8,128)S(1)} %get-tuple-element.85.short), channel_id=1, source_target_pairs={{0,2},{1,3},{2,0},{3,1},{4,6},{5,7},{6,4},{7,5},{8,10},{9,11},{10,... | collective-permute-start | bytes 12296 | tf_op jit(solution)/shard_map/ppermute | solution.py:776

commit v12 on v10

--- a/solution.py
+++ b/solution.py
@@ -415,6 +415,7 @@
     extra = slice(n, n + 16)
     first = c == 0
     came = jnp.where(has(1) == 1, near[...], 0.0)
+    far = jnp.where(has(1) == 1, far[...], 0.0)
     xn = jnp.where(first, came, own_near[...])
     xf = jnp.where(first, far[...], own_far[...])
     x = jnp.concatenate(
@@ -812,7 +813,7 @@
     (own_far,) = kernel(
         pack_far_kernel, vmem(vecs, from_core, from_chip, from_far), vmem(shape(r + 8, 2 * r))
     )
-    far = later(own_far, 1)
+    far = later(own_far, 1, cyclic=True)
     (picked,) = kernel(pick_kernel, vmem(turned, before), vmem(shape(6 * bs, r)))
     other = swap(picked, 2)
     own_half, before_half = kernel(
@@ -820,7 +821,7 @@
     )
     pairs = (own_half, swap(own_half, 1), before_half, swap(before_half, 1))
     third = later(own_half, 2, cyclic=True)
-    fourth = later(before_half, 2, cyclic=True)
+    fourth = later(before_half, 2)
     m1 = kernel(
         functools.partial(prepare_kernel, bs),
         vmem(pattern, *pairs),

time: 82.3 us -> 82.5 us (level)
  starting transfers between devices: 21.2 us -> 15.6 us
  waiting for transfers between devices: 45.7 us -> 50.8 us
    ppermute x6, starting transfers between devices: 12.5 us -> 7.28 us  [later(): lax.ppermute(value, 'tm', [(i, (i + distance) % tms) for i in range(count)])]
    ppermute x6, waiting for transfers between devices: 28.3 us -> 33.1 us  [later(): lax.ppermute(value, 'tm', [(i, (i + distance) % tms) for i in range(count)])]
where the time goes in v12:
time: 82.5 us; the launch traced here: 82.3 us
  waiting for transfers between devices  50.8 us (62%)
  starting transfers between devices  15.6 us (19%)
  Pallas kernels  14.3 us (17%)
  between operations  0.84 us (1%)
    ppermute x6, waiting for transfers between devices, later(): lax.ppermute(value, 'tm', [(i, (i + distance) % tms) for i in range(count)])  33.1 us
    ppermute x14, waiting for transfers between devices, swap(): return lax.ppermute(value, 'col', [(i, i ^ bit) for i in range(cols)])  17.7 us
    pallas_call x18, Pallas kernels, kernel(): call(*(pltpu.with_memory_space_constraint(x, kept[where]) if where in kep...  14.3 us
    ppermute x14, starting transfers between devices, swap(): return lax.ppermute(value, 'col', [(i, i ^ bit) for i in range(cols)])  8.35 us
    ppermute x6, starting transfers between devices, later(): lax.ppermute(value, 'tm', [(i, (i + distance) % tms) for i in range(count)])  7.28 us
  transfers between devices with their start and end apart: 20, of which 10 were waited for; matrix products, arithmetic and copies ran while one was open for 0% of the time, Pallas kernels for 11%

profile of v12, /device:TPU:0, one launch (start us, length us, event | category | flops | bytes accessed | tf_op | source)
XLA Modules:
  0.0 82.3 jit_solution(2490376354248142740)
XLA Ops:
  0.6 1.3 %shard_map.101 = (f32[136,384]{1,0:T(8,128)S(1)}, f32[136,256]{1,0:T(8,128)S(1)}, f32[136,128]{1,0:T(8,128)S(1)}, f32[128,512]{1,0:T(8,128)S(1)}, f32[8,128]{1,0:T(8,128)S(1)}) custom-call(f32[2,128,512]{2,1,0:T(8,128)} %cov.1, f32[2,128,512]{2,1,0:T(8,128)} %cost.1, f32[2,128]{1,0:T(2,128)} %drift.1, f32[2,128]{1,0:T(2,128)} %eta.1), custom_call_target="tpu_custom_call" | custom-call | tf_op jit(solution)/shard_map/pallas_call | solution.py:762
  2.5 2.5 %collective-permute-start.5 = (f32[2,192,128]{2,1,0:T(8,128)S(1)}, f32[2,192,128]{2,1,0:T(8,128)S(1)}, u32[]{:S(2)}, u32[]{:S(2)}) collective-permute-start(f32[2,192,128]{2,1,0:T(8,128)S(1)} %bitcast.1), channel_id=1, source_target_pairs={{0,4},{4,8},{8,12},{12,16},{16,20},{20,24},{24,28},{28,0},{1,5},{5... | collective-permute-start | bytes 589832 | tf_op jit(solution)/shard_map/ppermute | solution.py:780
  5.0 8.5 %collective-permute-done.5.before = f32[2,192,128]{2,1,0:T(8,128)S(1)} collective-permute-done((f32[2,192,128]{2,1,0:T(8,128)S(1)}, f32[2,192,128]{2,1,0:T(8,128)S(1)}, u32[]{:S(2)}, u32[]{:S(2)}) %collective-permute-start.5) | collective-permute-done | bytes 196640 | tf_op jit(solution)/shard_map/ppermute | solution.py:780
  13.6 1.6 %collective-permute-start.6 = (f32[384,128]{1,0:T(8,128)S(1)}, f32[384,128]{1,0:T(8,128)S(1)}, u32[]{:S(2)}, u32[]{:S(2)}) collective-permute-start(f32[384,128]{1,0:T(8,128)S(1)} %shard_map.104), channel_id=1, source_target_pairs={{0,2},{1,3},{2,0},{3,1},{4,6},{5,7},{6,4},{7,5},{8,10},{9,11},{10,... | collective-permute-start | bytes 589832 | tf_op jit(solution)/shard_map/ppermute | solution.py:776
  16.1 5.3 %collective-permute-done.6.other = f32[384,128]{1,0:T(8,128)S(1)} collective-permute-done((f32[384,128]{1,0:T(8,128)S(1)}, f32[384,128]{1,0:T(8,128)S(1)}, u32[]{:S(2)}, u32[]{:S(2)}) %collective-permute-start.6) | collective-permute-done | bytes 196640 | tf_op jit(solution)/shard_map/ppermute | solution.py:776
  22.0 1.6 %collective-permute-done.2.from_far = f32[136,128]{1,0:T(8,128)S(1)} collective-permute-done((f32[136,128]{1,0:T(8,128)S(1)}, f32[136,128]{1,0:T(8,128)S(1)}, u32[]{:S(2)}, u32[]{:S(2)}) %collective-permute-start.2) | collective-permute-done | bytes 69664 | tf_op jit(solution)/shard_map/ppermute | solution.py:776
  25.7 7.6 %collective-permute-done.4.far = f32[136,256]{1,0:T(8,128)S(1)} collective-permute-done((f32[136,256]{1,0:T(8,128)S(1)}, f32[136,256]{1,0:T(8,128)S(1)}, u32[]{:S(2)}, u32[]{:S(2)}) %collective-permute-start.4) | collective-permute-done | bytes 139296 | tf_op jit(solution)/shard_map/ppermute | solution.py:780
  33.3 1.9 %shard_map.107.own = f32[264,512]{1,0:T(8,128)S(1)} custom-call(f32[128,768]{1,0:T(8,128)S(1)} %shard_map.102.own_near, f32[136,256]{1,0:T(8,128)S(1)} %shard_map.103.own_far, f32[128,768]{1,0:T(8,128)S(1)} %collective-permute-done.3.near, f32[136,256]{1,0:T(8,128)S(1)} %collective-permute-done.4.far, bf16[512,512]{1,0:T(8,128)(2,1)S(1)} %get-tuple-element.58.mh, ...), custom_call_target="tpu_custom_call" | custom-call | tf_op jit(solution)/shard_map/pallas_call | solution.py:762
  35.2 1.3 %collective-permute-start.9 = (f32[264,512]{1,0:T(8,128)S(1)}, f32[264,512]{1,0:T(8,128)S(1)}, u32[]{:S(2)}, u32[]{:S(2)}) collective-permute-start(f32[264,512]{1,0:T(8,128)S(1)} %shard_map.107.own), channel_id=1, source_target_pairs={{0,8},{4,12},{8,16},{12,20},{16,24},{20,28},{1,9},{5,13},{9,17},{1... | collective-permute-start | bytes 1622024 | tf_op jit(solution)/shard_map/ppermute | solution.py:780
  36.6 3.3 %collective-permute-start.12 = (f32[384,128]{1,0:T(8,128)S(1)}, f32[384,128]{1,0:T(8,128)S(1)}, u32[]{:S(2)}, u32[]{:S(2)}) collective-permute-start(f32[384,128]{1,0:T(8,128)S(1)} %get-tuple-element.57.before), channel_id=1, source_target_pairs={{0,8},{4,12},{8,16},{12,20},{16,24},{20,28},{1,9},{5,13},{9,17},{1... | collective-permute-start | bytes 589832 | tf_op jit(solution)/shard_map/ppermute | solution.py:780
  39.8 13.5 %collective-permute-done.10.mine = f32[384,128]{1,0:T(8,128)S(1)} collective-permute-done((f32[384,128]{1,0:T(8,128)S(1)}, f32[384,128]{1,0:T(8,128)S(1)}, u32[]{:S(2)}, u32[]{:S(2)}) %collective-permute-start.10) | collective-permute-done | bytes 196640 | tf_op jit(solution)/shard_map/ppermute | solution.py:780
  53.3 3.5 %collective-permute-done.12.mine = f32[384,128]{1,0:T(8,128)S(1)} collective-permute-done((f32[384,128]{1,0:T(8,128)S(1)}, f32[384,128]{1,0:T(8,128)S(1)}, u32[]{:S(2)}, u32[]{:S(2)}) %collective-permute-start.12) | collective-permute-done | bytes 196640 | tf_op jit(solution)/shard_map/ppermute | solution.py:780
  56.9 1.4 %shard_map.108 = (bf16[512,512]{1,0:T(8,128)(2,1)S(1)}, bf16[512,512]{1,0:T(8,128)(2,1)S(1)}, bf16[512,512]{1,0:T(8,128)(2,1)S(1)}, bf16[512,512]{1,0:T(8,128)(2,1)S(1)}, f32[512,256]{1,0:T(8,128)S(1)}) custom-call(s32[8,3]{1,0:T(8,128)S(1)} %copy.13.pattern, f32[384,128]{1,0:T(8,128)S(1)} %get-tuple-element.56.own, ...), custom_call_target="tpu_custom_call" | custom-call | tf_op jit(solution)/shard_map/pallas_call | solution.py:762
  58.3 1.1 %shard_map.109 = (f32[512,256]{1,0:T(8,128)S(1)}, f32[512,512]{1,0:T(8,128)S(1)}, bf16[512,512]{1,0:T(8,128)(2,1)S(1)}, bf16[512,512]{1,0:T(8,128)(2,1)S(1)}) custom-call(s32[8,3]{1,0:T(8,128)S(1)} %copy.13.pattern, f32[384,128]{1,0:T(8,128)S(1)} %collective-permute-done.10.mine, f32[384,128]{1,0:T(8,128)S(1)} %collective-permute-done.11.theirs, ...), custom_call_target="tpu_custom_call" | custom-call | tf_op jit(solution)/shard_map/pallas_call | solution.py:762
  59.4 1.1 %shard_map.110 = (f32[128,512]{1,0:T(8,128)S(1)}, f32[128,512]{1,0:T(8,128)S(1)}, bf16[512,512]{1,0:T(8,128)(2,1)S(1)}, bf16[512,512]{1,0:T(8,128)(2,1)S(1)}) custom-call(s32[8,3]{1,0:T(8,128)S(1)} %copy.13.pattern, f32[384,128]{1,0:T(8,128)S(1)} %collective-permute-done.12.mine, f32[384,128]{1,0:T(8,128)S(1)} %collective-permute-done.13.theirs, ...), custom_call_target="tpu_custom_call" | custom-call | tf_op jit(solution)/shard_map/pallas_call | solution.py:762
  60.5 1.2 %shard_map.111 = (bf16[512,512]{1,0:T(8,128)(2,1)S(1)}, bf16[512,512]{1,0:T(8,128)(2,1)S(1)}, bf16[512,512]{1,0:T(8,128)(2,1)S(1)}, bf16[512,512]{1,0:T(8,128)(2,1)S(1)}) custom-call(bf16[512,512]{1,0:T(8,128)(2,1)S(1)} %get-tuple-element.62.a0h, bf16[512,512]{1,0:T(8,128)(2,1)S(1)} %get-tuple-element.63.a0l, bf16[512,512]{1,0:T(8,128)(2,1)S(1)} %get-tuple-element.64.a1h, ...), custom_call_target="tpu_custom_call" | custom-call | tf_op jit(solution)/shard_map/pallas_call | solution.py:762
  62.0 1.7 %shard_map.113 = (f32[520,128]{1,0:T(8,128)S(1)}, bf16[512,512]{1,0:T(8,128)(2,1)S(1)}, bf16[512,512]{1,0:T(8,128)(2,1)S(1)}) custom-call(f32[264,512]{1,0:T(8,128)S(1)} %shard_map.107.own, f32[264,512]{1,0:T(8,128)S(1)} %collective-permute-done.9.earlier, bf16[512,512]{1,0:T(8,128)(2,1)S(1)} %get-tuple-element.74.mh, ...), custom_call_target="tpu_custom_call" | custom-call | tf_op jit(solution)/shard_map/pallas_call | solution.py:762
  63.6 1.4 %collective-permute-start.16 = (f32[520,128]{1,0:T(8,128)S(1)}, f32[520,128]{1,0:T(8,128)S(1)}, u32[]{:S(2)}, u32[]{:S(2)}) collective-permute-start(f32[520,128]{1,0:T(8,128)S(1)} %get-tuple-element.86), channel_id=1, source_target_pairs={{0,2},{1,3},{2,0},{3,1},{4,6},{5,7},{6,4},{7,5},{8,10},{9,11},{10,... | collective-permute-start | bytes 798728 | tf_op jit(solution)/shard_map/ppermute | solution.py:776
  67.4 1.0 %collective-permute-start.19 = (f32[264,128]{1,0:T(8,128)S(1)}, f32[264,128]{1,0:T(8,128)S(1)}, u32[]{:S(2)}, u32[]{:S(2)}) collective-permute-start(f32[264,128]{1,0:T(8,128)S(1)} %get-tuple-element.92), channel_id=1, source_target_pairs={{0,3},{1,2},{2,1},{3,0},{4,7},{5,6},{6,5},{7,4},{8,11},{9,10},{10,... | collective-permute-start | bytes 405512 | tf_op jit(solution)/shard_map/ppermute | solution.py:776
  68.4 4.6 %collective-permute-done.16.from_chip = f32[520,128]{1,0:T(8,128)S(1)} collective-permute-done((f32[520,128]{1,0:T(8,128)S(1)}, f32[520,128]{1,0:T(8,128)S(1)}, u32[]{:S(2)}, u32[]{:S(2)}) %collective-permute-start.16) | collective-permute-done | bytes 266272 | tf_op jit(solution)/shard_map/ppermute | solution.py:776
  73.2 1.4 %collective-permute-start.17 = (f32[8,128]{1,0:T(8,128)S(1)}, f32[8,128]{1,0:T(8,128)S(1)}, u32[]{:S(2)}, u32[]{:S(2)}) collective-permute-start(f32[8,128]{1,0:T(8,128)S(1)} %get-tuple-element.81.short), channel_id=1, source_target_pairs={{0,2},{1,3},{2,0},{3,1},{4,6},{5,7},{6,4},{7,5},{8,10},{9,11},{10,... | collective-permute-start | bytes 12296 | tf_op jit(solution)/shard_map/ppermute | solution.py:776
  74.6 4.0 %collective-permute-done.15.dyn_recv = f32[128,512]{1,0:T(8,128)S(1)} collective-permute-done((f32[128,512]{1,0:T(8,128)S(1)}, f32[128,512]{1,0:T(8,128)S(1)}, u32[]{:S(2)}, u32[]{:S(2)}) %collective-permute-start.15) | collective-permute-done | bytes 262176 | tf_op jit(solution)/shard_map/ppermute | solution.py:776
  78.6 1.2 %shard_map.117 = (f32[2,128,512]{2,1,0:T(8,128)}, f32[2,128,512]{2,1,0:T(8,128)}, f32[2,128,512]{2,1,0:T(8,128)}) custom-call(f32[512,128]{1,0:T(8,128)S(1)} %get-tuple-element.82.keep, f32[520,128]{1,0:T(8,128)S(1)} %collective-permute-done.14.from_core, f32[128,512]{1,0:T(8,128)S(1)} %get-tuple-element.84.dyn_own, ...), custom_call_target="tpu_custom_call" | custom-call | tf_op jit(solution)/shard_map/pallas_call | solution.py:762
  79.8 1.7 %collective-permute-done.17.chip_short = f32[8,128]{1,0:T(8,128)S(1)} collective-permute-done((f32[8,128]{1,0:T(8,128)S(1)}, f32[8,128]{1,0:T(8,128)S(1)}, u32[]{:S(2)}, u32[]{:S(2)}) %collective-permute-start.17) | collective-permute-done | bytes 4128 | tf_op jit(solution)/shard_map/ppermute | solution.py:776
  (39 shorter events, 7.7 us)
Async XLA Ops:
  0.6 1.9 %copy-start = (f32[2,128,192]{1,2,0:T(8,128)S(1)}, f32[2,128,192]{1,2,0:T(8,128)}, u32[]{:S(2)}) copy-start(f32[2,128,192]{1,2,0:T(8,128)} %param.6) | copy-start | bytes 589828
  1.9 13.3 %collective-permute-start = (f32[136,384]{1,0:T(8,128)S(1)}, f32[136,384]{1,0:T(8,128)S(1)}, u32[]{:S(2)}, u32[]{:S(2)}) collective-permute-start(f32[136,384]{1,0:T(8,128)S(1)} %get-tuple-element.52), channel_id=1, source_target_pairs={{0,1},{1,0},{2,3},{3,2},{4,5},{5,4},{6,7},{7,6},{8,9},{9,8},{10,11... | collective-permute-start | bytes 626696 | tf_op jit(solution)/shard_map/ppermute | solution.py:776
  2.5 11.1 %collective-permute-start.5 = (f32[2,192,128]{2,1,0:T(8,128)S(1)}, f32[2,192,128]{2,1,0:T(8,128)S(1)}, u32[]{:S(2)}, u32[]{:S(2)}) collective-permute-start(f32[2,192,128]{2,1,0:T(8,128)S(1)} %bitcast.1), channel_id=1, source_target_pairs={{0,4},{4,8},{8,12},{12,16},{16,20},{20,24},{24,28},{28,0},{1,5},{5... | collective-permute-start | bytes 589832 | tf_op jit(solution)/shard_map/ppermute | solution.py:780
  13.6 7.8 %collective-permute-start.6 = (f32[384,128]{1,0:T(8,128)S(1)}, f32[384,128]{1,0:T(8,128)S(1)}, u32[]{:S(2)}, u32[]{:S(2)}) collective-permute-start(f32[384,128]{1,0:T(8,128)S(1)} %shard_map.104), channel_id=1, source_target_pairs={{0,2},{1,3},{2,0},{3,1},{4,6},{5,7},{6,4},{7,5},{8,10},{9,11},{10,... | collective-permute-start | bytes 589832 | tf_op jit(solution)/shard_map/ppermute | solution.py:776
  15.2 18.1 %collective-permute-start.3 = (f32[128,768]{1,0:T(8,128)S(1)}, f32[128,768]{1,0:T(8,128)S(1)}, u32[]{:S(2)}, u32[]{:S(2)}) collective-permute-start(f32[128,768]{1,0:T(8,128)S(1)} %shard_map.102.own_near), channel_id=1, source_target_pairs={{0,4},{4,8},{8,12},{12,16},{16,20},{20,24},{24,28},{28,0},{1,5},{5... | collective-permute-start | bytes 1179656 | tf_op jit(solution)/shard_map/ppermute | solution.py:780
  15.3 8.8 %collective-permute-start.1 = (f32[136,256]{1,0:T(8,128)S(1)}, f32[136,256]{1,0:T(8,128)S(1)}, u32[]{:S(2)}, u32[]{:S(2)}) collective-permute-start(f32[136,256]{1,0:T(8,128)S(1)} %get-tuple-element.54), channel_id=1, source_target_pairs={{0,2},{1,3},{2,0},{3,1},{4,6},{5,7},{6,4},{7,5},{8,10},{9,11},{10,... | collective-permute-start | bytes 417800 | tf_op jit(solution)/shard_map/ppermute | solution.py:776
  15.9 7.8 %collective-permute-start.2 = (f32[136,128]{1,0:T(8,128)S(1)}, f32[136,128]{1,0:T(8,128)S(1)}, u32[]{:S(2)}, u32[]{:S(2)}) collective-permute-start(f32[136,128]{1,0:T(8,128)S(1)} %get-tuple-element.55), channel_id=1, source_target_pairs={{0,3},{1,2},{2,1},{3,0},{4,7},{5,6},{6,5},{7,4},{8,11},{9,10},{10,... | collective-permute-start | bytes 208904 | tf_op jit(solution)/shard_map/ppermute | solution.py:776
  21.5 3.4 %collective-permute-start.7 = (f32[384,128]{1,0:T(8,128)S(1)}, f32[384,128]{1,0:T(8,128)S(1)}, u32[]{:S(2)}, u32[]{:S(2)}) collective-permute-start(f32[384,128]{1,0:T(8,128)S(1)} %get-tuple-element.56.own), channel_id=1, source_target_pairs={{0,1},{1,0},{2,3},{3,2},{4,5},{5,4},{6,7},{7,6},{8,9},{9,8},{10,11... | collective-permute-start | bytes 589832 | tf_op jit(solution)/shard_map/ppermute | solution.py:776
  21.5 3.3 %collective-permute-start.8 = (f32[384,128]{1,0:T(8,128)S(1)}, f32[384,128]{1,0:T(8,128)S(1)}, u32[]{:S(2)}, u32[]{:S(2)}) collective-permute-start(f32[384,128]{1,0:T(8,128)S(1)} %get-tuple-element.57.before), channel_id=1, source_target_pairs={{0,1},{1,0},{2,3},{3,2},{4,5},{5,4},{6,7},{7,6},{8,9},{9,8},{10,11... | collective-permute-start | bytes 589832 | tf_op jit(solution)/shard_map/ppermute | solution.py:776
  24.1 0.7 copy-start.1
  24.1 9.2 %collective-permute-start.4 = (f32[136,256]{1,0:T(8,128)S(1)}, f32[136,256]{1,0:T(8,128)S(1)}, u32[]{:S(2)}, u32[]{:S(2)}) collective-permute-start(f32[136,256]{1,0:T(8,128)S(1)} %shard_map.103.own_far), channel_id=1, source_target_pairs={{0,4},{4,8},{8,12},{12,16},{16,20},{20,24},{24,28},{28,0},{1,5},{5... | collective-permute-start | bytes 417800 | tf_op jit(solution)/shard_map/ppermute | solution.py:780
  35.2 26.8 %collective-permute-start.9 = (f32[264,512]{1,0:T(8,128)S(1)}, f32[264,512]{1,0:T(8,128)S(1)}, u32[]{:S(2)}, u32[]{:S(2)}) collective-permute-start(f32[264,512]{1,0:T(8,128)S(1)} %shard_map.107.own), channel_id=1, source_target_pairs={{0,8},{4,12},{8,16},{12,20},{16,24},{20,28},{1,9},{5,13},{9,17},{1... | collective-permute-start | bytes 1622024 | tf_op jit(solution)/shard_map/ppermute | solution.py:780
  36.5 16.8 %collective-permute-start.10 = (f32[384,128]{1,0:T(8,128)S(1)}, f32[384,128]{1,0:T(8,128)S(1)}, u32[]{:S(2)}, u32[]{:S(2)}) collective-permute-start(f32[384,128]{1,0:T(8,128)S(1)} %get-tuple-element.56.own), channel_id=1, source_target_pairs={{0,8},{4,12},{8,16},{12,20},{16,24},{20,28},{24,0},{28,4},{1,9},{5... | collective-permute-start | bytes 589832 | tf_op jit(solution)/shard_map/ppermute | solution.py:780
  36.6 20.3 %collective-permute-start.12 = (f32[384,128]{1,0:T(8,128)S(1)}, f32[384,128]{1,0:T(8,128)S(1)}, u32[]{:S(2)}, u32[]{:S(2)}) collective-permute-start(f32[384,128]{1,0:T(8,128)S(1)} %get-tuple-element.57.before), channel_id=1, source_target_pairs={{0,8},{4,12},{8,16},{12,20},{16,24},{20,28},{1,9},{5,13},{9,17},{1... | collective-permute-start | bytes 589832 | tf_op jit(solution)/shard_map/ppermute | solution.py:780
  53.3 4.9 %collective-permute-start.11 = (f32[384,128]{1,0:T(8,128)S(1)}, f32[384,128]{1,0:T(8,128)S(1)}, u32[]{:S(2)}, u32[]{:S(2)}) collective-permute-start(f32[384,128]{1,0:T(8,128)S(1)} %collective-permute-done.10.mine), channel_id=1, source_target_pairs={{0,1},{1,0},{2,3},{3,2},{4,5},{5,4},{6,7},{7,6},{8,9},{9,8},{10,11... | collective-permute-start | bytes 589832 | tf_op jit(solution)/shard_map/ppermute | solution.py:776
  56.9 2.5 %collective-permute-start.13 = (f32[384,128]{1,0:T(8,128)S(1)}, f32[384,128]{1,0:T(8,128)S(1)}, u32[]{:S(2)}, u32[]{:S(2)}) collective-permute-start(f32[384,128]{1,0:T(8,128)S(1)} %collective-permute-done.12.mine), channel_id=1, source_target_pairs={{0,1},{1,0},{2,3},{3,2},{4,5},{5,4},{6,7},{7,6},{8,9},{9,8},{10,11... | collective-permute-start | bytes 589832 | tf_op jit(solution)/shard_map/ppermute | solution.py:776
  63.6 9.3 %collective-permute-start.16 = (f32[520,128]{1,0:T(8,128)S(1)}, f32[520,128]{1,0:T(8,128)S(1)}, u32[]{:S(2)}, u32[]{:S(2)}) collective-permute-start(f32[520,128]{1,0:T(8,128)S(1)} %get-tuple-element.86), channel_id=1, source_target_pairs={{0,2},{1,3},{2,0},{3,1},{4,6},{5,7},{6,4},{7,5},{8,10},{9,11},{10,... | collective-permute-start | bytes 798728 | tf_op jit(solution)/shard_map/ppermute | solution.py:776
  66.5 12.1 %collective-permute-start.14 = (f32[520,128]{1,0:T(8,128)S(1)}, f32[520,128]{1,0:T(8,128)S(1)}, u32[]{:S(2)}, u32[]{:S(2)}) collective-permute-start(f32[520,128]{1,0:T(8,128)S(1)} %get-tuple-element.83), channel_id=1, source_target_pairs={{0,1},{1,0},{2,3},{3,2},{4,5},{5,4},{6,7},{7,6},{8,9},{9,8},{10,11... | collective-permute-start | bytes 798728 | tf_op jit(solution)/shard_map/ppermute | solution.py:776
  66.7 11.9 %collective-permute-start.15 = (f32[128,512]{1,0:T(8,128)S(1)}, f32[128,512]{1,0:T(8,128)S(1)}, u32[]{:S(2)}, u32[]{:S(2)}) collective-permute-start(f32[128,512]{1,0:T(8,128)S(1)} %get-tuple-element.85), channel_id=1, source_target_pairs={{0,2},{1,3},{2,0},{3,1},{4,6},{5,7},{6,4},{7,5},{8,10},{9,11},{10,... | collective-permute-start | bytes 786440 | tf_op jit(solution)/shard_map/ppermute | solution.py:776
  67.4 14.1 %collective-permute-start.19 = (f32[264,128]{1,0:T(8,128)S(1)}, f32[264,128]{1,0:T(8,128)S(1)}, u32[]{:S(2)}, u32[]{:S(2)}) collective-permute-start(f32[264,128]{1,0:T(8,128)S(1)} %get-tuple-element.92), channel_id=1, source_target_pairs={{0,3},{1,2},{2,1},{3,0},{4,7},{5,6},{6,5},{7,4},{8,11},{9,10},{10,... | collective-permute-start | bytes 405512 | tf_op jit(solution)/shard_map/ppermute | solution.py:776
  73.1 8.4 %collective-permute-start.18 = (f32[256,128]{1,0:T(8,128)S(1)}, f32[256,128]{1,0:T(8,128)S(1)}, u32[]{:S(2)}, u32[]{:S(2)}) collective-permute-start(f32[256,128]{1,0:T(8,128)S(1)} %get-tuple-element.91), channel_id=1, source_target_pairs={{0,1},{1,0},{2,3},{3,2},{4,5},{5,4},{6,7},{7,6},{8,9},{9,8},{10,11... | collective-permute-start | bytes 393224 | tf_op jit(solution)/shard_map/ppermute | solution.py:776
  73.2 8.3 %collective-permute-start.17 = (f32[8,128]{1,0:T(8,128)S(1)}, f32[8,128]{1,0:T(8,128)S(1)}, u32[]{:S(2)}, u32[]{:S(2)}) collective-permute-start(f32[8,128]{1,0:T(8,128)S(1)} %get-tuple-element.81.short), channel_id=1, source_target_pairs={{0,2},{1,3},{2,0},{3,1},{4,6},{5,7},{6,4},{7,5},{8,10},{9,11},{10,... | collective-permute-start | bytes 12296 | tf_op jit(solution)/shard_map/ppermute | solution.py:776
